TPU v7x, 32 devices: a whole 2x2x4 slice. The times are simulated.
32 devices in a mesh: slab: 2 (over x), dp: 8 (over z, y), mp: 2 (over core).
Axes of the slice: x: 2, y: 2, z: 4, core: 2. Of those that a mesh axis runs over, the one named last changes fastest.
Arguments:
- states: bfloat16 [2, 8, 1024, 768], P('slab', 'dp', 'mp'), may hold values from -6 to 6
- attn_gain: bfloat16 [2, 768], P('slab', 'dp'), may hold values from 0.099609375 to 1.8984375
- w_query: bfloat16 [2, 768, 768], P('slab', 'dp', 'mp'), may hold values from -0.21875 to 0.21875
- w_key: bfloat16 [2, 768, 768], P('slab', 'dp', 'mp'), may hold values from -0.21875 to 0.21875
- w_value: bfloat16 [2, 768, 768], P('slab', 'dp', 'mp'), may hold values from -0.21875 to 0.21875
- w_out: bfloat16 [2, 768, 768], P('slab', 'mp', 'dp'), may hold values from -3.5 to 3.5
- mlp_gain: bfloat16 [2, 768], P('slab', 'dp'), may hold values from 0.099609375 to 1.8984375
- w_gate: bfloat16 [2, 768, 2048], P('slab', 'dp', 'mp'), may hold values from -0.21875 to 0.21875
- w_up: bfloat16 [2, 768, 2048], P('slab', 'dp', 'mp'), may hold values from -0.21875 to 0.21875
- w_down: bfloat16 [2, 2048, 768], P('slab', 'mp', 'dp'), may hold values from -0.125 to 0.125
- final_gain: bfloat16 [2, 768], P('slab', 'dp'), may hold values from 0.099609375 to 1.8984375
- cross_gain: bfloat16 [768], P(('slab', 'dp')), may hold values from 0.099609375 to 1.8984375
- cross_query: bfloat16 [768, 768], P(('slab', 'dp'), 'mp'), may hold values from -0.21875 to 0.21875
- cross_key: bfloat16 [768, 768], P(('slab', 'dp'), 'mp'), may hold values from -0.21875 to 0.21875
- cross_value: bfloat16 [768, 768], P(('slab', 'dp'), 'mp'), may hold values from -0.21875 to 0.21875
- cross_out: bfloat16 [768, 768], P('mp', ('slab', 'dp')), may hold values from -3.5 to 3.5
- embedding: bfloat16 [16384, 768], P(('slab', 'dp', 'mp')), may hold values from -8 to 8
- source_len: int32 [8], replicated, may hold values from 512 to 1024, as said below
- target_len: int32 [8], replicated, may hold values from 512 to 1024, as said below
- target_ids: int32 [8, 1024], P('dp'), may hold values from 0 to 16383
- pairing: int32 [8], replicated, may hold values from 0 to 7, each once
Outputs:
- seq_loss: float32 [8], P('dp')
- d_states: float32 [2, 8, 1024, 768], P('slab', 'dp', 'mp')
- g_attn_gain: float32 [2, 768], P('slab', 'dp')
- g_w_query: float32 [2, 768, 768], P('slab', 'dp', 'mp')
- g_w_key: float32 [2, 768, 768], P('slab', 'dp', 'mp')
- g_w_value: float32 [2, 768, 768], P('slab', 'dp', 'mp')
- g_w_out: float32 [2, 768, 768], P('slab', 'mp', 'dp')
- g_mlp_gain: float32 [2, 768], P('slab', 'dp')
- g_w_gate: float32 [2, 768, 2048], P('slab', 'dp', 'mp')
- g_w_up: float32 [2, 768, 2048], P('slab', 'dp', 'mp')
- g_w_down: float32 [2, 2048, 768], P('slab', 'mp', 'dp')
- g_final_gain: float32 [2, 768], P('slab', 'dp')
- g_cross_gain: float32 [768], P(('slab', 'dp'))
- g_cross_query: float32 [768, 768], P(('slab', 'dp'), 'mp')
- g_cross_key: float32 [768, 768], P(('slab', 'dp'), 'mp')
- g_cross_value: float32 [768, 768], P(('slab', 'dp'), 'mp')
- g_cross_out: float32 [768, 768], P('mp', ('slab', 'dp'))
- g_embedding: float32 [16384, 768], P(('slab', 'dp', 'mp'))
- token_loss: float32 [8, 1024], P('dp')
Inputs may be any that keep to these rules, and one draw needn't show every extreme that they name: `source_len`: every source length lies between 512 and 1024, and some source sequence has exactly 1024 tokens. `target_len`: every target length lies between 512 and 1024, and some target sequence has exactly 1024 tokens. `pairing`: each source sequence is translated by exactly one target sequence.
All inputs are finite; a program needn't handle non-finite values.
Results may differ from a plain program's by a relative error of at most 0.025.
Values may be sent and summed in bfloat16 or wider, within the bound.
No kernel may reach another device: no remote copies, remote signals or barrier semaphores. Data moves between devices by JAX's collectives and lax.ppermute only.
A program may use at most 384 MiB of HBM per device.

v0:
```python
import jax
import jax.numpy as jnp
from jax import lax
from jax.sharding import PartitionSpec as P

DK = 64


epsilon = 1e-06
masked_out = -1000000000.0


def for_sending(value):

    def short(part):
        return part.astype(jnp.bfloat16) if part.dtype == jnp.float32 else part

    return jax.tree.map(short, value)


def from_behind(value, axis, steps):
    count = lax.axis_size(axis)
    initial, last = (max(0, -steps), min(count, count - steps))
    return lax.ppermute(value, axis, [(source, source + steps) for source in range(initial, last)])


def combined_all(value, axis, join):
    pieces = jax.tree.map(lambda part: lax.all_gather(part, axis), value)
    head = jax.tree.map(lambda part: part[0], pieces)
    tail = jax.tree.map(lambda part: part[1:], pieces)
    so_far, _ = lax.scan(lambda so_far, share: (join(so_far, share), None), head, tail)
    return so_far


def matmul(matrix_a, matrix_b):
    return jnp.dot(matrix_a, matrix_b, preferred_element_type=jnp.float32)


def contract_last(matrix_a, matrix_b):
    return lax.dot_general(
        matrix_a, matrix_b, (((1,), (1,)), ((), ())), preferred_element_type=jnp.float32
    )


def contract_first(matrix_a, matrix_b):
    return lax.dot_general(
        matrix_a, matrix_b, (((0,), (0,)), ((), ())), preferred_element_type=jnp.float32
    )


def rms_apply(hidden, scaling):
    return hidden * lax.rsqrt(jnp.mean(hidden * hidden, axis=-1, keepdims=True) + epsilon) * scaling


def norm_back(hidden, scaling, upstream):
    unused, pullback = jax.vjp(rms_apply, hidden, scaling)
    return pullback(upstream)


def on_slab(active, handler, *operands):
    return lax.cond(
        active,
        handler,
        lambda *spare_args: jax.tree.map(jnp.zeros_like, handler(*spare_args)),
        *operands
    )


def row_gather(block):
    return lax.all_gather(block, "mp", axis=0, tiled=True)


def row_sum(block):
    return jax.tree.map(
        lambda part: part.astype(jnp.float32),
        lax.psum_scatter(for_sending(block), "mp", scatter_dimension=0, tiled=True),
    )


def project(inputs, weight):
    product = matmul(inputs, weight).astype(jnp.bfloat16)
    return product.reshape(inputs.shape[0], -1, DK)


def attend(queries, key_rows, value_rows, allowed):
    scores = jnp.einsum(
        "qhd,khd->hqk", queries, key_rows, preferred_element_type=jnp.float32
    ) * DK ** (-0.5)
    scores = jnp.where(allowed[None], scores, masked_out)
    highest = jnp.max(scores, axis=-1, keepdims=True)
    shifted = jnp.exp(scores - highest)
    totals = jnp.sum(shifted, axis=-1, keepdims=True)
    weights = (shifted / totals).astype(jnp.bfloat16)
    context = jnp.einsum("hqk,khd->qhd", weights, value_rows, preferred_element_type=jnp.float32)
    context = context.reshape(queries.shape[0], -1).astype(jnp.bfloat16)
    return (context, highest + jnp.log(totals))


def flatten_heads(heads):
    return heads.reshape(heads.shape[0], -1).astype(jnp.bfloat16)


def attend_back(queries, key_rows, value_rows, allowed, log_total, grad_context):
    scale = DK ** (-0.5)
    scores = (
        jnp.einsum("qhd,khd->hqk", queries, key_rows, preferred_element_type=jnp.float32) * scale
    )
    scores = jnp.where(allowed[None], scores, masked_out)
    weights = jnp.exp(scores - log_total)
    grad_heads = grad_context.reshape(queries.shape)
    grad_weights = jnp.einsum(
        "qhd,khd->hqk", grad_heads, value_rows, preferred_element_type=jnp.float32
    )
    grad_scores = weights * (grad_weights - jnp.sum(grad_weights * weights, axis=-1, keepdims=True))
    grad_scores = grad_scores.astype(jnp.bfloat16)
    grad_query = (
        jnp.einsum("hqk,khd->qhd", grad_scores, key_rows, preferred_element_type=jnp.float32)
        * scale
    )
    grad_key = (
        jnp.einsum("hqk,qhd->khd", grad_scores, queries, preferred_element_type=jnp.float32) * scale
    )
    grad_value = jnp.einsum(
        "hqk,qhd->khd", weights.astype(jnp.bfloat16), grad_heads, preferred_element_type=jnp.float32
    )
    return (flatten_heads(grad_query), flatten_heads(grad_key), flatten_heads(grad_value))


def attention_back(
    query_in, queries, key_rows, value_rows, context, log_total, w_query, w_out, allowed, grad_rows
):
    grad_context = contract_last(grad_rows, w_out).astype(jnp.bfloat16)
    grad_w_out = contract_first(context, grad_rows)
    grad_query, grad_key, grad_value = attend_back(
        queries, key_rows, value_rows, allowed, log_total, grad_context
    )
    grad_w_query = contract_first(query_in, grad_query)
    grad_query_in = contract_last(grad_query, w_query)
    return (grad_query_in, grad_key, grad_value, grad_w_query, grad_w_out)


def key_side_back(memory_in, grad_key, grad_value, w_key, w_value):
    grad_memory = contract_last(grad_key, w_key) + contract_last(grad_value, w_value)
    return (grad_memory, contract_first(memory_in, grad_key), contract_first(memory_in, grad_value))


def gelu_gate(gate_out, up_out):
    return jax.nn.gelu(gate_out, approximate=True) * up_out


def mlp_forward(normed, w_gate, w_up, w_down):
    gate_out = matmul(normed, w_gate)
    up_out = matmul(normed, w_up)
    inner = gelu_gate(gate_out, up_out).astype(jnp.bfloat16)
    return (matmul(inner, w_down), gate_out, up_out, inner)


def mlp_back(normed, gate_out, up_out, inner, w_gate, w_up, w_down, grad_rows):
    grad_inner = contract_last(grad_rows, w_down)
    grad_w_down = contract_first(inner, grad_rows)
    unused, pullback = jax.vjp(gelu_gate, gate_out, up_out)
    grad_gate, grad_up = pullback(grad_inner)
    grad_gate = grad_gate.astype(jnp.bfloat16)
    grad_up = grad_up.astype(jnp.bfloat16)
    grad_normed = contract_last(grad_gate, w_gate) + contract_last(grad_up, w_up)
    return (
        grad_normed,
        contract_first(normed, grad_gate),
        contract_first(normed, grad_up),
        grad_w_down,
    )


def head_forward(final_rows, vocab_table, local_ids, owned):
    logits = contract_last(final_rows, vocab_table) * final_rows.shape[1] ** (-0.5)
    highest = jnp.max(logits, axis=-1)
    totals = jnp.sum(jnp.exp(logits - highest[:, None]), axis=-1)
    picked = jnp.where(owned, jnp.take_along_axis(logits, local_ids[:, None], axis=1)[:, 0], 0.0)
    return (logits, highest, totals, picked)


def head_back(logits, log_total, counted, final_rows, vocab_table, local_ids, owned):
    scale = final_rows.shape[1] ** (-0.5)
    weights = jnp.exp(logits - log_total[:, None])
    columns = jnp.arange(logits.shape[1], dtype=jnp.int32)
    target_hit = (columns[None, :] == local_ids[:, None]) & owned[:, None]
    grad_logits = jnp.where(counted[:, None], weights - target_hit.astype(jnp.float32), 0.0).astype(
        jnp.bfloat16
    )
    grad_final = matmul(grad_logits, vocab_table) * scale
    grad_table = contract_first(grad_logits, final_rows) * scale
    return (grad_final, grad_table)


def merge_softmax(first_part, second_part):
    highest = jnp.maximum(first_part[0], second_part[0])
    totals = first_part[1] * jnp.exp(first_part[0] - highest) + second_part[1] * jnp.exp(
        second_part[0] - highest
    )
    return (highest, totals, first_part[2] + second_part[2])


def deliver(block, pairing):
    crossed = from_behind(block, "slab", 1)
    count = lax.axis_size("dp")
    block_rows = block.shape[0]
    spread = lax.all_to_all(
        crossed.reshape(count, block_rows // count, block.shape[1]),
        "dp",
        split_axis=0,
        concat_axis=0,
        tiled=True,
    )
    routed = lax.all_to_all(spread[pairing], "dp", split_axis=0, concat_axis=0, tiled=True)
    return routed.reshape(block_rows, block.shape[1])


def send_back(block, pairing):
    count = lax.axis_size("dp")
    block_rows = block.shape[0]
    pieces = block.reshape(count, block_rows // count, block.shape[1])
    arrived = lax.all_to_all(pieces, "dp", split_axis=0, concat_axis=0, tiled=True)
    inverse = jnp.zeros((count,), jnp.int32).at[pairing].set(jnp.arange(count, dtype=jnp.int32))
    gathered = lax.all_to_all(arrived[inverse], "dp", split_axis=0, concat_axis=0, tiled=True)
    return from_behind(gathered.reshape(block_rows, block.shape[1]), "slab", -1)


def on_device(
    states,
    attn_gain,
    w_query,
    w_key,
    w_value,
    w_out,
    mlp_gain,
    w_gate,
    w_up,
    w_down,
    final_gain,
    cross_gain,
    cross_query,
    cross_key,
    cross_value,
    cross_out,
    embedding,
    source_len,
    target_len,
    target_ids,
    pairing,
):
    decoding = lax.axis_index("slab") == 1
    encoding = jnp.logical_not(decoding)
    seq_index = lax.axis_index("dp")
    vocab_part = lax.axis_index("mp")
    parts_mp = lax.axis_size("mp")
    layer = (
        lax.all_gather(attn_gain, "dp", axis=1, tiled=True),
        lax.all_gather(w_query, "dp", axis=1, tiled=True),
        lax.all_gather(w_key, "dp", axis=1, tiled=True),
        lax.all_gather(w_value, "dp", axis=1, tiled=True),
        lax.all_gather(w_out, "dp", axis=2, tiled=True),
        lax.all_gather(mlp_gain, "dp", axis=1, tiled=True),
        lax.all_gather(w_gate, "dp", axis=1, tiled=True),
        lax.all_gather(w_up, "dp", axis=1, tiled=True),
        lax.all_gather(w_down, "dp", axis=2, tiled=True),
        lax.all_gather(final_gain, "dp", axis=1, tiled=True),
    )
    gain_attn = layer[0][0].astype(jnp.float32)
    full_query = layer[1][0]
    full_key = layer[2][0]
    full_value = layer[3][0]
    full_out = layer[4][0]
    gain_mlp = layer[5][0].astype(jnp.float32)
    full_gate = layer[6][0]
    full_up = layer[7][0]
    full_down = layer[8][0]
    gain_final = layer[9][0].astype(jnp.float32)
    shared = (
        lax.all_gather(cross_gain, ("slab", "dp"), axis=0, tiled=True),
        lax.all_gather(cross_query, ("slab", "dp"), axis=0, tiled=True),
        lax.all_gather(cross_key, ("slab", "dp"), axis=0, tiled=True),
        lax.all_gather(cross_value, ("slab", "dp"), axis=0, tiled=True),
        lax.all_gather(cross_out, ("slab", "dp"), axis=1, tiled=True),
        lax.all_gather(embedding, ("slab", "dp"), axis=0, tiled=True),
    )
    gain_cross = shared[0].astype(jnp.float32)
    query_cross = shared[1]
    key_cross = shared[2]
    value_cross = shared[3]
    out_cross = shared[4]
    vocab_table = shared[5]
    seq_rows = states.shape[2] * parts_mp
    positions = jnp.arange(seq_rows, dtype=jnp.int32)
    own_length = jnp.where(decoding, target_len[seq_index], source_len[seq_index])
    later_keys = positions[None, :] > positions[:, None]
    self_allowed = (positions[None, :] < own_length) & jnp.logical_not(later_keys & decoding)
    cross_allowed = jnp.broadcast_to(
        positions[None, :] < source_len[pairing[seq_index]], (seq_rows, seq_rows)
    )
    block_rows = embedding.shape[0]
    wanted = target_ids[0]
    owned = wanted // block_rows % parts_mp == vocab_part
    local_ids = wanted // block_rows // parts_mp * block_rows + wanted % block_rows
    counted = decoding & (positions < target_len[seq_index])
    start_rows = states[0, 0].astype(jnp.float32)
    normed_attn = row_gather(rms_apply(start_rows, gain_attn).astype(jnp.bfloat16))
    self_queries = project(normed_attn, full_query)
    self_keys = project(normed_attn, full_key)
    self_values = project(normed_attn, full_value)
    self_context, self_log = attend(self_queries, self_keys, self_values, self_allowed)
    after_self = start_rows + row_sum(matmul(self_context, full_out))
    normed_enc = row_gather(rms_apply(after_self, gain_mlp).astype(jnp.bfloat16))
    enc_mlp = on_slab(encoding, mlp_forward, normed_enc, full_gate, full_up, full_down)
    after_enc = after_self + row_sum(enc_mlp[0])
    memory_half = jnp.where(encoding, rms_apply(after_enc, gain_final), 0.0).astype(jnp.bfloat16)
    memory_full = row_gather(deliver(memory_half, pairing))
    cross_keys = on_slab(decoding, project, memory_full, key_cross)
    cross_values = on_slab(decoding, project, memory_full, value_cross)
    normed_cross = row_gather(rms_apply(after_enc, gain_cross).astype(jnp.bfloat16))

    def cross_forward(query_in, key_rows, value_rows):
        queries = project(query_in, query_cross)
        context, log_total = attend(queries, key_rows, value_rows, cross_allowed)
        return (matmul(context, out_cross), queries, context, log_total)

    cross_result = on_slab(decoding, cross_forward, normed_cross, cross_keys, cross_values)
    after_cross = after_enc + row_sum(cross_result[0])
    normed_dec = row_gather(rms_apply(after_cross, gain_mlp).astype(jnp.bfloat16))
    dec_mlp = on_slab(decoding, mlp_forward, normed_dec, full_gate, full_up, full_down)
    after_mlp = after_cross + row_sum(dec_mlp[0])
    normed_final = row_gather(rms_apply(after_mlp, gain_final).astype(jnp.bfloat16))
    head_out = on_slab(decoding, head_forward, normed_final, vocab_table, local_ids, owned)
    totals_local = jnp.where(decoding, head_out[2], 1.0)
    merged = combined_all((head_out[1], totals_local, head_out[3]), "mp", merge_softmax)
    log_total = merged[0] + jnp.log(merged[1])
    token_ce = jnp.where(counted, log_total - merged[2], 0.0)
    loss_part = jnp.sum(token_ce)
    head_grads = on_slab(
        decoding,
        head_back,
        head_out[0],
        log_total,
        counted,
        normed_final,
        vocab_table,
        local_ids,
        owned,
    )
    grad_stream, grad_gain_final = norm_back(after_mlp, gain_final, row_sum(head_grads[0]))
    grad_rows = row_gather(grad_stream.astype(jnp.bfloat16))
    dec_back = on_slab(
        decoding,
        mlp_back,
        normed_dec,
        dec_mlp[1],
        dec_mlp[2],
        dec_mlp[3],
        full_gate,
        full_up,
        full_down,
        grad_rows,
    )
    stream_part, grad_gain_mlp = norm_back(after_cross, gain_mlp, row_sum(dec_back[0]))
    grad_stream = grad_stream + stream_part
    grad_rows = row_gather(grad_stream.astype(jnp.bfloat16))

    def cross_back(query_in, queries, key_rows, value_rows, context, log_cross, grad_in):
        return attention_back(
            query_in,
            queries,
            key_rows,
            value_rows,
            context,
            log_cross,
            query_cross,
            out_cross,
            cross_allowed,
            grad_in,
        )

    cross_grads = on_slab(
        decoding,
        cross_back,
        normed_cross,
        cross_result[1],
        cross_keys,
        cross_values,
        cross_result[2],
        cross_result[3],
        grad_rows,
    )
    grad_query_cross = cross_grads[3]
    grad_out_cross = cross_grads[4]
    key_grads = on_slab(
        decoding, key_side_back, memory_full, cross_grads[1], cross_grads[2], key_cross, value_cross
    )
    grad_cross_half, grad_memory_half = row_sum((cross_grads[0], key_grads[0]))
    returned = send_back(grad_memory_half.astype(jnp.bfloat16), pairing)
    grad_key_cross = key_grads[1]
    grad_value_cross = key_grads[2]
    stream_part, grad_gain_cross = norm_back(after_enc, gain_cross, grad_cross_half)
    grad_stream = grad_stream + stream_part
    grad_memory = jnp.where(encoding, returned.astype(jnp.float32), 0.0)
    stream_part, gain_part = norm_back(after_enc, gain_final, grad_memory)
    grad_stream = grad_stream + stream_part
    grad_gain_final = grad_gain_final + gain_part
    grad_rows = row_gather(grad_stream.astype(jnp.bfloat16))
    enc_back = on_slab(
        encoding,
        mlp_back,
        normed_enc,
        enc_mlp[1],
        enc_mlp[2],
        enc_mlp[3],
        full_gate,
        full_up,
        full_down,
        grad_rows,
    )
    stream_part, gain_part = norm_back(after_self, gain_mlp, row_sum(enc_back[0]))
    grad_stream = grad_stream + stream_part
    grad_gain_mlp = grad_gain_mlp + gain_part
    grad_rows = row_gather(grad_stream.astype(jnp.bfloat16))
    self_grads = attention_back(
        normed_attn,
        self_queries,
        self_keys,
        self_values,
        self_context,
        self_log,
        full_query,
        full_out,
        self_allowed,
        grad_rows,
    )
    self_keyside = key_side_back(normed_attn, self_grads[1], self_grads[2], full_key, full_value)
    stream_part, grad_gain_attn = norm_back(
        start_rows, gain_attn, row_sum(self_grads[0] + self_keyside[0])
    )
    grad_stream = grad_stream + stream_part
    gain_totals = lax.psum((grad_gain_attn, grad_gain_mlp, grad_gain_final, grad_gain_cross), "mp")
    stacked = (
        lax.psum_scatter(gain_totals[0][None], "dp", scatter_dimension=1, tiled=True),
        lax.psum_scatter(self_grads[3][None], "dp", scatter_dimension=1, tiled=True),
        lax.psum_scatter(self_keyside[1][None], "dp", scatter_dimension=1, tiled=True),
        lax.psum_scatter(self_keyside[2][None], "dp", scatter_dimension=1, tiled=True),
        lax.psum_scatter(self_grads[4][None], "dp", scatter_dimension=2, tiled=True),
        lax.psum_scatter(gain_totals[1][None], "dp", scatter_dimension=1, tiled=True),
        lax.psum_scatter((enc_back[1] + dec_back[1])[None], "dp", scatter_dimension=1, tiled=True),
        lax.psum_scatter((enc_back[2] + dec_back[2])[None], "dp", scatter_dimension=1, tiled=True),
        lax.psum_scatter((enc_back[3] + dec_back[3])[None], "dp", scatter_dimension=2, tiled=True),
        lax.psum_scatter(gain_totals[2][None], "dp", scatter_dimension=1, tiled=True),
    )
    count_dp = lax.axis_size("dp")
    slot_ids = jnp.arange(lax.axis_size("slab") * count_dp, dtype=jnp.int32)
    mine = decoding & (slot_ids % count_dp == seq_index)
    loss_spread = jnp.where(mine, loss_part, 0.0).astype(jnp.float32)
    token_spread = jnp.where(mine[:, None], token_ce[None, :], 0.0).astype(jnp.float32)
    decoder_sums = (
        lax.psum_scatter(gain_totals[3], ("slab", "dp"), scatter_dimension=0, tiled=True),
        lax.psum_scatter(grad_query_cross, ("slab", "dp"), scatter_dimension=0, tiled=True),
        lax.psum_scatter(grad_key_cross, ("slab", "dp"), scatter_dimension=0, tiled=True),
        lax.psum_scatter(grad_value_cross, ("slab", "dp"), scatter_dimension=0, tiled=True),
        lax.psum_scatter(grad_out_cross, ("slab", "dp"), scatter_dimension=1, tiled=True),
        lax.psum_scatter(head_grads[1], ("slab", "dp"), scatter_dimension=0, tiled=True),
        lax.psum_scatter(loss_spread, ("slab", "dp"), scatter_dimension=0, tiled=True),
        lax.psum_scatter(token_spread, ("slab", "dp"), scatter_dimension=0, tiled=True),
    )
    seq_loss = decoder_sums[6] / target_len[seq_index].astype(jnp.float32)
    return (
        seq_loss,
        grad_stream[None, None],
        stacked[0],
        stacked[1],
        stacked[2],
        stacked[3],
        stacked[4],
        stacked[5],
        stacked[6],
        stacked[7],
        stacked[8],
        stacked[9],
        decoder_sums[0],
        decoder_sums[1],
        decoder_sums[2],
        decoder_sums[3],
        decoder_sums[4],
        decoder_sums[5],
        decoder_sums[7],
    )


def solution(mesh):
    return jax.shard_map(
        on_device,
        mesh=mesh,
        in_specs=(
            P("slab", "dp", "mp", None),
            P("slab", "dp"),
            P("slab", "dp", "mp"),
            P("slab", "dp", "mp"),
            P("slab", "dp", "mp"),
            P("slab", "mp", "dp"),
            P("slab", "dp"),
            P("slab", "dp", "mp"),
            P("slab", "dp", "mp"),
            P("slab", "mp", "dp"),
            P("slab", "dp"),
            P(("slab", "dp")),
            P(("slab", "dp"), "mp"),
            P(("slab", "dp"), "mp"),
            P(("slab", "dp"), "mp"),
            P("mp", ("slab", "dp")),
            P(("slab", "dp", "mp"), None),
            P(),
            P(),
            P("dp", None),
            P(),
        ),
        out_specs=(
            P("dp"),
            P("slab", "dp", "mp", None),
            P("slab", "dp"),
            P("slab", "dp", "mp"),
            P("slab", "dp", "mp"),
            P("slab", "dp", "mp"),
            P("slab", "mp", "dp"),
            P("slab", "dp"),
            P("slab", "dp", "mp"),
            P("slab", "dp", "mp"),
            P("slab", "mp", "dp"),
            P("slab", "dp"),
            P(("slab", "dp")),
            P(("slab", "dp"), "mp"),
            P(("slab", "dp"), "mp"),
            P(("slab", "dp"), "mp"),
            P("mp", ("slab", "dp")),
            P(("slab", "dp", "mp"), None),
            P("dp", None),
        ),
        check_vma=False,
    )
```

profile of v0, /device:TPU:0, one launch (start us, length us, event | category | flops | bytes accessed | tf_op | source)
XLA Modules:
  0.0 2937.0 jit_solution(17969468341711650636)
XLA Ops:
  14.1 23.4 all-reduce.10
  45.5 31.8 %all_gather.99 = bf16[1,768,384]{2,1,0:T(8,128)(2,1)S(1)} all-gather(bf16[1,96,384]{2,1,0:T(8,128)(2,1)S(1)} %copy-done.54), channel_id=1, replica_groups=mesh['slab'=2,'dp'=8,'mp'=2] {'dp'}, dimensions={1}, use_global_device_ids=true | all-gather | bytes 663552 | tf_op jit(solution)/shard_map/all_gather | solution.py:258
  77.3 31.7 %all_gather.100 = bf16[1,768,384]{2,1,0:T(8,128)(2,1)S(1)} all-gather(bf16[1,96,384]{2,1,0:T(8,128)(2,1)S(1)} %copy-done.55), channel_id=1, replica_groups=mesh['slab'=2,'dp'=8,'mp'=2] {'dp'}, dimensions={1}, use_global_device_ids=true | all-gather | bytes 663552 | tf_op jit(solution)/shard_map/all_gather | solution.py:259
  109.0 31.7 %all_gather.98 = bf16[1,768,384]{2,1,0:T(8,128)(2,1)S(1)} all-gather(bf16[1,96,384]{2,1,0:T(8,128)(2,1)S(1)} %copy-done.56), channel_id=1, replica_groups=mesh['slab'=2,'dp'=8,'mp'=2] {'dp'}, dimensions={1}, use_global_device_ids=true | all-gather | bytes 663552 | tf_op jit(solution)/shard_map/all_gather | solution.py:260
  140.7 31.3 %all_gather.101 = bf16[1,384,768]{1,2,0:T(8,128)(2,1)S(1)} all-gather(bf16[1,384,96]{1,2,0:T(8,128)(2,1)S(1)} %copy-done.57), channel_id=1, replica_groups=mesh['slab'=2,'dp'=8,'mp'=2] {'dp'}, dimensions={2}, use_global_device_ids=true | all-gather | bytes 663552 | tf_op jit(solution)/shard_map/all_gather | solution.py:261
  175.7 10.6 fusion.132
  186.3 10.2 fusion.51
  197.4 10.8 fusion.92
  219.7 34.8 %all-gather.22.cloned.1.call-done = bf16[1,768,1024]{2,1,0:T(8,128)(2,1)} async-done(((bf16[1,96,1024]{2,1,0:T(8,128)(2,1)}), bf16[1,768,1024]{2,1,0:T(8,128)(2,1)}) %all-gather.22.cloned.1.call-update) | async-done | bytes 1572880 | tf_op jit(solution)/shard_map/all_gather | solution.py:263
  254.5 44.6 %all-gather.24.cloned.1.call-done = bf16[1,768,1024]{2,1,0:T(8,128)(2,1)} async-done(((bf16[1,96,1024]{2,1,0:T(8,128)(2,1)}), bf16[1,768,1024]{2,1,0:T(8,128)(2,1)}) %all-gather.24.cloned.1.call-update) | async-done | bytes 1572880 | tf_op jit(solution)/shard_map/all_gather | solution.py:264
  299.1 44.6 %all-gather.26.cloned.1.call-done = bf16[1,1024,768]{1,2,0:T(8,128)(2,1)} async-done(((bf16[1,1024,96]{1,2,0:T(8,128)(2,1)}), bf16[1,1024,768]{1,2,0:T(8,128)(2,1)}) %all-gather.26.cloned.1.call-update) | async-done | bytes 1572880 | tf_op jit(solution)/shard_map/all_gather | solution.py:265
  343.7 10.2 all-gather.20.cloned.1.call-done
  353.8 15.9 conditional.11
  371.8 38.3 %all-reduce.2 = bf16[768]{0:T(1024)(128)(2,1)S(1)} all-reduce(bf16[768]{0:T(1024)(128)(2,1)S(1)} %dynamic-update-slice.2), channel_id=1, replica_groups=mesh['slab'=2,'dp'=8,'mp'=2] {'slab','dp'}, use_global_device_ids=true, to_apply=%add.2 | all-reduce | flops 768 | bytes 3072
  413.2 7.1 collective-permute-start
  420.3 9.0 collective-permute-done
  433.5 15.2 all-to-all-done
  449.4 20.1 all_to_all.20
  470.9 43.3 %all_gather.109 = bf16[768,384]{1,0:T(8,128)(2,1)S(1)} all-gather(bf16[48,384]{1,0:T(8,128)(2,1)S(1)} %copy-done.64), channel_id=1, replica_groups=mesh['slab'=2,'dp'=8,'mp'=2] {'slab','dp'}, dimensions={0}, use_global_device_ids=true | all-gather | bytes 626688 | tf_op jit(solution)/shard_map/all_gather | solution.py:280
  514.1 41.2 %all_gather.112 = bf16[768,384]{1,0:T(8,128)(2,1)} all-gather(bf16[48,384]{1,0:T(8,128)(2,1)S(1)} %copy-done.65), channel_id=1, replica_groups=mesh['slab'=2,'dp'=8,'mp'=2] {'slab','dp'}, dimensions={0}, use_global_device_ids=true | all-gather | bytes 626688 | tf_op jit(solution)/shard_map/all_gather | solution.py:281
  555.4 41.4 %all_gather.113 = bf16[768,384]{1,0:T(8,128)(2,1)S(1)} all-gather(bf16[48,384]{1,0:T(8,128)(2,1)S(1)} %copy-done.66), channel_id=1, replica_groups=mesh['slab'=2,'dp'=8,'mp'=2] {'slab','dp'}, dimensions={0}, use_global_device_ids=true | all-gather | bytes 626688 | tf_op jit(solution)/shard_map/all_gather | solution.py:282
  596.8 40.9 %all_gather.114 = bf16[384,768]{0,1:T(8,128)(2,1)} all-gather(bf16[384,48]{0,1:T(8,128)(2,1)S(1)} %copy-done.67), channel_id=1, replica_groups=mesh['slab'=2,'dp'=8,'mp'=2] {'slab','dp'}, dimensions={1}, use_global_device_ids=true | all-gather | bytes 626688 | tf_op jit(solution)/shard_map/all_gather | solution.py:283
  643.0 49.5 %reduce-scatter.35.cloned.1.call-done = bf16[512,768]{1,0:T(8,128)(2,1)} async-done(((bf16[1024,768]{1,0:T(8,128)(2,1)}), bf16[512,768]{1,0:T(8,128)(2,1)}) %reduce-scatter.35.cloned.1.call-update) | async-done | bytes 786448 | tf_op jit(solution)/shard_map/reduce_scatter | solution.py:76
  695.1 11.1 all-gather.32.cloned.1.call-done
  706.2 7.1 conditional.15
  715.2 18.2 reduce-scatter.37.cloned.1.call-done
  736.9 142.8 %all-gather.36.cloned.1.call-done = bf16[8192,768]{1,0:T(8,128)(2,1)} async-done(((bf16[512,768]{1,0:T(8,128)(2,1)}), bf16[8192,768]{1,0:T(8,128)(2,1)}) %all-gather.36.cloned.1.call-update) | async-done | bytes 12582928 | tf_op jit(solution)/shard_map/all_gather | solution.py:284
  879.8 9.9 all-gather.34.cloned.1.call-done
  889.7 11.8 conditional.16
  890.3 11.2 broadcast.397
  908.8 11.8 conditional.17
  910.5 10.0 broadcast.401
  920.7 100.8 %reduce-scatter.39.cloned.1.call-done = bf16[512,768]{1,0:T(8,128)(2,1)} async-done(((bf16[1024,768]{1,0:T(8,128)(2,1)}), bf16[512,768]{1,0:T(8,128)(2,1)}) %reduce-scatter.39.cloned.1.call-update) | async-done | bytes 786448 | tf_op jit(solution)/shard_map/reduce_scatter | solution.py:76
  1025.5 11.1 all-gather.38.cloned.1.call-done
  1036.6 7.5 conditional.18
  1044.6 34.3 %reduce-scatter.41.cloned.1.call-done = bf16[512,768]{1,0:T(8,128)(2,1)} async-done(((bf16[1024,768]{1,0:T(8,128)(2,1)}), bf16[512,768]{1,0:T(8,128)(2,1)}) %reduce-scatter.41.cloned.1.call-update) | async-done | bytes 786448 | tf_op jit(solution)/shard_map/reduce_scatter | solution.py:76
  1084.8 11.1 all-gather.40.cloned.1.call-done
  1105.1 102.5 %reduce-scatter.45.cloned.1.call-done = bf16[512,768]{1,0:T(8,128)(2,1)} async-done(((bf16[1024,768]{1,0:T(8,128)(2,1)}), bf16[512,768]{1,0:T(8,128)(2,1)}) %reduce-scatter.45.cloned.1.call-update) | async-done | bytes 786448 | tf_op jit(solution)/shard_map/reduce_scatter | solution.py:76
  1215.0 19.0 all-to-all-done.2
  1234.6 23.8 all_to_all.21
  1259.9 18.9 collective-permute-done.1
  1284.7 9.0 all-gather.42.cloned.1.call-done
  1293.6 29.1 conditional.21
  1299.5 7.0 multiply_convert_fusion.1
  1323.2 9.0 reduce-scatter.47.cloned.1.call-done
  1337.3 11.1 all-gather.44.cloned.1.call-done
  1350.6 11.2 fusion.89
  1361.8 16.0 multiply_reduce_fusion.1
  1377.8 17.0 multiply_convert_fusion.5
  1462.6 56.6 %all-reduce.16.cloned.1.call-done = f32[16,1024]{1,0:T(8,128)} async-done(((f32[16,1024]{1,0:T(8,128)}), f32[16,1024]{1,0:T(8,128)}) %all-reduce.16.cloned.1.call-update) | async-done | bytes 65552
  1521.2 40.9 %all-reduce.8 = (f32[16]{0:T(128)S(1)}, f32[768]{0:T(1024)S(1)}) all-reduce(f32[16]{0:T(128)S(1)} %get-tuple-element.459, f32[768]{0:T(1024)S(1)} %get-tuple-element.434), channel_id=9, replica_groups=mesh['slab'=2,'dp'=8,'mp'=2] {'slab','dp'}, use_global_device_ids=true, to_apply=%region_28.29.clone | all-reduce | flops 784 | bytes 6272
  1565.8 37.4 %all-reduce.14.cloned.1.call-done = f32[1,384,768]{1,0,2:T(1,128)} async-done(((f32[1,384,768]{1,0,2:T(1,128)}), f32[1,384,768]{1,0,2:T(1,128)}) %all-reduce.14.cloned.1.call-update) | async-done | bytes 1179664
  1608.6 7.3 reduce-scatter.73.cloned.1.call-done
  1619.7 124.3 %reduce-scatter.65.cloned.1.call-done = f32[48,384]{1,0:T(8,128)} async-done(((f32[768,384]{1,0:T(8,128)}), f32[48,384]{1,0:T(8,128)}) %reduce-scatter.65.cloned.1.call-update) | async-done | bytes 73744 | tf_op jit(solution)/shard_map/reduce_scatter | solution.py:462
  1744.0 128.0 %reduce-scatter.67.cloned.1.call-done = f32[48,384]{1,0:T(8,128)} async-done(((f32[768,384]{1,0:T(8,128)}), f32[48,384]{1,0:T(8,128)}) %reduce-scatter.67.cloned.1.call-update) | async-done | bytes 73744 | tf_op jit(solution)/shard_map/reduce_scatter | solution.py:463
  1872.0 128.1 %reduce-scatter.63.cloned.1.call-done = f32[48,384]{1,0:T(8,128)} async-done(((f32[768,384]{1,0:T(8,128)}), f32[48,384]{1,0:T(8,128)}) %reduce-scatter.63.cloned.1.call-update) | async-done | bytes 73744 | tf_op jit(solution)/shard_map/reduce_scatter | solution.py:461
  2000.1 127.9 %reduce-scatter.69.cloned.1.call-done = f32[384,48]{0,1:T(8,128)} async-done(((f32[384,768]{0,1:T(8,128)}), f32[384,48]{0,1:T(8,128)}) %reduce-scatter.69.cloned.1.call-update) | async-done | bytes 73744 | tf_op jit(solution)/shard_map/reduce_scatter | solution.py:464
  2127.9 77.4 %reduce-scatter.57.cloned.1.call-done = f32[1,96,1024]{2,1,0:T(8,128)} async-done(((f32[1,768,1024]{2,1,0:T(8,128)}), f32[1,96,1024]{2,1,0:T(8,128)}) %reduce-scatter.57.cloned.1.call-update) | async-done | bytes 393232 | tf_op jit(solution)/shard_map/reduce_scatter | solution.py:449
  2205.3 77.4 %reduce-scatter.59.cloned.1.call-done = f32[1,96,1024]{2,1,0:T(8,128)} async-done(((f32[1,768,1024]{2,1,0:T(8,128)}), f32[1,96,1024]{2,1,0:T(8,128)}) %reduce-scatter.59.cloned.1.call-update) | async-done | bytes 393232 | tf_op jit(solution)/shard_map/reduce_scatter | solution.py:450
  2282.7 77.3 %reduce-scatter.61.cloned.1.call-done = f32[1,1024,96]{1,2,0:T(8,128)} async-done(((f32[1,1024,768]{1,2,0:T(8,128)}), f32[1,1024,96]{1,2,0:T(8,128)}) %reduce-scatter.61.cloned.1.call-update) | async-done | bytes 393232 | tf_op jit(solution)/shard_map/reduce_scatter | solution.py:451
  2360.1 67.1 %reduce-scatter.55.cloned.1.call-done = f32[1,96,384]{2,1,0:T(8,128)} async-done(((f32[1,768,384]{2,1,0:T(8,128)}), f32[1,96,384]{2,1,0:T(8,128)}) %reduce-scatter.55.cloned.1.call-update) | async-done | bytes 147472 | tf_op jit(solution)/shard_map/reduce_scatter | solution.py:446
  2427.2 67.0 %reduce-scatter.51.cloned.1.call-done = f32[1,96,384]{2,1,0:T(8,128)} async-done(((f32[1,768,384]{2,1,0:T(8,128)}), f32[1,96,384]{2,1,0:T(8,128)}) %reduce-scatter.51.cloned.1.call-update) | async-done | bytes 147472 | tf_op jit(solution)/shard_map/reduce_scatter | solution.py:444
  2494.2 66.9 %reduce-scatter.53.cloned.1.call-done = f32[1,96,384]{2,1,0:T(8,128)} async-done(((f32[1,768,384]{2,1,0:T(8,128)}), f32[1,96,384]{2,1,0:T(8,128)}) %reduce-scatter.53.cloned.1.call-update) | async-done | bytes 147472 | tf_op jit(solution)/shard_map/reduce_scatter | solution.py:445
  2561.1 367.0 %reduce-scatter.71.cloned.1.call-done = f32[512,768]{1,0:T(8,128)} async-done(((f32[8192,768]{1,0:T(8,128)}), f32[512,768]{1,0:T(8,128)}) %reduce-scatter.71.cloned.1.call-update) | async-done | bytes 1572880 | tf_op jit(solution)/shard_map/reduce_scatter | solution.py:465
  (430 shorter events, 243.1 us)
Async XLA Ops:
  8.0 164.4 %all-gather.18.cloned.1.call-start = ((), (), s32[]{:S(2)}) async-start(), calls=%async_computation.28 | async-start | bytes 2359296 | tf_op jit(solution)/shard_map/all_gather | solution.py:70
  8.1 37.4 %copy-start.54 = (bf16[1,96,384]{2,1,0:T(8,128)(2,1)S(1)}, bf16[1,96,384]{2,1,0:T(8,128)(2,1)}, u32[]{:S(2)}) copy-start(bf16[1,96,384]{2,1,0:T(8,128)(2,1)} %param.45) | copy-start | bytes 221188
  9.5 67.8 %copy-start.55 = (bf16[1,96,384]{2,1,0:T(8,128)(2,1)S(1)}, bf16[1,96,384]{2,1,0:T(8,128)(2,1)}, u32[]{:S(2)}) copy-start(bf16[1,96,384]{2,1,0:T(8,128)(2,1)} %param.46) | copy-start | bytes 221188
  38.1 70.9 %copy-start.56 = (bf16[1,96,384]{2,1,0:T(8,128)(2,1)S(1)}, bf16[1,96,384]{2,1,0:T(8,128)(2,1)}, u32[]{:S(2)}) copy-start(bf16[1,96,384]{2,1,0:T(8,128)(2,1)} %param.47) | copy-start | bytes 221188
  40.4 100.4 %copy-start.57 = (bf16[1,384,96]{1,2,0:T(8,128)(2,1)S(1)}, bf16[1,384,96]{1,2,0:T(8,128)(2,1)}, u32[]{:S(2)}) copy-start(bf16[1,384,96]{1,2,0:T(8,128)(2,1)} %param.48) | copy-start | bytes 221188
  40.4 176.4 %reduce-scatter.31.cloned.1.call-start = ((), (), s32[]{:S(2)}) async-start(), calls=%async_computation.29 | async-start | bytes 2359296 | tf_op jit(solution)/shard_map/reduce_scatter | solution.py:76
  77.3 97.4 %copy-start.37 = (bf16[1,768,384]{2,1,0:T(8,128)(2,1)}, bf16[1,768,384]{2,1,0:T(8,128)(2,1)S(1)}, u32[]{:S(2)}) copy-start(bf16[1,768,384]{2,1,0:T(8,128)(2,1)S(1)} %all_gather.99) | copy-start | bytes 1769476
  109.0 65.8 %copy-start.35 = (bf16[1,768,384]{2,1,0:T(8,128)(2,1)}, bf16[1,768,384]{2,1,0:T(8,128)(2,1)S(1)}, u32[]{:S(2)}) copy-start(bf16[1,768,384]{2,1,0:T(8,128)(2,1)S(1)} %all_gather.100) | copy-start | bytes 1769476
  140.7 55.8 %copy-start.33 = (bf16[1,768,384]{2,1,0:T(8,128)(2,1)}, bf16[1,768,384]{2,1,0:T(8,128)(2,1)S(1)}, u32[]{:S(2)}) copy-start(bf16[1,768,384]{2,1,0:T(8,128)(2,1)S(1)} %all_gather.98) | copy-start | bytes 1769476
  210.4 44.2 %all-gather.22.cloned.1.call-start = ((), (), s32[]{:S(2)}) async-start(), calls=%async_computation.31 | async-start | bytes 1769472 | tf_op jit(solution)/shard_map/all_gather | solution.py:263
  211.0 88.1 %all-gather.24.cloned.1.call-start = ((), (), s32[]{:S(2)}) async-start(), calls=%async_computation.32 | async-start | bytes 1769472 | tf_op jit(solution)/shard_map/all_gather | solution.py:264
  211.6 132.1 %all-gather.26.cloned.1.call-start = ((), (), s32[]{:S(2)}) async-start(), calls=%async_computation.33 | async-start | bytes 1769472 | tf_op jit(solution)/shard_map/all_gather | solution.py:265
  212.1 141.7 %all-gather.20.cloned.1.call-start = ((), (), s32[]{:S(2)}) async-start(), calls=%async_computation.30 | async-start | bytes 2359296 | tf_op jit(solution)/shard_map/all_gather | solution.py:70
  212.2 481.7 %copy-start.50 = (f32[768]{0:T(1024)}, f32[768]{0:T(1024)S(1)}, u32[]{:S(2)}) copy-start(f32[768]{0:T(1024)S(1)} %mul.625) | copy-start | bytes 9220
  219.7 190.5 %reduce-scatter.33.cloned.1.call-start = ((), (), s32[]{:S(2)}) async-start(), calls=%async_computation.34 | async-start | bytes 2359296 | tf_op jit(solution)/shard_map/reduce_scatter | solution.py:76
  413.2 16.1 collective-permute-start
  429.3 19.4 all-to-all-start
  432.9 204.8 %all-gather.30.cloned.1.call-start = ((), (), s32[]{:S(2)}) async-start(), calls=%async_computation.36 | async-start | bytes 2359296 | tf_op jit(solution)/shard_map/all_gather | solution.py:70
  449.4 64.7 %copy-start.65 = (bf16[48,384]{1,0:T(8,128)(2,1)S(1)}, bf16[48,384]{1,0:T(8,128)(2,1)}, u32[]{:S(2)}) copy-start(bf16[48,384]{1,0:T(8,128)(2,1)} %param.56) | copy-start | bytes 110596
  469.5 85.9 %copy-start.66 = (bf16[48,384]{1,0:T(8,128)(2,1)S(1)}, bf16[48,384]{1,0:T(8,128)(2,1)}, u32[]{:S(2)}) copy-start(bf16[48,384]{1,0:T(8,128)(2,1)} %param.57) | copy-start | bytes 110596
  469.5 127.3 %copy-start.67 = (bf16[384,48]{0,1:T(8,128)(2,1)S(1)}, bf16[384,48]{0,1:T(8,128)(2,1)}, u32[]{:S(2)}) copy-start(bf16[384,48]{0,1:T(8,128)(2,1)} %param.58) | copy-start | bytes 110596
  469.5 168.4 %all-gather.28.cloned.1.call-start = ((), (), s32[]{:S(2)}) async-start(), calls=%async_computation.35 | async-start | bytes 2359296 | tf_op jit(solution)/shard_map/all_gather | solution.py:70
  470.1 222.3 %reduce-scatter.35.cloned.1.call-start = ((), (), s32[]{:S(2)}) async-start(), calls=%async_computation.37 | async-start | bytes 2359296 | tf_op jit(solution)/shard_map/reduce_scatter | solution.py:76
  470.9 167.1 %copy-start.68 = (pred[1,1024]{1,0:T(4,128)(4,1)}, pred[1,1024]{1,0:T(4,128)(4,1)S(1)}, u32[]{:S(2)}) copy-start(pred[1,1024]{1,0:T(4,128)(4,1)S(1)} %iota_compare_fusion.2) | copy-start | bytes 3076
  514.1 123.8 %copy-start.44 = (bf16[768,384]{1,0:T(8,128)(2,1)}, bf16[768,384]{1,0:T(8,128)(2,1)S(1)}, u32[]{:S(2)}) copy-start(bf16[768,384]{1,0:T(8,128)(2,1)S(1)} %all_gather.109) | copy-start | bytes 1769476
  596.8 41.0 %copy-start.39 = (bf16[768,384]{1,0:T(8,128)(2,1)}, bf16[768,384]{1,0:T(8,128)(2,1)S(1)}, u32[]{:S(2)}) copy-start(bf16[768,384]{1,0:T(8,128)(2,1)S(1)} %all_gather.113) | copy-start | bytes 1769476
  642.1 50.4 %copy-start.4 = (f32[512,768]{1,0:T(8,128)S(1)}, f32[512,768]{1,0:T(8,128)}, u32[]{:S(2)}) copy-start(f32[512,768]{1,0:T(8,128)} %copy-done.3) | copy-start | bytes 4718596
  642.1 64.1 %all-gather.32.cloned.1.call-start = ((), (), s32[]{:S(2)}) async-start(), calls=%async_computation.38 | async-start | bytes 2359296 | tf_op jit(solution)/shard_map/all_gather | solution.py:70
  695.1 38.4 %reduce-scatter.37.cloned.1.call-start = ((), (), s32[]{:S(2)}) async-start(), calls=%async_computation.39 | async-start | bytes 2359296 | tf_op jit(solution)/shard_map/reduce_scatter | solution.py:76
  714.5 165.3 %all-gather.36.cloned.1.call-start = ((), (), s32[]{:S(2)}) async-start(), calls=%async_computation.41 | async-start | bytes 13369344 | tf_op jit(solution)/shard_map/all_gather | solution.py:284
  715.2 174.5 %all-gather.34.cloned.1.call-start = ((), (), s32[]{:S(2)}) async-start(), calls=%async_computation.40 | async-start | bytes 2359296 | tf_op jit(solution)/shard_map/all_gather | solution.py:70
  736.2 285.3 %reduce-scatter.39.cloned.1.call-start = ((), (), s32[]{:S(2)}) async-start(), calls=%async_computation.42 | async-start | bytes 2359296 | tf_op jit(solution)/shard_map/reduce_scatter | solution.py:76
  920.7 116.0 %all-gather.38.cloned.1.call-start = ((), (), s32[]{:S(2)}) async-start(), calls=%async_computation.43 | async-start | bytes 2359296 | tf_op jit(solution)/shard_map/all_gather | solution.py:70
  1025.5 53.4 %reduce-scatter.41.cloned.1.call-start = ((), (), s32[]{:S(2)}) async-start(), calls=%async_computation.44 | async-start | bytes 2359296 | tf_op jit(solution)/shard_map/reduce_scatter | solution.py:76
  1044.2 51.8 %all-gather.40.cloned.1.call-start = ((), (), s32[]{:S(2)}) async-start(), calls=%async_computation.45 | async-start | bytes 2359296 | tf_op jit(solution)/shard_map/all_gather | solution.py:70
  1084.8 122.8 %reduce-scatter.45.cloned.1.call-start = ((), (), s32[]{:S(2)}) async-start(), calls=%async_computation.47 | async-start | bytes 2359296 | tf_op jit(solution)/shard_map/reduce_scatter | solution.py:76
  1207.6 26.4 all-to-all-start.2
  1213.4 46.5 %reduce-scatter.43.cloned.1.call-start = ((), (), s32[]{:S(2)}) async-start(), calls=%async_computation.46 | async-start | bytes 2359296 | tf_op jit(solution)/shard_map/reduce_scatter | solution.py:76
  1214.2 79.5 %all-gather.42.cloned.1.call-start = ((), (), s32[]{:S(2)}) async-start(), calls=%async_computation.48 | async-start | bytes 2359296 | tf_op jit(solution)/shard_map/all_gather | solution.py:70
  1215.0 63.8 %copy-start.5 = (f32[512,768]{1,0:T(8,128)S(1)}, f32[512,768]{1,0:T(8,128)}, u32[]{:S(2)}) copy-start(f32[512,768]{1,0:T(8,128)} %copy-done.3) | copy-start | bytes 4718596
  1215.0 63.8 %copy-start.61 = (f32[768]{0:T(1024)S(1)}, f32[768]{0:T(1024)}, u32[]{:S(2)}) copy-start(f32[768]{0:T(1024)} %copy-done.60) | copy-start | bytes 9220
  1215.0 63.8 %copy-start.73 = (f32[512]{0:T(512)S(1)}, f32[512]{0:T(512)}, u32[]{:S(2)}) copy-start(f32[512]{0:T(512)} %copy-done.72) | copy-start | bytes 6148
  1258.4 20.3 collective-permute-start.1
  1284.6 47.6 %reduce-scatter.47.cloned.1.call-start = ((), (), s32[]{:S(2)}) async-start(), calls=%async_computation.49 | async-start | bytes 2359296 | tf_op jit(solution)/shard_map/reduce_scatter | solution.py:76
  1322.7 25.7 all-gather.44.cloned.1.call-start
  1337.2 84.8 %reduce-scatter.49.cloned.1.call-start = ((), (), s32[]{:S(2)}) async-start(), calls=%async_computation.51 | async-start | bytes 2359296 | tf_op jit(solution)/shard_map/reduce_scatter | solution.py:76
  1409.5 109.7 %all-reduce.16.cloned.1.call-start = ((), (), s32[]{:S(2)}) async-start(), calls=%async_computation.67 | async-start | bytes 131072
  1411.7 152.4 %reduce-scatter.77.cloned.1.call-start = ((), (), s32[]{:S(2)}) async-start(), calls=%async_computation.65 | async-start | bytes 442368
  1412.7 152.3 %reduce-scatter.75.cloned.1.call-start = ((), (), s32[]{:S(2)}) async-start(), calls=%async_computation.64 | async-start | bytes 442368
  1413.7 189.5 %all-reduce.14.cloned.1.call-start = ((), (), s32[]{:S(2)}) async-start(), calls=%async_computation.66 | async-start | bytes 2359296
  1422.0 193.9 %reduce-scatter.73.cloned.1.call-start = ((), (), s32[]{:S(2)}) async-start(), calls=%async_computation.63 | async-start | bytes 442368
  1424.9 319.1 %reduce-scatter.65.cloned.1.call-start = ((), (), s32[]{:S(2)}) async-start(), calls=%async_computation.59 | async-start | bytes 1253376 | tf_op jit(solution)/shard_map/reduce_scatter | solution.py:462
  1425.7 446.3 %reduce-scatter.67.cloned.1.call-start = ((), (), s32[]{:S(2)}) async-start(), calls=%async_computation.60 | async-start | bytes 1253376 | tf_op jit(solution)/shard_map/reduce_scatter | solution.py:463
  1426.4 573.7 %reduce-scatter.63.cloned.1.call-start = ((), (), s32[]{:S(2)}) async-start(), calls=%async_computation.58 | async-start | bytes 1253376 | tf_op jit(solution)/shard_map/reduce_scatter | solution.py:461
  1429.2 698.7 %reduce-scatter.69.cloned.1.call-start = ((), (), s32[]{:S(2)}) async-start(), calls=%async_computation.61 | async-start | bytes 1253376 | tf_op jit(solution)/shard_map/reduce_scatter | solution.py:464
  1432.0 773.4 %reduce-scatter.57.cloned.1.call-start = ((), (), s32[]{:S(2)}) async-start(), calls=%async_computation.55 | async-start | bytes 3538944 | tf_op jit(solution)/shard_map/reduce_scatter | solution.py:449
  1437.5 845.2 %reduce-scatter.59.cloned.1.call-start = ((), (), s32[]{:S(2)}) async-start(), calls=%async_computation.56 | async-start | bytes 3538944 | tf_op jit(solution)/shard_map/reduce_scatter | solution.py:450
  1443.1 917.0 %reduce-scatter.61.cloned.1.call-start = ((), (), s32[]{:S(2)}) async-start(), calls=%async_computation.57 | async-start | bytes 3538944 | tf_op jit(solution)/shard_map/reduce_scatter | solution.py:451
  1449.0 978.2 %reduce-scatter.55.cloned.1.call-start = ((), (), s32[]{:S(2)}) async-start(), calls=%async_computation.54 | async-start | bytes 1327104 | tf_op jit(solution)/shard_map/reduce_scatter | solution.py:446
  1452.6 1041.7 %reduce-scatter.51.cloned.1.call-start = ((), (), s32[]{:S(2)}) async-start(), calls=%async_computation.52 | async-start | bytes 1327104 | tf_op jit(solution)/shard_map/reduce_scatter | solution.py:444
  1456.4 1104.7 %reduce-scatter.53.cloned.1.call-start = ((), (), s32[]{:S(2)}) async-start(), calls=%async_computation.53 | async-start | bytes 1327104 | tf_op jit(solution)/shard_map/reduce_scatter | solution.py:445
  1459.9 1468.1 %reduce-scatter.71.cloned.1.call-start = ((), (), s32[]{:S(2)}) async-start(), calls=%async_computation.62 | async-start | bytes 26738688 | tf_op jit(solution)/shard_map/reduce_scatter | solution.py:465
  1460.0 144.9 %copy-start.81 = (f32[512]{0:T(512)S(1)}, f32[512]{0:T(512)}, u32[]{:S(2)}) copy-start(f32[512]{0:T(512)} %copy-done.80) | copy-start | bytes 6148
  1460.0 144.9 %copy-start.16 = (bf16[512,768]{1,0:T(8,128)(2,1)S(1)}, bf16[512,768]{1,0:T(8,128)(2,1)}, u32[]{:S(2)}) copy-start(bf16[512,768]{1,0:T(8,128)(2,1)} %reduce-scatter.47.cloned.1.call-done) | copy-start | bytes 2359300
  (77 other events, 630.0 us)
Sparse Core Ops, SparseCore 0:
  40.5 7.0 all-gather.17
  210.5 6.3 reduce-scatter.30
  371.1 9.4 reduce-scatter.32
  469.7 9.8 all-gather.29
  481.6 10.9 all-gather.27
  695.2 10.9 all-gather.31
  714.6 18.8 reduce-scatter.36
  920.8 100.6 reduce-scatter.38
  1025.6 10.9 all-gather.37
  1044.3 34.5 reduce-scatter.40
  1084.9 11.0 all-gather.39
  1105.2 102.3 reduce-scatter.44
  1216.6 10.4 reduce-scatter.42
  1284.7 8.8 all-gather.41
  1322.8 9.2 reduce-scatter.46
  1337.3 11.0 all-gather.43
  1409.6 10.2 reduce-scatter.48
  1423.0 62.6 reduce-scatter.76
  1489.0 61.5 reduce-scatter.74
  1553.7 62.1 reduce-scatter.72
  1621.2 122.7 reduce-scatter.64
  1749.3 122.6 reduce-scatter.66
  1877.3 122.7 reduce-scatter.62
  2005.3 122.6 reduce-scatter.68
  2132.1 73.1 reduce-scatter.56
  2209.3 73.3 reduce-scatter.58
  2286.7 73.2 reduce-scatter.60
  2364.0 63.1 reduce-scatter.54
  2431.2 63.0 reduce-scatter.50
  2498.0 62.9 reduce-scatter.52
  2567.4 360.6 reduce-scatter.70
Sparse Core Ops, SparseCore 1:
  213.0 41.4 all-gather.21
  256.6 42.4 all-gather.23
  301.2 42.4 all-gather.25
  345.9 7.9 all-gather.19
  642.2 50.2 reduce-scatter.34
  718.4 161.4 all-gather.35
  881.8 7.9 all-gather.33
  1416.0 103.1 all-reduce.15
  1522.9 80.2 all-reduce.13
where the time goes:
time: 2950 us; the launch traced here: 2940 us
  waiting for transfers between devices  2140 us (73%)
  blocking collectives  448 us (15%)
  matrix products  123 us (4%)
  other arithmetic  90.1 us (3%)
  local copies, waits for them, and re-layouts  89.9 us (3%)
    reduce_scatter x1, waiting for transfers between devices, on_device(): lax.psum_scatter(head_grads[1], ('slab', 'dp'), scatter_dimension=0, tile...  367 us
    reduce_scatter x10, waiting for transfers between devices, row_sum(): lax.psum_scatter(for_sending(block), 'mp', scatter_dimension=0, tiled=True)  319 us
    all_gather x1, waiting for transfers between devices, on_device(): lax.all_gather(embedding, ('slab', 'dp'), axis=0, tiled=True)  143 us
    reduce_scatter x1, waiting for transfers between devices, on_device(): lax.psum_scatter(grad_query_cross, ('slab', 'dp'), scatter_dimension=0, t...  128 us
    reduce_scatter x1, waiting for transfers between devices, on_device(): lax.psum_scatter(grad_value_cross, ('slab', 'dp'), scatter_dimension=0, t...  128 us
    reduce_scatter x1, waiting for transfers between devices, on_device(): lax.psum_scatter(grad_out_cross, ('slab', 'dp'), scatter_dimension=1, til...  128 us
    reduce_scatter x1, waiting for transfers between devices, on_device(): lax.psum_scatter(grad_key_cross, ('slab', 'dp'), scatter_dimension=0, til...  124 us
    unnamed x45, waiting for transfers between devices  107 us
  transfers between devices with their start and end apart: 44, of which 36 were waited for; matrix products, arithmetic and copies ran while one was open for 2% of the time, Pallas kernels for 0%

commit v1 on v0

v1 whole, which is shorter than its diff:
```python
import jax
import jax.numpy as jnp
from jax import lax
from jax.experimental import pallas as pl
from jax.experimental.pallas import tpu as pltpu
from jax.sharding import PartitionSpec as P

DK = 64
f32 = jnp.float32
bf16 = jnp.bfloat16
epsilon = 1e-06
masked_out = -1000000000.0


def loop_order(count):
    return [0, 2, 4, 6, 7, 5, 3, 1] if count == 8 else None


def swap_core(value):
    return lax.ppermute(value, "mp", [(0, 1), (1, 0)])


def swap_slab(value):
    return lax.ppermute(value, "slab", [(0, 1), (1, 0)])


def to_encoder(value):
    return lax.ppermute(value, "slab", [(1, 0)])


def to_decoder(value):
    return lax.ppermute(value, "slab", [(0, 1)])


def loop_step(value, order, step):
    count = len(order)
    return lax.ppermute(
        value, "dp", [(order[i], order[(i + step) % count]) for i in range(count)]
    )


def held_after(value, earlier):
    return value if earlier is None else lax.optimization_barrier((value, earlier))[0]


def loop_index(offset):
    order = loop_order(lax.axis_size("dp"))
    place_of = jnp.array([order.index(i) for i in range(len(order))], jnp.int32)
    place = place_of[lax.axis_index("dp")]
    return jnp.array(order, jnp.int32)[(place + offset) % len(order)]


def loop_gather(block):
    order = loop_order(lax.axis_size("dp"))
    half = block.shape[0] // 2
    behind, ahead = [block], [block]
    for _ in range(3):
        behind.append(loop_step(behind[-1], order, 1))
        ahead.append(loop_step(ahead[-1], order, -1))
    far = jnp.concatenate(
        [loop_step(behind[3][:half], order, 1), loop_step(ahead[3][half:], order, -1)], 0
    )
    offsets = [0, -1, 1, -2, 2, -3, 3, 4]
    blocks = [block, behind[1], ahead[1], behind[2], ahead[2], behind[3], ahead[3], far]
    return offsets, blocks


def loop_scatter(chunk, rows):
    order = loop_order(lax.axis_size("dp"))
    half = rows // 2
    first = chunk(4)
    right = loop_step(first[:half].astype(bf16), order, 1)
    left = loop_step(first[half:].astype(bf16), order, -1)
    mine = chunk(3)
    right = jnp.concatenate([(mine[:half] + right).astype(bf16), mine[half:].astype(bf16)], 0)
    right = loop_step(right, order, 1)
    mine = chunk(-3)
    left = jnp.concatenate([mine[:half].astype(bf16), (mine[half:] + left).astype(bf16)], 0)
    left = loop_step(left, order, -1)
    for offset in (2, 1):
        right = loop_step((chunk(offset) + right).astype(bf16), order, 1)
        left = loop_step((chunk(-offset) + left).astype(bf16), order, -1)
    return chunk(0) + right.astype(f32) + left.astype(f32)


def assemble(blocks, indices, widths):
    count, (rows, _) = len(blocks), blocks[0].shape

    def body(index_ref, *refs):
        sources, targets = refs[:count], refs[count:]
        for turn in range(count):

            @pl.when(pl.program_id(0) == turn)
            def _():
                first = 0
                for target, width in zip(targets, widths):
                    target[0] = sources[turn][:, first : first + width]
                    first += width

    whole = [pl.BlockSpec(block.shape, lambda i, index: (0, 0)) for block in blocks]
    parts = [pl.BlockSpec((1, rows, width), lambda i, index: (index[i], 0, 0)) for width in widths]
    size = sum(block.size for block in blocks) * 4
    out = pl.pallas_call(
        body,
        out_shape=[jax.ShapeDtypeStruct((count, rows, w), blocks[0].dtype) for w in widths],
        grid_spec=pltpu.PrefetchScalarGridSpec(
            num_scalar_prefetch=1, grid=(count,), in_specs=whole, out_specs=parts
        ),
        cost_estimate=pl.CostEstimate(flops=0, bytes_accessed=size, transcendentals=0),
        name="assemble",
    )(jnp.stack(indices), *blocks)
    return [part.reshape(count * rows, part.shape[2]) for part in out]


def gather_columns(block, widths, earlier=None):
    block = held_after(block, earlier)
    if loop_order(lax.axis_size("dp")) is None:
        rows = lax.all_gather(block, "dp", axis=0, tiled=True)
        cuts = [sum(widths[:i]) for i in range(1, len(widths))]
        return jnp.split(rows, cuts, axis=1), None
    offsets, blocks = loop_gather(block)
    parts = assemble(blocks, [loop_index(offset) for offset in offsets], widths)
    return parts, blocks[-1]


def gather_table(block, first_id, step_id, earlier=None):
    block = held_after(block, earlier)
    rows = block.shape[0]
    line = jnp.arange(rows, dtype=jnp.int32)
    if loop_order(lax.axis_size("dp")) is None:
        table = lax.all_gather(block, "dp", axis=0, tiled=True)
        starts = first_id + step_id * jnp.arange(lax.axis_size("dp"), dtype=jnp.int32)
        return [table], [(starts[:, None] + line[None, :]).reshape(-1)]
    offsets, blocks = loop_gather(block)
    return blocks, [first_id + step_id * loop_index(offset) + line for offset in offsets]


def scatter_rows(parts):
    count = lax.axis_size("dp")
    rows, columns = parts[0].shape[0] // count, parts[0].shape[1]
    if loop_order(count) is None:
        total = sum(part.astype(f32) for part in parts).astype(bf16)
        return lax.psum_scatter(total, "dp", scatter_dimension=0, tiled=True).astype(f32)
    stacks = [part.reshape(count, rows, columns) for part in parts]

    def chunk(offset):
        where = loop_index(offset)
        return sum(
            lax.dynamic_index_in_dim(stack, where, 0, keepdims=False).astype(f32) for stack in stacks
        )

    return loop_scatter(chunk, rows)


def scatter_table(pieces):
    if loop_order(lax.axis_size("dp")) is None:
        return lax.psum_scatter(
            pieces[0].astype(bf16), "dp", scatter_dimension=0, tiled=True
        ).astype(f32)
    offsets = [0, -1, 1, -2, 2, -3, 3, 4]
    return loop_scatter(lambda offset: pieces[offsets.index(offset)].astype(f32), pieces[0].shape[0])


def to_distance(value, distance):
    count = lax.axis_size("dp")
    return lax.ppermute(value, "dp", [(i, (i + distance) % count) for i in range(count)])


def gather_small(value):
    count = lax.axis_size("dp")
    if loop_order(count) is None:
        return lax.all_gather(value, "dp")
    me = lax.axis_index("dp")
    received = [to_distance(value, distance) for distance in range(count - 1, 0, -1)] + [value]
    twice = jnp.stack(received + received)
    return lax.dynamic_slice_in_dim(twice, (count - 1 - me) % count, count, 0)


def scatter_small(pieces):
    count = lax.axis_size("dp")
    if loop_order(count) is None:
        return lax.psum_scatter(pieces, "dp", scatter_dimension=0)
    me = lax.axis_index("dp")
    total = lax.dynamic_index_in_dim(pieces, me, 0, keepdims=False)
    for distance in range(1, count):
        piece = lax.dynamic_index_in_dim(pieces, (me + distance) % count, 0, keepdims=False)
        total = total + to_distance(piece, distance)
    return total


def reroute_plane(rows, source_of):
    count = lax.axis_size("dp")
    pieces = rows.reshape(count, rows.shape[0] // count, rows.shape[1])
    if loop_order(count) is None:
        spread = lax.all_to_all(pieces, "dp", split_axis=0, concat_axis=0, tiled=True)
        back = lax.all_to_all(spread[source_of], "dp", split_axis=0, concat_axis=0, tiled=True)
        return back.reshape(rows.shape)
    me = lax.axis_index("dp")

    def piece_at(stack, where):
        return lax.dynamic_index_in_dim(stack, where, 0, keepdims=False)

    received = [piece_at(pieces, me)]
    for distance in range(1, count):
        received.append(to_distance(piece_at(pieces, (me + distance) % count), distance))
    held = jnp.stack(received)
    final = [piece_at(held, (me - source_of[me]) % count)]
    for distance in range(1, count):
        goal = (me + distance) % count
        final.append(to_distance(piece_at(held, (me - source_of[goal]) % count), distance))
    return assemble(final, [(me - distance) % count for distance in range(count)], [rows.shape[1]])[0]


def reroute_decoder(rows, source_of, decoding):
    half = rows.shape[0] // 2
    lent = jnp.where(decoding, rows[half:], to_encoder(rows[:half]))
    moved = reroute_plane(lent, source_of)
    return jnp.concatenate([to_decoder(moved), moved], 0)


def matmul(a, b):
    return jnp.dot(a, b, preferred_element_type=f32)


def contract_last(a, b):
    return lax.dot_general(a, b, (((1,), (1,)), ((), ())), preferred_element_type=f32)


def contract_first(a, b):
    return lax.dot_general(a, b, (((0,), (0,)), ((), ())), preferred_element_type=f32)


def rms_apply(hidden, gain):
    return hidden * lax.rsqrt(jnp.mean(hidden * hidden, axis=-1, keepdims=True) + epsilon) * gain


def norm_back(hidden, gain, upstream):
    scale = lax.rsqrt(jnp.mean(hidden * hidden, axis=-1, keepdims=True) + epsilon)
    weighted = upstream * gain
    dot = jnp.mean(weighted * hidden, axis=-1, keepdims=True)
    grad = scale * weighted - hidden * (scale * scale * scale * dot)
    return grad, jnp.sum(upstream * hidden * scale, axis=0)


def side(a, pair):
    return jnp.concatenate([matmul(a, pair[0]), matmul(a, pair[1])], 1)


def heads(rows):
    return rows.reshape(rows.shape[0], -1, DK)


def attend(queries, key_rows, value_rows, allowed):
    scores = jnp.einsum("qhd,khd->hqk", heads(queries), heads(key_rows), preferred_element_type=f32)
    scores = jnp.where(allowed[None], scores * DK ** (-0.5), masked_out)
    highest = jnp.max(scores, axis=-1, keepdims=True)
    shifted = jnp.exp(scores - highest)
    totals = jnp.sum(shifted, axis=-1, keepdims=True)
    weights = (shifted / totals).astype(bf16)
    context = jnp.einsum("hqk,khd->qhd", weights, heads(value_rows), preferred_element_type=f32)
    return context.reshape(queries.shape).astype(bf16), highest + jnp.log(totals)


def attend_back(queries, key_rows, value_rows, allowed, log_total, grad_context):
    scale = DK ** (-0.5)
    queries, key_rows, value_rows = heads(queries), heads(key_rows), heads(value_rows)
    grad_heads = heads(grad_context)
    scores = jnp.einsum("qhd,khd->hqk", queries, key_rows, preferred_element_type=f32) * scale
    scores = jnp.where(allowed[None], scores, masked_out)
    weights = jnp.exp(scores - log_total)
    grad_weights = jnp.einsum("qhd,khd->hqk", grad_heads, value_rows, preferred_element_type=f32)
    grad_scores = weights * (grad_weights - jnp.sum(grad_weights * weights, axis=-1, keepdims=True))
    grad_scores = grad_scores.astype(bf16)

    def flat(grad):
        return grad.reshape(grad.shape[0], -1).astype(bf16)

    grad_query = jnp.einsum("hqk,khd->qhd", grad_scores, key_rows, preferred_element_type=f32)
    grad_key = jnp.einsum("hqk,qhd->khd", grad_scores, queries, preferred_element_type=f32)
    grad_value = jnp.einsum(
        "hqk,qhd->khd", weights.astype(bf16), grad_heads, preferred_element_type=f32
    )
    return flat(grad_query * scale), flat(grad_key * scale), flat(grad_value)


def attention_forward(query_in, memory_in, qkv, out, allowed):
    width = qkv[0].shape[1] // 3
    queries = side(query_in, [part[:, :width] for part in qkv]).astype(bf16)
    key_rows = side(memory_in, [part[:, width : 2 * width] for part in qkv]).astype(bf16)
    value_rows = side(memory_in, [part[:, 2 * width :] for part in qkv]).astype(bf16)
    context, log_total = attend(queries, key_rows, value_rows, allowed)
    branch = contract_last(context[:, :width], out[0]) + contract_last(context[:, width:], out[1])
    return branch, (queries, key_rows, value_rows, context, log_total)


def attention_back(kept, qkv, out, allowed, grad_rows):
    queries, key_rows, value_rows, context, log_total = kept
    width = qkv[0].shape[1] // 3
    grad_context = side(grad_rows, out).astype(bf16)
    grads = attend_back(queries, key_rows, value_rows, allowed, log_total, grad_context)

    def into(grad, start):
        return sum(
            contract_last(grad[:, i * width : (i + 1) * width], qkv[i][:, start : start + width])
            for i in range(2)
        )

    grad_query_in = into(grads[0], 0)
    grad_memory = into(grads[1], width) + into(grads[2], 2 * width)
    return grads, grad_query_in, grad_memory


def attention_weight_grads(query_in, memory_in, context, grads, grad_rows):
    width = context.shape[1] // 2
    parts = []
    for i in range(2):
        cut = slice(i * width, (i + 1) * width)
        parts.append(
            jnp.concatenate(
                [
                    contract_first(query_in, grads[0][:, cut]).astype(bf16),
                    contract_first(memory_in, grads[1][:, cut]).astype(bf16),
                    contract_first(memory_in, grads[2][:, cut]).astype(bf16),
                    contract_first(grad_rows, context[:, cut]).astype(bf16),
                ],
                1,
            )
        )
    return parts


def mlp_forward(normed, gate_up, down):
    width = down[0].shape[1]
    both = [matmul(normed, part) for part in gate_up]
    gate_out = [part[:, :width] for part in both]
    up_out = [part[:, width:] for part in both]
    inner = [
        (jax.nn.gelu(gate, approximate=True) * up).astype(bf16) for gate, up in zip(gate_out, up_out)
    ]
    branch = contract_last(inner[0], down[0]) + contract_last(inner[1], down[1])
    return branch, (both, inner)


def gelu_gate(gate_out, up_out):
    return jax.nn.gelu(gate_out, approximate=True) * up_out


def mlp_back(kept, gate_up, down, grad_rows):
    both, _ = kept
    width = down[0].shape[1]
    grads, total = [], 0.0
    for i in range(2):
        grad_inner = matmul(grad_rows, down[i])
        _, pullback = jax.vjp(gelu_gate, both[i][:, :width], both[i][:, width:])
        grad = jnp.concatenate([part.astype(bf16) for part in pullback(grad_inner)], 1)
        grads.append(grad)
        total = total + contract_last(grad, gate_up[i])
    return grads, total


def mlp_weight_grads(normed, inner, grads, grad_rows):
    return [
        jnp.concatenate(
            [
                contract_first(normed, grads[i]).astype(bf16),
                contract_first(grad_rows, inner[i]).astype(bf16),
            ],
            1,
        )
        for i in range(2)
    ]


def merge_stats(first, second):
    highest = jnp.maximum(first[0], second[0])
    totals = first[1] * jnp.exp(first[0] - highest) + second[1] * jnp.exp(second[0] - highest)
    return jnp.stack([highest, totals, first[2] + second[2]])


def on_device(
    states,
    attn_gain,
    w_query,
    w_key,
    w_value,
    w_out,
    mlp_gain,
    w_gate,
    w_up,
    w_down,
    final_gain,
    cross_gain,
    cross_query,
    cross_key,
    cross_value,
    cross_out,
    embedding,
    source_len,
    target_len,
    target_ids,
    pairing,
):
    slab, me, core = (lax.axis_index(name) for name in ("slab", "dp", "mp"))
    decoding = slab == 1
    count = lax.axis_size("dp")
    numbers = jnp.arange(count, dtype=jnp.int32)
    target_of = jnp.sum(
        jnp.where(pairing[None, :] == numbers[:, None], numbers[None, :], 0), axis=1
    )
    target = target_of[me]
    source_length, target_length = source_len[me], target_len[target]

    gain_rows = attn_gain.shape[1]
    cross_rows = cross_gain.shape[0]
    gains = gather_small(
        jnp.concatenate([attn_gain[0], mlp_gain[0], final_gain[0], cross_gain], 0)
    ).astype(f32)
    gain_attn, gain_mlp, gain_final = (
        gains[:, i * gain_rows : (i + 1) * gain_rows].reshape(-1) for i in range(3)
    )
    cross_part = gains[:, 3 * gain_rows :].reshape(-1)
    gain_cross = jnp.concatenate([to_decoder(cross_part), cross_part], 0)
    wanted = lax.dynamic_index_in_dim(gather_small(target_ids[0]), target, 0, keepdims=False)

    rows = states[0, 0]
    own = jnp.where(decoding, reroute_decoder(rows, target_of, decoding), rows)
    other = swap_core(own)

    width, hidden = w_query.shape[2], w_gate.shape[2]
    (qkv, out), last = gather_columns(
        jnp.concatenate([w_query[0], w_key[0], w_value[0], w_out[0].T], 1), [3 * width, width]
    )
    qkv, out = (qkv, swap_core(qkv)), (out, swap_core(out))
    (gate_up, down), last = gather_columns(
        jnp.concatenate([w_gate[0], w_up[0], w_down[0].T], 1), [2 * hidden, hidden], last
    )
    gate_up, down = (gate_up, swap_core(gate_up)), (down, swap_core(down))
    (cross_qkv, cross_o), last = gather_columns(
        jnp.concatenate([cross_query, cross_key, cross_value, cross_out.T], 1),
        [3 * width, width],
        last,
    )
    cross_qkv = jnp.concatenate([to_decoder(cross_qkv), cross_qkv], 0)
    cross_o = jnp.concatenate([to_decoder(cross_o), cross_o], 0)
    cross_qkv, cross_o = (cross_qkv, swap_core(cross_qkv)), (cross_o, swap_core(cross_o))
    vocab_rows = embedding.shape[0]
    cores = lax.axis_size("mp")
    tables, entries = gather_table(
        embedding,
        (slab * count * cores + core) * vocab_rows,
        cores * vocab_rows,
        last,
    )

    half = rows.shape[0]
    line = jnp.arange(half, dtype=jnp.int32)
    query_at = core * half + line
    key_at = jnp.concatenate([query_at, (1 - core) * half + line])
    own_length = jnp.where(decoding, target_length, source_length)
    later = key_at[None, :] > query_at[:, None]
    self_allowed = (key_at[None, :] < own_length) & jnp.logical_not(later & decoding)
    cross_allowed = jnp.broadcast_to(key_at[None, :] < source_length, (half, 2 * half))

    start = own.astype(f32)
    normed = rms_apply(start, gain_attn).astype(bf16)
    normed_all = jnp.concatenate([normed, rms_apply(other.astype(f32), gain_attn).astype(bf16)], 0)
    branch, self_kept = attention_forward(normed, normed_all, qkv, out, self_allowed)
    after_self = start + branch

    normed_enc = rms_apply(after_self, gain_mlp).astype(bf16)
    branch, enc_kept = mlp_forward(normed_enc, gate_up, down)
    after_enc = after_self + branch
    memory = to_decoder(rms_apply(after_enc, gain_final).astype(bf16))
    memory = jnp.concatenate([memory, swap_core(memory)], 0)

    normed_cross = rms_apply(after_self, gain_cross).astype(bf16)
    branch, cross_kept = attention_forward(normed_cross, memory, cross_qkv, cross_o, cross_allowed)
    after_cross = after_self + branch
    normed_dec = rms_apply(after_cross, gain_mlp).astype(bf16)
    branch, dec_kept = mlp_forward(normed_dec, gate_up, down)
    after_mlp = after_cross + branch
    final = rms_apply(after_mlp, gain_final).astype(bf16)

    final = jnp.where(decoding, final, to_encoder(final))
    final = jnp.concatenate([final, swap_core(final)], 0)
    wanted = jnp.where(core == 0, wanted, jnp.roll(wanted, half))
    counted = key_at < target_length
    width_scale = final.shape[1] ** (-0.5)
    logits = [contract_last(final, table) * width_scale for table in tables]
    hits = [ids[None, :] == wanted[:, None] for ids in entries]
    highest = jnp.max(jnp.stack([jnp.max(part, axis=1) for part in logits]), axis=0)
    totals = sum(jnp.sum(jnp.exp(part - highest[:, None]), axis=1) for part in logits)
    picked = sum(jnp.sum(jnp.where(hit, part, 0.0), axis=1) for hit, part in zip(hits, logits))
    stats = jnp.stack([highest, totals, picked])
    flipped = jnp.roll(swap_core(stats), half, axis=1)
    stats = merge_stats(stats, flipped)
    stats = merge_stats(stats, swap_slab(stats))
    log_total = stats[0] + jnp.log(stats[1])
    token_ce = jnp.where(counted, log_total - stats[2], 0.0)
    in_order = jnp.where(core == 0, token_ce, jnp.roll(token_ce, half))
    token_loss = lax.dynamic_index_in_dim(gather_small(in_order), pairing[me], 0, keepdims=True)
    seq_loss = jnp.sum(token_loss, axis=1) / target_len[me].astype(f32)

    grad_logits = [
        jnp.where(
            counted[:, None], jnp.exp(part - log_total[:, None]) - hit.astype(f32), 0.0
        ).astype(bf16)
        for hit, part in zip(hits, logits)
    ]
    grad_final = sum(matmul(part, table) for part, table in zip(grad_logits, tables)) * width_scale
    grad_final = grad_final[:half] + swap_core(grad_final[half:].astype(bf16)).astype(f32)
    grad_final = grad_final + to_decoder(grad_final.astype(bf16)).astype(f32)
    grad_final = jnp.where(decoding, grad_final, 0.0)
    grad_table = [contract_first(part, final) * width_scale for part in grad_logits]
    g_embedding = scatter_table(grad_table)

    stream, grad_gain_final = norm_back(after_mlp, gain_final, grad_final)
    dec_rows = stream.astype(bf16)
    dec_grads, grad_normed = mlp_back(dec_kept, gate_up, down, dec_rows)
    part, grad_gain_mlp = norm_back(after_cross, gain_mlp, grad_normed)
    stream = stream + part
    cross_in = stream.astype(bf16)
    cross_grads, grad_normed, grad_memory = attention_back(
        cross_kept, cross_qkv, cross_o, cross_allowed, cross_in
    )
    grad_memory = grad_memory[:half] + swap_core(grad_memory[half:].astype(bf16)).astype(f32)
    grad_memory = to_encoder(grad_memory.astype(bf16)).astype(f32)
    part, grad_gain_cross = norm_back(after_self, gain_cross, grad_normed)
    stream = stream + part
    cross_weights = attention_weight_grads(
        normed_cross, memory, cross_kept[3], cross_grads, cross_in
    )

    enc_stream, gain_part = norm_back(after_enc, gain_final, grad_memory)
    grad_gain_final = grad_gain_final + gain_part
    enc_rows = enc_stream.astype(bf16)
    enc_grads, grad_normed = mlp_back(enc_kept, gate_up, down, enc_rows)
    part, gain_part = norm_back(after_self, gain_mlp, grad_normed)
    grad_gain_mlp = grad_gain_mlp + gain_part
    stream = stream + enc_stream + part
    mlp_weights = lax.cond(
        decoding,
        lambda dec, enc: mlp_weight_grads(*dec),
        lambda dec, enc: mlp_weight_grads(*enc),
        (normed_dec, dec_kept[1], dec_grads, dec_rows),
        (normed_enc, enc_kept[1], enc_grads, enc_rows),
    )

    self_in = stream.astype(bf16)
    self_grads, grad_normed, grad_keyside = attention_back(
        self_kept, qkv, out, self_allowed, self_in
    )
    grad_normed = grad_normed + grad_keyside[:half]
    grad_normed = grad_normed + swap_core(grad_keyside[half:].astype(bf16)).astype(f32)
    part, grad_gain_attn = norm_back(start, gain_attn, grad_normed)
    stream = stream + part
    self_weights = attention_weight_grads(normed, normed_all, self_kept[3], self_grads, self_in)
    d_states = jnp.where(
        decoding, reroute_decoder(stream.astype(bf16), pairing, decoding).astype(f32), stream
    )

    def owned(parts):
        return scatter_rows([parts[0], swap_core(parts[1])])

    def plane_half(value):
        top, bottom = value[: value.shape[0] // 2], value[value.shape[0] // 2 :]
        return jnp.where(decoding, bottom, to_encoder(top))

    g_cross = owned([plane_half(part) for part in cross_weights])
    g_mlp = owned(mlp_weights)
    g_attn = owned(self_weights)

    gain_grads = jnp.stack([grad_gain_attn, grad_gain_mlp, grad_gain_final, grad_gain_cross])
    gain_grads = gain_grads + swap_core(gain_grads)
    packed = jnp.concatenate(
        [gain_grads[i].reshape(count, gain_rows) for i in range(3)]
        + [plane_half(gain_grads[3]).reshape(count, cross_rows)],
        1,
    )
    gain_own = scatter_small(packed)[None]

    return (
        seq_loss,
        d_states[None, None],
        gain_own[:, :gain_rows],
        g_attn[None, :, :width],
        g_attn[None, :, width : 2 * width],
        g_attn[None, :, 2 * width : 3 * width],
        g_attn[:, 3 * width :].T[None],
        gain_own[:, gain_rows : 2 * gain_rows],
        g_mlp[None, :, :hidden],
        g_mlp[None, :, hidden : 2 * hidden],
        g_mlp[:, 2 * hidden :].T[None],
        gain_own[:, 2 * gain_rows : 3 * gain_rows],
        gain_own[0, 3 * gain_rows :],
        g_cross[:, :width],
        g_cross[:, width : 2 * width],
        g_cross[:, 2 * width : 3 * width],
        g_cross[:, 3 * width :].T,
        g_embedding,
        token_loss,
    )


def solution(mesh):
    layer = P("slab", "dp", "mp")
    shared = P(("slab", "dp"), "mp")
    gain = P("slab", "dp")
    turned = P("slab", "mp", "dp")
    tokens = P("slab", "dp", "mp", None)
    weights = (gain, layer, layer, layer, turned, gain, layer, layer, turned, gain)
    crossing = (P(("slab", "dp")), shared, shared, shared, P("mp", ("slab", "dp")))
    table = P(("slab", "dp", "mp"), None)
    return jax.shard_map(
        on_device,
        mesh=mesh,
        in_specs=(tokens,) + weights + crossing + (table, P(), P(), P("dp", None), P()),
        out_specs=(P("dp"), tokens) + weights + crossing + (table, P("dp", None)),
        check_vma=False,
    )
```

time: 2950 us -> 1100 us (0.37)
  waiting for transfers between devices: 2140 us -> 253 us
  blocking collectives: 448 us -> 0 us
  matrix products: 123 us -> 322 us
  starting transfers between devices: 20.5 us -> 182 us
  other arithmetic: 90.1 us -> 154 us
    reduce_scatter x21 -> x0, waiting for transfers between devices: 1630 us -> none  [the longest x1 367 us: on_device(): lax.psum_scatter(head_grads[1], ('slab', 'dp'), scatter_dimension=0, tile...]
    all_gather x14 -> x0, waiting for transfers between devices: 340 us -> none  [the longest x1 143 us: on_device(): lax.all_gather(embedding, ('slab', 'dp'), axis=0, tiled=True)]
    all_gather x11 -> x0, blocking collectives: 299 us -> none  [the longest x1 43.3 us: on_device(): lax.all_gather(cross_query, ('slab', 'dp'), axis=0, tiled=True)]
    ppermute x2 -> x152, waiting for transfers between devices: 27.9 us -> 253 us  [the longest x64 102 us: loop_step(): lax.ppermute(value, 'dp', [(order[i], order[(i + step) % count]) for i in...]
    ppermute x2 -> x152, starting transfers between devices: 8.52 us -> 182 us  [the longest x56 84.2 us: to_distance(): lax.ppermute(value, 'dp', [(i, (i + distance) % count) for i in range(cou...]
    dot_general x24 -> x100, matrix products: 97.9 us -> 266 us  [the longest x32 67.3 us: matmul(): return jnp.dot(a, b, preferred_element_type=f32)]
    unnamed x45 -> x0, waiting for transfers between devices: 107 us -> none
    unnamed x3 -> x0, blocking collectives: 103 us -> none
  transfers between devices with their start and end apart: 44 -> 152, of which waited for: 36 -> 56; matrix products, arithmetic and copies ran while one was open for 2% -> 46% of each run, Pallas kernels for 0% -> 2%
where the time goes in v1:
time: 1100 us; the launch traced here: 1080 us
  matrix products  322 us (29%)
  waiting for transfers between devices  253 us (23%)
  starting transfers between devices  182 us (17%)
  other arithmetic  154 us (14%)
  local copies, waits for them, and re-layouts  95.4 us (9%)
  between operations  50.5 us (5%)
  Pallas kernels  25.7 us (2%)
    ppermute x64, waiting for transfers between devices, loop_step(): lax.ppermute(value, 'dp', [(order[i], order[(i + step) % count]) for i in...  102 us
    ppermute x56, starting transfers between devices, to_distance(): lax.ppermute(value, 'dp', [(i, (i + distance) % count) for i in range(cou...  84.2 us
    ppermute x64, starting transfers between devices, loop_step(): lax.ppermute(value, 'dp', [(order[i], order[(i + step) % count]) for i in...  67.6 us
    dot_general x32, matrix products, matmul(): return jnp.dot(a, b, preferred_element_type=f32)  67.3 us
    dot_general x32, matrix products, contract_last(): lax.dot_general(a, b, (((1,), (1,)), ((), ())), preferred_element_type=f32)  66.3 us
    ppermute x56, waiting for transfers between devices, to_distance(): lax.ppermute(value, 'dp', [(i, (i + distance) % count) for i in range(cou...  62 us
    ppermute x7, waiting for transfers between devices, to_encoder(): return lax.ppermute(value, 'slab', [(1, 0)])  54.4 us
    dot_general x28, matrix products, contract_first(): lax.dot_general(a, b, (((0,), (0,)), ((), ())), preferred_element_type=f32)  53.7 us
  transfers between devices with their start and end apart: 152, of which 56 were waited for; matrix products, arithmetic and copies ran while one was open for 46% of the time, Pallas kernels for 2%

profile of v1, /device:TPU:0, one launch (start us, length us, event | category | flops | bytes accessed | tf_op | source)
XLA Modules:
  0.0 1083.1 jit_solution(1660942535861225100)
XLA Ops:
  1.5 6.0 collective-permute-start.16
  32.2 5.9 collective-permute-done.2
  38.1 5.9 collective-permute-done.3
  44.0 5.1 collective-permute-done.4
  49.8 4.3 collective-permute-done.5
  93.2 5.8 stack.252.index_ref
  101.2 4.2 assemble.5
  105.4 4.9 collective-permute-start.15
  130.0 5.5 assemble.6
  149.5 8.7 collective-permute-done.36.refs_3_
  166.6 10.9 %fusion.13 = (f32[12,512]{1,0:T(8,128)S(1)}, f32[12,512,1024]{2,1,0:T(8,128)}) fusion(pred[512,1024]{1,0:T(8,128)(4,1)S(1)} %not_and_fusion, bf16[1024,6,64]{0,2,1:T(8,128)(2,1)S(1)} %bitcast.597, bf16[1024,6,64]{0,2,1:T(8,128)(2,1)S(1)} %bitcast.595, bf16[512,6,64]{0,2,1:T(8,128)(2,1)S(1)} %convolution_convert_fusion.38, ...), kind=kOutput, calls=%fused_computation.35 | convolution fusion | flops 825354240 | bytes 28073984 | tf_op jit(solution)/shard_map/qhd,khd->hqk/dot_general | solution.py:254
  179.3 11.8 %fusion = f32[12,512]{1,0:T(8,128)S(1)} fusion(f32[12,512]{1,0:T(8,128)S(1)} %get-tuple-element.278, f32[12,512,1024]{2,1,0:T(8,128)} %get-tuple-element.279, pred[512,1024]{1,0:T(8,128)(4,1)S(1)} %not_and_fusion), kind=kLoop, calls=%fused_computation.24 | loop fusion | flops 25159680 | bytes 25739264 | tf_op jit(solution)/shard_map/reduce_sum | solution.py:258
  196.2 5.4 collective-permute-done.41
  202.5 6.8 assemble.7
  211.3 12.3 %fusion.100 = bf16[12,64,512]{2,1,0:T(8,128)(2,1)S(1)} fusion(f32[12,512]{1,0:T(8,128)S(1)} %fusion, f32[12,512]{1,0:T(8,128)S(1)} %get-tuple-element.278, f32[12,512,1024]{2,1,0:T(8,128)} %get-tuple-element.279, pred[512,1024]{1,0:T(8,128)(4,1)S(1)} %not_and_fusion, bf16[1024,6,64]{0,2,1:T(8,128)(2,1)} %bitcast.609, bf16[1024,6,64]{0,2,1:T(8,128)(2,1)S(1)} %bitcast.607), kind=kOutput, calls=%fused_computation.260 | convolution fusion | flops 837943296 | bytes 28098560 | tf_op jit(solution)/shard_map/hqk,khd->qhd/dot_general | solution.py:260
  245.5 5.1 assemble.8
  252.6 4.2 fusion.309
  258.8 9.1 collective-permute-done.54
  276.5 4.5 collective-permute-start.44
  284.4 14.4 %collective-permute-done.44 = bf16[512,768]{1,0:T(8,128)(2,1)S(1)} collective-permute-done((bf16[512,768]{1,0:T(8,128)(2,1)S(1)}, bf16[512,768]{1,0:T(8,128)(2,1)S(1)}, u32[]{:S(2)}, u32[]{:S(2)}) %collective-permute-start.44) | collective-permute-done | bytes 786464 | tf_op jit(solution)/shard_map/ppermute | solution.py:32
  298.8 5.8 collective-permute-done.57
  310.0 10.4 fusion.12
  320.4 11.2 %fusion.1 = f32[12,512]{1,0:T(8,128)S(1)} fusion(f32[12,512]{1,0:T(8,128)S(1)} %get-tuple-element.284, f32[12,512,1024]{2,1,0:T(8,128)} %get-tuple-element.285, pred[1024]{0:T(1024)(128)(4,1)S(1)} %copy-done.205), kind=kLoop, calls=%fused_computation.25 | loop fusion | flops 25159680 | bytes 25216000 | tf_op jit(solution)/shard_map/reduce_sum | solution.py:258
  333.4 11.9 %fusion.99 = bf16[12,64,512]{2,1,0:T(8,128)(2,1)S(1)} fusion(f32[12,512]{1,0:T(8,128)S(1)} %fusion.1, f32[12,512]{1,0:T(8,128)S(1)} %get-tuple-element.284, f32[12,512,1024]{2,1,0:T(8,128)} %get-tuple-element.285, pred[1024]{0:T(1024)(128)(4,1)S(1)} %copy-done.205, bf16[1024,6,64]{0,2,1:T(8,128)(2,1)S(1)} %bitcast.613, bf16[1024,6,64]{0,2,1:T(8,128)(2,1)S(1)} %bitcast.611), kind=kOutput, calls=%fused_computation.259 | convolution fusion | flops 837943296 | bytes 27575296 | tf_op jit(solution)/shard_map/hqk,khd->qhd/dot_general | solution.py:260
  352.4 4.1 fusion.313
  378.8 6.1 collective-permute-done.59
  460.4 5.8 exponential_reduce_fusion
  474.7 4.2 collective-permute-start.78
  513.4 4.1 fusion.263
  517.5 5.2 add_multiply_fusion
  522.8 4.9 fusion.275
  556.1 9.8 collective-permute-done.145
  585.1 4.5 fusion.284
  596.0 21.3 %multiply_reduce_fusion.1 = (f32[12,512]{1,0:T(8,128)S(1)}, f32[12,512,1024]{2,1,0:T(8,128)}) fusion(f32[12,512]{1,0:T(8,128)S(1)} %copy-done.149, f32[12,512,1024]{2,1,0:T(8,128)} %get-tuple-element.285, pred[1024]{0:T(1024)(128)(4,1)S(1)} %copy-done.206, bf16[1024,6,64]{0,2,1:T(8,128)(2,1)S(1)} %bitcast.614, bf16[1024,6,64]{0,2,1:T(8,128)(2,1)S(1)} %bitcast.612, ...), kind=kOutput, calls=%fused_computation.16 | convolution fusion | flops 837937152 | bytes 52741120 | tf_op jit(solution)/shard_map/qhd,khd->hqk/dot_general | solution.py:271
  617.3 11.1 %fusion.76 = bf16[12,64,1024]{2,1,0:T(8,128)(2,1)S(1)} fusion(f32[12,512]{1,0:T(8,128)S(1)} %copy-done.149, f32[12,512,1024]{2,1,0:T(8,128)} %get-tuple-element.285, pred[1024]{0:T(1024)(128)(4,1)S(1)} %copy-done.206, bf16[512,6,64]{0,2,1:T(8,128)(2,1)S(1)} %bitcast.623, bf16[512,6,64]{0,2,1:T(8,128)(2,1)S(1)} %bitcast.621), kind=kOutput, calls=%fused_computation.181 | convolution fusion | flops 831651840 | bytes 27550720 | tf_op jit(solution)/shard_map/hqk,qhd->khd/dot_general | solution.py:280
  629.0 17.2 %multiply_convert_fusion.1 = bf16[12,512,1024]{2,1,0:T(8,128)(2,1)S(1)} fusion(f32[12,512,1024]{2,1,0:T(8,128)} %get-tuple-element.308, f32[12,512]{1,0:T(8,128)S(1)} %get-tuple-element.307, f32[12,512]{1,0:T(8,128)S(1)} %copy-done.149, f32[12,512,1024]{2,1,0:T(8,128)} %get-tuple-element.285, pred[1024]{0:T(1024)(128)(4,1)S(1)} %copy-done.206), kind=kLoop, calls=%fused_computation.15 | loop fusion | flops 37748736 | bytes 62964736 | tf_op jit(solution)/shard_map/convert_element_type | solution.py:273
  646.2 4.5 copy-done
  653.1 8.6 multiply_convert_fusion.14
  692.2 7.4 collective-permute-done.133
  703.1 21.8 %collective-permute-done.134 = bf16[384,1536]{0,1:T(8,128)(2,1)} collective-permute-done((bf16[384,1536]{0,1:T(8,128)(2,1)}, bf16[384,1536]{0,1:T(8,128)(2,1)}, u32[]{:S(2)}, u32[]{:S(2)}) %collective-permute-start.134) | collective-permute-done | bytes 1179680 | tf_op jit(solution)/shard_map/ppermute | solution.py:28
  730.5 9.5 collective-permute-done.88
  761.8 18.0 %multiply_reduce_fusion = (f32[12,512]{1,0:T(8,128)S(1)}, f32[12,512,1024]{2,1,0:T(8,128)}) fusion(f32[12,512]{1,0:T(8,128)S(1)} %copy-done.152, f32[12,512,1024]{2,1,0:T(8,128)} %get-tuple-element.279, pred[512,1024]{1,0:T(8,128)(4,1)S(1)} %copy-done.18, bf16[1024,6,64]{0,2,1:T(8,128)(2,1)} %bitcast.610, bf16[1024,6,64]{0,2,1:T(8,128)(2,1)S(1)} %bitcast.608, ...), kind=kOutput, calls=%fused_computation.13 | convolution fusion | flops 837937152 | bytes 53264384 | tf_op jit(solution)/shard_map/qhd,khd->hqk/dot_general | solution.py:271
  779.9 21.7 %multiply_convert_fusion = bf16[12,512,1024]{2,1,0:T(8,128)(2,1)} fusion(f32[12,512,1024]{2,1,0:T(8,128)} %get-tuple-element.311, f32[12,512]{1,0:T(8,128)S(1)} %get-tuple-element.310, f32[12,512]{1,0:T(8,128)S(1)} %copy-done.152, f32[12,512,1024]{2,1,0:T(8,128)} %get-tuple-element.279, pred[512,1024]{1,0:T(8,128)(4,1)S(1)} %copy-done.18), kind=kLoop, calls=%fused_computation.12 | loop fusion | flops 37748736 | bytes 63488000 | tf_op jit(solution)/shard_map/convert_element_type | solution.py:273
  801.6 8.6 multiply_convert_fusion.13
  810.2 7.2 multiply_convert_fusion.2
  817.4 12.1 %fusion.79 = bf16[12,64,1024]{2,1,0:T(8,128)(2,1)S(1)} fusion(f32[12,512]{1,0:T(8,128)S(1)} %copy-done.152, f32[12,512,1024]{2,1,0:T(8,128)} %get-tuple-element.279, pred[512,1024]{1,0:T(8,128)(4,1)S(1)} %copy-done.18, bf16[512,6,64]{0,2,1:T(8,128)(2,1)S(1)} %bitcast.619, bf16[512,6,64]{0,2,1:T(8,128)(2,1)S(1)} %convolution_convert_fusion.33), kind=kOutput, calls=%fused_computation.182 | convolution fusion | flops 831651840 | bytes 28073984 | tf_op jit(solution)/shard_map/hqk,qhd->khd/dot_general | solution.py:280
  844.8 4.4 copy.197
  852.2 10.1 conditional.1
  877.0 4.7 fusion.96
  912.5 7.9 collective-permute-done.90
  922.9 4.9 collective-permute-done.91
  927.8 5.9 collective-permute-done.92
  933.7 5.9 collective-permute-done.93
  939.6 5.2 collective-permute-done.94
  944.8 5.0 collective-permute-done.95
  977.7 4.6 collective-permute-done.98.refs_1_
  984.0 4.2 assemble.9
  992.3 4.3 copy.198
  1000.6 5.7 collective-permute-done.116
  1008.5 6.2 collective-permute-done.117
  1020.7 7.9 collective-permute-done.125
  1031.0 8.2 collective-permute-done.126
  1043.5 12.8 %collective-permute-done.127 = bf16[96,3072]{1,0:T(8,128)(2,1)S(1)} collective-permute-done((bf16[96,3072]{1,0:T(8,128)(2,1)S(1)}, bf16[96,3072]{1,0:T(8,128)(2,1)S(1)}, u32[]{:S(2)}, u32[]{:S(2)}) %collective-permute-start.127) | collective-permute-done | bytes 589856 | tf_op jit(solution)/shard_map/ppermute | solution.py:37
  1074.5 4.8 collective-permute-done.132
  (1085 shorter events, 532.1 us)
Async XLA Ops:
  1.5 62.4 %collective-permute-start.16 = (bf16[336]{0:T(512)(128)(2,1)S(1)}, bf16[336]{0:T(512)(128)(2,1)S(1)}, u32[]{:S(2)}, u32[]{:S(2)}) collective-permute-start(bf16[336]{0:T(512)(128)(2,1)S(1)} %pad_maximum_fusion.59), channel_id=1, source_target_pairs={{0,14},{2,0},{4,2},{6,4},{8,6},{10,8},{12,10},{14,12},{1,15},{3,1}... | collective-permute-start | bytes 2024 | tf_op jit(solution)/shard_map/ppermute | solution.py:166
  7.5 58.4 %collective-permute-start.17 = (bf16[336]{0:T(512)(128)(2,1)S(1)}, bf16[336]{0:T(512)(128)(2,1)S(1)}, u32[]{:S(2)}, u32[]{:S(2)}) collective-permute-start(bf16[336]{0:T(512)(128)(2,1)S(1)} %pad_maximum_fusion.59), channel_id=1, source_target_pairs={{0,12},{2,14},{4,0},{6,2},{8,4},{10,6},{12,8},{14,10},{1,13},{3,15... | collective-permute-start | bytes 2024 | tf_op jit(solution)/shard_map/ppermute | solution.py:166
  8.0 60.0 %collective-permute-start.18 = (bf16[336]{0:T(512)(128)(2,1)S(1)}, bf16[336]{0:T(512)(128)(2,1)S(1)}, u32[]{:S(2)}, u32[]{:S(2)}) collective-permute-start(bf16[336]{0:T(512)(128)(2,1)S(1)} %pad_maximum_fusion.59), channel_id=1, source_target_pairs={{0,10},{2,12},{4,14},{6,0},{8,2},{10,4},{12,6},{14,8},{1,11},{3,13... | collective-permute-start | bytes 2024 | tf_op jit(solution)/shard_map/ppermute | solution.py:166
  8.0 61.9 %collective-permute-start.19 = (bf16[336]{0:T(512)(128)(2,1)S(1)}, bf16[336]{0:T(512)(128)(2,1)S(1)}, u32[]{:S(2)}, u32[]{:S(2)}) collective-permute-start(bf16[336]{0:T(512)(128)(2,1)S(1)} %pad_maximum_fusion.59), channel_id=1, source_target_pairs={{0,8},{2,10},{4,12},{6,14},{8,0},{10,2},{12,4},{14,6},{1,9},{3,11}... | collective-permute-start | bytes 2024 | tf_op jit(solution)/shard_map/ppermute | solution.py:166
  77.0 34.9 %collective-permute-start.26 = (bf16[96,1536]{1,0:T(8,128)(2,1)S(1)}, bf16[96,1536]{1,0:T(8,128)(2,1)S(1)}, u32[]{:S(2)}, u32[]{:S(2)}) collective-permute-start(bf16[96,1536]{1,0:T(8,128)(2,1)S(1)} %collective-permute-done.24.refs_1_), channel_id=1, source_target_pairs={{0,4},{4,8},{8,12},{12,14},{14,10},{10,6},{6,2},{2,0},{1,5},{5,9},... | collective-permute-start | bytes 884744 | tf_op jit(solution)/shard_map/ppermute | solution.py:37
  78.8 20.3 %collective-permute-start.13 = (bf16[32,768]{1,0:T(8,128)(2,1)S(1)}, bf16[32,768]{1,0:T(8,128)(2,1)S(1)}, u32[]{:S(2)}, u32[]{:S(2)}) collective-permute-start(bf16[32,768]{1,0:T(8,128)(2,1)S(1)} %get-tuple-element.206), channel_id=1, source_target_pairs={{0,12},{2,14},{4,0},{6,2},{8,4},{10,6},{12,8},{14,10},{1,13},{3,15... | collective-permute-start | bytes 147464 | tf_op jit(solution)/shard_map/ppermute | solution.py:166
  80.8 19.8 %collective-permute-start.14 = (bf16[32,768]{1,0:T(8,128)(2,1)S(1)}, bf16[32,768]{1,0:T(8,128)(2,1)S(1)}, u32[]{:S(2)}, u32[]{:S(2)}) collective-permute-start(bf16[32,768]{1,0:T(8,128)(2,1)S(1)} %get-tuple-element.205), channel_id=1, source_target_pairs={{0,14},{2,0},{4,2},{6,4},{8,6},{10,8},{12,10},{14,12},{1,15},{3,1}... | collective-permute-start | bytes 147464 | tf_op jit(solution)/shard_map/ppermute | solution.py:166
  82.3 18.2 %collective-permute-start.8 = (bf16[32,768]{1,0:T(8,128)(2,1)S(1)}, bf16[32,768]{1,0:T(8,128)(2,1)S(1)}, u32[]{:S(2)}, u32[]{:S(2)}) collective-permute-start(bf16[32,768]{1,0:T(8,128)(2,1)S(1)} %get-tuple-element.211), channel_id=1, source_target_pairs={{0,2},{2,4},{4,6},{6,8},{8,10},{10,12},{12,14},{14,0},{1,3},{3,5},... | collective-permute-start | bytes 147464 | tf_op jit(solution)/shard_map/ppermute | solution.py:166
  82.9 17.7 %collective-permute-start.9 = (bf16[32,768]{1,0:T(8,128)(2,1)S(1)}, bf16[32,768]{1,0:T(8,128)(2,1)S(1)}, u32[]{:S(2)}, u32[]{:S(2)}) collective-permute-start(bf16[32,768]{1,0:T(8,128)(2,1)S(1)} %get-tuple-element.210), channel_id=1, source_target_pairs={{0,4},{2,6},{4,8},{6,10},{8,12},{10,14},{12,0},{14,2},{1,5},{3,7},... | collective-permute-start | bytes 147464 | tf_op jit(solution)/shard_map/ppermute | solution.py:166
  120.9 24.4 %collective-permute-start.23 = (bf16[512,768]{1,0:T(8,128)(2,1)S(1)}, bf16[512,768]{1,0:T(8,128)(2,1)S(1)}, u32[]{:S(2)}, u32[]{:S(2)}) collective-permute-start(bf16[512,768]{1,0:T(8,128)(2,1)S(1)} %get-tuple-element.152), channel_id=1, source_target_pairs={{0,1},{1,0},{2,3},{3,2},{4,5},{5,4},{6,7},{7,6},{8,9},{9,8},{10,11... | collective-permute-start | bytes 2359304 | tf_op jit(solution)/shard_map/ppermute | solution.py:20
  128.0 15.2 %collective-permute-start.34 = (bf16[96,3072]{1,0:T(8,128)(2,1)}, bf16[96,3072]{1,0:T(8,128)(2,1)}, u32[]{:S(2)}, u32[]{:S(2)}) collective-permute-start(bf16[96,3072]{1,0:T(8,128)(2,1)} %pad_maximum_fusion.33.refs_0_), channel_id=1, source_target_pairs={{0,4},{4,8},{8,12},{12,14},{14,10},{10,6},{6,2},{2,0},{1,5},{5,9},... | collective-permute-start | bytes 1769480 | tf_op jit(solution)/shard_map/ppermute | solution.py:37
  128.1 15.9 %collective-permute-start.35 = (bf16[96,3072]{1,0:T(8,128)(2,1)}, bf16[96,3072]{1,0:T(8,128)(2,1)}, u32[]{:S(2)}, u32[]{:S(2)}) collective-permute-start(bf16[96,3072]{1,0:T(8,128)(2,1)} %pad_maximum_fusion.33.refs_0_), channel_id=1, source_target_pairs={{0,2},{4,0},{8,4},{12,8},{14,12},{10,14},{6,10},{2,6},{1,3},{5,1},... | collective-permute-start | bytes 1769480 | tf_op jit(solution)/shard_map/ppermute | solution.py:37
  135.5 24.9 %collective-permute-start.32 = (bf16[768,1152]{1,0:T(8,128)(2,1)}, bf16[768,1152]{1,0:T(8,128)(2,1)}, u32[]{:S(2)}, u32[]{:S(2)}) collective-permute-start(bf16[768,1152]{1,0:T(8,128)(2,1)} %bitcast.563), channel_id=1, source_target_pairs={{0,1},{1,0},{2,3},{3,2},{4,5},{5,4},{6,7},{7,6},{8,9},{9,8},{10,11... | collective-permute-start | bytes 5308424 | tf_op jit(solution)/shard_map/ppermute | solution.py:20
  139.5 86.2 %collective-permute-start.33 = (bf16[768,384]{1,0:T(8,128)(2,1)}, bf16[768,384]{1,0:T(8,128)(2,1)}, u32[]{:S(2)}, u32[]{:S(2)}) collective-permute-start(bf16[768,384]{1,0:T(8,128)(2,1)} %bitcast.570), channel_id=1, source_target_pairs={{0,1},{1,0},{2,3},{3,2},{4,5},{5,4},{6,7},{7,6},{8,9},{9,8},{10,11... | collective-permute-start | bytes 1769480 | tf_op jit(solution)/shard_map/ppermute | solution.py:20
  143.2 14.9 %collective-permute-start.36 = (bf16[96,3072]{1,0:T(8,128)(2,1)}, bf16[96,3072]{1,0:T(8,128)(2,1)}, u32[]{:S(2)}, u32[]{:S(2)}) collective-permute-start(bf16[96,3072]{1,0:T(8,128)(2,1)} %collective-permute-done.34.refs_1_), channel_id=1, source_target_pairs={{0,4},{4,8},{8,12},{12,14},{14,10},{10,6},{6,2},{2,0},{1,5},{5,9},... | collective-permute-start | bytes 1769480 | tf_op jit(solution)/shard_map/ppermute | solution.py:37
  144.1 14.8 %collective-permute-start.37 = (bf16[96,3072]{1,0:T(8,128)(2,1)}, bf16[96,3072]{1,0:T(8,128)(2,1)}, u32[]{:S(2)}, u32[]{:S(2)}) collective-permute-start(bf16[96,3072]{1,0:T(8,128)(2,1)} %collective-permute-done.35.refs_2_), channel_id=1, source_target_pairs={{0,2},{4,0},{8,4},{12,8},{14,12},{10,14},{6,10},{2,6},{1,3},{5,1},... | collective-permute-start | bytes 1769480 | tf_op jit(solution)/shard_map/ppermute | solution.py:37
  158.1 19.4 %collective-permute-start.38 = (bf16[96,3072]{1,0:T(8,128)(2,1)}, bf16[96,3072]{1,0:T(8,128)(2,1)}, u32[]{:S(2)}, u32[]{:S(2)}) collective-permute-start(bf16[96,3072]{1,0:T(8,128)(2,1)} %collective-permute-done.36.refs_3_), channel_id=1, source_target_pairs={{0,4},{4,8},{8,12},{12,14},{14,10},{10,6},{6,2},{2,0},{1,5},{5,9},... | collective-permute-start | bytes 1769480 | tf_op jit(solution)/shard_map/ppermute | solution.py:37
  158.8 35.0 %collective-permute-start.39 = (bf16[96,3072]{1,0:T(8,128)(2,1)}, bf16[96,3072]{1,0:T(8,128)(2,1)}, u32[]{:S(2)}, u32[]{:S(2)}) collective-permute-start(bf16[96,3072]{1,0:T(8,128)(2,1)} %collective-permute-done.37.refs_4_), channel_id=1, source_target_pairs={{0,2},{4,0},{8,4},{12,8},{14,12},{10,14},{6,10},{2,6},{1,3},{5,1},... | collective-permute-start | bytes 1769480 | tf_op jit(solution)/shard_map/ppermute | solution.py:37
  178.5 17.7 %collective-permute-start.40 = (bf16[48,3072]{1,0:T(8,128)(2,1)S(1)}, bf16[48,3072]{1,0:T(8,128)(2,1)S(1)}, u32[]{:S(2)}, u32[]{:S(2)}) collective-permute-start(bf16[48,3072]{1,0:T(8,128)(2,1)S(1)} %slice.604), channel_id=1, source_target_pairs={{0,4},{4,8},{8,12},{12,14},{14,10},{10,6},{6,2},{2,0},{1,5},{5,9},... | collective-permute-start | bytes 884744 | tf_op jit(solution)/shard_map/ppermute | solution.py:37
  209.3 58.9 %collective-permute-start.42 = (bf16[768,2048]{1,0:T(8,128)(2,1)}, bf16[768,2048]{1,0:T(8,128)(2,1)}, u32[]{:S(2)}, u32[]{:S(2)}) collective-permute-start(bf16[768,2048]{1,0:T(8,128)(2,1)} %bitcast.687), channel_id=1, source_target_pairs={{0,1},{1,0},{2,3},{3,2},{4,5},{5,4},{6,7},{7,6},{8,9},{9,8},{10,11... | collective-permute-start | bytes 9437192 | tf_op jit(solution)/shard_map/ppermute | solution.py:20
  209.3 14.5 %collective-permute-start.46 = (bf16[48,1536]{1,0:T(8,128)(2,1)S(1)}, bf16[48,1536]{1,0:T(8,128)(2,1)S(1)}, u32[]{:S(2)}, u32[]{:S(2)}) collective-permute-start(bf16[48,1536]{1,0:T(8,128)(2,1)S(1)} %pad_maximum_fusion.48.refs_0_), channel_id=1, source_target_pairs={{0,4},{4,8},{8,12},{12,14},{14,10},{10,6},{6,2},{2,0},{1,5},{5,9},... | collective-permute-start | bytes 442376 | tf_op jit(solution)/shard_map/ppermute | solution.py:37
  250.5 17.4 %collective-permute-start.54 = (bf16[384,1152]{1,0:T(8,128)(2,1)}, bf16[384,1152]{1,0:T(8,128)(2,1)S(1)}, u32[]{:S(2)}, u32[]{:S(2)}) collective-permute-start(bf16[384,1152]{1,0:T(8,128)(2,1)} %bitcast.504), channel_id=1, source_target_pairs={{0,16},{1,17},{2,18},{3,19},{4,20},{5,21},{6,22},{7,23},{8,24},{9,... | collective-permute-start | bytes 2654216 | tf_op jit(solution)/shard_map/ppermute | solution.py:32
  252.6 21.4 %collective-permute-start.43 = (bf16[768,1024]{1,0:T(8,128)(2,1)S(1)}, bf16[768,1024]{1,0:T(8,128)(2,1)S(1)}, u32[]{:S(2)}, u32[]{:S(2)}) collective-permute-start(bf16[768,1024]{1,0:T(8,128)(2,1)S(1)} %bitcast.534), channel_id=1, source_target_pairs={{0,1},{1,0},{2,3},{3,2},{4,5},{5,4},{6,7},{7,6},{8,9},{9,8},{10,11... | collective-permute-start | bytes 4718600 | tf_op jit(solution)/shard_map/ppermute | solution.py:20
  268.1 39.5 %collective-permute-start.55 = (bf16[768,1152]{1,0:T(8,128)(2,1)S(1)}, bf16[768,1152]{1,0:T(8,128)(2,1)S(1)}, u32[]{:S(2)}, u32[]{:S(2)}) collective-permute-start(bf16[768,1152]{1,0:T(8,128)(2,1)S(1)} %pad_maximum_fusion.4), channel_id=1, source_target_pairs={{0,1},{1,0},{2,3},{3,2},{4,5},{5,4},{6,7},{7,6},{8,9},{9,8},{10,11... | collective-permute-start | bytes 5308424 | tf_op jit(solution)/shard_map/ppermute | solution.py:20
  276.5 22.3 %collective-permute-start.44 = (bf16[512,768]{1,0:T(8,128)(2,1)S(1)}, bf16[512,768]{1,0:T(8,128)(2,1)S(1)}, u32[]{:S(2)}, u32[]{:S(2)}) collective-permute-start(bf16[512,768]{1,0:T(8,128)(2,1)S(1)} %multiply_convert_fusion.18), channel_id=1, source_target_pairs={{0,16},{1,17},{2,18},{3,19},{4,20},{5,21},{6,22},{7,23},{8,24},{9,... | collective-permute-start | bytes 2359304 | tf_op jit(solution)/shard_map/ppermute | solution.py:32
  281.0 23.8 %collective-permute-start.61 = (bf16[512,768]{1,0:T(8,128)(2,1)S(1)}, bf16[512,768]{1,0:T(8,128)(2,1)}, u32[]{:S(2)}, u32[]{:S(2)}) collective-permute-start(bf16[512,768]{1,0:T(8,128)(2,1)S(1)} %copy-done.248), channel_id=1, source_target_pairs={{0,4},{4,8},{8,12},{12,14},{14,10},{10,6},{6,2},{2,0},{1,5},{5,9},... | collective-permute-start | bytes 2359304 | tf_op jit(solution)/shard_map/ppermute | solution.py:37
  282.3 23.8 %collective-permute-start.62 = (bf16[512,768]{1,0:T(8,128)(2,1)S(1)}, bf16[512,768]{1,0:T(8,128)(2,1)}, u32[]{:S(2)}, u32[]{:S(2)}) collective-permute-start(bf16[512,768]{1,0:T(8,128)(2,1)S(1)} %copy-done.248), channel_id=1, source_target_pairs={{0,2},{4,0},{8,4},{12,8},{14,12},{10,14},{6,10},{2,6},{1,3},{5,1},... | collective-permute-start | bytes 2359304 | tf_op jit(solution)/shard_map/ppermute | solution.py:37
  283.0 21.6 %collective-permute-start.57 = (bf16[384,384]{1,0:T(8,128)(2,1)S(1)}, bf16[384,384]{1,0:T(8,128)(2,1)S(1)}, u32[]{:S(2)}, u32[]{:S(2)}) collective-permute-start(bf16[384,384]{1,0:T(8,128)(2,1)S(1)} %bitcast.591), channel_id=1, source_target_pairs={{0,16},{1,17},{2,18},{3,19},{4,20},{5,21},{6,22},{7,23},{8,24},{9,... | collective-permute-start | bytes 884744 | tf_op jit(solution)/shard_map/ppermute | solution.py:32
  304.7 40.6 %collective-permute-start.58 = (bf16[768,384]{1,0:T(8,128)(2,1)S(1)}, bf16[768,384]{1,0:T(8,128)(2,1)S(1)}, u32[]{:S(2)}, u32[]{:S(2)}) collective-permute-start(bf16[768,384]{1,0:T(8,128)(2,1)S(1)} %pad_maximum_fusion.34), channel_id=1, source_target_pairs={{0,1},{1,0},{2,3},{3,2},{4,5},{5,4},{6,7},{7,6},{8,9},{9,8},{10,11... | collective-permute-start | bytes 1769480 | tf_op jit(solution)/shard_map/ppermute | solution.py:20
  304.8 66.9 %collective-permute-start.63 = (bf16[512,768]{1,0:T(8,128)(2,1)}, bf16[512,768]{1,0:T(8,128)(2,1)}, u32[]{:S(2)}, u32[]{:S(2)}) collective-permute-start(bf16[512,768]{1,0:T(8,128)(2,1)} %collective-permute-done.61), channel_id=1, source_target_pairs={{0,4},{4,8},{8,12},{12,14},{14,10},{10,6},{6,2},{2,0},{1,5},{5,9},... | collective-permute-start | bytes 2359304 | tf_op jit(solution)/shard_map/ppermute | solution.py:37
  306.1 68.8 %collective-permute-start.64 = (bf16[512,768]{1,0:T(8,128)(2,1)}, bf16[512,768]{1,0:T(8,128)(2,1)}, u32[]{:S(2)}, u32[]{:S(2)}) collective-permute-start(bf16[512,768]{1,0:T(8,128)(2,1)} %collective-permute-done.62), channel_id=1, source_target_pairs={{0,2},{4,0},{8,4},{12,8},{14,12},{10,14},{6,10},{2,6},{1,3},{5,1},... | collective-permute-start | bytes 2359304 | tf_op jit(solution)/shard_map/ppermute | solution.py:37
  363.1 21.8 %collective-permute-start.59 = (bf16[512,768]{1,0:T(8,128)(2,1)}, bf16[512,768]{1,0:T(8,128)(2,1)}, u32[]{:S(2)}, u32[]{:S(2)}) collective-permute-start(bf16[512,768]{1,0:T(8,128)(2,1)} %multiply_convert_fusion.15), channel_id=1, source_target_pairs={{16,0},{17,1},{18,2},{19,3},{20,4},{21,5},{22,6},{23,7},{24,8},{25... | collective-permute-start | bytes 2359304 | tf_op jit(solution)/shard_map/ppermute | solution.py:28
  364.6 24.3 %collective-permute-start.69 = (s32[1024]{0:T(1024)S(1)}, s32[1024]{0:T(1024)S(1)}, u32[]{:S(2)}, u32[]{:S(2)}) collective-permute-start(s32[1024]{0:T(1024)S(1)} %bitcast.644), channel_id=1, source_target_pairs={{0,14},{2,0},{4,2},{6,4},{8,6},{10,8},{12,10},{14,12},{1,15},{3,1}... | collective-permute-start | bytes 12296 | tf_op jit(solution)/shard_map/ppermute | solution.py:166
  367.3 32.5 %collective-permute-start.70 = (s32[1024]{0:T(1024)S(1)}, s32[1024]{0:T(1024)S(1)}, u32[]{:S(2)}, u32[]{:S(2)}) collective-permute-start(s32[1024]{0:T(1024)S(1)} %bitcast.645), channel_id=1, source_target_pairs={{0,12},{2,14},{4,0},{6,2},{8,4},{10,6},{12,8},{14,10},{1,13},{3,15... | collective-permute-start | bytes 12296 | tf_op jit(solution)/shard_map/ppermute | solution.py:166
  371.7 49.0 %collective-permute-start.65 = (bf16[512,768]{1,0:T(8,128)(2,1)}, bf16[512,768]{1,0:T(8,128)(2,1)}, u32[]{:S(2)}, u32[]{:S(2)}) collective-permute-start(bf16[512,768]{1,0:T(8,128)(2,1)} %collective-permute-done.63), channel_id=1, source_target_pairs={{0,4},{4,8},{8,12},{12,14},{14,10},{10,6},{6,2},{2,0},{1,5},{5,9},... | collective-permute-start | bytes 2359304 | tf_op jit(solution)/shard_map/ppermute | solution.py:37
  374.9 48.5 %collective-permute-start.66 = (bf16[512,768]{1,0:T(8,128)(2,1)}, bf16[512,768]{1,0:T(8,128)(2,1)}, u32[]{:S(2)}, u32[]{:S(2)}) collective-permute-start(bf16[512,768]{1,0:T(8,128)(2,1)} %collective-permute-done.64), channel_id=1, source_target_pairs={{0,2},{4,0},{8,4},{12,8},{14,12},{10,14},{6,10},{2,6},{1,3},{5,1},... | collective-permute-start | bytes 2359304 | tf_op jit(solution)/shard_map/ppermute | solution.py:37
  384.9 16.2 %collective-permute-start.71 = (s32[1024]{0:T(1024)S(1)}, s32[1024]{0:T(1024)S(1)}, u32[]{:S(2)}, u32[]{:S(2)}) collective-permute-start(s32[1024]{0:T(1024)S(1)} %bitcast.646), channel_id=1, source_target_pairs={{0,10},{2,12},{4,14},{6,0},{8,2},{10,4},{12,6},{14,8},{1,11},{3,13... | collective-permute-start | bytes 12296 | tf_op jit(solution)/shard_map/ppermute | solution.py:166
  388.8 48.4 %collective-permute-start.60 = (bf16[512,768]{1,0:T(8,128)(2,1)}, bf16[512,768]{1,0:T(8,128)(2,1)}, u32[]{:S(2)}, u32[]{:S(2)}) collective-permute-start(bf16[512,768]{1,0:T(8,128)(2,1)} %broadcast_select_fusion), channel_id=1, source_target_pairs={{0,1},{1,0},{2,3},{3,2},{4,5},{5,4},{6,7},{7,6},{8,9},{9,8},{10,11... | collective-permute-start | bytes 2359304 | tf_op jit(solution)/shard_map/ppermute | solution.py:20
  474.7 53.0 %collective-permute-start.78 = (f32[1024]{0:T(1024)S(1)}, f32[1024]{0:T(1024)S(1)}, u32[]{:S(2)}, u32[]{:S(2)}) collective-permute-start(f32[1024]{0:T(1024)S(1)} %maximum_select_fusion.2), channel_id=1, source_target_pairs={{0,14},{2,0},{4,2},{6,4},{8,6},{10,8},{12,10},{14,12},{1,15},{3,1}... | collective-permute-start | bytes 12296 | tf_op jit(solution)/shard_map/ppermute | solution.py:166
  478.9 50.9 %collective-permute-start.79 = (f32[1024]{0:T(1024)S(1)}, f32[1024]{0:T(1024)S(1)}, u32[]{:S(2)}, u32[]{:S(2)}) collective-permute-start(f32[1024]{0:T(1024)S(1)} %maximum_select_fusion.2), channel_id=1, source_target_pairs={{0,12},{2,14},{4,0},{6,2},{8,4},{10,6},{12,8},{14,10},{1,13},{3,15... | collective-permute-start | bytes 12296 | tf_op jit(solution)/shard_map/ppermute | solution.py:166
  479.2 50.6 %collective-permute-start.80 = (f32[1024]{0:T(1024)S(1)}, f32[1024]{0:T(1024)S(1)}, u32[]{:S(2)}, u32[]{:S(2)}) collective-permute-start(f32[1024]{0:T(1024)S(1)} %maximum_select_fusion.2), channel_id=1, source_target_pairs={{0,10},{2,12},{4,14},{6,0},{8,2},{10,4},{12,6},{14,8},{1,11},{3,13... | collective-permute-start | bytes 12296 | tf_op jit(solution)/shard_map/ppermute | solution.py:166
  479.2 57.2 %collective-permute-start.81 = (f32[1024]{0:T(1024)S(1)}, f32[1024]{0:T(1024)S(1)}, u32[]{:S(2)}, u32[]{:S(2)}) collective-permute-start(f32[1024]{0:T(1024)S(1)} %maximum_select_fusion.2), channel_id=1, source_target_pairs={{0,8},{2,10},{4,12},{6,14},{8,0},{10,2},{12,4},{14,6},{1,9},{3,11}... | collective-permute-start | bytes 12296 | tf_op jit(solution)/shard_map/ppermute | solution.py:166
  486.8 53.7 %collective-permute-start.144 = (bf16[256,768]{1,0:T(8,128)(2,1)}, bf16[256,768]{1,0:T(8,128)(2,1)}, u32[]{:S(2)}, u32[]{:S(2)}) collective-permute-start(bf16[256,768]{1,0:T(8,128)(2,1)} %get-tuple-element.181), channel_id=1, source_target_pairs={{0,4},{4,8},{8,12},{12,14},{14,10},{10,6},{6,2},{2,0},{1,5},{5,9},... | collective-permute-start | bytes 1179656 | tf_op jit(solution)/shard_map/ppermute | solution.py:37
  543.9 22.0 %collective-permute-start.145 = (bf16[512,768]{1,0:T(8,128)(2,1)}, bf16[512,768]{1,0:T(8,128)(2,1)}, u32[]{:S(2)}, u32[]{:S(2)}) collective-permute-start(bf16[512,768]{1,0:T(8,128)(2,1)} %pad_maximum_fusion.31), channel_id=1, source_target_pairs={{0,4},{4,8},{8,12},{12,14},{14,10},{10,6},{6,2},{2,0},{1,5},{5,9},... | collective-permute-start | bytes 2359304 | tf_op jit(solution)/shard_map/ppermute | solution.py:37
  547.4 22.3 %collective-permute-start.149 = (bf16[512,768]{1,0:T(8,128)(2,1)}, bf16[512,768]{1,0:T(8,128)(2,1)}, u32[]{:S(2)}, u32[]{:S(2)}) collective-permute-start(bf16[512,768]{1,0:T(8,128)(2,1)} %pad_maximum_fusion.32), channel_id=1, source_target_pairs={{0,2},{4,0},{8,4},{12,8},{14,12},{10,14},{6,10},{2,6},{1,3},{5,1},... | collective-permute-start | bytes 2359304 | tf_op jit(solution)/shard_map/ppermute | solution.py:37
  554.0 21.7 %collective-permute-start.86 = (bf16[512,768]{1,0:T(8,128)(2,1)S(1)}, bf16[512,768]{1,0:T(8,128)(2,1)S(1)}, u32[]{:S(2)}, u32[]{:S(2)}) collective-permute-start(bf16[512,768]{1,0:T(8,128)(2,1)S(1)} %fusion.110), channel_id=1, source_target_pairs={{0,16},{1,17},{2,18},{3,19},{4,20},{5,21},{6,22},{7,23},{8,24},{9,... | collective-permute-start | bytes 2359304 | tf_op jit(solution)/shard_map/ppermute | solution.py:32
  569.7 113.0 %collective-permute-start.146 = (bf16[512,768]{1,0:T(8,128)(2,1)}, bf16[512,768]{1,0:T(8,128)(2,1)}, u32[]{:S(2)}, u32[]{:S(2)}) collective-permute-start(bf16[512,768]{1,0:T(8,128)(2,1)} %add_convert_fusion.3), channel_id=1, source_target_pairs={{0,4},{4,8},{8,12},{12,14},{14,10},{10,6},{6,2},{2,0},{1,5},{5,9},... | collective-permute-start | bytes 2359304 | tf_op jit(solution)/shard_map/ppermute | solution.py:37
  573.7 111.4 %collective-permute-start.150 = (bf16[512,768]{1,0:T(8,128)(2,1)}, bf16[512,768]{1,0:T(8,128)(2,1)}, u32[]{:S(2)}, u32[]{:S(2)}) collective-permute-start(bf16[512,768]{1,0:T(8,128)(2,1)} %add_convert_fusion.1), channel_id=1, source_target_pairs={{0,2},{4,0},{8,4},{12,8},{14,12},{10,14},{6,10},{2,6},{1,3},{5,1},... | collective-permute-start | bytes 2359304 | tf_op jit(solution)/shard_map/ppermute | solution.py:37
  668.7 30.8 %collective-permute-start.133 = (bf16[384,1536]{0,1:T(8,128)(2,1)S(1)}, bf16[384,1536]{0,1:T(8,128)(2,1)S(1)}, u32[]{:S(2)}, u32[]{:S(2)}) collective-permute-start(bf16[384,1536]{0,1:T(8,128)(2,1)S(1)} %slice.685), channel_id=1, source_target_pairs={{16,0},{17,1},{18,2},{19,3},{20,4},{21,5},{22,6},{23,7},{24,8},{25... | collective-permute-start | bytes 3538952 | tf_op jit(solution)/shard_map/ppermute | solution.py:28
  671.3 53.6 %collective-permute-start.134 = (bf16[384,1536]{0,1:T(8,128)(2,1)}, bf16[384,1536]{0,1:T(8,128)(2,1)}, u32[]{:S(2)}, u32[]{:S(2)}) collective-permute-start(bf16[384,1536]{0,1:T(8,128)(2,1)} %slice.687), channel_id=1, source_target_pairs={{16,0},{17,1},{18,2},{19,3},{20,4},{21,5},{22,6},{23,7},{24,8},{25... | collective-permute-start | bytes 3538952 | tf_op jit(solution)/shard_map/ppermute | solution.py:28
  685.1 42.3 %collective-permute-start.147 = (bf16[512,768]{1,0:T(8,128)(2,1)}, bf16[512,768]{1,0:T(8,128)(2,1)}, u32[]{:S(2)}, u32[]{:S(2)}) collective-permute-start(bf16[512,768]{1,0:T(8,128)(2,1)} %add_convert_fusion.2), channel_id=1, source_target_pairs={{0,4},{4,8},{8,12},{12,14},{14,10},{10,6},{6,2},{2,0},{1,5},{5,9},... | collective-permute-start | bytes 2359304 | tf_op jit(solution)/shard_map/ppermute | solution.py:37
  687.3 40.1 %collective-permute-start.151 = (bf16[512,768]{1,0:T(8,128)(2,1)}, bf16[512,768]{1,0:T(8,128)(2,1)}, u32[]{:S(2)}, u32[]{:S(2)}) collective-permute-start(bf16[512,768]{1,0:T(8,128)(2,1)} %add_convert_fusion), channel_id=1, source_target_pairs={{0,2},{4,0},{8,4},{12,8},{14,12},{10,14},{6,10},{2,6},{1,3},{5,1},... | collective-permute-start | bytes 2359304 | tf_op jit(solution)/shard_map/ppermute | solution.py:37
  690.5 49.5 %collective-permute-start.88 = (bf16[512,768]{1,0:T(8,128)(2,1)}, bf16[512,768]{1,0:T(8,128)(2,1)S(1)}, u32[]{:S(2)}, u32[]{:S(2)}) collective-permute-start(bf16[512,768]{1,0:T(8,128)(2,1)} %fusion.98), channel_id=1, source_target_pairs={{16,0},{17,1},{18,2},{19,3},{20,4},{21,5},{22,6},{23,7},{24,8},{25... | collective-permute-start | bytes 2359304 | tf_op jit(solution)/shard_map/ppermute | solution.py:28
  727.4 144.2 %collective-permute-start.135 = (bf16[384,1536]{0,1:T(8,128)(2,1)}, bf16[384,1536]{0,1:T(8,128)(2,1)}, u32[]{:S(2)}, u32[]{:S(2)}) collective-permute-start(bf16[384,1536]{0,1:T(8,128)(2,1)} %slice_select_fusion), channel_id=1, source_target_pairs={{0,1},{1,0},{2,3},{3,2},{4,5},{5,4},{6,7},{7,6},{8,9},{9,8},{10,11... | collective-permute-start | bytes 3538952 | tf_op jit(solution)/shard_map/ppermute | solution.py:20
  851.6 25.3 %collective-permute-start.89 = (bf16[512,768]{1,0:T(8,128)(2,1)}, bf16[512,768]{1,0:T(8,128)(2,1)}, u32[]{:S(2)}, u32[]{:S(2)}) collective-permute-start(bf16[512,768]{1,0:T(8,128)(2,1)} %slice.982), channel_id=1, source_target_pairs={{0,1},{1,0},{2,3},{3,2},{4,5},{5,4},{6,7},{7,6},{8,9},{9,8},{10,11... | collective-permute-start | bytes 2359304 | tf_op jit(solution)/shard_map/ppermute | solution.py:20
  905.3 110.0 %collective-permute-start.124 = (bf16[768,3072]{1,0:T(8,128)(2,1)}, bf16[768,3072]{1,0:T(8,128)(2,1)}, u32[]{:S(2)}, u32[]{:S(2)}) collective-permute-start(bf16[768,3072]{1,0:T(8,128)(2,1)} %copy-done.26), channel_id=1, source_target_pairs={{0,1},{1,0},{2,3},{3,2},{4,5},{5,4},{6,7},{7,6},{8,9},{9,8},{10,11... | collective-permute-start | bytes 14155784 | tf_op jit(solution)/shard_map/ppermute | solution.py:20
  905.4 86.9 %collective-permute-start.115 = (bf16[768,1536]{0,1:T(8,128)(2,1)}, bf16[768,1536]{0,1:T(8,128)(2,1)}, u32[]{:S(2)}, u32[]{:S(2)}) collective-permute-start(bf16[768,1536]{0,1:T(8,128)(2,1)} %pad_maximum_fusion.6), channel_id=1, source_target_pairs={{0,1},{1,0},{2,3},{3,2},{4,5},{5,4},{6,7},{7,6},{8,9},{9,8},{10,11... | collective-permute-start | bytes 7077896 | tf_op jit(solution)/shard_map/ppermute | solution.py:20
  910.3 50.2 %collective-permute-start.141 = (bf16[48,1536]{1,0:T(8,128)(2,1)S(1)}, bf16[48,1536]{1,0:T(8,128)(2,1)S(1)}, u32[]{:S(2)}, u32[]{:S(2)}) collective-permute-start(bf16[48,1536]{1,0:T(8,128)(2,1)S(1)} %pad_maximum_fusion.50), channel_id=1, source_target_pairs={{0,2},{4,0},{8,4},{12,8},{14,12},{10,14},{6,10},{2,6},{1,3},{5,1},... | collective-permute-start | bytes 442376 | tf_op jit(solution)/shard_map/ppermute | solution.py:37
  922.0 38.6 %collective-permute-start.138 = (bf16[48,1536]{1,0:T(8,128)(2,1)S(1)}, bf16[48,1536]{1,0:T(8,128)(2,1)S(1)}, u32[]{:S(2)}, u32[]{:S(2)}) collective-permute-start(bf16[48,1536]{1,0:T(8,128)(2,1)S(1)} %fusion.194), channel_id=1, source_target_pairs={{0,4},{4,8},{8,12},{12,14},{14,10},{10,6},{6,2},{2,0},{1,5},{5,9},... | collective-permute-start | bytes 442376 | tf_op jit(solution)/shard_map/ppermute | solution.py:37
  988.2 70.6 %collective-permute-start.105 = (bf16[256,768]{1,0:T(8,128)(2,1)}, bf16[256,768]{1,0:T(8,128)(2,1)}, u32[]{:S(2)}, u32[]{:S(2)}) collective-permute-start(bf16[256,768]{1,0:T(8,128)(2,1)} %bitcast.573), channel_id=1, source_target_pairs={{0,16},{1,17},{2,18},{3,19},{4,20},{5,21},{6,22},{7,23},{8,24},{9,... | collective-permute-start | bytes 1179656 | tf_op jit(solution)/shard_map/ppermute | solution.py:32
  1006.5 35.8 %collective-permute-start.121 = (bf16[96,1536]{1,0:T(8,128)(2,1)S(1)}, bf16[96,1536]{1,0:T(8,128)(2,1)S(1)}, u32[]{:S(2)}, u32[]{:S(2)}) collective-permute-start(bf16[96,1536]{1,0:T(8,128)(2,1)S(1)} %pad_maximum_fusion.47), channel_id=1, source_target_pairs={{0,2},{4,0},{8,4},{12,8},{14,12},{10,14},{6,10},{2,6},{1,3},{5,1},... | collective-permute-start | bytes 884744 | tf_op jit(solution)/shard_map/ppermute | solution.py:37
  1014.9 27.4 %collective-permute-start.118 = (bf16[96,1536]{1,0:T(8,128)(2,1)S(1)}, bf16[96,1536]{1,0:T(8,128)(2,1)S(1)}, u32[]{:S(2)}, u32[]{:S(2)}) collective-permute-start(bf16[96,1536]{1,0:T(8,128)(2,1)S(1)} %fusion.147), channel_id=1, source_target_pairs={{0,4},{4,8},{8,12},{12,14},{14,10},{10,6},{6,2},{2,0},{1,5},{5,9},... | collective-permute-start | bytes 884744 | tf_op jit(solution)/shard_map/ppermute | solution.py:37
  1040.4 15.9 %collective-permute-start.127 = (bf16[96,3072]{1,0:T(8,128)(2,1)S(1)}, bf16[96,3072]{1,0:T(8,128)(2,1)S(1)}, u32[]{:S(2)}, u32[]{:S(2)}) collective-permute-start(bf16[96,3072]{1,0:T(8,128)(2,1)S(1)} %fusion.103), channel_id=1, source_target_pairs={{0,4},{4,8},{8,12},{12,14},{14,10},{10,6},{6,2},{2,0},{1,5},{5,9},... | collective-permute-start | bytes 1769480 | tf_op jit(solution)/shard_map/ppermute | solution.py:37
  1042.5 20.3 %collective-permute-start.122 = (bf16[96,1536]{1,0:T(8,128)(2,1)S(1)}, bf16[96,1536]{1,0:T(8,128)(2,1)S(1)}, u32[]{:S(2)}, u32[]{:S(2)}) collective-permute-start(bf16[96,1536]{1,0:T(8,128)(2,1)S(1)} %get-tuple-element.167), channel_id=1, source_target_pairs={{0,2},{4,0},{8,4},{12,8},{14,12},{10,14},{6,10},{2,6},{1,3},{5,1},... | collective-permute-start | bytes 884744 | tf_op jit(solution)/shard_map/ppermute | solution.py:37
  (336 other events, 4242.9 us)

commit v2 on v1

v2 whole, which is shorter than its diff:
```python
import jax
import jax.numpy as jnp
from jax import lax
from jax.experimental import pallas as pl
from jax.experimental.pallas import tpu as pltpu
from jax.sharding import PartitionSpec as P

DK = 64
f32 = jnp.float32
bf16 = jnp.bfloat16
epsilon = 1e-06
masked_out = -1000000000.0


def loop_order(count):
    return [0, 2, 4, 6, 7, 5, 3, 1] if count == 8 else None


def swap_core(value):
    return lax.ppermute(value, "mp", [(0, 1), (1, 0)])


def swap_slab(value):
    return lax.ppermute(value, "slab", [(0, 1), (1, 0)])


def to_encoder(value):
    return lax.ppermute(value, "slab", [(1, 0)])


def to_decoder(value):
    return lax.ppermute(value, "slab", [(0, 1)])


def loop_step(value, step):
    order = loop_order(lax.axis_size("dp"))
    count = len(order)
    pairs = [(order[i], order[(i + step) % count]) for i in range(count)]
    return lax.ppermute(value, "dp", pairs)


def held_after(value, earlier):
    return value if earlier is None else lax.optimization_barrier((value, earlier))[0]


def loop_index(offset):
    me, count = lax.axis_index("dp"), lax.axis_size("dp")
    place = jnp.where(me % 2 == 0, me // 2, count - 1 - me // 2)
    place = (place + offset + count) % count
    return jnp.where(place < count // 2, 2 * place, 2 * (count - 1 - place) + 1)


OFFSETS = [0, -1, 1, -2, 2, -3, 3, 4]


class Gathering:
    def __init__(self, block, earlier=None):
        self.block = held_after(block, earlier)
        self.half = block.shape[0] // 2
        self.whole = None
        self.last = None
        if loop_order(lax.axis_size("dp")) is None:
            self.whole = lax.all_gather(self.block, "dp")
        self.behind, self.ahead = [self.block], [self.block]
        self.step()

    def step(self, token=None):
        if self.whole is not None:
            return
        behind = held_after(self.behind[-1], token)
        ahead = held_after(self.ahead[-1], token)
        if len(self.behind) == 4:
            behind, ahead = behind[: self.half], ahead[self.half :]
        self.behind.append(loop_step(behind, 1))
        self.ahead.append(loop_step(ahead, -1))
        self.last = self.ahead[-1]

    def blocks(self):
        far = jnp.concatenate([self.behind[4], self.ahead[4]], 0)
        near = [self.behind[i] if side == 0 else self.ahead[i] for i in (1, 2, 3) for side in (0, 1)]
        return [self.block] + near + [far]

    def both_parts(self, cuts):
        if self.whole is not None:
            parts = []
            for r, rows, c, columns, groups in cuts:
                part = self.whole[:, r : r + rows, c : c + columns]
                part = part.reshape(part.shape[0], groups, rows // groups, columns)
                parts.append(part.transpose(1, 0, 2, 3))
            return parts, [swap_core(part) for part in parts]
        indices = loop_index(jnp.array(OFFSETS, jnp.int32))
        blocks = self.blocks()
        early = assemble(blocks[:-1], indices[:-1], cuts, len(OFFSETS))
        other = [swap_core(part) for part in early]
        other_block = swap_core(blocks[-1])
        return (
            patch(early, blocks[-1], indices[-1:], cuts),
            patch(other, other_block, indices[-1:], cuts),
        )


class Scattering:
    def __init__(self, chunk, rows):
        self.chunk, self.half = chunk, rows // 2
        self.offset = 4
        self.step()

    def step(self, token=None):
        half = self.half
        if self.offset == 4:
            far = self.chunk(4)
            right, left = far[:half], far[half:]
        else:
            right, left = self.chunk(self.offset), self.chunk(-self.offset)
            if self.offset == 3:
                right = jnp.concatenate([right[:half] + self.right, right[half:]], 0)
                left = jnp.concatenate([left[:half], left[half:] + self.left], 0)
            else:
                right, left = right + self.right, left + self.left
        right = held_after(right.astype(bf16), token)
        left = held_after(left.astype(bf16), token)
        self.right = loop_step(right, 1)
        self.left = self.last = loop_step(left, -1)
        self.offset -= 1

    def total(self):
        return self.chunk(0) + self.right.astype(f32) + self.left.astype(f32)


class Scattered:
    def __init__(self, value):
        self.value, self.last = value, None

    def step(self, token=None):
        pass

    def total(self):
        return self.value


def lay(source, targets, cuts):
    for target, (row, rows, column, columns, groups) in zip(targets, cuts):
        size = rows // groups
        for group in range(groups):
            first = row + group * size
            target[group, 0] = source[first : first + size, column : column + columns]


def slot_spec(cut):
    row, rows, column, columns, groups = cut
    return pl.BlockSpec(
        (groups, 1, rows // groups, columns), lambda i, index: (0, index[i], 0, 0)
    )


def assemble(blocks, indices, cuts, count):
    def body(index_ref, *refs):
        sources, targets = refs[: len(blocks)], refs[len(blocks) :]
        for turn in range(len(blocks)):

            @pl.when(pl.program_id(0) == turn)
            def _():
                lay(sources[turn], targets, cuts)

    whole = [pl.BlockSpec(block.shape, lambda i, index: (0, 0)) for block in blocks]
    shapes = [(groups, count, rows // groups, columns) for _, rows, _, columns, groups in cuts]
    size = sum(block.size for block in blocks) * 4
    return pl.pallas_call(
        body,
        out_shape=[jax.ShapeDtypeStruct(shape, blocks[0].dtype) for shape in shapes],
        grid_spec=pltpu.PrefetchScalarGridSpec(
            num_scalar_prefetch=1,
            grid=(len(blocks),),
            in_specs=whole,
            out_specs=[slot_spec(cut) for cut in cuts],
        ),
        cost_estimate=pl.CostEstimate(flops=0, bytes_accessed=size, transcendentals=0),
        name="assemble",
    )(indices, *blocks)


def patch(parts, block, index, cuts):
    count = len(parts)

    def body(index_ref, *refs):
        lay(refs[count], refs[count + 1 :], cuts)

    return pl.pallas_call(
        body,
        out_shape=[jax.ShapeDtypeStruct(part.shape, part.dtype) for part in parts],
        grid_spec=pltpu.PrefetchScalarGridSpec(
            num_scalar_prefetch=1,
            grid=(1,),
            in_specs=[pl.BlockSpec(memory_space=pl.ANY)] * count
            + [pl.BlockSpec(block.shape, lambda i, index: (0, 0))],
            out_specs=[slot_spec(cut) for cut in cuts],
        ),
        input_output_aliases={i + 1: i for i in range(count)},
        cost_estimate=pl.CostEstimate(flops=0, bytes_accessed=block.size * 4, transcendentals=0),
        name="patch",
    )(index, *parts, block)


def column_cuts(rows, widths, first=0, groups=1):
    return [
        (0, rows, first + sum(widths[:i]), width, groups) for i, width in enumerate(widths)
    ]


def flat_rows(part):
    return part.reshape(-1, part.shape[3])


def scatter_stacks(stacks):
    if loop_order(lax.axis_size("dp")) is None:
        total = sum(jnp.concatenate(stack, 1).astype(f32) for stack in stacks).astype(bf16)
        return Scattered(lax.psum_scatter(total, "dp", scatter_dimension=0).astype(f32))

    def chunk(offset):
        where = loop_index(offset)
        return sum(
            jnp.concatenate(
                [lax.dynamic_index_in_dim(piece, where, 0, keepdims=False) for piece in stack], 0
            ).astype(f32)
            for stack in stacks
        )

    return Scattering(chunk, sum(piece.shape[1] for piece in stacks[0]))


def reroute_plane(pieces, source_of):
    spread = lax.all_to_all(pieces, "dp", split_axis=0, concat_axis=0, tiled=True)
    return lax.all_to_all(spread[source_of], "dp", split_axis=0, concat_axis=0, tiled=True)


def matmul(a, b):
    return jnp.dot(a, b, preferred_element_type=f32)


def contract_last(a, b):
    return lax.dot_general(a, b, (((1,), (1,)), ((), ())), preferred_element_type=f32)


def contract_first(a, b):
    return lax.dot_general(a, b, (((0,), (0,)), ((), ())), preferred_element_type=f32)


def rms_apply(hidden, gain):
    return hidden * lax.rsqrt(jnp.mean(hidden * hidden, axis=-1, keepdims=True) + epsilon) * gain


def norm_back(hidden, gain, upstream):
    scale = lax.rsqrt(jnp.mean(hidden * hidden, axis=-1, keepdims=True) + epsilon)
    weighted = upstream * gain
    dot = jnp.mean(weighted * hidden, axis=-1, keepdims=True)
    grad = scale * weighted - hidden * (scale * scale * scale * dot)
    return grad, jnp.sum(upstream * hidden * scale, axis=0)


PAIR = 2 * DK


def paired(key_columns, value_columns):
    rows, width = key_columns.shape
    both = [part.reshape(rows, width // PAIR, 1, PAIR) for part in (key_columns, value_columns)]
    return jnp.concatenate(both, 2).reshape(rows, 2 * width)


def unpaired(columns):
    rows, width = columns.shape
    both = columns.reshape(rows, width // (2 * PAIR), 2, PAIR)
    return both[:, :, 0].reshape(rows, width // 2), both[:, :, 1].reshape(rows, width // 2)


def lanes_of(head, value):
    lane = lax.broadcasted_iota(jnp.int32, value.shape, 1)
    return jnp.where(lane // DK == head, value, jnp.zeros_like(value))


def dot_last(a, b):
    return lax.dot_general(a, b, (((1,), (1,)), ((), ())), preferred_element_type=f32)


def dot_first(a, b):
    return lax.dot_general(a, b, (((0,), (0,)), ((), ())), preferred_element_type=f32)


def masked_scores(keys, queries, reach):
    scores = dot_last(keys, queries)
    row = lax.broadcasted_iota(jnp.int32, scores.shape, 0)
    return jnp.where(row <= reach, scores, masked_out)


def attend_body(start_ref, query_ref, pair_ref, limit_ref, context_ref, log_ref):
    half = pair_ref.shape[0] // 2
    scaled = query_ref[...] * jnp.asarray(DK ** (-0.5), bf16)
    reach = [limit_ref[...] - start_ref[part] for part in range(2)]
    rows = [pl.ds(part * half, half) for part in range(2)]
    turned = []
    for head in range(2):
        queries = lanes_of(head, scaled)
        scores = [masked_scores(pair_ref[rows[i], :PAIR], queries, reach[i]) for i in range(2)]
        highest = jnp.max(jnp.maximum(scores[0], scores[1]), axis=0, keepdims=True)
        shifted = [jnp.exp(part - highest) for part in scores]
        totals = jnp.sum(shifted[0] + shifted[1], axis=0, keepdims=True)
        context = sum(
            dot_first(pair_ref[rows[i], PAIR:], shifted[i].astype(bf16)) for i in range(2)
        )
        turned.append(context[head * DK : (head + 1) * DK] / totals)
        log_ref[0, head : head + 1] = highest + jnp.log(totals)
    context_ref[...] = jnp.concatenate(turned, 0).T.astype(bf16)


def attend_back_body(
    start_ref, query_ref, pair_ref, limit_ref, log_ref, grad_ref, grad_query_ref, grad_pair_ref
):
    half = pair_ref.shape[0] // 2
    scale = DK ** (-0.5)
    scaled = query_ref[...] * jnp.asarray(scale, bf16)
    reach = [limit_ref[...] - start_ref[part] for part in range(2)]
    rows = [pl.ds(part * half, half) for part in range(2)]
    grad_query = 0.0
    grad_key, grad_value = [0.0, 0.0], [0.0, 0.0]
    for head in range(2):
        queries = lanes_of(head, scaled)
        grad_context = lanes_of(head, grad_ref[...])
        log_total = log_ref[0, head : head + 1]
        weights, grad_weights = [], []
        for i in range(2):
            scores = masked_scores(pair_ref[rows[i], :PAIR], queries, reach[i])
            weights.append(jnp.exp(scores - log_total))
            grad_weights.append(dot_last(pair_ref[rows[i], PAIR:], grad_context))
        inner = jnp.sum(
            weights[0] * grad_weights[0] + weights[1] * grad_weights[1], axis=0, keepdims=True
        )
        for i in range(2):
            grad_scores = (weights[i] * (grad_weights[i] - inner)).astype(bf16)
            grad_value[i] += jnp.dot(
                weights[i].astype(bf16), grad_context, preferred_element_type=f32
            )
            grad_key[i] += jnp.dot(grad_scores, queries, preferred_element_type=f32)
            grad_query += dot_first(lanes_of(head, pair_ref[rows[i], :PAIR]), grad_scores)
    for i in range(2):
        grad_pair_ref[rows[i], :PAIR] = grad_key[i].astype(bf16)
        grad_pair_ref[rows[i], PAIR:] = grad_value[i].astype(bf16)
    grad_query_ref[...] = (grad_query * scale).T.astype(bf16)


def attend_specs(queries, pairs):
    query_spec = pl.BlockSpec((queries.shape[0], PAIR), lambda i, start: (0, i))
    pair_spec = pl.BlockSpec((pairs.shape[0], 2 * PAIR), lambda i, start: (0, i))
    limit_spec = pl.BlockSpec((1, queries.shape[0]), lambda i, start: (0, 0))
    log_spec = pl.BlockSpec((1, 2, queries.shape[0]), lambda i, start: (i, 0, 0))
    return query_spec, pair_spec, limit_spec, log_spec


def attend(queries, pairs, limit, starts):
    query_spec, pair_spec, limit_spec, log_spec = attend_specs(queries, pairs)
    rows, width = queries.shape
    area = rows * pairs.shape[0] * width
    return pl.pallas_call(
        attend_body,
        out_shape=[
            jax.ShapeDtypeStruct((rows, width), bf16),
            jax.ShapeDtypeStruct((width // PAIR, 2, rows), f32),
        ],
        grid_spec=pltpu.PrefetchScalarGridSpec(
            num_scalar_prefetch=1,
            grid=(width // PAIR,),
            in_specs=[query_spec, pair_spec, limit_spec],
            out_specs=[query_spec, log_spec],
        ),
        cost_estimate=pl.CostEstimate(
            flops=area // 64, bytes_accessed=pairs.size // 64, transcendentals=0
        ),
        name="attend",
    )(starts, queries, pairs, limit)


def attend_back(queries, pairs, limit, starts, log_total, grad_context):
    query_spec, pair_spec, limit_spec, log_spec = attend_specs(queries, pairs)
    rows, width = queries.shape
    area = rows * pairs.shape[0] * width
    return pl.pallas_call(
        attend_back_body,
        out_shape=[
            jax.ShapeDtypeStruct((rows, width), bf16),
            jax.ShapeDtypeStruct(pairs.shape, bf16),
        ],
        grid_spec=pltpu.PrefetchScalarGridSpec(
            num_scalar_prefetch=1,
            grid=(width // PAIR,),
            in_specs=[query_spec, pair_spec, limit_spec, log_spec, query_spec],
            out_specs=[query_spec, pair_spec],
        ),
        cost_estimate=pl.CostEstimate(
            flops=area // 64, bytes_accessed=pairs.size // 64, transcendentals=0
        ),
        name="attend_back",
    )(starts, queries, pairs, limit, log_total, grad_context)


def attention_forward(query_in, memory_in, weights, limit, starts, ring=None):
    query_w, pair_w, out_w = weights
    branch, kept = 0.0, []
    for i in range(2):
        queries = matmul(query_in, query_w[i]).astype(bf16)
        pairs = matmul(memory_in, pair_w[i]).astype(bf16)
        if ring is not None:
            queries = held_after(queries, ring.last)
            ring.step()
        context, log_total = attend(queries, pairs, limit, starts)
        branch = branch + contract_last(context, out_w[i])
        kept.append((queries, pairs, context, log_total))
    return branch, kept


def attention_back(kept, weights, limit, starts, grad_rows):
    query_w, pair_w, out_w = weights
    grad_query_in, grad_memory, grads = 0.0, 0.0, []
    for i in range(2):
        queries, pairs, _, log_total = kept[i]
        grad_context = matmul(grad_rows, out_w[i]).astype(bf16)
        grad = attend_back(queries, pairs, limit, starts, log_total, grad_context)
        grad_query_in = grad_query_in + contract_last(grad[0], query_w[i])
        grad_memory = grad_memory + contract_last(grad[1], pair_w[i])
        grads.append(grad)
    return grads, grad_query_in, grad_memory


def attention_weight_grads(query_in, memory_in, kept, grads, grad_rows):
    return [
        jnp.concatenate(
            [
                contract_first(query_in, grads[i][0]).astype(bf16),
                contract_first(memory_in, grads[i][1]).astype(bf16),
                contract_first(grad_rows, kept[i][2]).astype(bf16),
            ],
            1,
        )
        for i in range(2)
    ]


def mlp_forward(normed, gate_up, down):
    width = down[0].shape[1]
    both = [matmul(normed, part) for part in gate_up]
    gate_out = [part[:, :width] for part in both]
    up_out = [part[:, width:] for part in both]
    inner = [
        (jax.nn.gelu(gate, approximate=True) * up).astype(bf16) for gate, up in zip(gate_out, up_out)
    ]
    branch = contract_last(inner[0], down[0]) + contract_last(inner[1], down[1])
    return branch, (both, inner)


def gelu_gate(gate_out, up_out):
    return jax.nn.gelu(gate_out, approximate=True) * up_out


def mlp_back(kept, gate_up, down, grad_rows):
    both, _ = kept
    width = down[0].shape[1]
    grads, total = [], 0.0
    for i in range(2):
        grad_inner = matmul(grad_rows, down[i])
        _, pullback = jax.vjp(gelu_gate, both[i][:, :width], both[i][:, width:])
        grad = jnp.concatenate([part.astype(bf16) for part in pullback(grad_inner)], 1)
        grads.append(grad)
        total = total + contract_last(grad, gate_up[i])
    return grads, total


def mlp_weight_grads(normed, inner, grads, grad_rows):
    return [
        jnp.concatenate(
            [
                contract_first(normed, grads[i]).astype(bf16),
                contract_first(grad_rows, inner[i]).astype(bf16),
            ],
            1,
        )
        for i in range(2)
    ]


def merge_stats(first, second):
    highest = jnp.maximum(first[0], second[0])
    totals = first[1] * jnp.exp(first[0] - highest) + second[1] * jnp.exp(second[0] - highest)
    return jnp.stack([highest, totals, first[2] + second[2]])


def on_device(
    states,
    attn_gain,
    w_query,
    w_key,
    w_value,
    w_out,
    mlp_gain,
    w_gate,
    w_up,
    w_down,
    final_gain,
    cross_gain,
    cross_query,
    cross_key,
    cross_value,
    cross_out,
    embedding,
    source_len,
    target_len,
    target_ids,
    pairing,
):
    slab, me, core = (lax.axis_index(name) for name in ("slab", "dp", "mp"))
    decoding = slab == 1
    count = lax.axis_size("dp")
    numbers = jnp.arange(count, dtype=jnp.int32)
    target_of = jnp.sum(
        jnp.where(pairing[None, :] == numbers[:, None], numbers[None, :], 0), axis=1
    )
    target = target_of[me]
    source_length, target_length = source_len[me], target_len[target]

    gain_rows, cross_rows = attn_gain.shape[1], cross_gain.shape[0]
    width, hidden = w_query.shape[2], w_gate.shape[2]
    half = states.shape[2]
    model = states.shape[3]

    def line_of(value):
        return jnp.pad(value[None], ((0, 0), (0, 4 * width - value.shape[0])))

    extra = jnp.concatenate(
        [
            line_of(jnp.concatenate([attn_gain[0], mlp_gain[0], final_gain[0], cross_gain], 0)),
            line_of((target_ids[0] // 128).astype(bf16)),
            line_of((target_ids[0] % 128).astype(bf16)),
            jnp.zeros((13, 4 * width), bf16),
        ],
        0,
    )

    def attention_block(query_w, key_w, value_w, out_w):
        return jnp.concatenate([query_w, paired(key_w, value_w), out_w.T], 1)

    attention_widths = [width, 2 * width, width]
    cross_block = attention_block(cross_query, cross_key, cross_value, cross_out)
    cross_block = jnp.concatenate([to_decoder(cross_block), cross_block], 0)
    gathering = Gathering(
        jnp.concatenate([attention_block(w_query[0], w_key[0], w_value[0], w_out[0]), extra], 0)
    )
    for _ in range(3):
        gathering.step()
    parts, other_parts = gathering.both_parts(
        column_cuts(gain_rows, attention_widths) + [(gain_rows, 16, 0, 4 * width, 1)]
    )
    self_weights = [
        (flat_rows(part), flat_rows(other)) for part, other in zip(parts[:3], other_parts)
    ]
    extra = parts[3][0]
    gains = extra[:, 0].astype(f32)
    gain_attn, gain_mlp, gain_final = (
        gains[:, i * gain_rows : (i + 1) * gain_rows].reshape(-1) for i in range(3)
    )
    cross_part = gains[:, 3 * gain_rows : 3 * gain_rows + cross_rows].reshape(-1)
    gain_cross = jnp.concatenate([to_decoder(cross_part), cross_part], 0)
    tokens = lax.dynamic_index_in_dim(extra, target, 0, keepdims=False)[:, : 2 * half].astype(f32)
    wanted = (tokens[1] * 128 + tokens[2]).astype(jnp.int32)

    rows = states[0, 0]

    def lend(value):
        cut = value.shape[0] // 2
        lent = jnp.where(decoding, value[cut:], to_encoder(value[:cut]))
        return lent.reshape(count, cut // count, value.shape[1])

    moved = reroute_plane(lend(rows), target_of).reshape(half // 2, model)
    own = jnp.where(decoding, jnp.concatenate([to_decoder(moved), moved], 0), rows)
    other = swap_core(own)

    mlp_gathering = Gathering(
        jnp.concatenate([w_gate[0], w_up[0], w_down[0].T, cross_block], 1), gathering.last
    )

    line = jnp.arange(half, dtype=jnp.int32)
    query_at = core * half + line
    key_at = jnp.concatenate([query_at, (1 - core) * half + line])
    starts = jnp.stack([core * half, (1 - core) * half])
    self_limit = jnp.where(
        decoding, jnp.minimum(query_at, target_length - 1), source_length - 1
    )[None]
    cross_limit = jnp.broadcast_to(source_length - 1, (1, half))

    start = own.astype(f32)
    normed = rms_apply(start, gain_attn).astype(bf16)
    normed_all = jnp.concatenate([normed, rms_apply(other.astype(f32), gain_attn).astype(bf16)], 0)
    branch, self_kept = attention_forward(
        normed,
        normed_all,
        self_weights,
        self_limit,
        starts,
        mlp_gathering,
    )
    after_self = start + branch
    after_self = held_after(after_self, mlp_gathering.last)
    mlp_gathering.step()
    parts, other_parts = mlp_gathering.both_parts(
        column_cuts(gain_rows, [2 * hidden, hidden])
        + column_cuts(2 * cross_rows, attention_widths, 3 * hidden, 2)
    )
    gate_up, down, *cross_weights = [
        (flat_rows(part), flat_rows(other)) for part, other in zip(parts, other_parts)
    ]
    table = lax.all_gather(held_after(embedding, mlp_gathering.last), "dp", axis=0, tiled=True)

    normed_enc = rms_apply(after_self, gain_mlp).astype(bf16)
    branch, enc_kept = mlp_forward(normed_enc, gate_up, down)
    after_enc = after_self + branch
    memory = rms_apply(after_enc, gain_final).astype(bf16)
    memory = to_decoder(memory)
    memory = jnp.concatenate([memory, swap_core(memory)], 0)

    normed_cross = rms_apply(after_self, gain_cross).astype(bf16)
    branch, cross_kept = attention_forward(
        normed_cross,
        memory,
        cross_weights,
        cross_limit,
        starts,
    )
    after_cross = after_self + branch
    normed_dec = rms_apply(after_cross, gain_mlp).astype(bf16)
    branch, dec_kept = mlp_forward(normed_dec, gate_up, down)
    after_mlp = after_cross + branch
    final = rms_apply(after_mlp, gain_final).astype(bf16)

    vocab_rows, cores = embedding.shape[0], lax.axis_size("mp")
    line = jnp.arange(count * vocab_rows, dtype=jnp.int32)
    device = slab * count + line // vocab_rows
    entries = (device * cores + core) * vocab_rows + line % vocab_rows

    final = jnp.where(decoding, final, to_encoder(final))
    final = jnp.concatenate([final, swap_core(final)], 0)
    wanted = jnp.where(core == 0, wanted, jnp.roll(wanted, half))
    counted = key_at < target_length
    width_scale = final.shape[1] ** (-0.5)
    logits = contract_last(final, table) * width_scale
    hits = entries[None, :] == wanted[:, None]
    highest = jnp.max(logits, axis=1)
    totals = jnp.sum(jnp.exp(logits - highest[:, None]), axis=1)
    picked = jnp.sum(jnp.where(hits, logits, 0.0), axis=1)
    stats = jnp.stack([highest, totals, picked])
    flipped = jnp.roll(swap_core(stats), half, axis=1)
    stats = merge_stats(stats, flipped)
    stats = merge_stats(stats, swap_slab(stats))
    log_total = stats[0] + jnp.log(stats[1])
    token_ce = jnp.where(counted, log_total - stats[2], 0.0)
    grad_logits = jnp.where(
        counted[:, None], jnp.exp(logits - log_total[:, None]) - hits.astype(f32), 0.0
    ).astype(bf16)
    grad_final = matmul(grad_logits, table) * width_scale
    grad_final = grad_final[:half] + swap_core(grad_final[half:].astype(bf16)).astype(f32)
    grad_logits = held_after(grad_logits, grad_final)
    grad_final = grad_final + to_decoder(grad_final.astype(bf16)).astype(f32)
    grad_final = jnp.where(decoding, grad_final, 0.0)
    grad_table = (contract_first(grad_logits, final) * width_scale).astype(bf16)
    g_embedding = lax.psum_scatter(grad_table, "dp", scatter_dimension=0, tiled=True)

    stream, grad_gain_final = norm_back(after_mlp, gain_final, grad_final)
    dec_rows = stream.astype(bf16)
    dec_grads, grad_normed = mlp_back(dec_kept, gate_up, down, dec_rows)
    part, grad_gain_mlp = norm_back(after_cross, gain_mlp, grad_normed)
    stream = stream + part
    cross_in = stream.astype(bf16)
    cross_grads, grad_normed, grad_memory = attention_back(
        cross_kept,
        cross_weights,
        cross_limit,
        starts,
        cross_in,
    )
    grad_memory = grad_memory[:half] + swap_core(grad_memory[half:].astype(bf16)).astype(f32)
    cross_in = held_after(cross_in, grad_memory)
    grad_memory = to_encoder(grad_memory.astype(bf16)).astype(f32)
    part, grad_gain_cross = norm_back(after_self, gain_cross, grad_normed)
    stream = stream + part
    cross_sums = attention_weight_grads(normed_cross, memory, cross_kept, cross_grads, cross_in)

    def stacked(part):
        return part.reshape(count, -1, part.shape[1])

    cross_sum = (cross_sums[0].astype(f32) + swap_core(cross_sums[1]).astype(f32)).astype(bf16)
    cut = cross_sum.shape[0] // 2
    cross_sum = jnp.where(decoding, cross_sum[cut:], to_encoder(cross_sum[:cut]))

    enc_stream, gain_part = norm_back(after_enc, gain_final, grad_memory)
    grad_gain_final = grad_gain_final + gain_part
    enc_rows = enc_stream.astype(bf16)
    enc_grads, grad_normed = mlp_back(enc_kept, gate_up, down, enc_rows)
    part, gain_part = norm_back(after_self, gain_mlp, grad_normed)
    grad_gain_mlp = grad_gain_mlp + gain_part
    stream = stream + enc_stream + part
    mlp_sums = lax.cond(
        decoding,
        lambda dec, enc: mlp_weight_grads(*dec),
        lambda dec, enc: mlp_weight_grads(*enc),
        (normed_dec, dec_kept[1], dec_grads, dec_rows),
        (normed_enc, enc_kept[1], enc_grads, held_after(enc_rows, cross_sum)),
    )

    mlp_sum = stacked(mlp_sums[0]).astype(f32) + stacked(swap_core(mlp_sums[1])).astype(f32)
    cross_sum = stacked(cross_sum)
    fold = mlp_sum.shape[1] // cross_sum.shape[1]
    size = cross_sum.shape[2] // fold
    cross_sum = [cross_sum[:, :, i * size : (i + 1) * size] for i in range(fold)]
    packed = jnp.concatenate([mlp_sum.astype(bf16), jnp.concatenate(cross_sum, 1)], 2)
    g_mlp = lax.psum_scatter(packed, "dp", scatter_dimension=0).astype(f32)
    g_cross = jnp.concatenate(jnp.split(g_mlp[:, 3 * hidden :], fold, 0), 1)
    g_mlp = g_mlp[:, : 3 * hidden]

    self_in = held_after(stream.astype(bf16), mlp_sums[0])
    self_grads, grad_normed, grad_keyside = attention_back(
        self_kept,
        self_weights,
        self_limit,
        starts,
        self_in,
    )
    grad_normed = grad_normed + grad_keyside[:half]
    grad_normed = grad_normed + swap_core(grad_keyside[half:].astype(bf16)).astype(f32)
    part, grad_gain_attn = norm_back(start, gain_attn, grad_normed)
    stream = stream + part
    self_sums = attention_weight_grads(normed, normed_all, self_kept, self_grads, self_in)

    in_order = jnp.where(core == 0, token_ce, jnp.roll(token_ce, half)).reshape(count, 1, -1)
    coarse = in_order.astype(bf16)
    fine = (in_order - coarse.astype(f32)).astype(bf16)
    losses = jnp.concatenate([coarse, fine], 2)
    losses = jnp.pad(losses, ((0, 0), (0, 0), (0, model - losses.shape[2])))
    moved = reroute_plane(jnp.concatenate([lend(stream.astype(bf16)), losses], 1), pairing)
    piece = in_order.shape[2]
    losses = moved[:, -1].astype(f32)
    token_loss = (losses[:, :piece] + losses[:, piece : 2 * piece]).reshape(1, -1)
    seq_loss = jnp.sum(token_loss, axis=1) / target_len[me].astype(f32)
    moved = moved[:, :-1].reshape(half // 2, model)
    d_states = jnp.where(
        decoding, jnp.concatenate([to_decoder(moved), moved], 0).astype(f32), stream
    )

    cut = grad_gain_cross.shape[0] // 2
    lent_gains = to_encoder(grad_gain_cross[:cut])
    gain_grads = [grad_gain_attn, grad_gain_mlp, grad_gain_final]
    gain_grads.append(jnp.where(decoding, grad_gain_cross[cut:], lent_gains))
    packed = jnp.concatenate([grad.reshape(count, 1, -1) for grad in gain_grads], 2).astype(bf16)
    packed = jnp.pad(packed, ((0, 0), (0, 15), (0, 4 * width - packed.shape[2])))
    self_scattering = scatter_stacks(
        [[stacked(self_sums[0]), packed], [stacked(swap_core(self_sums[1])), swap_core(packed)]],
    )
    for _ in range(3):
        self_scattering.step()
    g_attn = self_scattering.total()
    gain_own = g_attn[gain_rows : gain_rows + 1]
    g_attn = g_attn[:gain_rows]
    g_key, g_value = unpaired(g_attn[:, width : 3 * width])
    g_cross_key, g_cross_value = unpaired(g_cross[:, width : 3 * width])

    return (
        seq_loss,
        d_states[None, None],
        gain_own[:, :gain_rows],
        g_attn[None, :, :width],
        g_key[None],
        g_value[None],
        g_attn[:, 3 * width :].T[None],
        gain_own[:, gain_rows : 2 * gain_rows],
        g_mlp[None, :, :hidden],
        g_mlp[None, :, hidden : 2 * hidden],
        g_mlp[:, 2 * hidden :].T[None],
        gain_own[:, 2 * gain_rows : 3 * gain_rows],
        gain_own[0, 3 * gain_rows : 3 * gain_rows + cross_rows],
        g_cross[:, :width],
        g_cross_key,
        g_cross_value,
        g_cross[:, 3 * width :].T,
        g_embedding.astype(f32),
        token_loss,
    )


def solution(mesh):
    layer = P("slab", "dp", "mp")
    shared = P(("slab", "dp"), "mp")
    gain = P("slab", "dp")
    turned = P("slab", "mp", "dp")
    tokens = P("slab", "dp", "mp", None)
    weights = (gain, layer, layer, layer, turned, gain, layer, layer, turned, gain)
    crossing = (P(("slab", "dp")), shared, shared, shared, P("mp", ("slab", "dp")))
    table = P(("slab", "dp", "mp"), None)
    return jax.shard_map(
        on_device,
        mesh=mesh,
        in_specs=(tokens,) + weights + crossing + (table, P(), P(), P("dp", None), P()),
        out_specs=(P("dp"), tokens) + weights + crossing + (table, P("dp", None)),
        check_vma=False,
    )
```

time: 1100 us -> 755 us (0.69)
  matrix products: 322 us -> 158 us
  starting transfers between devices: 182 us -> 82.7 us
  Pallas kernels: 25.7 us -> 121 us
  waiting for transfers between devices: 253 us -> 184 us
  other arithmetic: 154 us -> 92 us
  between operations: 50.5 us -> 22.7 us
  local copies, waits for them, and re-layouts: 95.4 us -> 82.9 us
    dot_general x12 -> x0, matrix products: 135 us -> none  [the longest x2 39.3 us: attend_back(): jnp.einsum('qhd,khd->hqk', grad_heads, value_rows, preferred_element_type...]
    ppermute x120 -> x24, starting transfers between devices: 152 us -> 27.6 us  [loop_step(): return lax.ppermute(value, 'dp', pairs)]
    pallas_call x5 -> x14, Pallas kernels: 25.7 us -> 121 us  [the longest x4 59.2 us: attend_back(): pl.pallas_call(attend_back_body, out_shape=[jax.ShapeDtypeStruct((rows, w...]
    ppermute x120 -> x24, waiting for transfers between devices: 164 us -> 82.7 us  [loop_step(): return lax.ppermute(value, 'dp', pairs)]
    dot_general x28 -> x17, matrix products: 53.7 us -> 27.1 us  [contract_first(): lax.dot_general(a, b, (((0,), (0,)), ((), ())), preferred_element_type=f32)]
    convert_element_type x26 -> x20, other arithmetic: 55.4 us -> 28.7 us  [the longest x1 9.03 us: on_device(): grad_logits = jnp.where(counted[:, None], jnp.exp(logits - log_total[:, N...]
    reduce_sum x3 -> x1, other arithmetic: 28.8 us -> 7.62 us  [on_device(): totals = jnp.sum(jnp.exp(logits - highest[:, None]), axis=1)]
    all_to_all x0 -> x4, starting transfers between devices: none -> 18.2 us  [the longest x2 10.7 us: reroute_plane(): lax.all_to_all(pieces, 'dp', split_axis=0, concat_axis=0, tiled=True)]
  transfers between devices with their start and end apart: 152 -> 66, of which waited for: 56 -> 25; matrix products, arithmetic and copies ran while one was open for 46% -> 36% of each run, Pallas kernels for 2% -> 15%
where the time goes in v2:
time: 755 us; the launch traced here: 745 us
  waiting for transfers between devices  184 us (24%)
  matrix products  158 us (21%)
  Pallas kernels  121 us (16%)
  other arithmetic  92 us (12%)
  local copies, waits for them, and re-layouts  82.9 us (11%)
  starting transfers between devices  82.7 us (11%)
  between operations  22.7 us (3%)
    ppermute x24, waiting for transfers between devices, loop_step(): return lax.ppermute(value, 'dp', pairs)  82.7 us
    dot_general x21, matrix products, matmul(): return jnp.dot(a, b, preferred_element_type=f32)  73.2 us
    ppermute x6, waiting for transfers between devices, to_encoder(): return lax.ppermute(value, 'slab', [(1, 0)])  61 us
    pallas_call x4, Pallas kernels, attend_back(): pl.pallas_call(attend_back_body, out_shape=[jax.ShapeDtypeStruct((rows, w...  59.2 us
    dot_general x21, matrix products, contract_last(): lax.dot_general(a, b, (((1,), (1,)), ((), ())), preferred_element_type=f32)  57.9 us
    pallas_call x4, Pallas kernels, attend(): pl.pallas_call(attend_body, out_shape=[jax.ShapeDtypeStruct((rows, width)...  38.5 us
    unnamed x385, local copies, waits for them, and re-layouts  33.9 us
    ppermute x24, starting transfers between devices, loop_step(): return lax.ppermute(value, 'dp', pairs)  27.6 us
  transfers between devices with their start and end apart: 66, of which 25 were waited for; matrix products, arithmetic and copies ran while one was open for 36% of the time, Pallas kernels for 15%

profile of v2, /device:TPU:0, one launch (start us, length us, event | category | flops | bytes accessed | tf_op | source)
XLA Modules:
  0.0 744.5 jit_solution(11553201562968640643)
XLA Ops:
  17.3 7.9 %collective-permute-done.3.refs_2_ = bf16[112,1536]{1,0:T(8,128)(2,1)S(1)} collective-permute-done((bf16[112,1536]{1,0:T(8,128)(2,1)S(1)}, bf16[112,1536]{1,0:T(8,128)(2,1)S(1)}, u32[]{:S(2)}, u32[]{:S(2)}) %collective-permute-start.3) | collective-permute-done | bytes 344096 | tf_op jit(solution)/shard_map/ppermute | solution.py:39
  28.0 6.0 all-to-all-start
  34.9 4.9 collective-permute-start.10
  42.2 3.2 all-to-all-done
  46.7 4.0 all-to-all-start.1
  54.8 5.5 assemble.2
  62.1 3.4 collective-permute-start.21
  65.5 3.9 collective-permute-start.1
  91.5 4.4 collective-permute-start.20
  98.3 7.2 collective-permute-done.22.refs_3_
  113.1 12.8 %collective-permute-done.23.refs_5_ = bf16[96,4608]{1,0:T(8,128)(2,1)} collective-permute-done((bf16[96,4608]{1,0:T(8,128)(2,1)}, bf16[96,4608]{1,0:T(8,128)(2,1)}, u32[]{:S(2)}, u32[]{:S(2)}) %collective-permute-start.23) | collective-permute-done | bytes 884768 | tf_op jit(solution)/shard_map/ppermute | solution.py:39
  126.6 7.6 %assemble.3 = (bf16[1,8,96,2048]{3,2,1,0:T(8,128)(2,1)}, bf16[1,8,96,1024]{3,2,1,0:T(8,128)(2,1)}, bf16[2,8,48,384]{3,2,1,0:T(8,128)(2,1)}, bf16[2,8,48,768]{3,2,1,0:T(8,128)(2,1)}, bf16[2,8,48,384]{3,2,1,0:T(8,128)(2,1)}) custom-call(s32[7]{0:T(128)} %bitcast.468, bf16[96,4608]{1,0:T(8,128)(2,1)} %copy-done.34, ...), custom_call_target="tpu_custom_call" | custom-call | bytes 12386304 | tf_op jit(solution)/shard_map/assemble/pallas_call | solution.py:168
  134.6 4.4 convolution_convert_fusion.10.pair_ref
  144.6 9.6 %attend.4 = (bf16[512,384]{1,0:T(8,128)(2,1)}, f32[3,2,512]{2,1,0:T(2,128)}) custom-call(s32[2]{0:T(128)} %pad_add_fusion.start_ref, bf16[512,384]{1,0:T(8,128)(2,1)} %convolution_convert_fusion.31.query_ref, bf16[1024,768]{1,0:T(8,128)(2,1)} %convolution_convert_fusion.11.pair_ref, s32[1,512]{1,0:T(1,128)} %broadcast_select_fusion.2.limit_ref), custom_call_target="tpu_custom_call" | custom-call | flops 3145728 | bytes 12288 | tf_op jit(solution)/shard_map/attend/pallas_call | solution.py:361
  154.2 9.4 %attend.5 = (bf16[512,384]{1,0:T(8,128)(2,1)}, f32[3,2,512]{2,1,0:T(2,128)}) custom-call(s32[2]{0:T(128)} %pad_add_fusion.start_ref, bf16[512,384]{1,0:T(8,128)(2,1)} %convolution_convert_fusion.30.query_ref, bf16[1024,768]{1,0:T(8,128)(2,1)} %convolution_convert_fusion.10.pair_ref, s32[1,512]{1,0:T(1,128)} %broadcast_select_fusion.2.limit_ref), custom_call_target="tpu_custom_call" | custom-call | flops 3145728 | bytes 12288 | tf_op jit(solution)/shard_map/attend/pallas_call | solution.py:361
  168.1 10.7 %collective-permute-done.25 = bf16[48,4608]{1,0:T(8,128)(2,1)S(1)} collective-permute-done((bf16[48,4608]{1,0:T(8,128)(2,1)S(1)}, bf16[48,4608]{1,0:T(8,128)(2,1)S(1)}, u32[]{:S(2)}, u32[]{:S(2)}) %collective-permute-start.25) | collective-permute-done | bytes 442400 | tf_op jit(solution)/shard_map/ppermute | solution.py:39
  189.6 3.7 fusion.134
  193.3 5.2 fusion.135
  200.6 3.2 fusion.136
  206.6 5.7 collective-permute-start.32
  212.3 16.1 %collective-permute-done.32 = bf16[512,768]{1,0:T(8,128)(2,1)} collective-permute-done((bf16[512,768]{1,0:T(8,128)(2,1)S(1)}, bf16[512,768]{1,0:T(8,128)(2,1)}, u32[]{:S(2)}, u32[]{:S(2)}) %collective-permute-start.32) | collective-permute-done | bytes 786464 | tf_op jit(solution)/shard_map/ppermute | solution.py:32
  236.6 4.4 convolution_convert_fusion.8.pair_ref
  241.6 9.5 %attend.7 = (bf16[512,384]{1,0:T(8,128)(2,1)}, f32[3,2,512]{2,1,0:T(2,128)}) custom-call(s32[2]{0:T(128)} %pad_add_fusion.start_ref, bf16[512,384]{1,0:T(8,128)(2,1)} %convolution_convert_fusion.28.query_ref, bf16[1024,768]{1,0:T(8,128)(2,1)} %convolution_convert_fusion.8.pair_ref, s32[1,512]{1,0:T(1,128)} %broadcast_in_dim.60.limit_ref), custom_call_target="tpu_custom_call" | custom-call | flops 3145728 | bytes 12288 | tf_op jit(solution)/shard_map/attend/pallas_call | solution.py:361
  251.0 4.3 convolution_convert_fusion.9.pair_ref
  255.4 10.0 %attend.6 = (bf16[512,384]{1,0:T(8,128)(2,1)}, f32[3,2,512]{2,1,0:T(2,128)}) custom-call(s32[2]{0:T(128)} %pad_add_fusion.start_ref, bf16[512,384]{1,0:T(8,128)(2,1)} %convolution_convert_fusion.29.query_ref, bf16[1024,768]{1,0:T(8,128)(2,1)} %convolution_convert_fusion.9.pair_ref, s32[1,512]{1,0:T(1,128)} %broadcast_in_dim.60.limit_ref), custom_call_target="tpu_custom_call" | custom-call | flops 3145728 | bytes 12288 | tf_op jit(solution)/shard_map/attend/pallas_call | solution.py:361
  269.6 4.0 fusion.139
  289.3 18.2 %collective-permute-done.34 = bf16[512,768]{1,0:T(8,128)(2,1)S(1)} collective-permute-done((bf16[512,768]{1,0:T(8,128)(2,1)S(1)}, bf16[512,768]{1,0:T(8,128)(2,1)S(1)}, u32[]{:S(2)}, u32[]{:S(2)}) %collective-permute-start.34) | collective-permute-done | bytes 786464 | tf_op jit(solution)/shard_map/ppermute | solution.py:28
  311.2 9.6 %multiply_reduce_fusion = (f32[1024]{0:T(1024)S(1)}, f32[1024,4096]{1,0:T(8,128)S(1)}) fusion(bf16[4096,768]{1,0:T(8,128)(2,1)} %all-gather.2.cloned.1.call-done, bf16[512,768]{1,0:T(8,128)(2,1)} %collective-permute-done.35, bf16[512,768]{1,0:T(8,128)(2,1)} %copy-done.108), kind=kOutput, calls=%fused_computation.21 | convolution fusion | flops 6453984256 | bytes 24645632 | tf_op jit(solution)/shard_map/dot_general | solution.py:241
  320.8 7.6 %exponential_reduce_fusion = (f32[1024]{0:T(1024)S(1)}, f32[1024]{0:T(1024)S(1)}) fusion(f32[1024,4096]{1,0:T(8,128)S(1)} %get-tuple-element.289, f32[1024]{0:T(1024)S(1)} %get-tuple-element.288, s32[1024]{0:T(1024)S(1)} %copy-done.150, s32[4096]{0:T(1024)S(1)} %copy-done.131), kind=kLoop, calls=%fused_computation.20 | loop fusion | flops 25163776 | bytes 16809984 | tf_op jit(solution)/shard_map/reduce_sum | solution.py:652
  336.6 9.0 %fusion.3 = bf16[1024,4096]{1,0:T(8,128)(2,1)S(1)} fusion(f32[1024,4096]{1,0:T(8,128)} %copy-done, f32[1024]{0:T(1024)S(1)} %log_add_fusion, s32[4096]{0:T(1024)} %fusion.78, s32[1024]{0:T(1024)} %add_select_fusion.2, pred[1024]{0:T(1024)(128)(4,1)} %add_compare_fusion), kind=kLoop, calls=%fused_computation.19 | loop fusion | flops 29360128 | bytes 25191424 | tf_op jit(solution)/shard_map/convert_element_type | solution.py:662
  345.7 9.0 %convolution_multiply_fusion = f32[1024,768]{1,0:T(8,128)S(1)} fusion(bf16[1024,4096]{1,0:T(8,128)(2,1)S(1)} %fusion.3, bf16[4096,768]{1,0:T(8,128)(2,1)} %all-gather.2.cloned.1.call-done), kind=kOutput, calls=%fused_computation.91 | convolution fusion | flops 6443237376 | bytes 17825792 | tf_op jit(solution)/shard_map/dot_general | solution.py:237
  361.5 10.1 %multiply_convert_fusion = bf16[4096,768]{1,0:T(8,128)(2,1)} fusion(bf16[1024,4096]{1,0:T(8,128)(2,1)S(1)} %fusion.3, bf16[512,768]{1,0:T(8,128)(2,1)} %collective-permute-done.35, bf16[512,768]{1,0:T(8,128)(2,1)S(1)} %copy-done.109), kind=kOutput, calls=%fused_computation.22 | convolution fusion | flops 6451888128 | bytes 16252928 | tf_op jit(solution)/shard_map/dot_general | solution.py:245
  371.9 6.4 collective-permute-done.39
  383.6 4.1 fusion.24
  387.7 4.5 fusion.31
  392.2 4.5 fusion.114
  399.5 3.1 fusion.119
  406.3 15.0 %attend_back.5 = (bf16[512,384]{1,0:T(8,128)(2,1)}, bf16[1024,768]{1,0:T(8,128)(2,1)}) custom-call(s32[2]{0:T(128)} %pad_add_fusion.start_ref, bf16[512,384]{1,0:T(8,128)(2,1)} %convolution_convert_fusion.28.query_ref, bf16[1024,768]{1,0:T(8,128)(2,1)} %convolution_convert_fusion.8.pair_ref, s32[1,512]{1,0:T(1,128)} %broadcast_in_dim.60.limit_ref, ...), custom_call_target="tpu_custom_call" | custom-call | flops 3145728 | bytes 12288 | tf_op jit(solution)/shard_map/attend_back/pallas_call | solution.py:384
  421.3 4.9 fusion.142
  426.3 14.7 %attend_back.4 = (bf16[512,384]{1,0:T(8,128)(2,1)}, bf16[1024,768]{1,0:T(8,128)(2,1)}) custom-call(s32[2]{0:T(128)} %pad_add_fusion.start_ref, bf16[512,384]{1,0:T(8,128)(2,1)} %convolution_convert_fusion.29.query_ref, bf16[1024,768]{1,0:T(8,128)(2,1)} %convolution_convert_fusion.9.pair_ref, s32[1,512]{1,0:T(1,128)} %broadcast_in_dim.60.limit_ref, ...), custom_call_target="tpu_custom_call" | custom-call | flops 3145728 | bytes 12288 | tf_op jit(solution)/shard_map/attend_back/pallas_call | solution.py:384
  441.0 4.4 convolution_add_fusion.1
  458.3 17.2 %collective-permute-done.41 = bf16[512,768]{1,0:T(8,128)(2,1)S(1)} collective-permute-done((bf16[512,768]{1,0:T(8,128)(2,1)S(1)}, bf16[512,768]{1,0:T(8,128)(2,1)S(1)}, u32[]{:S(2)}, u32[]{:S(2)}) %collective-permute-start.41) | collective-permute-done | bytes 786464 | tf_op jit(solution)/shard_map/ppermute | solution.py:28
  477.7 3.8 fusion.10
  486.1 3.8 fusion.17
  491.3 19.9 %collective-permute-done.43 = bf16[384,1536]{0,1:T(8,128)(2,1)S(1)} collective-permute-done((bf16[384,1536]{0,1:T(8,128)(2,1)S(1)}, bf16[384,1536]{0,1:T(8,128)(2,1)S(1)}, u32[]{:S(2)}, u32[]{:S(2)}) %collective-permute-start.43) | collective-permute-done | bytes 1179680 | tf_op jit(solution)/shard_map/ppermute | solution.py:28
  512.4 10.1 %conditional.1 = ((bf16[768,3072]{1,0:T(8,128)(2,1)}, bf16[768,3072]{1,0:T(8,128)(2,1)})) conditional(s32[]{:T(128)} %convert_element_type.490, (bf16[512,768]{1,0:T(8,128)(2,1)S(1)}, bf16[512,2048]{1,0:T(8,128)(2,1)S(1)}, bf16[512,768]{1,0:T(8,128)(2,1)S(1)}, bf16[512,1024]{1,0:T(8,128)(2,1)S(1)}, bf16[512,2048]{1,0:T(8,128)(2,1)S(1)}, ...), branch_computations={%region_15.16_spmd, %region_16.17_spmd} | conditional | flops 4855431168 | bytes 60817556 | solution.py:705
  518.2 4.0 pad_maximum_fusion
  525.3 3.9 fusion.113
  540.7 14.7 %attend_back.7 = (bf16[512,384]{1,0:T(8,128)(2,1)}, bf16[1024,768]{1,0:T(8,128)(2,1)}) custom-call(s32[2]{0:T(128)} %pad_add_fusion.start_ref, bf16[512,384]{1,0:T(8,128)(2,1)} %convolution_convert_fusion.30.query_ref, bf16[1024,768]{1,0:T(8,128)(2,1)} %convolution_convert_fusion.10.pair_ref, s32[1,512]{1,0:T(1,128)} %broadcast_select_fusion.2.limit_ref, ...), custom_call_target="tpu_custom_call" | custom-call | flops 3145728 | bytes 12288 | tf_op jit(solution)/shard_map/attend_back/pallas_call | solution.py:384
  557.7 14.8 %attend_back.6 = (bf16[512,384]{1,0:T(8,128)(2,1)}, bf16[1024,768]{1,0:T(8,128)(2,1)}) custom-call(s32[2]{0:T(128)} %pad_add_fusion.start_ref, bf16[512,384]{1,0:T(8,128)(2,1)} %convolution_convert_fusion.31.query_ref, bf16[1024,768]{1,0:T(8,128)(2,1)} %convolution_convert_fusion.11.pair_ref, s32[1,512]{1,0:T(1,128)} %broadcast_select_fusion.2.limit_ref, ...), custom_call_target="tpu_custom_call" | custom-call | flops 3145728 | bytes 12288 | tf_op jit(solution)/shard_map/attend_back/pallas_call | solution.py:384
  577.0 5.4 add_convert_fusion
  582.4 4.4 maximum_maximum_fusion
  604.1 4.3 copy.98
  610.2 4.6 collective-permute-done.45
  617.4 4.7 all-to-all-start.2
  631.1 3.3 constant_dynamic-slice_fusion.14
  639.5 10.1 %all-to-all-done.2 = bf16[8,33,768]{2,1,0:T(8,128)(2,1)S(1)} async-done(((bf16[8,33,768]{2,1,0:T(8,128)(2,1)}), bf16[8,33,768]{2,1,0:T(8,128)(2,1)S(1)}, u32[]{:S(2)}, u32[]{:S(2)}) %all-to-all-start.2) | async-done | bytes 405536 | tf_op jit(solution)/shard_map/all_to_all | solution.py:232
  651.1 3.5 all-to-all-start.3
  654.6 4.3 copy.99
  664.2 6.7 collective-permute-done.50
  679.4 7.0 collective-permute-done.51
  691.2 5.7 collective-permute-done.52
  704.3 9.7 %collective-permute-done.53 = bf16[112,1536]{1,0:T(8,128)(2,1)S(1)} collective-permute-done((bf16[112,1536]{1,0:T(8,128)(2,1)S(1)}, bf16[112,1536]{1,0:T(8,128)(2,1)S(1)}, u32[]{:S(2)}, u32[]{:S(2)}) %collective-permute-start.53) | collective-permute-done | bytes 344096 | tf_op jit(solution)/shard_map/ppermute | solution.py:39
  713.9 10.7 %collective-permute-done.57 = bf16[112,1536]{1,0:T(8,128)(2,1)S(1)} collective-permute-done((bf16[112,1536]{1,0:T(8,128)(2,1)S(1)}, bf16[112,1536]{1,0:T(8,128)(2,1)S(1)}, u32[]{:S(2)}, u32[]{:S(2)}) %collective-permute-start.57) | collective-permute-done | bytes 344096 | tf_op jit(solution)/shard_map/ppermute | solution.py:39
  (711 shorter events, 258.9 us)
Async XLA Ops:
  8.4 18.8 %collective-permute-start = (bf16[256,768]{1,0:T(8,128)(2,1)S(1)}, bf16[256,768]{1,0:T(8,128)(2,1)S(1)}, u32[]{:S(2)}, u32[]{:S(2)}) collective-permute-start(bf16[256,768]{1,0:T(8,128)(2,1)S(1)} %slice_bitcast_fusion.3), channel_id=1, source_target_pairs={{16,0},{17,1},{18,2},{19,3},{20,4},{21,5},{22,6},{23,7},{24,8},{25... | collective-permute-start | bytes 1179656 | tf_op jit(solution)/shard_map/ppermute | solution.py:28
  14.1 11.1 %collective-permute-start.3 = (bf16[112,1536]{1,0:T(8,128)(2,1)S(1)}, bf16[112,1536]{1,0:T(8,128)(2,1)S(1)}, u32[]{:S(2)}, u32[]{:S(2)}) collective-permute-start(bf16[112,1536]{1,0:T(8,128)(2,1)S(1)} %concatenate.252.refs_0_), channel_id=1, source_target_pairs={{0,2},{4,0},{8,4},{12,8},{14,12},{10,14},{6,10},{2,6},{1,3},{5,1},... | collective-permute-start | bytes 1032200 | tf_op jit(solution)/shard_map/ppermute | solution.py:39
  17.1 9.8 %collective-permute-start.2 = (bf16[112,1536]{1,0:T(8,128)(2,1)S(1)}, bf16[112,1536]{1,0:T(8,128)(2,1)S(1)}, u32[]{:S(2)}, u32[]{:S(2)}) collective-permute-start(bf16[112,1536]{1,0:T(8,128)(2,1)S(1)} %concatenate.252.refs_0_), channel_id=1, source_target_pairs={{0,4},{4,8},{8,12},{12,14},{14,10},{10,6},{6,2},{2,0},{1,5},{5,9},... | collective-permute-start | bytes 1032200 | tf_op jit(solution)/shard_map/ppermute | solution.py:39
  25.2 14.8 %collective-permute-start.5 = (bf16[112,1536]{1,0:T(8,128)(2,1)S(1)}, bf16[112,1536]{1,0:T(8,128)(2,1)}, u32[]{:S(2)}, u32[]{:S(2)}) collective-permute-start(bf16[112,1536]{1,0:T(8,128)(2,1)S(1)} %collective-permute-done.3.refs_2_), channel_id=1, source_target_pairs={{0,2},{4,0},{8,4},{12,8},{14,12},{10,14},{6,10},{2,6},{1,3},{5,1},... | collective-permute-start | bytes 1032200 | tf_op jit(solution)/shard_map/ppermute | solution.py:39
  26.9 15.2 %collective-permute-start.4 = (bf16[112,1536]{1,0:T(8,128)(2,1)S(1)}, bf16[112,1536]{1,0:T(8,128)(2,1)}, u32[]{:S(2)}, u32[]{:S(2)}) collective-permute-start(bf16[112,1536]{1,0:T(8,128)(2,1)S(1)} %collective-permute-done.2.refs_1_), channel_id=1, source_target_pairs={{0,4},{4,8},{8,12},{12,14},{14,10},{10,6},{6,2},{2,0},{1,5},{5,9},... | collective-permute-start | bytes 1032200 | tf_op jit(solution)/shard_map/ppermute | solution.py:39
  28.0 17.3 %all-to-all-start = ((bf16[8,32,768]{2,1,0:T(8,128)(2,1)}), bf16[8,32,768]{2,1,0:T(8,128)(2,1)S(1)}, u32[]{:S(2)}, u32[]{:S(2)}) async-start(bf16[8,32,768]{2,1,0:T(8,128)(2,1)} %bitcast.2), calls=%async_computation | async-start | bytes 786432 | tf_op jit(solution)/shard_map/all_to_all | solution.py:232
  34.9 25.5 %collective-permute-start.10 = (bf16[48,1536]{1,0:T(8,128)(2,1)}, bf16[48,1536]{1,0:T(8,128)(2,1)}, u32[]{:S(2)}, u32[]{:S(2)}) collective-permute-start(bf16[48,1536]{1,0:T(8,128)(2,1)} %pad_maximum_fusion.21), channel_id=1, source_target_pairs={{0,16},{1,17},{2,18},{3,19},{4,20},{5,21},{6,22},{7,23},{8,24},{9,... | collective-permute-start | bytes 442376 | tf_op jit(solution)/shard_map/ppermute | solution.py:32
  40.0 11.3 %collective-permute-start.7 = (bf16[112,1536]{1,0:T(8,128)(2,1)}, bf16[112,1536]{1,0:T(8,128)(2,1)S(1)}, u32[]{:S(2)}, u32[]{:S(2)}) collective-permute-start(bf16[112,1536]{1,0:T(8,128)(2,1)} %collective-permute-done.5.refs_4_), channel_id=1, source_target_pairs={{0,2},{4,0},{8,4},{12,8},{14,12},{10,14},{6,10},{2,6},{1,3},{5,1},... | collective-permute-start | bytes 1032200 | tf_op jit(solution)/shard_map/ppermute | solution.py:39
  42.1 11.9 %collective-permute-start.6 = (bf16[112,1536]{1,0:T(8,128)(2,1)}, bf16[112,1536]{1,0:T(8,128)(2,1)S(1)}, u32[]{:S(2)}, u32[]{:S(2)}) collective-permute-start(bf16[112,1536]{1,0:T(8,128)(2,1)} %collective-permute-done.4.refs_3_), channel_id=1, source_target_pairs={{0,4},{4,8},{8,12},{12,14},{14,10},{10,6},{6,2},{2,0},{1,5},{5,9},... | collective-permute-start | bytes 1032200 | tf_op jit(solution)/shard_map/ppermute | solution.py:39
  46.7 18.8 %all-to-all-start.1 = ((bf16[8,32,768]{2,1,0:T(8,128)(2,1)}), bf16[8,32,768]{2,1,0:T(8,128)(2,1)S(1)}, u32[]{:S(2)}, u32[]{:S(2)}) async-start(bf16[8,32,768]{2,1,0:T(8,128)(2,1)} %gather_fusion), calls=%async_computation.1 | async-start | bytes 786432 | tf_op jit(solution)/shard_map/all_to_all | solution.py:233
  50.7 260.4 %all-gather.2.cloned.1.call-start = ((), (), s32[]{:S(2)}) async-start(), calls=%async_computation.6 | async-start | bytes 7077888 | tf_op jit(solution)/shard_map/all_gather | solution.py:616
  52.0 10.1 %collective-permute-start.9 = (bf16[56,1536]{1,0:T(8,128)(2,1)}, bf16[56,1536]{1,0:T(8,128)(2,1)}, u32[]{:S(2)}, u32[]{:S(2)}) collective-permute-start(bf16[56,1536]{1,0:T(8,128)(2,1)} %slice.390), channel_id=1, source_target_pairs={{0,2},{4,0},{8,4},{12,8},{14,12},{10,14},{6,10},{2,6},{1,3},{5,1},... | collective-permute-start | bytes 516104 | tf_op jit(solution)/shard_map/ppermute | solution.py:39
  54.8 10.7 %collective-permute-start.8 = (bf16[56,1536]{1,0:T(8,128)(2,1)}, bf16[56,1536]{1,0:T(8,128)(2,1)}, u32[]{:S(2)}, u32[]{:S(2)}) collective-permute-start(bf16[56,1536]{1,0:T(8,128)(2,1)} %slice.389), channel_id=1, source_target_pairs={{0,4},{4,8},{8,12},{12,14},{14,10},{10,6},{6,2},{2,0},{1,5},{5,9},... | collective-permute-start | bytes 516104 | tf_op jit(solution)/shard_map/ppermute | solution.py:39
  60.4 27.4 %collective-permute-start.14 = (bf16[1,8,96,768]{3,2,1,0:T(8,128)(2,1)}, bf16[1,8,96,768]{3,2,1,0:T(8,128)(2,1)}, u32[]{:S(2)}, u32[]{:S(2)}) collective-permute-start(bf16[1,8,96,768]{3,2,1,0:T(8,128)(2,1)} %get-tuple-element.109.refs_1_), channel_id=1, source_target_pairs={{0,1},{1,0},{2,3},{3,2},{4,5},{5,4},{6,7},{7,6},{8,9},{9,8},{10,11... | collective-permute-start | bytes 3538952 | tf_op jit(solution)/shard_map/ppermute | solution.py:20
  61.6 16.1 %collective-permute-start.16 = (bf16[1,8,16,1536]{3,2,1,0:T(8,128)(2,1)}, bf16[1,8,16,1536]{3,2,1,0:T(8,128)(2,1)S(1)}, u32[]{:S(2)}, u32[]{:S(2)}) collective-permute-start(bf16[1,8,16,1536]{3,2,1,0:T(8,128)(2,1)} %get-tuple-element.111.refs_3_), channel_id=1, source_target_pairs={{0,1},{1,0},{2,3},{3,2},{4,5},{5,4},{6,7},{7,6},{8,9},{9,8},{10,11... | collective-permute-start | bytes 1179656 | tf_op jit(solution)/shard_map/ppermute | solution.py:20
  62.1 22.0 %collective-permute-start.21 = (bf16[96,4608]{1,0:T(8,128)(2,1)S(1)}, bf16[96,4608]{1,0:T(8,128)(2,1)}, u32[]{:S(2)}, u32[]{:S(2)}) collective-permute-start(bf16[96,4608]{1,0:T(8,128)(2,1)S(1)} %maximum_maximum_fusion.1.refs_0_), channel_id=1, source_target_pairs={{0,4},{4,8},{8,12},{12,14},{14,10},{10,6},{6,2},{2,0},{1,5},{5,9},... | collective-permute-start | bytes 2654216 | tf_op jit(solution)/shard_map/ppermute | solution.py:39
  65.5 20.4 %collective-permute-start.11 = (bf16[96,4608]{1,0:T(8,128)(2,1)S(1)}, bf16[96,4608]{1,0:T(8,128)(2,1)}, u32[]{:S(2)}, u32[]{:S(2)}) collective-permute-start(bf16[96,4608]{1,0:T(8,128)(2,1)S(1)} %maximum_maximum_fusion.1.refs_0_), channel_id=1, source_target_pairs={{0,2},{4,0},{8,4},{12,8},{14,12},{10,14},{6,10},{2,6},{1,3},{5,1},... | collective-permute-start | bytes 2654216 | tf_op jit(solution)/shard_map/ppermute | solution.py:39
  65.5 12.3 %collective-permute-start.1 = (bf16[256,768]{1,0:T(8,128)(2,1)S(1)}, bf16[256,768]{1,0:T(8,128)(2,1)}, u32[]{:S(2)}, u32[]{:S(2)}) collective-permute-start(bf16[256,768]{1,0:T(8,128)(2,1)S(1)} %bitcast.413), channel_id=1, source_target_pairs={{0,16},{1,17},{2,18},{3,19},{4,20},{5,21},{6,22},{7,23},{8,24},{9,... | collective-permute-start | bytes 1179656 | tf_op jit(solution)/shard_map/ppermute | solution.py:32
  77.8 8.4 %collective-permute-start.13 = (bf16[1,8,96,384]{3,2,1,0:T(8,128)(2,1)S(1)}, bf16[1,8,96,384]{3,2,1,0:T(8,128)(2,1)S(1)}, u32[]{:S(2)}, u32[]{:S(2)}) collective-permute-start(bf16[1,8,96,384]{3,2,1,0:T(8,128)(2,1)S(1)} %copy-done.39), channel_id=1, source_target_pairs={{0,1},{1,0},{2,3},{3,2},{4,5},{5,4},{6,7},{7,6},{8,9},{9,8},{10,11... | collective-permute-start | bytes 1769480 | tf_op jit(solution)/shard_map/ppermute | solution.py:20
  77.8 8.4 %collective-permute-start.15 = (bf16[1,8,96,384]{3,2,1,0:T(8,128)(2,1)}, bf16[1,8,96,384]{3,2,1,0:T(8,128)(2,1)S(1)}, u32[]{:S(2)}, u32[]{:S(2)}) collective-permute-start(bf16[1,8,96,384]{3,2,1,0:T(8,128)(2,1)} %get-tuple-element.110.refs_2_), channel_id=1, source_target_pairs={{0,1},{1,0},{2,3},{3,2},{4,5},{5,4},{6,7},{7,6},{8,9},{9,8},{10,11... | collective-permute-start | bytes 1769480 | tf_op jit(solution)/shard_map/ppermute | solution.py:20
  84.1 21.4 %collective-permute-start.22 = (bf16[96,4608]{1,0:T(8,128)(2,1)}, bf16[96,4608]{1,0:T(8,128)(2,1)}, u32[]{:S(2)}, u32[]{:S(2)}) collective-permute-start(bf16[96,4608]{1,0:T(8,128)(2,1)} %collective-permute-done.21.refs_1_), channel_id=1, source_target_pairs={{0,4},{4,8},{8,12},{12,14},{14,10},{10,6},{6,2},{2,0},{1,5},{5,9},... | collective-permute-start | bytes 2654216 | tf_op jit(solution)/shard_map/ppermute | solution.py:39
  85.8 20.5 %collective-permute-start.18 = (bf16[96,4608]{1,0:T(8,128)(2,1)}, bf16[96,4608]{1,0:T(8,128)(2,1)}, u32[]{:S(2)}, u32[]{:S(2)}) collective-permute-start(bf16[96,4608]{1,0:T(8,128)(2,1)} %collective-permute-done.11.refs_2_), channel_id=1, source_target_pairs={{0,2},{4,0},{8,4},{12,8},{14,12},{10,14},{6,10},{2,6},{1,3},{5,1},... | collective-permute-start | bytes 2654216 | tf_op jit(solution)/shard_map/ppermute | solution.py:39
  86.1 9.8 %collective-permute-start.17 = (bf16[112,1536]{1,0:T(8,128)(2,1)}, bf16[112,1536]{1,0:T(8,128)(2,1)}, u32[]{:S(2)}, u32[]{:S(2)}) collective-permute-start(bf16[112,1536]{1,0:T(8,128)(2,1)} %constant_dynamic-update-slice_fusion.refs_4_), channel_id=1, source_target_pairs={{0,1},{1,0},{2,3},{3,2},{4,5},{5,4},{6,7},{7,6},{8,9},{9,8},{10,11... | collective-permute-start | bytes 1032200 | tf_op jit(solution)/shard_map/ppermute | solution.py:20
  87.8 25.0 %collective-permute-start.12 = (bf16[512,768]{1,0:T(8,128)(2,1)S(1)}, bf16[512,768]{1,0:T(8,128)(2,1)S(1)}, u32[]{:S(2)}, u32[]{:S(2)}) collective-permute-start(bf16[512,768]{1,0:T(8,128)(2,1)S(1)} %get-tuple-element.198), channel_id=1, source_target_pairs={{0,1},{1,0},{2,3},{3,2},{4,5},{5,4},{6,7},{7,6},{8,9},{9,8},{10,11... | collective-permute-start | bytes 2359304 | tf_op jit(solution)/shard_map/ppermute | solution.py:20
  91.5 21.3 %collective-permute-start.20 = (f32[384]{0:T(512)S(1)}, f32[384]{0:T(512)S(1)}, u32[]{:S(2)}, u32[]{:S(2)}) collective-permute-start(f32[384]{0:T(512)S(1)} %reshape.964), channel_id=1, source_target_pairs={{0,16},{1,17},{2,18},{3,19},{4,20},{5,21},{6,22},{7,23},{8,24},{9,... | collective-permute-start | bytes 4616 | tf_op jit(solution)/shard_map/ppermute | solution.py:32
  105.5 20.5 %collective-permute-start.23 = (bf16[96,4608]{1,0:T(8,128)(2,1)}, bf16[96,4608]{1,0:T(8,128)(2,1)}, u32[]{:S(2)}, u32[]{:S(2)}) collective-permute-start(bf16[96,4608]{1,0:T(8,128)(2,1)} %collective-permute-done.22.refs_3_), channel_id=1, source_target_pairs={{0,4},{4,8},{8,12},{12,14},{14,10},{10,6},{6,2},{2,0},{1,5},{5,9},... | collective-permute-start | bytes 2654216 | tf_op jit(solution)/shard_map/ppermute | solution.py:39
  106.4 20.2 %collective-permute-start.19 = (bf16[96,4608]{1,0:T(8,128)(2,1)}, bf16[96,4608]{1,0:T(8,128)(2,1)}, u32[]{:S(2)}, u32[]{:S(2)}) collective-permute-start(bf16[96,4608]{1,0:T(8,128)(2,1)} %collective-permute-done.18.refs_4_), channel_id=1, source_target_pairs={{0,2},{4,0},{8,4},{12,8},{14,12},{10,14},{6,10},{2,6},{1,3},{5,1},... | collective-permute-start | bytes 2654216 | tf_op jit(solution)/shard_map/ppermute | solution.py:39
  134.2 49.6 %collective-permute-start.26 = (bf16[1,8,96,2048]{3,2,1,0:T(8,128)(2,1)}, bf16[1,8,96,2048]{3,2,1,0:T(8,128)(2,1)}, u32[]{:S(2)}, u32[]{:S(2)}) collective-permute-start(bf16[1,8,96,2048]{3,2,1,0:T(8,128)(2,1)} %get-tuple-element.125.refs_0_), channel_id=1, source_target_pairs={{0,1},{1,0},{2,3},{3,2},{4,5},{5,4},{6,7},{7,6},{8,9},{9,8},{10,11... | collective-permute-start | bytes 9437192 | tf_op jit(solution)/shard_map/ppermute | solution.py:20
  140.1 27.2 %collective-permute-start.24 = (bf16[48,4608]{1,0:T(8,128)(2,1)S(1)}, bf16[48,4608]{1,0:T(8,128)(2,1)S(1)}, u32[]{:S(2)}, u32[]{:S(2)}) collective-permute-start(bf16[48,4608]{1,0:T(8,128)(2,1)S(1)} %slice.394), channel_id=1, source_target_pairs={{0,4},{4,8},{8,12},{12,14},{14,10},{10,6},{6,2},{2,0},{1,5},{5,9},... | collective-permute-start | bytes 1327112 | tf_op jit(solution)/shard_map/ppermute | solution.py:39
  166.4 12.3 %collective-permute-start.25 = (bf16[48,4608]{1,0:T(8,128)(2,1)S(1)}, bf16[48,4608]{1,0:T(8,128)(2,1)S(1)}, u32[]{:S(2)}, u32[]{:S(2)}) collective-permute-start(bf16[48,4608]{1,0:T(8,128)(2,1)S(1)} %slice.395), channel_id=1, source_target_pairs={{0,2},{4,0},{8,4},{12,8},{14,12},{10,14},{6,10},{2,6},{1,3},{5,1},... | collective-permute-start | bytes 1327112 | tf_op jit(solution)/shard_map/ppermute | solution.py:39
  166.7 14.5 %collective-permute-start.28 = (bf16[2,8,48,384]{3,2,1,0:T(8,128)(2,1)S(1)}, bf16[2,8,48,384]{3,2,1,0:T(8,128)(2,1)S(1)}, u32[]{:S(2)}, u32[]{:S(2)}) collective-permute-start(bf16[2,8,48,384]{3,2,1,0:T(8,128)(2,1)S(1)} %copy-done.46), channel_id=1, source_target_pairs={{0,1},{1,0},{2,3},{3,2},{4,5},{5,4},{6,7},{7,6},{8,9},{9,8},{10,11... | collective-permute-start | bytes 1769480 | tf_op jit(solution)/shard_map/ppermute | solution.py:20
  166.8 17.0 %collective-permute-start.29 = (bf16[2,8,48,768]{3,2,1,0:T(8,128)(2,1)}, bf16[2,8,48,768]{3,2,1,0:T(8,128)(2,1)}, u32[]{:S(2)}, u32[]{:S(2)}) collective-permute-start(bf16[2,8,48,768]{3,2,1,0:T(8,128)(2,1)} %get-tuple-element.128.refs_3_), channel_id=1, source_target_pairs={{0,1},{1,0},{2,3},{3,2},{4,5},{5,4},{6,7},{7,6},{8,9},{9,8},{10,11... | collective-permute-start | bytes 3538952 | tf_op jit(solution)/shard_map/ppermute | solution.py:20
  167.2 16.6 %collective-permute-start.27 = (bf16[1,8,96,1024]{3,2,1,0:T(8,128)(2,1)}, bf16[1,8,96,1024]{3,2,1,0:T(8,128)(2,1)}, u32[]{:S(2)}, u32[]{:S(2)}) collective-permute-start(bf16[1,8,96,1024]{3,2,1,0:T(8,128)(2,1)} %get-tuple-element.126.refs_1_), channel_id=1, source_target_pairs={{0,1},{1,0},{2,3},{3,2},{4,5},{5,4},{6,7},{7,6},{8,9},{9,8},{10,11... | collective-permute-start | bytes 4718600 | tf_op jit(solution)/shard_map/ppermute | solution.py:20
  179.5 7.1 collective-permute-start.31
  181.2 2.5 collective-permute-start.30
  183.5 545.8 %reduce-scatter.5.cloned.1.call-start = ((), (), s32[]{:S(2)}) async-start(), calls=%async_computation.8 | async-start | bytes 7077888 | tf_op jit(solution)/shard_map/reduce_scatter | solution.py:669
  206.6 21.7 %collective-permute-start.32 = (bf16[512,768]{1,0:T(8,128)(2,1)S(1)}, bf16[512,768]{1,0:T(8,128)(2,1)}, u32[]{:S(2)}, u32[]{:S(2)}) collective-permute-start(bf16[512,768]{1,0:T(8,128)(2,1)S(1)} %multiply_convert_fusion.11), channel_id=1, source_target_pairs={{0,16},{1,17},{2,18},{3,19},{4,20},{5,21},{6,22},{7,23},{8,24},{9,... | collective-permute-start | bytes 2359304 | tf_op jit(solution)/shard_map/ppermute | solution.py:32
  228.4 7.0 collective-permute-start.33
  285.4 22.1 %collective-permute-start.34 = (bf16[512,768]{1,0:T(8,128)(2,1)S(1)}, bf16[512,768]{1,0:T(8,128)(2,1)S(1)}, u32[]{:S(2)}, u32[]{:S(2)}) collective-permute-start(bf16[512,768]{1,0:T(8,128)(2,1)S(1)} %multiply_convert_fusion.9), channel_id=1, source_target_pairs={{16,0},{17,1},{18,2},{19,3},{20,4},{21,5},{22,6},{23,7},{24,8},{25... | collective-permute-start | bytes 2359304 | tf_op jit(solution)/shard_map/ppermute | solution.py:28
  308.7 2.4 collective-permute-start.35
  331.0 4.1 collective-permute-start.37
  358.7 19.6 %collective-permute-start.39 = (bf16[512,768]{1,0:T(8,128)(2,1)}, bf16[512,768]{1,0:T(8,128)(2,1)}, u32[]{:S(2)}, u32[]{:S(2)}) collective-permute-start(bf16[512,768]{1,0:T(8,128)(2,1)} %get-tuple-element.187), channel_id=1, source_target_pairs={{0,16},{1,17},{2,18},{3,19},{4,20},{5,21},{6,22},{7,23},{8,24},{9,... | collective-permute-start | bytes 2359304 | tf_op jit(solution)/shard_map/ppermute | solution.py:32
  371.7 360.0 %reduce-scatter.3.cloned.1.call-start = ((), (), s32[]{:S(2)}) async-start(), calls=%async_computation.7 | async-start | bytes 6635520 | tf_op jit(solution)/shard_map/reduce_scatter | solution.py:719
  445.5 4.7 collective-permute-start.40
  451.6 30.0 %collective-permute-start.42 = (bf16[768,1536]{0,1:T(8,128)(2,1)S(1)}, bf16[768,1536]{0,1:T(8,128)(2,1)S(1)}, u32[]{:S(2)}, u32[]{:S(2)}) collective-permute-start(bf16[768,1536]{0,1:T(8,128)(2,1)S(1)} %pad_maximum_fusion.4), channel_id=1, source_target_pairs={{0,1},{1,0},{2,3},{3,2},{4,5},{5,4},{6,7},{7,6},{8,9},{9,8},{10,11... | collective-permute-start | bytes 7077896 | tf_op jit(solution)/shard_map/ppermute | solution.py:20
  454.4 21.1 %collective-permute-start.41 = (bf16[512,768]{1,0:T(8,128)(2,1)S(1)}, bf16[512,768]{1,0:T(8,128)(2,1)S(1)}, u32[]{:S(2)}, u32[]{:S(2)}) collective-permute-start(bf16[512,768]{1,0:T(8,128)(2,1)S(1)} %slice_add_fusion.1), channel_id=1, source_target_pairs={{16,0},{17,1},{18,2},{19,3},{20,4},{21,5},{22,6},{23,7},{24,8},{25... | collective-permute-start | bytes 2359304 | tf_op jit(solution)/shard_map/ppermute | solution.py:28
  482.4 28.8 %collective-permute-start.43 = (bf16[384,1536]{0,1:T(8,128)(2,1)S(1)}, bf16[384,1536]{0,1:T(8,128)(2,1)S(1)}, u32[]{:S(2)}, u32[]{:S(2)}) collective-permute-start(bf16[384,1536]{0,1:T(8,128)(2,1)S(1)} %slice.420), channel_id=1, source_target_pairs={{16,0},{17,1},{18,2},{19,3},{20,4},{21,5},{22,6},{23,7},{24,8},{25... | collective-permute-start | bytes 3538952 | tf_op jit(solution)/shard_map/ppermute | solution.py:28
  522.5 54.4 %collective-permute-start.58 = (bf16[768,3072]{1,0:T(8,128)(2,1)}, bf16[768,3072]{1,0:T(8,128)(2,1)}, u32[]{:S(2)}, u32[]{:S(2)}) collective-permute-start(bf16[768,3072]{1,0:T(8,128)(2,1)} %get-tuple-element.159), channel_id=1, source_target_pairs={{0,1},{1,0},{2,3},{3,2},{4,5},{5,4},{6,7},{7,6},{8,9},{9,8},{10,11... | collective-permute-start | bytes 14155784 | tf_op jit(solution)/shard_map/ppermute | solution.py:20
  531.6 5.5 collective-permute-start.47
  589.7 8.2 %collective-permute-start.44 = (bf16[512,768]{1,0:T(8,128)(2,1)S(1)}, bf16[512,768]{1,0:T(8,128)(2,1)S(1)}, u32[]{:S(2)}, u32[]{:S(2)}) collective-permute-start(bf16[512,768]{1,0:T(8,128)(2,1)S(1)} %slice.560), channel_id=1, source_target_pairs={{0,1},{1,0},{2,3},{3,2},{4,5},{5,4},{6,7},{7,6},{8,9},{9,8},{10,11... | collective-permute-start | bytes 2359304 | tf_op jit(solution)/shard_map/ppermute | solution.py:20
  594.3 60.2 %collective-permute-start.48 = (bf16[768,1536]{0,1:T(8,128)(2,1)}, bf16[768,1536]{0,1:T(8,128)(2,1)}, u32[]{:S(2)}, u32[]{:S(2)}) collective-permute-start(bf16[768,1536]{0,1:T(8,128)(2,1)} %pad_maximum_fusion.6), channel_id=1, source_target_pairs={{0,1},{1,0},{2,3},{3,2},{4,5},{5,4},{6,7},{7,6},{8,9},{9,8},{10,11... | collective-permute-start | bytes 7077896 | tf_op jit(solution)/shard_map/ppermute | solution.py:20
  600.9 13.9 %collective-permute-start.45 = (bf16[256,768]{1,0:T(8,128)(2,1)}, bf16[256,768]{1,0:T(8,128)(2,1)}, u32[]{:S(2)}, u32[]{:S(2)}) collective-permute-start(bf16[256,768]{1,0:T(8,128)(2,1)} %slice.424), channel_id=1, source_target_pairs={{16,0},{17,1},{18,2},{19,3},{20,4},{21,5},{22,6},{23,7},{24,8},{25... | collective-permute-start | bytes 1179656 | tf_op jit(solution)/shard_map/ppermute | solution.py:28
  609.8 21.3 %collective-permute-start.49 = (bf16[8,16,1536]{2,0,1:T(8,128)(2,1)S(1)}, bf16[8,16,1536]{2,0,1:T(8,128)(2,1)}, u32[]{:S(2)}, u32[]{:S(2)}) collective-permute-start(bf16[8,16,1536]{2,0,1:T(8,128)(2,1)S(1)} %fusion.61), channel_id=1, source_target_pairs={{0,1},{1,0},{2,3},{3,2},{4,5},{5,4},{6,7},{7,6},{8,9},{9,8},{10,11... | collective-permute-start | bytes 1179656 | tf_op jit(solution)/shard_map/ppermute | solution.py:20
  617.4 32.1 %all-to-all-start.2 = ((bf16[8,33,768]{2,1,0:T(8,128)(2,1)}), bf16[8,33,768]{2,1,0:T(8,128)(2,1)S(1)}, u32[]{:S(2)}, u32[]{:S(2)}) async-start(bf16[8,33,768]{2,1,0:T(8,128)(2,1)} %pad_maximum_fusion.15), calls=%async_computation.2 | async-start | bytes 983040 | tf_op jit(solution)/shard_map/all_to_all | solution.py:232
  651.1 23.5 %all-to-all-start.3 = ((bf16[8,33,768]{2,1,0:T(8,128)(2,1)}), bf16[8,33,768]{2,1,0:T(8,128)(2,1)S(1)}, u32[]{:S(2)}, u32[]{:S(2)}) async-start(bf16[8,33,768]{2,1,0:T(8,128)(2,1)} %gather_fusion.1), calls=%async_computation.3 | async-start | bytes 983040 | tf_op jit(solution)/shard_map/all_to_all | solution.py:233
  661.8 9.1 %collective-permute-start.50 = (bf16[56,1536]{1,0:T(8,128)(2,1)S(1)}, bf16[56,1536]{1,0:T(8,128)(2,1)S(1)}, u32[]{:S(2)}, u32[]{:S(2)}) collective-permute-start(bf16[56,1536]{1,0:T(8,128)(2,1)S(1)} %get-tuple-element.261), channel_id=1, source_target_pairs={{0,4},{4,8},{8,12},{12,14},{14,10},{10,6},{6,2},{2,0},{1,5},{5,9},... | collective-permute-start | bytes 516104 | tf_op jit(solution)/shard_map/ppermute | solution.py:39
  663.8 7.9 %collective-permute-start.54 = (bf16[56,1536]{1,0:T(8,128)(2,1)S(1)}, bf16[56,1536]{1,0:T(8,128)(2,1)S(1)}, u32[]{:S(2)}, u32[]{:S(2)}) collective-permute-start(bf16[56,1536]{1,0:T(8,128)(2,1)S(1)} %get-tuple-element.262), channel_id=1, source_target_pairs={{0,2},{4,0},{8,4},{12,8},{14,12},{10,14},{6,10},{2,6},{1,3},{5,1},... | collective-permute-start | bytes 516104 | tf_op jit(solution)/shard_map/ppermute | solution.py:39
  671.7 14.7 %collective-permute-start.51 = (bf16[112,1536]{1,0:T(8,128)(2,1)}, bf16[112,1536]{1,0:T(8,128)(2,1)}, u32[]{:S(2)}, u32[]{:S(2)}) collective-permute-start(bf16[112,1536]{1,0:T(8,128)(2,1)} %pad_maximum_fusion.16), channel_id=1, source_target_pairs={{0,4},{4,8},{8,12},{12,14},{14,10},{10,6},{6,2},{2,0},{1,5},{5,9},... | collective-permute-start | bytes 1032200 | tf_op jit(solution)/shard_map/ppermute | solution.py:39
  672.5 15.3 %collective-permute-start.55 = (bf16[112,1536]{1,0:T(8,128)(2,1)}, bf16[112,1536]{1,0:T(8,128)(2,1)}, u32[]{:S(2)}, u32[]{:S(2)}) collective-permute-start(bf16[112,1536]{1,0:T(8,128)(2,1)} %pad_maximum_fusion.17), channel_id=1, source_target_pairs={{0,2},{4,0},{8,4},{12,8},{14,12},{10,14},{6,10},{2,6},{1,3},{5,1},... | collective-permute-start | bytes 1032200 | tf_op jit(solution)/shard_map/ppermute | solution.py:39
  674.7 27.0 %collective-permute-start.46 = (bf16[256,768]{1,0:T(8,128)(2,1)S(1)}, bf16[256,768]{1,0:T(8,128)(2,1)}, u32[]{:S(2)}, u32[]{:S(2)}) collective-permute-start(bf16[256,768]{1,0:T(8,128)(2,1)S(1)} %bitcast.410), channel_id=1, source_target_pairs={{0,16},{1,17},{2,18},{3,19},{4,20},{5,21},{6,22},{7,23},{8,24},{9,... | collective-permute-start | bytes 1179656 | tf_op jit(solution)/shard_map/ppermute | solution.py:32
  687.8 9.1 %collective-permute-start.52 = (bf16[112,1536]{1,0:T(8,128)(2,1)S(1)}, bf16[112,1536]{1,0:T(8,128)(2,1)S(1)}, u32[]{:S(2)}, u32[]{:S(2)}) collective-permute-start(bf16[112,1536]{1,0:T(8,128)(2,1)S(1)} %add_convert_fusion.5), channel_id=1, source_target_pairs={{0,4},{4,8},{8,12},{12,14},{14,10},{10,6},{6,2},{2,0},{1,5},{5,9},... | collective-permute-start | bytes 1032200 | tf_op jit(solution)/shard_map/ppermute | solution.py:39
  689.3 9.6 %collective-permute-start.56 = (bf16[112,1536]{1,0:T(8,128)(2,1)S(1)}, bf16[112,1536]{1,0:T(8,128)(2,1)S(1)}, u32[]{:S(2)}, u32[]{:S(2)}) collective-permute-start(bf16[112,1536]{1,0:T(8,128)(2,1)S(1)} %add_convert_fusion.3), channel_id=1, source_target_pairs={{0,2},{4,0},{8,4},{12,8},{14,12},{10,14},{6,10},{2,6},{1,3},{5,1},... | collective-permute-start | bytes 1032200 | tf_op jit(solution)/shard_map/ppermute | solution.py:39
  697.9 16.1 %collective-permute-start.53 = (bf16[112,1536]{1,0:T(8,128)(2,1)S(1)}, bf16[112,1536]{1,0:T(8,128)(2,1)S(1)}, u32[]{:S(2)}, u32[]{:S(2)}) collective-permute-start(bf16[112,1536]{1,0:T(8,128)(2,1)S(1)} %add_convert_fusion.4), channel_id=1, source_target_pairs={{0,4},{4,8},{8,12},{12,14},{14,10},{10,6},{6,2},{2,0},{1,5},{5,9},... | collective-permute-start | bytes 1032200 | tf_op jit(solution)/shard_map/ppermute | solution.py:39
  699.1 25.6 %collective-permute-start.57 = (bf16[112,1536]{1,0:T(8,128)(2,1)S(1)}, bf16[112,1536]{1,0:T(8,128)(2,1)S(1)}, u32[]{:S(2)}, u32[]{:S(2)}) collective-permute-start(bf16[112,1536]{1,0:T(8,128)(2,1)S(1)} %add_convert_fusion.2), channel_id=1, source_target_pairs={{0,2},{4,0},{8,4},{12,8},{14,12},{10,14},{6,10},{2,6},{1,3},{5,1},... | collective-permute-start | bytes 1032200 | tf_op jit(solution)/shard_map/ppermute | solution.py:39
  (183 other events, 1710.4 us)
Sparse Core Ops, SparseCore 0:
  183.6 100.3 all-gather.1
  371.8 117.1 reduce-scatter.4
  587.0 144.2 reduce-scatter.2

commit v3 on v2

--- a/solution.py
+++ b/solution.py
@@ -285,64 +285,60 @@
     return lax.dot_general(a, b, (((0,), (0,)), ((), ())), preferred_element_type=f32)
 
 
-def masked_scores(keys, queries, reach):
-    scores = dot_last(keys, queries)
-    row = lax.broadcasted_iota(jnp.int32, scores.shape, 0)
-    return jnp.where(row <= reach, scores, masked_out)
-
-
-def attend_body(start_ref, query_ref, pair_ref, limit_ref, context_ref, log_ref):
-    half = pair_ref.shape[0] // 2
+def mask_keys(mask_ref, start_ref, limit_ref):
+    half = mask_ref.shape[0] // 2
+
+    @pl.when(pl.program_id(0) == 0)
+    def _():
+        for part in range(2):
+            row = lax.broadcasted_iota(jnp.int32, (half, mask_ref.shape[1]), 0)
+            reach = limit_ref[...] - start_ref[part]
+            mask_ref[part * half : (part + 1) * half] = jnp.where(row <= reach, 0.0, masked_out)
+
+
+def attend_body(start_ref, query_ref, pair_ref, limit_ref, context_ref, log_ref, mask_ref):
+    mask_keys(mask_ref, start_ref, limit_ref)
     scaled = query_ref[...] * jnp.asarray(DK ** (-0.5), bf16)
-    reach = [limit_ref[...] - start_ref[part] for part in range(2)]
-    rows = [pl.ds(part * half, half) for part in range(2)]
     turned = []
     for head in range(2):
-        queries = lanes_of(head, scaled)
-        scores = [masked_scores(pair_ref[rows[i], :PAIR], queries, reach[i]) for i in range(2)]
-        highest = jnp.max(jnp.maximum(scores[0], scores[1]), axis=0, keepdims=True)
-        shifted = [jnp.exp(part - highest) for part in scores]
-        totals = jnp.sum(shifted[0] + shifted[1], axis=0, keepdims=True)
-        context = sum(
-            dot_first(pair_ref[rows[i], PAIR:], shifted[i].astype(bf16)) for i in range(2)
-        )
+        scores = dot_last(pair_ref[:, :PAIR], lanes_of(head, scaled)) + mask_ref[...]
+        highest = jnp.max(scores, axis=0, keepdims=True)
+        shifted = jnp.exp(scores - highest)
+        totals = jnp.sum(shifted, axis=0, keepdims=True)
+        context = dot_first(pair_ref[:, PAIR:], shifted.astype(bf16))
         turned.append(context[head * DK : (head + 1) * DK] / totals)
         log_ref[0, head : head + 1] = highest + jnp.log(totals)
     context_ref[...] = jnp.concatenate(turned, 0).T.astype(bf16)
 
 
 def attend_back_body(
-    start_ref, query_ref, pair_ref, limit_ref, log_ref, grad_ref, grad_query_ref, grad_pair_ref
+    start_ref,
+    query_ref,
+    pair_ref,
+    limit_ref,
+    log_ref,
+    grad_ref,
+    grad_query_ref,
+    grad_pair_ref,
+    mask_ref,
 ):
-    half = pair_ref.shape[0] // 2
+    mask_keys(mask_ref, start_ref, limit_ref)
     scale = DK ** (-0.5)
     scaled = query_ref[...] * jnp.asarray(scale, bf16)
-    reach = [limit_ref[...] - start_ref[part] for part in range(2)]
-    rows = [pl.ds(part * half, half) for part in range(2)]
-    grad_query = 0.0
-    grad_key, grad_value = [0.0, 0.0], [0.0, 0.0]
+    grad_query, grad_key, grad_value = 0.0, 0.0, 0.0
     for head in range(2):
         queries = lanes_of(head, scaled)
         grad_context = lanes_of(head, grad_ref[...])
-        log_total = log_ref[0, head : head + 1]
-        weights, grad_weights = [], []
-        for i in range(2):
-            scores = masked_scores(pair_ref[rows[i], :PAIR], queries, reach[i])
-            weights.append(jnp.exp(scores - log_total))
-            grad_weights.append(dot_last(pair_ref[rows[i], PAIR:], grad_context))
-        inner = jnp.sum(
-            weights[0] * grad_weights[0] + weights[1] * grad_weights[1], axis=0, keepdims=True
-        )
-        for i in range(2):
-            grad_scores = (weights[i] * (grad_weights[i] - inner)).astype(bf16)
-            grad_value[i] += jnp.dot(
-                weights[i].astype(bf16), grad_context, preferred_element_type=f32
-            )
-            grad_key[i] += jnp.dot(grad_scores, queries, preferred_element_type=f32)
-            grad_query += dot_first(lanes_of(head, pair_ref[rows[i], :PAIR]), grad_scores)
-    for i in range(2):
-        grad_pair_ref[rows[i], :PAIR] = grad_key[i].astype(bf16)
-        grad_pair_ref[rows[i], PAIR:] = grad_value[i].astype(bf16)
+        scores = dot_last(pair_ref[:, :PAIR], queries) + mask_ref[...]
+        weights = jnp.exp(scores - log_ref[0, head : head + 1])
+        grad_weights = dot_last(pair_ref[:, PAIR:], grad_context)
+        inner = jnp.sum(weights * grad_weights, axis=0, keepdims=True)
+        grad_scores = (weights * (grad_weights - inner)).astype(bf16)
+        grad_value += jnp.dot(weights.astype(bf16), grad_context, preferred_element_type=f32)
+        grad_key += jnp.dot(grad_scores, queries, preferred_element_type=f32)
+        grad_query += dot_first(lanes_of(head, pair_ref[:, :PAIR]), grad_scores)
+    grad_pair_ref[:, :PAIR] = grad_key.astype(bf16)
+    grad_pair_ref[:, PAIR:] = grad_value.astype(bf16)
     grad_query_ref[...] = (grad_query * scale).T.astype(bf16)
 
 
@@ -369,6 +365,7 @@
             grid=(width // PAIR,),
             in_specs=[query_spec, pair_spec, limit_spec],
             out_specs=[query_spec, log_spec],
+            scratch_shapes=[pltpu.VMEM((pairs.shape[0], rows), f32)],
         ),
         cost_estimate=pl.CostEstimate(
             flops=area // 64, bytes_accessed=pairs.size // 64, transcendentals=0
@@ -392,6 +389,7 @@
             grid=(width // PAIR,),
             in_specs=[query_spec, pair_spec, limit_spec, log_spec, query_spec],
             out_specs=[query_spec, pair_spec],
+            scratch_shapes=[pltpu.VMEM((pairs.shape[0], rows), f32)],
         ),
         cost_estimate=pl.CostEstimate(
             flops=area // 64, bytes_accessed=pairs.size // 64, transcendentals=0
@@ -428,18 +426,43 @@
     return grads, grad_query_in, grad_memory
 
 
+def row_products(lefts, rights):
+    tile = 256
+    flat = [right for group in rights for _, right in group]
+    widths = [sum(right.shape[1] for _, right in group) for group in rights]
+    height = lefts[0].shape[1]
+
+    def body(*refs):
+        turned = [ref[...].T for ref in refs[: len(lefts)]]
+        sources = iter(refs[len(lefts) : len(lefts) + len(flat)])
+        for target, group in zip(refs[len(lefts) + len(flat) :], rights):
+            first = 0
+            for left, right in group:
+                product = jnp.dot(turned[left], next(sources)[...], preferred_element_type=f32)
+                target[:, first : first + right.shape[1]] = product.astype(bf16)
+                first += right.shape[1]
+
+    return pl.pallas_call(
+        body,
+        out_shape=[jax.ShapeDtypeStruct((height, width), bf16) for width in widths],
+        grid=(height // tile,),
+        in_specs=[pl.BlockSpec((left.shape[0], tile), lambda i: (0, i)) for left in lefts]
+        + [pl.BlockSpec(right.shape, lambda i: (0, 0)) for right in flat],
+        out_specs=[pl.BlockSpec((tile, width), lambda i: (i, 0)) for width in widths],
+        cost_estimate=pl.CostEstimate(
+            flops=sum(2 * height * right.size for right in flat),
+            bytes_accessed=2 * height * sum(widths),
+            transcendentals=0,
+        ),
+        name="row_products",
+    )(*lefts, *flat)
+
+
 def attention_weight_grads(query_in, memory_in, kept, grads, grad_rows):
-    return [
-        jnp.concatenate(
-            [
-                contract_first(query_in, grads[i][0]).astype(bf16),
-                contract_first(memory_in, grads[i][1]).astype(bf16),
-                contract_first(grad_rows, kept[i][2]).astype(bf16),
-            ],
-            1,
-        )
-        for i in range(2)
-    ]
+    return row_products(
+        [query_in, memory_in, grad_rows],
+        [[(0, grads[i][0]), (1, grads[i][1]), (2, kept[i][2])] for i in range(2)],
+    )
 
 
 def mlp_forward(normed, gate_up, down):
@@ -472,16 +495,9 @@
 
 
 def mlp_weight_grads(normed, inner, grads, grad_rows):
-    return [
-        jnp.concatenate(
-            [
-                contract_first(normed, grads[i]).astype(bf16),
-                contract_first(grad_rows, inner[i]).astype(bf16),
-            ],
-            1,
-        )
-        for i in range(2)
-    ]
+    return row_products(
+        [normed, grad_rows], [[(0, grads[i]), (1, inner[i])] for i in range(2)]
+    )
 
 
 def merge_stats(first, second):
@@ -669,7 +685,7 @@
     g_embedding = lax.psum_scatter(grad_table, "dp", scatter_dimension=0, tiled=True)
 
     stream, grad_gain_final = norm_back(after_mlp, gain_final, grad_final)
-    dec_rows = stream.astype(bf16)
+    dec_rows = held_after(stream.astype(bf16), grad_table)
     dec_grads, grad_normed = mlp_back(dec_kept, gate_up, down, dec_rows)
     part, grad_gain_mlp = norm_back(after_cross, gain_mlp, grad_normed)
     stream = stream + part
@@ -692,8 +708,6 @@
         return part.reshape(count, -1, part.shape[1])
 
     cross_sum = (cross_sums[0].astype(f32) + swap_core(cross_sums[1]).astype(f32)).astype(bf16)
-    cut = cross_sum.shape[0] // 2
-    cross_sum = jnp.where(decoding, cross_sum[cut:], to_encoder(cross_sum[:cut]))
 
     enc_stream, gain_part = norm_back(after_enc, gain_final, grad_memory)
     grad_gain_final = grad_gain_final + gain_part
@@ -707,20 +721,20 @@
         lambda dec, enc: mlp_weight_grads(*dec),
         lambda dec, enc: mlp_weight_grads(*enc),
         (normed_dec, dec_kept[1], dec_grads, dec_rows),
-        (normed_enc, enc_kept[1], enc_grads, held_after(enc_rows, cross_sum)),
+        (normed_enc, enc_kept[1], enc_grads, enc_rows),
     )
 
     mlp_sum = stacked(mlp_sums[0]).astype(f32) + stacked(swap_core(mlp_sums[1])).astype(f32)
-    cross_sum = stacked(cross_sum)
-    fold = mlp_sum.shape[1] // cross_sum.shape[1]
-    size = cross_sum.shape[2] // fold
-    cross_sum = [cross_sum[:, :, i * size : (i + 1) * size] for i in range(fold)]
-    packed = jnp.concatenate([mlp_sum.astype(bf16), jnp.concatenate(cross_sum, 1)], 2)
-    g_mlp = lax.psum_scatter(packed, "dp", scatter_dimension=0).astype(f32)
-    g_cross = jnp.concatenate(jnp.split(g_mlp[:, 3 * hidden :], fold, 0), 1)
-    g_mlp = g_mlp[:, : 3 * hidden]
-
-    self_in = held_after(stream.astype(bf16), mlp_sums[0])
+    cut = cross_sum.shape[0] // 2
+    halves = jnp.concatenate([stacked(cross_sum[:cut]), stacked(cross_sum[cut:])], 1)
+    packed = jnp.concatenate([mlp_sum.astype(bf16), halves], 2)
+    summed = lax.psum_scatter(packed, "dp", scatter_dimension=0)
+    g_mlp = summed[:, : 3 * hidden].astype(f32)
+    g_cross = summed[:, 3 * hidden :]
+    g_cross = jnp.where(decoding, g_cross[cross_rows:], to_encoder(g_cross[:cross_rows]))
+    g_cross = g_cross.astype(f32)
+
+    self_in = held_after(stream.astype(bf16), packed)
     self_grads, grad_normed, grad_keyside = attention_back(
         self_kept,
         self_weights,
@@ -753,10 +767,10 @@
     lent_gains = to_encoder(grad_gain_cross[:cut])
     gain_grads = [grad_gain_attn, grad_gain_mlp, grad_gain_final]
     gain_grads.append(jnp.where(decoding, grad_gain_cross[cut:], lent_gains))
-    packed = jnp.concatenate([grad.reshape(count, 1, -1) for grad in gain_grads], 2).astype(bf16)
-    packed = jnp.pad(packed, ((0, 0), (0, 15), (0, 4 * width - packed.shape[2])))
+    lines = jnp.concatenate([grad.reshape(count, 1, -1) for grad in gain_grads], 2).astype(bf16)
+    lines = jnp.pad(lines, ((0, 0), (0, 15), (0, 4 * width - lines.shape[2])))
     self_scattering = scatter_stacks(
-        [[stacked(self_sums[0]), packed], [stacked(swap_core(self_sums[1])), swap_core(packed)]],
+        [[stacked(self_sums[0]), lines], [stacked(swap_core(self_sums[1])), swap_core(lines)]],
     )
     for _ in range(3):
         self_scattering.step()

time: 755 us -> 729 us (0.966)
  waiting for transfers between devices: 184 us -> 162 us
  matrix products: 158 us -> 141 us
  Pallas kernels: 121 us -> 137 us
  local copies, waits for them, and re-layouts: 82.9 us -> 69.2 us
  starting transfers between devices: 82.7 us -> 90.9 us
    pallas_call x0 -> x3, Pallas kernels: none -> 26.9 us  [row_products(): pl.pallas_call(body, out_shape=[jax.ShapeDtypeStruct((height, width), bf1...]
    dot_general x17 -> x1, matrix products: 27.1 us -> 11.1 us  [contract_first(): lax.dot_general(a, b, (((0,), (0,)), ((), ())), preferred_element_type=f32)]
    ppermute x24, waiting for transfers between devices: 82.7 us -> 69.6 us  [loop_step(): return lax.ppermute(value, 'dp', pairs)]
    convert_element_type x4 -> x6, other arithmetic: 10.4 us -> 21.9 us  [the longest x1 7.25 us: on_device(): stacked(mlp_sums[0]).astype(f32)]
    ppermute x6, waiting for transfers between devices: 61 us -> 50.4 us  [to_encoder(): return lax.ppermute(value, 'slab', [(1, 0)])]
    ppermute x24, starting transfers between devices: 27.6 us -> 35.7 us  [loop_step(): return lax.ppermute(value, 'dp', pairs)]
    unnamed x385 -> x317, local copies, waits for them, and re-layouts: 33.9 us -> 28.5 us
  transfers between devices with their start and end apart: 66 -> 66, of which waited for: 25 -> 24; matrix products, arithmetic and copies ran while one was open for 36% -> 34% of each run, Pallas kernels for 15% -> 18%
where the time goes in v3:
time: 729 us; the launch traced here: 719 us
  waiting for transfers between devices  162 us (22%)
  matrix products  141 us (19%)
  Pallas kernels  137 us (19%)
  other arithmetic  95.9 us (13%)
  starting transfers between devices  90.9 us (12%)
  local copies, waits for them, and re-layouts  69.2 us (9%)
  between operations  22.3 us (3%)
    ppermute x24, waiting for transfers between devices, loop_step(): return lax.ppermute(value, 'dp', pairs)  69.6 us
    dot_general x21, matrix products, matmul(): return jnp.dot(a, b, preferred_element_type=f32)  69.5 us
    dot_general x21, matrix products, contract_last(): lax.dot_general(a, b, (((1,), (1,)), ((), ())), preferred_element_type=f32)  60.4 us
    pallas_call x4, Pallas kernels, attend_back(): pl.pallas_call(attend_back_body, out_shape=[jax.ShapeDtypeStruct((rows, w...  52.3 us
    ppermute x6, waiting for transfers between devices, to_encoder(): return lax.ppermute(value, 'slab', [(1, 0)])  50.4 us
    ppermute x24, starting transfers between devices, loop_step(): return lax.ppermute(value, 'dp', pairs)  35.7 us
    pallas_call x4, Pallas kernels, attend(): pl.pallas_call(attend_body, out_shape=[jax.ShapeDtypeStruct((rows, width)...  34.4 us
    unnamed x317, local copies, waits for them, and re-layouts  28.5 us
  transfers between devices with their start and end apart: 66, of which 24 were waited for; matrix products, arithmetic and copies ran while one was open for 34% of the time, Pallas kernels for 18%

profile of v3, /device:TPU:0, one launch (start us, length us, event | category | flops | bytes accessed | tf_op | source)
XLA Modules:
  0.0 718.9 jit_solution(2182834244993956634)
XLA Ops:
  15.9 7.9 %collective-permute-done.3.refs_2_ = bf16[112,1536]{1,0:T(8,128)(2,1)S(1)} collective-permute-done((bf16[112,1536]{1,0:T(8,128)(2,1)S(1)}, bf16[112,1536]{1,0:T(8,128)(2,1)S(1)}, u32[]{:S(2)}, u32[]{:S(2)}) %collective-permute-start.3) | collective-permute-done | bytes 344096 | tf_op jit(solution)/shard_map/ppermute | solution.py:39
  26.6 6.1 all-to-all-start
  33.7 4.9 collective-permute-start.10
  45.4 4.0 all-to-all-start.1
  53.5 5.5 assemble.2
  63.9 3.5 collective-permute-done.8
  67.4 5.0 collective-permute-start.1
  91.9 4.4 collective-permute-start.20
  98.6 7.8 %collective-permute-done.18.refs_4_ = bf16[96,4608]{1,0:T(8,128)(2,1)} collective-permute-done((bf16[96,4608]{1,0:T(8,128)(2,1)}, bf16[96,4608]{1,0:T(8,128)(2,1)}, u32[]{:S(2)}, u32[]{:S(2)}) %collective-permute-start.18) | collective-permute-done | bytes 884768 | tf_op jit(solution)/shard_map/ppermute | solution.py:39
  114.1 13.5 %collective-permute-done.19.refs_6_ = bf16[96,4608]{1,0:T(8,128)(2,1)} collective-permute-done((bf16[96,4608]{1,0:T(8,128)(2,1)}, bf16[96,4608]{1,0:T(8,128)(2,1)}, u32[]{:S(2)}, u32[]{:S(2)}) %collective-permute-start.19) | collective-permute-done | bytes 884768 | tf_op jit(solution)/shard_map/ppermute | solution.py:39
  129.5 7.6 %assemble.3 = (bf16[1,8,96,2048]{3,2,1,0:T(8,128)(2,1)}, bf16[1,8,96,1024]{3,2,1,0:T(8,128)(2,1)}, bf16[2,8,48,384]{3,2,1,0:T(8,128)(2,1)}, bf16[2,8,48,768]{3,2,1,0:T(8,128)(2,1)}, bf16[2,8,48,384]{3,2,1,0:T(8,128)(2,1)}) custom-call(s32[7]{0:T(128)} %bitcast.436, bf16[96,4608]{1,0:T(8,128)(2,1)} %copy-done.26, ...), custom_call_target="tpu_custom_call" | custom-call | bytes 12386304 | tf_op jit(solution)/shard_map/assemble/pallas_call | solution.py:168
  137.6 4.4 convolution_convert_fusion.2.pair_ref
  146.1 8.7 %attend.4 = (bf16[512,384]{1,0:T(8,128)(2,1)}, f32[3,2,512]{2,1,0:T(2,128)}) custom-call(s32[2]{0:T(128)} %pad_add_fusion.start_ref, bf16[512,384]{1,0:T(8,128)(2,1)} %convolution_convert_fusion.11.query_ref, bf16[1024,768]{1,0:T(8,128)(2,1)} %convolution_convert_fusion.3.pair_ref, s32[1,512]{1,0:T(1,128)} %broadcast_select_fusion.2.limit_ref), custom_call_target="tpu_custom_call" | custom-call | flops 3145728 | bytes 12288 | tf_op jit(solution)/shard_map/attend/pallas_call | solution.py:357
  154.8 8.5 %attend.5 = (bf16[512,384]{1,0:T(8,128)(2,1)}, f32[3,2,512]{2,1,0:T(2,128)}) custom-call(s32[2]{0:T(128)} %pad_add_fusion.start_ref, bf16[512,384]{1,0:T(8,128)(2,1)} %convolution_convert_fusion.10.query_ref, bf16[1024,768]{1,0:T(8,128)(2,1)} %convolution_convert_fusion.2.pair_ref, s32[1,512]{1,0:T(1,128)} %broadcast_select_fusion.2.limit_ref), custom_call_target="tpu_custom_call" | custom-call | flops 3145728 | bytes 12288 | tf_op jit(solution)/shard_map/attend/pallas_call | solution.py:357
  169.3 9.2 %collective-permute-done.25 = bf16[48,4608]{1,0:T(8,128)(2,1)S(1)} collective-permute-done((bf16[48,4608]{1,0:T(8,128)(2,1)S(1)}, bf16[48,4608]{1,0:T(8,128)(2,1)S(1)}, u32[]{:S(2)}, u32[]{:S(2)}) %collective-permute-start.25) | collective-permute-done | bytes 442400 | tf_op jit(solution)/shard_map/ppermute | solution.py:39
  189.6 4.0 fusion.136
  197.6 3.2 fusion.137
  203.7 4.2 collective-permute-start.32
  207.9 16.8 %collective-permute-done.32 = bf16[512,768]{1,0:T(8,128)(2,1)S(1)} collective-permute-done((bf16[512,768]{1,0:T(8,128)(2,1)S(1)}, bf16[512,768]{1,0:T(8,128)(2,1)S(1)}, u32[]{:S(2)}, u32[]{:S(2)}) %collective-permute-start.32) | collective-permute-done | bytes 786464 | tf_op jit(solution)/shard_map/ppermute | solution.py:32
  227.5 4.4 convolution_convert_fusion.pair_ref
  232.5 8.5 %attend.7 = (bf16[512,384]{1,0:T(8,128)(2,1)}, f32[3,2,512]{2,1,0:T(2,128)}) custom-call(s32[2]{0:T(128)} %pad_add_fusion.start_ref, bf16[512,384]{1,0:T(8,128)(2,1)} %convolution_convert_fusion.8.query_ref, bf16[1024,768]{1,0:T(8,128)(2,1)} %convolution_convert_fusion.pair_ref, s32[1,512]{1,0:T(1,128)} %broadcast_in_dim.60.limit_ref), custom_call_target="tpu_custom_call" | custom-call | flops 3145728 | bytes 12288 | tf_op jit(solution)/shard_map/attend/pallas_call | solution.py:357
  241.0 4.3 convolution_convert_fusion.1.pair_ref
  245.3 8.7 %attend.6 = (bf16[512,384]{1,0:T(8,128)(2,1)}, f32[3,2,512]{2,1,0:T(2,128)}) custom-call(s32[2]{0:T(128)} %pad_add_fusion.start_ref, bf16[512,384]{1,0:T(8,128)(2,1)} %convolution_convert_fusion.9.query_ref, bf16[1024,768]{1,0:T(8,128)(2,1)} %convolution_convert_fusion.1.pair_ref, s32[1,512]{1,0:T(1,128)} %broadcast_in_dim.60.limit_ref), custom_call_target="tpu_custom_call" | custom-call | flops 3145728 | bytes 12288 | tf_op jit(solution)/shard_map/attend/pallas_call | solution.py:357
  257.9 4.3 fusion.140
  277.2 20.1 %collective-permute-done.34 = bf16[512,768]{1,0:T(8,128)(2,1)} collective-permute-done((bf16[512,768]{1,0:T(8,128)(2,1)}, bf16[512,768]{1,0:T(8,128)(2,1)}, u32[]{:S(2)}, u32[]{:S(2)}) %collective-permute-start.34) | collective-permute-done | bytes 786464 | tf_op jit(solution)/shard_map/ppermute | solution.py:28
  302.1 9.8 %multiply_reduce_fusion = (f32[1024]{0:T(1024)S(1)}, f32[1024,4096]{1,0:T(8,128)S(1)}) fusion(bf16[4096,768]{1,0:T(8,128)(2,1)} %all-gather.2.cloned.1.call-done, bf16[512,768]{1,0:T(8,128)(2,1)} %collective-permute-done.35, bf16[512,768]{1,0:T(8,128)(2,1)} %copy-done.89), kind=kOutput, calls=%fused_computation.9 | convolution fusion | flops 6453984256 | bytes 24645632 | tf_op jit(solution)/shard_map/dot_general | solution.py:241
  311.9 7.6 %exponential_reduce_fusion = (f32[1024]{0:T(1024)S(1)}, f32[1024]{0:T(1024)S(1)}) fusion(f32[1024,4096]{1,0:T(8,128)S(1)} %get-tuple-element.308, f32[1024]{0:T(1024)S(1)} %get-tuple-element.307, s32[1024]{0:T(1024)S(1)} %add_select_fusion.2, s32[4096]{0:T(1024)S(1)} %fusion.80), kind=kLoop, calls=%fused_computation.8 | loop fusion | flops 25163776 | bytes 16809984 | tf_op jit(solution)/shard_map/reduce_sum | solution.py:668
  324.7 6.3 fusion.3
  331.0 10.7 %convolution_multiply_fusion = f32[1024,768]{1,0:T(8,128)S(1)} fusion(bf16[1024,4096]{1,0:T(8,128)(2,1)S(1)} %fusion.3, bf16[4096,768]{1,0:T(8,128)(2,1)} %all-gather.2.cloned.1.call-done), kind=kOutput, calls=%fused_computation.77 | convolution fusion | flops 6443237376 | bytes 17825792 | tf_op jit(solution)/shard_map/dot_general | solution.py:237
  348.5 11.1 %multiply_convert_fusion = bf16[4096,768]{1,0:T(8,128)(2,1)} fusion(bf16[1024,4096]{1,0:T(8,128)(2,1)} %copy-done.10, bf16[512,768]{1,0:T(8,128)(2,1)} %collective-permute-done.35, bf16[512,768]{1,0:T(8,128)(2,1)S(1)} %copy-done.90), kind=kOutput, calls=%fused_computation.10 | convolution fusion | flops 6451888128 | bytes 16252928 | tf_op jit(solution)/shard_map/dot_general | solution.py:245
  359.9 5.1 collective-permute-done.39
  369.9 4.1 fusion.32
  374.0 4.5 fusion.25
  378.6 4.5 fusion.116
  389.7 13.2 %attend_back.5 = (bf16[512,384]{1,0:T(8,128)(2,1)}, bf16[1024,768]{1,0:T(8,128)(2,1)}) custom-call(s32[2]{0:T(128)} %pad_add_fusion.start_ref, bf16[512,384]{1,0:T(8,128)(2,1)} %convolution_convert_fusion.8.query_ref, bf16[1024,768]{1,0:T(8,128)(2,1)} %convolution_convert_fusion.pair_ref, s32[1,512]{1,0:T(1,128)} %broadcast_in_dim.60.limit_ref, ...), custom_call_target="tpu_custom_call" | custom-call | flops 3145728 | bytes 12288 | tf_op jit(solution)/shard_map/attend_back/pallas_call | solution.py:381
  405.3 13.1 %attend_back.4 = (bf16[512,384]{1,0:T(8,128)(2,1)}, bf16[1024,768]{1,0:T(8,128)(2,1)}) custom-call(s32[2]{0:T(128)} %pad_add_fusion.start_ref, bf16[512,384]{1,0:T(8,128)(2,1)} %convolution_convert_fusion.9.query_ref, bf16[1024,768]{1,0:T(8,128)(2,1)} %convolution_convert_fusion.1.pair_ref, s32[1,512]{1,0:T(1,128)} %broadcast_in_dim.60.limit_ref, ...), custom_call_target="tpu_custom_call" | custom-call | flops 3145728 | bytes 12288 | tf_op jit(solution)/shard_map/attend_back/pallas_call | solution.py:381
  433.9 15.7 %collective-permute-done.41 = bf16[512,768]{1,0:T(8,128)(2,1)S(1)} collective-permute-done((bf16[512,768]{1,0:T(8,128)(2,1)}, bf16[512,768]{1,0:T(8,128)(2,1)S(1)}, u32[]{:S(2)}, u32[]{:S(2)}) %collective-permute-start.41) | collective-permute-done | bytes 786464 | tf_op jit(solution)/shard_map/ppermute | solution.py:28
  452.0 3.7 fusion.11
  459.5 3.7 fusion.18
  466.2 17.7 %conditional.3 = (bf16[768,3072]{1,0:T(8,128)(2,1)}, f32[8,96,3072]{2,1,0:T(8,128)}) conditional(s32[]{:T(128)} %convert_element_type.433, (bf16[512,768]{1,0:T(8,128)(2,1)}, bf16[512,768]{1,0:T(8,128)(2,1)S(1)}, bf16[512,2048]{1,0:T(8,128)(2,1)}, bf16[512,1024]{1,0:T(8,128)(2,1)S(1)}, bf16[512,2048]{1,0:T(8,128)(2,1)}, ...), branch_computations={%region_15.16_spmd, %region_16.17_spmd} | conditional | flops 4834197504 | bytes 26738732
  467.0 9.4 %row_products.4 = (bf16[768,3072]{1,0:T(8,128)(2,1)}, bf16[768,3072]{1,0:T(8,128)(2,1)}) custom-call(bf16[512,768]{1,0:T(8,128)(2,1)} %get-tuple-element.36.refs_0_, bf16[512,768]{1,0:T(8,128)(2,1)} %copy-done.91, bf16[512,2048]{1,0:T(8,128)(2,1)} %get-tuple-element.38.refs_2_, bf16[512,1024]{1,0:T(8,128)(2,1)S(1)} %get-tuple-element.39.refs_3_, ...), custom_call_target="tpu_custom_call" | custom-call | flops 4831838208 | bytes 9437184 | tf_op jit(solution)/shard_map/cond/branch_0_fun/row_products/pallas_call | solution.py:445
  476.4 7.3 %convert.58 = f32[8,96,3072]{2,1,0:T(8,128)} convert(bf16[8,96,3072]{2,1,0:T(8,128)(2,1)} %bitcast.354) | non-fusion elementwise | flops 2359296 | bytes 14155776 | tf_op jit(solution)/shard_map/convert_element_type | solution.py:727
  484.0 8.7 %row_products.6 = (bf16[768,1536]{1,0:T(8,128)(2,1)}, bf16[768,1536]{1,0:T(8,128)(2,1)}) custom-call(bf16[512,768]{1,0:T(8,128)(2,1)} %get-tuple-element.253.refs_0_, bf16[1024,768]{1,0:T(8,128)(2,1)} %copy-done.98, bf16[512,768]{1,0:T(8,128)(2,1)} %copy-done.80, bf16[512,384]{1,0:T(8,128)(2,1)} %get-tuple-element.166.refs_3_, ...), custom_call_target="tpu_custom_call" | custom-call | flops 3623878656 | bytes 4718592 | tf_op jit(solution)/shard_map/row_products/pallas_call | solution.py:445
  502.2 6.8 fusion.4
  509.0 4.7 maximum_maximum_fusion
  515.8 4.3 fusion.115
  520.3 3.5 multiply_reduce_fusion.3
  525.9 4.1 fusion.120
  531.3 13.1 %attend_back.7 = (bf16[512,384]{1,0:T(8,128)(2,1)}, bf16[1024,768]{1,0:T(8,128)(2,1)}) custom-call(s32[2]{0:T(128)} %pad_add_fusion.start_ref, bf16[512,384]{1,0:T(8,128)(2,1)} %convolution_convert_fusion.10.query_ref, bf16[1024,768]{1,0:T(8,128)(2,1)} %convolution_convert_fusion.2.pair_ref, s32[1,512]{1,0:T(1,128)} %broadcast_select_fusion.2.limit_ref, ...), custom_call_target="tpu_custom_call" | custom-call | flops 3145728 | bytes 12288 | tf_op jit(solution)/shard_map/attend_back/pallas_call | solution.py:381
  546.8 12.9 %attend_back.6 = (bf16[512,384]{1,0:T(8,128)(2,1)}, bf16[1024,768]{1,0:T(8,128)(2,1)}) custom-call(s32[2]{0:T(128)} %pad_add_fusion.start_ref, bf16[512,384]{1,0:T(8,128)(2,1)} %convolution_convert_fusion.11.query_ref, bf16[1024,768]{1,0:T(8,128)(2,1)} %convolution_convert_fusion.3.pair_ref, s32[1,512]{1,0:T(1,128)} %broadcast_select_fusion.2.limit_ref, ...), custom_call_target="tpu_custom_call" | custom-call | flops 3145728 | bytes 12288 | tf_op jit(solution)/shard_map/attend_back/pallas_call | solution.py:381
  559.7 3.4 fusion.145
  567.2 8.9 %row_products.7 = (bf16[768,1536]{1,0:T(8,128)(2,1)}, bf16[768,1536]{1,0:T(8,128)(2,1)}) custom-call(bf16[512,768]{1,0:T(8,128)(2,1)} %copy-done.32, bf16[1024,768]{1,0:T(8,128)(2,1)} %pad_maximum_fusion.4.refs_1_, bf16[512,768]{1,0:T(8,128)(2,1)} %copy-done.84, bf16[512,384]{1,0:T(8,128)(2,1)} %get-tuple-element.178.refs_3_, ...), custom_call_target="tpu_custom_call" | custom-call | flops 3623878656 | bytes 4718592 | tf_op jit(solution)/shard_map/row_products/pallas_call | solution.py:445
  586.4 9.9 %collective-permute-done.45 = bf16[256,768]{1,0:T(8,128)(2,1)} collective-permute-done((bf16[256,768]{1,0:T(8,128)(2,1)}, bf16[256,768]{1,0:T(8,128)(2,1)}, u32[]{:S(2)}, u32[]{:S(2)}) %collective-permute-start.45) | collective-permute-done | bytes 393248 | tf_op jit(solution)/shard_map/ppermute | solution.py:28
  598.9 4.8 all-to-all-start.2
  612.5 3.5 constant_dynamic-slice_fusion.14
  621.0 5.9 all-to-all-done.2
  628.4 3.5 all-to-all-start.3
  638.0 12.0 %collective-permute-done.54 = bf16[56,1536]{1,0:T(8,128)(2,1)S(1)} collective-permute-done((bf16[56,1536]{1,0:T(8,128)(2,1)S(1)}, bf16[56,1536]{1,0:T(8,128)(2,1)S(1)}, u32[]{:S(2)}, u32[]{:S(2)}) %collective-permute-start.54) | collective-permute-done | bytes 172064 | tf_op jit(solution)/shard_map/ppermute | solution.py:39
  650.8 5.2 collective-permute-start.55
  656.8 5.5 collective-permute-start.51
  666.5 3.6 collective-permute-done.55
  675.1 5.9 collective-permute-done.56
  687.2 3.6 collective-permute-done.57
  702.7 4.7 collective-permute-done.58
  (625 shorter events, 248.5 us)
Async XLA Ops:
  8.4 17.4 %collective-permute-start = (bf16[256,768]{1,0:T(8,128)(2,1)S(1)}, bf16[256,768]{1,0:T(8,128)(2,1)S(1)}, u32[]{:S(2)}, u32[]{:S(2)}) collective-permute-start(bf16[256,768]{1,0:T(8,128)(2,1)S(1)} %slice_bitcast_fusion.3), channel_id=1, source_target_pairs={{16,0},{17,1},{18,2},{19,3},{20,4},{21,5},{22,6},{23,7},{24,8},{25... | collective-permute-start | bytes 1179656 | tf_op jit(solution)/shard_map/ppermute | solution.py:28
  12.7 11.1 %collective-permute-start.3 = (bf16[112,1536]{1,0:T(8,128)(2,1)S(1)}, bf16[112,1536]{1,0:T(8,128)(2,1)S(1)}, u32[]{:S(2)}, u32[]{:S(2)}) collective-permute-start(bf16[112,1536]{1,0:T(8,128)(2,1)S(1)} %concatenate.225.refs_0_), channel_id=1, source_target_pairs={{0,2},{4,0},{8,4},{12,8},{14,12},{10,14},{6,10},{2,6},{1,3},{5,1},... | collective-permute-start | bytes 1032200 | tf_op jit(solution)/shard_map/ppermute | solution.py:39
  15.7 9.8 %collective-permute-start.2 = (bf16[112,1536]{1,0:T(8,128)(2,1)S(1)}, bf16[112,1536]{1,0:T(8,128)(2,1)S(1)}, u32[]{:S(2)}, u32[]{:S(2)}) collective-permute-start(bf16[112,1536]{1,0:T(8,128)(2,1)S(1)} %concatenate.225.refs_0_), channel_id=1, source_target_pairs={{0,4},{4,8},{8,12},{12,14},{14,10},{10,6},{6,2},{2,0},{1,5},{5,9},... | collective-permute-start | bytes 1032200 | tf_op jit(solution)/shard_map/ppermute | solution.py:39
  23.8 14.9 %collective-permute-start.5 = (bf16[112,1536]{1,0:T(8,128)(2,1)S(1)}, bf16[112,1536]{1,0:T(8,128)(2,1)}, u32[]{:S(2)}, u32[]{:S(2)}) collective-permute-start(bf16[112,1536]{1,0:T(8,128)(2,1)S(1)} %collective-permute-done.3.refs_2_), channel_id=1, source_target_pairs={{0,2},{4,0},{8,4},{12,8},{14,12},{10,14},{6,10},{2,6},{1,3},{5,1},... | collective-permute-start | bytes 1032200 | tf_op jit(solution)/shard_map/ppermute | solution.py:39
  25.5 15.3 %collective-permute-start.4 = (bf16[112,1536]{1,0:T(8,128)(2,1)S(1)}, bf16[112,1536]{1,0:T(8,128)(2,1)}, u32[]{:S(2)}, u32[]{:S(2)}) collective-permute-start(bf16[112,1536]{1,0:T(8,128)(2,1)S(1)} %collective-permute-done.2.refs_1_), channel_id=1, source_target_pairs={{0,4},{4,8},{8,12},{12,14},{14,10},{10,6},{6,2},{2,0},{1,5},{5,9},... | collective-permute-start | bytes 1032200 | tf_op jit(solution)/shard_map/ppermute | solution.py:39
  26.6 17.5 %all-to-all-start = ((bf16[8,32,768]{2,1,0:T(8,128)(2,1)}), bf16[8,32,768]{2,1,0:T(8,128)(2,1)S(1)}, u32[]{:S(2)}, u32[]{:S(2)}) async-start(bf16[8,32,768]{2,1,0:T(8,128)(2,1)} %bitcast.4), calls=%async_computation | async-start | bytes 786432 | tf_op jit(solution)/shard_map/all_to_all | solution.py:232
  33.7 26.5 %collective-permute-start.10 = (bf16[48,1536]{1,0:T(8,128)(2,1)}, bf16[48,1536]{1,0:T(8,128)(2,1)}, u32[]{:S(2)}, u32[]{:S(2)}) collective-permute-start(bf16[48,1536]{1,0:T(8,128)(2,1)} %pad_maximum_fusion.13), channel_id=1, source_target_pairs={{0,16},{1,17},{2,18},{3,19},{4,20},{5,21},{6,22},{7,23},{8,24},{9,... | collective-permute-start | bytes 442376 | tf_op jit(solution)/shard_map/ppermute | solution.py:32
  38.8 11.3 %collective-permute-start.7 = (bf16[112,1536]{1,0:T(8,128)(2,1)}, bf16[112,1536]{1,0:T(8,128)(2,1)S(1)}, u32[]{:S(2)}, u32[]{:S(2)}) collective-permute-start(bf16[112,1536]{1,0:T(8,128)(2,1)} %collective-permute-done.5.refs_4_), channel_id=1, source_target_pairs={{0,2},{4,0},{8,4},{12,8},{14,12},{10,14},{6,10},{2,6},{1,3},{5,1},... | collective-permute-start | bytes 1032200 | tf_op jit(solution)/shard_map/ppermute | solution.py:39
  40.8 11.9 %collective-permute-start.6 = (bf16[112,1536]{1,0:T(8,128)(2,1)}, bf16[112,1536]{1,0:T(8,128)(2,1)S(1)}, u32[]{:S(2)}, u32[]{:S(2)}) collective-permute-start(bf16[112,1536]{1,0:T(8,128)(2,1)} %collective-permute-done.4.refs_3_), channel_id=1, source_target_pairs={{0,4},{4,8},{8,12},{12,14},{14,10},{10,6},{6,2},{2,0},{1,5},{5,9},... | collective-permute-start | bytes 1032200 | tf_op jit(solution)/shard_map/ppermute | solution.py:39
  45.4 22.0 %all-to-all-start.1 = ((bf16[8,32,768]{2,1,0:T(8,128)(2,1)}), bf16[8,32,768]{2,1,0:T(8,128)(2,1)S(1)}, u32[]{:S(2)}, u32[]{:S(2)}) async-start(bf16[8,32,768]{2,1,0:T(8,128)(2,1)} %gather_fusion), calls=%async_computation.1 | async-start | bytes 786432 | tf_op jit(solution)/shard_map/all_to_all | solution.py:233
  49.5 252.7 %all-gather.2.cloned.1.call-start = ((), (), s32[]{:S(2)}) async-start(), calls=%async_computation.6 | async-start | bytes 7077888 | tf_op jit(solution)/shard_map/all_gather | solution.py:632
  50.8 11.1 %collective-permute-start.9 = (bf16[56,1536]{1,0:T(8,128)(2,1)}, bf16[56,1536]{1,0:T(8,128)(2,1)}, u32[]{:S(2)}, u32[]{:S(2)}) collective-permute-start(bf16[56,1536]{1,0:T(8,128)(2,1)} %slice.388), channel_id=1, source_target_pairs={{0,2},{4,0},{8,4},{12,8},{14,12},{10,14},{6,10},{2,6},{1,3},{5,1},... | collective-permute-start | bytes 516104 | tf_op jit(solution)/shard_map/ppermute | solution.py:39
  59.0 29.2 %collective-permute-start.14 = (bf16[1,8,96,768]{3,2,1,0:T(8,128)(2,1)}, bf16[1,8,96,768]{3,2,1,0:T(8,128)(2,1)}, u32[]{:S(2)}, u32[]{:S(2)}) collective-permute-start(bf16[1,8,96,768]{3,2,1,0:T(8,128)(2,1)} %get-tuple-element.129.refs_1_), channel_id=1, source_target_pairs={{0,1},{1,0},{2,3},{3,2},{4,5},{5,4},{6,7},{7,6},{8,9},{9,8},{10,11... | collective-permute-start | bytes 3538952 | tf_op jit(solution)/shard_map/ppermute | solution.py:20
  60.1 7.3 %collective-permute-start.8 = (bf16[56,1536]{1,0:T(8,128)(2,1)S(1)}, bf16[56,1536]{1,0:T(8,128)(2,1)}, u32[]{:S(2)}, u32[]{:S(2)}) collective-permute-start(bf16[56,1536]{1,0:T(8,128)(2,1)S(1)} %slice.387), channel_id=1, source_target_pairs={{0,4},{4,8},{8,12},{12,14},{14,10},{10,6},{6,2},{2,0},{1,5},{5,9},... | collective-permute-start | bytes 516104 | tf_op jit(solution)/shard_map/ppermute | solution.py:39
  61.4 19.4 %collective-permute-start.16 = (bf16[1,8,16,1536]{3,2,1,0:T(8,128)(2,1)S(1)}, bf16[1,8,16,1536]{3,2,1,0:T(8,128)(2,1)}, u32[]{:S(2)}, u32[]{:S(2)}) collective-permute-start(bf16[1,8,16,1536]{3,2,1,0:T(8,128)(2,1)S(1)} %copy-done.94), channel_id=1, source_target_pairs={{0,1},{1,0},{2,3},{3,2},{4,5},{5,4},{6,7},{7,6},{8,9},{9,8},{10,11... | collective-permute-start | bytes 1179656 | tf_op jit(solution)/shard_map/ppermute | solution.py:20
  61.9 22.6 %collective-permute-start.11 = (bf16[96,4608]{1,0:T(8,128)(2,1)S(1)}, bf16[96,4608]{1,0:T(8,128)(2,1)}, u32[]{:S(2)}, u32[]{:S(2)}) collective-permute-start(bf16[96,4608]{1,0:T(8,128)(2,1)S(1)} %maximum_maximum_fusion.1.refs_0_), channel_id=1, source_target_pairs={{0,2},{4,0},{8,4},{12,8},{14,12},{10,14},{6,10},{2,6},{1,3},{5,1},... | collective-permute-start | bytes 2654216 | tf_op jit(solution)/shard_map/ppermute | solution.py:39
  63.6 22.9 %collective-permute-start.21 = (bf16[96,4608]{1,0:T(8,128)(2,1)S(1)}, bf16[96,4608]{1,0:T(8,128)(2,1)}, u32[]{:S(2)}, u32[]{:S(2)}) collective-permute-start(bf16[96,4608]{1,0:T(8,128)(2,1)S(1)} %maximum_maximum_fusion.1.refs_0_), channel_id=1, source_target_pairs={{0,4},{4,8},{8,12},{12,14},{14,10},{10,6},{6,2},{2,0},{1,5},{5,9},... | collective-permute-start | bytes 2654216 | tf_op jit(solution)/shard_map/ppermute | solution.py:39
  67.4 13.4 %collective-permute-start.1 = (bf16[256,768]{1,0:T(8,128)(2,1)S(1)}, bf16[256,768]{1,0:T(8,128)(2,1)}, u32[]{:S(2)}, u32[]{:S(2)}) collective-permute-start(bf16[256,768]{1,0:T(8,128)(2,1)S(1)} %bitcast.378), channel_id=1, source_target_pairs={{0,16},{1,17},{2,18},{3,19},{4,20},{5,21},{6,22},{7,23},{8,24},{9,... | collective-permute-start | bytes 1179656 | tf_op jit(solution)/shard_map/ppermute | solution.py:32
  80.8 5.7 collective-permute-start.13
  80.8 5.8 collective-permute-start.15
  84.4 22.0 %collective-permute-start.18 = (bf16[96,4608]{1,0:T(8,128)(2,1)}, bf16[96,4608]{1,0:T(8,128)(2,1)}, u32[]{:S(2)}, u32[]{:S(2)}) collective-permute-start(bf16[96,4608]{1,0:T(8,128)(2,1)} %collective-permute-done.11.refs_2_), channel_id=1, source_target_pairs={{0,2},{4,0},{8,4},{12,8},{14,12},{10,14},{6,10},{2,6},{1,3},{5,1},... | collective-permute-start | bytes 2654216 | tf_op jit(solution)/shard_map/ppermute | solution.py:39
  86.5 21.9 %collective-permute-start.22 = (bf16[96,4608]{1,0:T(8,128)(2,1)}, bf16[96,4608]{1,0:T(8,128)(2,1)}, u32[]{:S(2)}, u32[]{:S(2)}) collective-permute-start(bf16[96,4608]{1,0:T(8,128)(2,1)} %collective-permute-done.21.refs_1_), channel_id=1, source_target_pairs={{0,4},{4,8},{8,12},{12,14},{14,10},{10,6},{6,2},{2,0},{1,5},{5,9},... | collective-permute-start | bytes 2654216 | tf_op jit(solution)/shard_map/ppermute | solution.py:39
  86.6 9.7 %collective-permute-start.17 = (bf16[112,1536]{1,0:T(8,128)(2,1)}, bf16[112,1536]{1,0:T(8,128)(2,1)}, u32[]{:S(2)}, u32[]{:S(2)}) collective-permute-start(bf16[112,1536]{1,0:T(8,128)(2,1)} %constant_dynamic-update-slice_fusion.refs_4_), channel_id=1, source_target_pairs={{0,1},{1,0},{2,3},{3,2},{4,5},{5,4},{6,7},{7,6},{8,9},{9,8},{10,11... | collective-permute-start | bytes 1032200 | tf_op jit(solution)/shard_map/ppermute | solution.py:20
  88.2 25.6 %collective-permute-start.12 = (bf16[512,768]{1,0:T(8,128)(2,1)S(1)}, bf16[512,768]{1,0:T(8,128)(2,1)S(1)}, u32[]{:S(2)}, u32[]{:S(2)}) collective-permute-start(bf16[512,768]{1,0:T(8,128)(2,1)S(1)} %get-tuple-element.223), channel_id=1, source_target_pairs={{0,1},{1,0},{2,3},{3,2},{4,5},{5,4},{6,7},{7,6},{8,9},{9,8},{10,11... | collective-permute-start | bytes 2359304 | tf_op jit(solution)/shard_map/ppermute | solution.py:20
  91.9 21.9 %collective-permute-start.20 = (f32[384]{0:T(512)S(1)}, f32[384]{0:T(512)S(1)}, u32[]{:S(2)}, u32[]{:S(2)}) collective-permute-start(f32[384]{0:T(512)S(1)} %reshape.969), channel_id=1, source_target_pairs={{0,16},{1,17},{2,18},{3,19},{4,20},{5,21},{6,22},{7,23},{8,24},{9,... | collective-permute-start | bytes 4616 | tf_op jit(solution)/shard_map/ppermute | solution.py:32
  106.4 21.1 %collective-permute-start.19 = (bf16[96,4608]{1,0:T(8,128)(2,1)}, bf16[96,4608]{1,0:T(8,128)(2,1)}, u32[]{:S(2)}, u32[]{:S(2)}) collective-permute-start(bf16[96,4608]{1,0:T(8,128)(2,1)} %collective-permute-done.18.refs_4_), channel_id=1, source_target_pairs={{0,2},{4,0},{8,4},{12,8},{14,12},{10,14},{6,10},{2,6},{1,3},{5,1},... | collective-permute-start | bytes 2654216 | tf_op jit(solution)/shard_map/ppermute | solution.py:39
  108.5 21.0 %collective-permute-start.23 = (bf16[96,4608]{1,0:T(8,128)(2,1)}, bf16[96,4608]{1,0:T(8,128)(2,1)}, u32[]{:S(2)}, u32[]{:S(2)}) collective-permute-start(bf16[96,4608]{1,0:T(8,128)(2,1)} %collective-permute-done.22.refs_3_), channel_id=1, source_target_pairs={{0,4},{4,8},{8,12},{12,14},{14,10},{10,6},{6,2},{2,0},{1,5},{5,9},... | collective-permute-start | bytes 2654216 | tf_op jit(solution)/shard_map/ppermute | solution.py:39
  137.1 46.8 %collective-permute-start.26 = (bf16[1,8,96,2048]{3,2,1,0:T(8,128)(2,1)}, bf16[1,8,96,2048]{3,2,1,0:T(8,128)(2,1)}, u32[]{:S(2)}, u32[]{:S(2)}) collective-permute-start(bf16[1,8,96,2048]{3,2,1,0:T(8,128)(2,1)} %get-tuple-element.145.refs_0_), channel_id=1, source_target_pairs={{0,1},{1,0},{2,3},{3,2},{4,5},{5,4},{6,7},{7,6},{8,9},{9,8},{10,11... | collective-permute-start | bytes 9437192 | tf_op jit(solution)/shard_map/ppermute | solution.py:20
  143.0 25.4 %collective-permute-start.24 = (bf16[48,4608]{1,0:T(8,128)(2,1)S(1)}, bf16[48,4608]{1,0:T(8,128)(2,1)S(1)}, u32[]{:S(2)}, u32[]{:S(2)}) collective-permute-start(bf16[48,4608]{1,0:T(8,128)(2,1)S(1)} %slice.392), channel_id=1, source_target_pairs={{0,4},{4,8},{8,12},{12,14},{14,10},{10,6},{6,2},{2,0},{1,5},{5,9},... | collective-permute-start | bytes 1327112 | tf_op jit(solution)/shard_map/ppermute | solution.py:39
  166.0 12.4 %collective-permute-start.25 = (bf16[48,4608]{1,0:T(8,128)(2,1)S(1)}, bf16[48,4608]{1,0:T(8,128)(2,1)S(1)}, u32[]{:S(2)}, u32[]{:S(2)}) collective-permute-start(bf16[48,4608]{1,0:T(8,128)(2,1)S(1)} %slice.393), channel_id=1, source_target_pairs={{0,2},{4,0},{8,4},{12,8},{14,12},{10,14},{6,10},{2,6},{1,3},{5,1},... | collective-permute-start | bytes 1327112 | tf_op jit(solution)/shard_map/ppermute | solution.py:39
  167.9 16.0 %collective-permute-start.27 = (bf16[1,8,96,1024]{3,2,1,0:T(8,128)(2,1)}, bf16[1,8,96,1024]{3,2,1,0:T(8,128)(2,1)}, u32[]{:S(2)}, u32[]{:S(2)}) collective-permute-start(bf16[1,8,96,1024]{3,2,1,0:T(8,128)(2,1)} %get-tuple-element.146.refs_1_), channel_id=1, source_target_pairs={{0,1},{1,0},{2,3},{3,2},{4,5},{5,4},{6,7},{7,6},{8,9},{9,8},{10,11... | collective-permute-start | bytes 4718600 | tf_op jit(solution)/shard_map/ppermute | solution.py:20
  167.9 13.1 %collective-permute-start.28 = (bf16[2,8,48,384]{3,2,1,0:T(8,128)(2,1)S(1)}, bf16[2,8,48,384]{3,2,1,0:T(8,128)(2,1)S(1)}, u32[]{:S(2)}, u32[]{:S(2)}) collective-permute-start(bf16[2,8,48,384]{3,2,1,0:T(8,128)(2,1)S(1)} %copy-done.45), channel_id=1, source_target_pairs={{0,1},{1,0},{2,3},{3,2},{4,5},{5,4},{6,7},{7,6},{8,9},{9,8},{10,11... | collective-permute-start | bytes 1769480 | tf_op jit(solution)/shard_map/ppermute | solution.py:20
  168.4 15.4 %collective-permute-start.29 = (bf16[2,8,48,768]{3,2,1,0:T(8,128)(2,1)}, bf16[2,8,48,768]{3,2,1,0:T(8,128)(2,1)}, u32[]{:S(2)}, u32[]{:S(2)}) collective-permute-start(bf16[2,8,48,768]{3,2,1,0:T(8,128)(2,1)} %get-tuple-element.148.refs_3_), channel_id=1, source_target_pairs={{0,1},{1,0},{2,3},{3,2},{4,5},{5,4},{6,7},{7,6},{8,9},{9,8},{10,11... | collective-permute-start | bytes 3538952 | tf_op jit(solution)/shard_map/ppermute | solution.py:20
  179.3 7.4 %collective-permute-start.31 = (bf16[96,4608]{1,0:T(8,128)(2,1)}, bf16[96,4608]{1,0:T(8,128)(2,1)}, u32[]{:S(2)}, u32[]{:S(2)}) collective-permute-start(bf16[96,4608]{1,0:T(8,128)(2,1)} %constant_dynamic-update-slice_fusion.2.refs_5_), channel_id=1, source_target_pairs={{0,1},{1,0},{2,3},{3,2},{4,5},{5,4},{6,7},{7,6},{8,9},{9,8},{10,11... | collective-permute-start | bytes 2654216 | tf_op jit(solution)/shard_map/ppermute | solution.py:20
  181.0 2.8 collective-permute-start.30
  183.3 512.7 %reduce-scatter.5.cloned.1.call-start = ((), (), s32[]{:S(2)}) async-start(), calls=%async_computation.8 | async-start | bytes 7077888 | tf_op jit(solution)/shard_map/reduce_scatter | solution.py:685
  203.7 21.1 %collective-permute-start.32 = (bf16[512,768]{1,0:T(8,128)(2,1)S(1)}, bf16[512,768]{1,0:T(8,128)(2,1)S(1)}, u32[]{:S(2)}, u32[]{:S(2)}) collective-permute-start(bf16[512,768]{1,0:T(8,128)(2,1)S(1)} %multiply_convert_fusion.11), channel_id=1, source_target_pairs={{0,16},{1,17},{2,18},{3,19},{4,20},{5,21},{6,22},{7,23},{8,24},{9,... | collective-permute-start | bytes 2359304 | tf_op jit(solution)/shard_map/ppermute | solution.py:32
  224.7 2.7 collective-permute-start.33
  275.1 22.3 %collective-permute-start.34 = (bf16[512,768]{1,0:T(8,128)(2,1)}, bf16[512,768]{1,0:T(8,128)(2,1)}, u32[]{:S(2)}, u32[]{:S(2)}) collective-permute-start(bf16[512,768]{1,0:T(8,128)(2,1)} %multiply_convert_fusion.9), channel_id=1, source_target_pairs={{16,0},{17,1},{18,2},{19,3},{20,4},{21,5},{22,6},{23,7},{24,8},{25... | collective-permute-start | bytes 2359304 | tf_op jit(solution)/shard_map/ppermute | solution.py:28
  299.7 2.4 collective-permute-start.35
  320.9 3.8 collective-permute-start.37
  341.8 2.4 collective-permute-start.38
  345.7 19.3 %collective-permute-start.39 = (bf16[512,768]{1,0:T(8,128)(2,1)}, bf16[512,768]{1,0:T(8,128)(2,1)}, u32[]{:S(2)}, u32[]{:S(2)}) collective-permute-start(bf16[512,768]{1,0:T(8,128)(2,1)} %get-tuple-element.212), channel_id=1, source_target_pairs={{0,16},{1,17},{2,18},{3,19},{4,20},{5,21},{6,22},{7,23},{8,24},{9,... | collective-permute-start | bytes 2359304 | tf_op jit(solution)/shard_map/ppermute | solution.py:32
  359.7 338.6 %reduce-scatter.3.cloned.1.call-start = ((), (), s32[]{:S(2)}) async-start(), calls=%async_computation.7 | async-start | bytes 7962624 | tf_op jit(solution)/shard_map/reduce_scatter | solution.py:731
  427.6 22.0 %collective-permute-start.41 = (bf16[512,768]{1,0:T(8,128)(2,1)}, bf16[512,768]{1,0:T(8,128)(2,1)S(1)}, u32[]{:S(2)}, u32[]{:S(2)}) collective-permute-start(bf16[512,768]{1,0:T(8,128)(2,1)} %slice_add_fusion.1), channel_id=1, source_target_pairs={{16,0},{17,1},{18,2},{19,3},{20,4},{21,5},{22,6},{23,7},{24,8},{25... | collective-permute-start | bytes 2359304 | tf_op jit(solution)/shard_map/ppermute | solution.py:28
  483.8 18.4 %collective-permute-start.42 = (bf16[768,3072]{1,0:T(8,128)(2,1)}, bf16[768,3072]{1,0:T(8,128)(2,1)}, u32[]{:S(2)}, u32[]{:S(2)}) collective-permute-start(bf16[768,3072]{1,0:T(8,128)(2,1)} %get-tuple-element.173), channel_id=1, source_target_pairs={{0,1},{1,0},{2,3},{3,2},{4,5},{5,4},{6,7},{7,6},{8,9},{9,8},{10,11... | collective-permute-start | bytes 14155784 | tf_op jit(solution)/shard_map/ppermute | solution.py:20
  492.6 6.1 collective-permute-start.43
  524.3 59.0 %collective-permute-start.47 = (bf16[384]{0:T(512)(128)(2,1)}, bf16[384]{0:T(512)(128)(2,1)}, u32[]{:S(2)}, u32[]{:S(2)}) collective-permute-start(bf16[384]{0:T(512)(128)(2,1)} %slice.356), channel_id=1, source_target_pairs={{16,0},{17,1},{18,2},{19,3},{20,4},{21,5},{22,6},{23,7},{24,8},{25... | collective-permute-start | bytes 2312 | tf_op jit(solution)/shard_map/ppermute | solution.py:28
  566.4 10.9 %collective-permute-start.44 = (bf16[512,768]{1,0:T(8,128)(2,1)S(1)}, bf16[512,768]{1,0:T(8,128)(2,1)S(1)}, u32[]{:S(2)}, u32[]{:S(2)}) collective-permute-start(bf16[512,768]{1,0:T(8,128)(2,1)S(1)} %slice.563), channel_id=1, source_target_pairs={{0,1},{1,0},{2,3},{3,2},{4,5},{5,4},{6,7},{7,6},{8,9},{9,8},{10,11... | collective-permute-start | bytes 2359304 | tf_op jit(solution)/shard_map/ppermute | solution.py:20
  576.1 55.8 %collective-permute-start.48 = (bf16[768,1536]{1,0:T(8,128)(2,1)}, bf16[768,1536]{1,0:T(8,128)(2,1)}, u32[]{:S(2)}, u32[]{:S(2)}) collective-permute-start(bf16[768,1536]{1,0:T(8,128)(2,1)} %get-tuple-element.184), channel_id=1, source_target_pairs={{0,1},{1,0},{2,3},{3,2},{4,5},{5,4},{6,7},{7,6},{8,9},{9,8},{10,11... | collective-permute-start | bytes 7077896 | tf_op jit(solution)/shard_map/ppermute | solution.py:20
  582.0 14.3 %collective-permute-start.45 = (bf16[256,768]{1,0:T(8,128)(2,1)}, bf16[256,768]{1,0:T(8,128)(2,1)}, u32[]{:S(2)}, u32[]{:S(2)}) collective-permute-start(bf16[256,768]{1,0:T(8,128)(2,1)} %slice.422), channel_id=1, source_target_pairs={{16,0},{17,1},{18,2},{19,3},{20,4},{21,5},{22,6},{23,7},{24,8},{25... | collective-permute-start | bytes 1179656 | tf_op jit(solution)/shard_map/ppermute | solution.py:28
  586.1 26.4 %collective-permute-start.49 = (bf16[8,16,1536]{2,0,1:T(8,128)(2,1)S(1)}, bf16[8,16,1536]{2,0,1:T(8,128)(2,1)}, u32[]{:S(2)}, u32[]{:S(2)}) collective-permute-start(bf16[8,16,1536]{2,0,1:T(8,128)(2,1)S(1)} %fusion.62), channel_id=1, source_target_pairs={{0,1},{1,0},{2,3},{3,2},{4,5},{5,4},{6,7},{7,6},{8,9},{9,8},{10,11... | collective-permute-start | bytes 1179656 | tf_op jit(solution)/shard_map/ppermute | solution.py:20
  598.9 28.1 %all-to-all-start.2 = ((bf16[8,33,768]{2,1,0:T(8,128)(2,1)}), bf16[8,33,768]{2,1,0:T(8,128)(2,1)S(1)}, u32[]{:S(2)}, u32[]{:S(2)}) async-start(bf16[8,33,768]{2,1,0:T(8,128)(2,1)} %pad_maximum_fusion.8), calls=%async_computation.2 | async-start | bytes 983040 | tf_op jit(solution)/shard_map/all_to_all | solution.py:232
  628.4 34.0 %all-to-all-start.3 = ((bf16[8,33,768]{2,1,0:T(8,128)(2,1)}), bf16[8,33,768]{2,1,0:T(8,128)(2,1)S(1)}, u32[]{:S(2)}, u32[]{:S(2)}) async-start(bf16[8,33,768]{2,1,0:T(8,128)(2,1)} %gather_fusion.1), calls=%async_computation.3 | async-start | bytes 983040 | tf_op jit(solution)/shard_map/all_to_all | solution.py:233
  635.0 15.0 %collective-permute-start.54 = (bf16[56,1536]{1,0:T(8,128)(2,1)S(1)}, bf16[56,1536]{1,0:T(8,128)(2,1)S(1)}, u32[]{:S(2)}, u32[]{:S(2)}) collective-permute-start(bf16[56,1536]{1,0:T(8,128)(2,1)S(1)} %get-tuple-element.279), channel_id=1, source_target_pairs={{0,2},{4,0},{8,4},{12,8},{14,12},{10,14},{6,10},{2,6},{1,3},{5,1},... | collective-permute-start | bytes 516104 | tf_op jit(solution)/shard_map/ppermute | solution.py:39
  637.2 18.8 %collective-permute-start.50 = (bf16[56,1536]{1,0:T(8,128)(2,1)S(1)}, bf16[56,1536]{1,0:T(8,128)(2,1)S(1)}, u32[]{:S(2)}, u32[]{:S(2)}) collective-permute-start(bf16[56,1536]{1,0:T(8,128)(2,1)S(1)} %get-tuple-element.278), channel_id=1, source_target_pairs={{0,4},{4,8},{8,12},{12,14},{14,10},{10,6},{6,2},{2,0},{1,5},{5,9},... | collective-permute-start | bytes 516104 | tf_op jit(solution)/shard_map/ppermute | solution.py:39
  650.8 19.3 %collective-permute-start.55 = (bf16[112,1536]{1,0:T(8,128)(2,1)}, bf16[112,1536]{1,0:T(8,128)(2,1)}, u32[]{:S(2)}, u32[]{:S(2)}) collective-permute-start(bf16[112,1536]{1,0:T(8,128)(2,1)} %pad_maximum_fusion.10), channel_id=1, source_target_pairs={{0,2},{4,0},{8,4},{12,8},{14,12},{10,14},{6,10},{2,6},{1,3},{5,1},... | collective-permute-start | bytes 1032200 | tf_op jit(solution)/shard_map/ppermute | solution.py:39
  656.8 14.7 %collective-permute-start.51 = (bf16[112,1536]{1,0:T(8,128)(2,1)}, bf16[112,1536]{1,0:T(8,128)(2,1)}, u32[]{:S(2)}, u32[]{:S(2)}) collective-permute-start(bf16[112,1536]{1,0:T(8,128)(2,1)} %pad_maximum_fusion.9), channel_id=1, source_target_pairs={{0,4},{4,8},{8,12},{12,14},{14,10},{10,6},{6,2},{2,0},{1,5},{5,9},... | collective-permute-start | bytes 1032200 | tf_op jit(solution)/shard_map/ppermute | solution.py:39
  662.5 22.0 %collective-permute-start.46 = (bf16[256,768]{1,0:T(8,128)(2,1)S(1)}, bf16[256,768]{1,0:T(8,128)(2,1)}, u32[]{:S(2)}, u32[]{:S(2)}) collective-permute-start(bf16[256,768]{1,0:T(8,128)(2,1)S(1)} %bitcast.375), channel_id=1, source_target_pairs={{0,16},{1,17},{2,18},{3,19},{4,20},{5,21},{6,22},{7,23},{8,24},{9,... | collective-permute-start | bytes 1179656 | tf_op jit(solution)/shard_map/ppermute | solution.py:32
  671.5 9.5 %collective-permute-start.56 = (bf16[112,1536]{1,0:T(8,128)(2,1)S(1)}, bf16[112,1536]{1,0:T(8,128)(2,1)S(1)}, u32[]{:S(2)}, u32[]{:S(2)}) collective-permute-start(bf16[112,1536]{1,0:T(8,128)(2,1)S(1)} %add_convert_fusion.2), channel_id=1, source_target_pairs={{0,2},{4,0},{8,4},{12,8},{14,12},{10,14},{6,10},{2,6},{1,3},{5,1},... | collective-permute-start | bytes 1032200 | tf_op jit(solution)/shard_map/ppermute | solution.py:39
  673.0 9.5 %collective-permute-start.52 = (bf16[112,1536]{1,0:T(8,128)(2,1)S(1)}, bf16[112,1536]{1,0:T(8,128)(2,1)S(1)}, u32[]{:S(2)}, u32[]{:S(2)}) collective-permute-start(bf16[112,1536]{1,0:T(8,128)(2,1)S(1)} %add_convert_fusion.4), channel_id=1, source_target_pairs={{0,4},{4,8},{8,12},{12,14},{14,10},{10,6},{6,2},{2,0},{1,5},{5,9},... | collective-permute-start | bytes 1032200 | tf_op jit(solution)/shard_map/ppermute | solution.py:39
  682.2 8.6 %collective-permute-start.57 = (bf16[112,1536]{1,0:T(8,128)(2,1)S(1)}, bf16[112,1536]{1,0:T(8,128)(2,1)S(1)}, u32[]{:S(2)}, u32[]{:S(2)}) collective-permute-start(bf16[112,1536]{1,0:T(8,128)(2,1)S(1)} %add_convert_fusion.1), channel_id=1, source_target_pairs={{0,2},{4,0},{8,4},{12,8},{14,12},{10,14},{6,10},{2,6},{1,3},{5,1},... | collective-permute-start | bytes 1032200 | tf_op jit(solution)/shard_map/ppermute | solution.py:39
  682.7 8.6 %collective-permute-start.53 = (bf16[112,1536]{1,0:T(8,128)(2,1)S(1)}, bf16[112,1536]{1,0:T(8,128)(2,1)S(1)}, u32[]{:S(2)}, u32[]{:S(2)}) collective-permute-start(bf16[112,1536]{1,0:T(8,128)(2,1)S(1)} %add_convert_fusion.3), channel_id=1, source_target_pairs={{0,4},{4,8},{8,12},{12,14},{14,10},{10,6},{6,2},{2,0},{1,5},{5,9},... | collective-permute-start | bytes 1032200 | tf_op jit(solution)/shard_map/ppermute | solution.py:39
  700.4 7.0 collective-permute-start.58
  (150 other events, 1340.1 us)
Sparse Core Ops, SparseCore 0:
  183.4 99.7 all-gather.1
  359.8 117.2 reduce-scatter.4
  513.9 144.6 reduce-scatter.2

commit v4 on v3

--- a/solution.py
+++ b/solution.py
@@ -724,6 +724,7 @@
         (normed_enc, enc_kept[1], enc_grads, enc_rows),
     )
 
+    mlp_sums = lax.optimization_barrier(mlp_sums)
     mlp_sum = stacked(mlp_sums[0]).astype(f32) + stacked(swap_core(mlp_sums[1])).astype(f32)
     cut = cross_sum.shape[0] // 2
     halves = jnp.concatenate([stacked(cross_sum[:cut]), stacked(cross_sum[cut:])], 1)
@@ -748,21 +749,6 @@
     stream = stream + part
     self_sums = attention_weight_grads(normed, normed_all, self_kept, self_grads, self_in)
 
-    in_order = jnp.where(core == 0, token_ce, jnp.roll(token_ce, half)).reshape(count, 1, -1)
-    coarse = in_order.astype(bf16)
-    fine = (in_order - coarse.astype(f32)).astype(bf16)
-    losses = jnp.concatenate([coarse, fine], 2)
-    losses = jnp.pad(losses, ((0, 0), (0, 0), (0, model - losses.shape[2])))
-    moved = reroute_plane(jnp.concatenate([lend(stream.astype(bf16)), losses], 1), pairing)
-    piece = in_order.shape[2]
-    losses = moved[:, -1].astype(f32)
-    token_loss = (losses[:, :piece] + losses[:, piece : 2 * piece]).reshape(1, -1)
-    seq_loss = jnp.sum(token_loss, axis=1) / target_len[me].astype(f32)
-    moved = moved[:, :-1].reshape(half // 2, model)
-    d_states = jnp.where(
-        decoding, jnp.concatenate([to_decoder(moved), moved], 0).astype(f32), stream
-    )
-
     cut = grad_gain_cross.shape[0] // 2
     lent_gains = to_encoder(grad_gain_cross[:cut])
     gain_grads = [grad_gain_attn, grad_gain_mlp, grad_gain_final]
@@ -772,8 +758,25 @@
     self_scattering = scatter_stacks(
         [[stacked(self_sums[0]), lines], [stacked(swap_core(self_sums[1])), swap_core(lines)]],
     )
-    for _ in range(3):
-        self_scattering.step()
+    self_scattering.step()
+
+    in_order = jnp.where(core == 0, token_ce, jnp.roll(token_ce, half)).reshape(count, 1, -1)
+    coarse = in_order.astype(bf16)
+    fine = (in_order - coarse.astype(f32)).astype(bf16)
+    losses = jnp.concatenate([coarse, fine], 2)
+    losses = jnp.pad(losses, ((0, 0), (0, 0), (0, model - losses.shape[2])))
+    moved = reroute_plane(jnp.concatenate([lend(held_after(stream.astype(bf16), self_scattering.last)), losses], 1), pairing)
+    piece = in_order.shape[2]
+    losses = moved[:, -1].astype(f32)
+    token_loss = (losses[:, :piece] + losses[:, piece : 2 * piece]).reshape(1, -1)
+    seq_loss = jnp.sum(token_loss, axis=1) / target_len[me].astype(f32)
+    moved = moved[:, :-1].reshape(half // 2, model)
+    d_states = jnp.where(
+        decoding, jnp.concatenate([to_decoder(moved), moved], 0).astype(f32), stream
+    )
+
+    self_scattering.step()
+    self_scattering.step()
     g_attn = self_scattering.total()
     gain_own = g_attn[gain_rows : gain_rows + 1]
     g_attn = g_attn[:gain_rows]

time: 729 us -> 723 us (level)
  waiting for transfers between devices: 162 us -> 177 us
  local copies, waits for them, and re-layouts: 69.2 us -> 59.8 us
  other arithmetic: 95.9 us -> 86.8 us
    ppermute x24, waiting for transfers between devices: 69.6 us -> 89.5 us  [loop_step(): return lax.ppermute(value, 'dp', pairs)]
    ppermute x6, waiting for transfers between devices: 50.4 us -> 40.7 us  [to_encoder(): return lax.ppermute(value, 'slab', [(1, 0)])]
    ppermute x24, starting transfers between devices: 35.7 us -> 27.6 us  [loop_step(): return lax.ppermute(value, 'dp', pairs)]
    unnamed x317 -> x343, local copies, waits for them, and re-layouts: 28.5 us -> 22.2 us
  transfers between devices with their start and end apart: 66 -> 66, of which waited for: 24 -> 26; matrix products, arithmetic and copies ran while one was open for 34% -> 32% of each run, Pallas kernels for 18% -> 18%
where the time goes in v4:
time: 723 us; the launch traced here: 713 us
  waiting for transfers between devices  177 us (24%)
  matrix products  140 us (19%)
  Pallas kernels  138 us (19%)
  starting transfers between devices  89.3 us (12%)
  other arithmetic  86.8 us (12%)
  local copies, waits for them, and re-layouts  59.8 us (8%)
  between operations  22.5 us (3%)
    ppermute x24, waiting for transfers between devices, loop_step(): return lax.ppermute(value, 'dp', pairs)  89.5 us
    dot_general x21, matrix products, matmul(): return jnp.dot(a, b, preferred_element_type=f32)  70.5 us
    dot_general x21, matrix products, contract_last(): lax.dot_general(a, b, (((1,), (1,)), ((), ())), preferred_element_type=f32)  58.3 us
    pallas_call x4, Pallas kernels, attend_back(): pl.pallas_call(attend_back_body, out_shape=[jax.ShapeDtypeStruct((rows, w...  52.4 us
    ppermute x6, waiting for transfers between devices, to_encoder(): return lax.ppermute(value, 'slab', [(1, 0)])  40.7 us
    pallas_call x4, Pallas kernels, attend(): pl.pallas_call(attend_body, out_shape=[jax.ShapeDtypeStruct((rows, width)...  34.5 us
    ppermute x24, starting transfers between devices, loop_step(): return lax.ppermute(value, 'dp', pairs)  27.6 us
    pallas_call x3, Pallas kernels, row_products(): pl.pallas_call(body, out_shape=[jax.ShapeDtypeStruct((height, width), bf1...  27.3 us
  transfers between devices with their start and end apart: 66, of which 26 were waited for; matrix products, arithmetic and copies ran while one was open for 32% of the time, Pallas kernels for 18%

profile of v4, /device:TPU:0, one launch (start us, length us, event | category | flops | bytes accessed | tf_op | source)
XLA Modules:
  0.0 713.3 jit_solution(12182935482803287052)
XLA Ops:
  15.9 7.9 %collective-permute-done.3.refs_2_ = bf16[112,1536]{1,0:T(8,128)(2,1)S(1)} collective-permute-done((bf16[112,1536]{1,0:T(8,128)(2,1)S(1)}, bf16[112,1536]{1,0:T(8,128)(2,1)S(1)}, u32[]{:S(2)}, u32[]{:S(2)}) %collective-permute-start.3) | collective-permute-done | bytes 344096 | tf_op jit(solution)/shard_map/ppermute | solution.py:39
  26.6 6.1 all-to-all-start
  33.7 4.3 collective-permute-start.10
  40.3 4.4 all-to-all-done
  46.0 3.5 all-to-all-start.1
  53.6 5.5 assemble.2
  67.1 5.0 collective-permute-start.1
  92.0 4.9 collective-permute-start.20
  100.0 6.0 collective-permute-done.18.refs_4_
  113.9 13.0 %collective-permute-done.19.refs_6_ = bf16[96,4608]{1,0:T(8,128)(2,1)} collective-permute-done((bf16[96,4608]{1,0:T(8,128)(2,1)}, bf16[96,4608]{1,0:T(8,128)(2,1)}, u32[]{:S(2)}, u32[]{:S(2)}) %collective-permute-start.19) | collective-permute-done | bytes 884768 | tf_op jit(solution)/shard_map/ppermute | solution.py:39
  129.1 7.7 %assemble.3 = (bf16[1,8,96,2048]{3,2,1,0:T(8,128)(2,1)}, bf16[1,8,96,1024]{3,2,1,0:T(8,128)(2,1)}, bf16[2,8,48,384]{3,2,1,0:T(8,128)(2,1)}, bf16[2,8,48,768]{3,2,1,0:T(8,128)(2,1)}, bf16[2,8,48,384]{3,2,1,0:T(8,128)(2,1)}) custom-call(s32[7]{0:T(128)} %bitcast.432, bf16[96,4608]{1,0:T(8,128)(2,1)} %copy-done.27, ...), custom_call_target="tpu_custom_call" | custom-call | bytes 12386304 | tf_op jit(solution)/shard_map/assemble/pallas_call | solution.py:168
  137.2 4.4 convolution_convert_fusion.2.pair_ref
  146.6 8.6 %attend.4 = (bf16[512,384]{1,0:T(8,128)(2,1)}, f32[3,2,512]{2,1,0:T(2,128)}) custom-call(s32[2]{0:T(128)} %pad_add_fusion.start_ref, bf16[512,384]{1,0:T(8,128)(2,1)} %convolution_convert_fusion.11.query_ref, bf16[1024,768]{1,0:T(8,128)(2,1)} %convolution_convert_fusion.3.pair_ref, s32[1,512]{1,0:T(1,128)} %broadcast_select_fusion.2.limit_ref), custom_call_target="tpu_custom_call" | custom-call | flops 3145728 | bytes 12288 | tf_op jit(solution)/shard_map/attend/pallas_call | solution.py:357
  155.2 8.5 %attend.5 = (bf16[512,384]{1,0:T(8,128)(2,1)}, f32[3,2,512]{2,1,0:T(2,128)}) custom-call(s32[2]{0:T(128)} %pad_add_fusion.start_ref, bf16[512,384]{1,0:T(8,128)(2,1)} %convolution_convert_fusion.10.query_ref, bf16[1024,768]{1,0:T(8,128)(2,1)} %convolution_convert_fusion.2.pair_ref, s32[1,512]{1,0:T(1,128)} %broadcast_select_fusion.2.limit_ref), custom_call_target="tpu_custom_call" | custom-call | flops 3145728 | bytes 12288 | tf_op jit(solution)/shard_map/attend/pallas_call | solution.py:357
  170.8 8.2 %collective-permute-done.25 = bf16[48,4608]{1,0:T(8,128)(2,1)S(1)} collective-permute-done((bf16[48,4608]{1,0:T(8,128)(2,1)S(1)}, bf16[48,4608]{1,0:T(8,128)(2,1)S(1)}, u32[]{:S(2)}, u32[]{:S(2)}) %collective-permute-start.25) | collective-permute-done | bytes 442400 | tf_op jit(solution)/shard_map/ppermute | solution.py:39
  190.0 3.9 fusion.135
  198.0 3.2 fusion.136
  204.1 4.8 collective-permute-start.32
  208.9 16.7 %collective-permute-done.32 = bf16[512,768]{1,0:T(8,128)(2,1)S(1)} collective-permute-done((bf16[512,768]{1,0:T(8,128)(2,1)S(1)}, bf16[512,768]{1,0:T(8,128)(2,1)S(1)}, u32[]{:S(2)}, u32[]{:S(2)}) %collective-permute-start.32) | collective-permute-done | bytes 786464 | tf_op jit(solution)/shard_map/ppermute | solution.py:32
  229.4 4.4 convolution_convert_fusion.pair_ref
  234.3 8.5 %attend.7 = (bf16[512,384]{1,0:T(8,128)(2,1)}, f32[3,2,512]{2,1,0:T(2,128)}) custom-call(s32[2]{0:T(128)} %pad_add_fusion.start_ref, bf16[512,384]{1,0:T(8,128)(2,1)} %convolution_convert_fusion.8.query_ref, bf16[1024,768]{1,0:T(8,128)(2,1)} %convolution_convert_fusion.pair_ref, s32[1,512]{1,0:T(1,128)} %broadcast_in_dim.60.limit_ref), custom_call_target="tpu_custom_call" | custom-call | flops 3145728 | bytes 12288 | tf_op jit(solution)/shard_map/attend/pallas_call | solution.py:357
  242.8 4.0 convolution_convert_fusion.1.pair_ref
  246.8 8.9 %attend.6 = (bf16[512,384]{1,0:T(8,128)(2,1)}, f32[3,2,512]{2,1,0:T(2,128)}) custom-call(s32[2]{0:T(128)} %pad_add_fusion.start_ref, bf16[512,384]{1,0:T(8,128)(2,1)} %convolution_convert_fusion.9.query_ref, bf16[1024,768]{1,0:T(8,128)(2,1)} %convolution_convert_fusion.1.pair_ref, s32[1,512]{1,0:T(1,128)} %broadcast_in_dim.60.limit_ref), custom_call_target="tpu_custom_call" | custom-call | flops 3145728 | bytes 12288 | tf_op jit(solution)/shard_map/attend/pallas_call | solution.py:357
  258.8 4.4 fusion.139
  278.1 20.3 %collective-permute-done.34 = bf16[512,768]{1,0:T(8,128)(2,1)} collective-permute-done((bf16[512,768]{1,0:T(8,128)(2,1)}, bf16[512,768]{1,0:T(8,128)(2,1)}, u32[]{:S(2)}, u32[]{:S(2)}) %collective-permute-start.34) | collective-permute-done | bytes 786464 | tf_op jit(solution)/shard_map/ppermute | solution.py:28
  303.1 9.8 %multiply_reduce_fusion = (f32[1024]{0:T(1024)S(1)}, f32[1024,4096]{1,0:T(8,128)S(1)}) fusion(bf16[4096,768]{1,0:T(8,128)(2,1)} %all-gather.2.cloned.1.call-done, bf16[512,768]{1,0:T(8,128)(2,1)} %collective-permute-done.35, bf16[512,768]{1,0:T(8,128)(2,1)} %copy-done.86), kind=kOutput, calls=%fused_computation.9 | convolution fusion | flops 6453984256 | bytes 24645632 | tf_op jit(solution)/shard_map/dot_general | solution.py:241
  313.0 7.6 %exponential_reduce_fusion = (f32[1024]{0:T(1024)S(1)}, f32[1024]{0:T(1024)S(1)}) fusion(f32[1024,4096]{1,0:T(8,128)S(1)} %get-tuple-element.293, f32[1024]{0:T(1024)S(1)} %get-tuple-element.292, s32[1024]{0:T(1024)S(1)} %add_select_fusion.2, s32[4096]{0:T(1024)S(1)} %fusion.79), kind=kLoop, calls=%fused_computation.8 | loop fusion | flops 25163776 | bytes 16809984 | tf_op jit(solution)/shard_map/reduce_sum | solution.py:668
  323.2 3.1 collective-permute-done.37
  326.3 6.3 fusion.3
  332.6 10.7 %convolution_multiply_fusion = f32[1024,768]{1,0:T(8,128)S(1)} fusion(bf16[1024,4096]{1,0:T(8,128)(2,1)S(1)} %fusion.3, bf16[4096,768]{1,0:T(8,128)(2,1)} %all-gather.2.cloned.1.call-done), kind=kOutput, calls=%fused_computation.76 | convolution fusion | flops 6443237376 | bytes 17825792 | tf_op jit(solution)/shard_map/dot_general | solution.py:237
  350.2 11.1 %multiply_convert_fusion = bf16[4096,768]{1,0:T(8,128)(2,1)} fusion(bf16[1024,4096]{1,0:T(8,128)(2,1)} %copy-done.10, bf16[512,768]{1,0:T(8,128)(2,1)} %collective-permute-done.35, bf16[512,768]{1,0:T(8,128)(2,1)S(1)} %copy-done.87), kind=kOutput, calls=%fused_computation.10 | convolution fusion | flops 6451888128 | bytes 16252928 | tf_op jit(solution)/shard_map/dot_general | solution.py:245
  361.6 5.1 collective-permute-done.39
  366.7 3.1 multiply_reduce_fusion.2
  372.2 4.1 fusion.31
  376.4 4.5 fusion.24
  380.9 4.5 fusion.115
  388.1 3.1 fusion.120
  392.6 13.3 %attend_back.5 = (bf16[512,384]{1,0:T(8,128)(2,1)}, bf16[1024,768]{1,0:T(8,128)(2,1)}) custom-call(s32[2]{0:T(128)} %pad_add_fusion.start_ref, bf16[512,384]{1,0:T(8,128)(2,1)} %convolution_convert_fusion.8.query_ref, bf16[1024,768]{1,0:T(8,128)(2,1)} %convolution_convert_fusion.pair_ref, s32[1,512]{1,0:T(1,128)} %broadcast_in_dim.60.limit_ref, ...), custom_call_target="tpu_custom_call" | custom-call | flops 3145728 | bytes 12288 | tf_op jit(solution)/shard_map/attend_back/pallas_call | solution.py:381
  408.3 13.1 %attend_back.4 = (bf16[512,384]{1,0:T(8,128)(2,1)}, bf16[1024,768]{1,0:T(8,128)(2,1)}) custom-call(s32[2]{0:T(128)} %pad_add_fusion.start_ref, bf16[512,384]{1,0:T(8,128)(2,1)} %convolution_convert_fusion.9.query_ref, bf16[1024,768]{1,0:T(8,128)(2,1)} %convolution_convert_fusion.1.pair_ref, s32[1,512]{1,0:T(1,128)} %broadcast_in_dim.60.limit_ref, ...), custom_call_target="tpu_custom_call" | custom-call | flops 3145728 | bytes 12288 | tf_op jit(solution)/shard_map/attend_back/pallas_call | solution.py:381
  435.5 15.7 %collective-permute-done.41 = bf16[512,768]{1,0:T(8,128)(2,1)} collective-permute-done((bf16[512,768]{1,0:T(8,128)(2,1)}, bf16[512,768]{1,0:T(8,128)(2,1)}, u32[]{:S(2)}, u32[]{:S(2)}) %collective-permute-start.41) | collective-permute-done | bytes 786464 | tf_op jit(solution)/shard_map/ppermute | solution.py:28
  456.0 4.0 fusion.10
  463.7 4.0 fusion.17
  469.8 9.9 %conditional.1 = ((bf16[768,3072]{1,0:T(8,128)(2,1)}, bf16[768,3072]{1,0:T(8,128)(2,1)})) conditional(s32[]{:T(128)} %convert_element_type.429, (bf16[512,768]{1,0:T(8,128)(2,1)}, bf16[512,768]{1,0:T(8,128)(2,1)}, bf16[512,2048]{1,0:T(8,128)(2,1)}, bf16[512,1024]{1,0:T(8,128)(2,1)}, bf16[512,2048]{1,0:T(8,128)(2,1)}, ...), branch_computations={%region_15.16_spmd, %region_16.17_spmd} | conditional | flops 4831838208 | bytes 9437192 | solution.py:719
  469.8 9.8 %row_products.4 = (bf16[768,3072]{1,0:T(8,128)(2,1)}, bf16[768,3072]{1,0:T(8,128)(2,1)}) custom-call(bf16[512,768]{1,0:T(8,128)(2,1)} %get-tuple-element.24.refs_0_, bf16[512,768]{1,0:T(8,128)(2,1)} %get-tuple-element.25.refs_1_, bf16[512,2048]{1,0:T(8,128)(2,1)} %get-tuple-element.26.refs_2_, bf16[512,1024]{1,0:T(8,128)(2,1)} %get-tuple-element.27.refs_3_, ...), custom_call_target="tpu_custom_call" | custom-call | flops 4831838208 | bytes 9437184 | tf_op jit(solution)/shard_map/cond/branch_0_fun/row_products/pallas_call | solution.py:445
  479.8 8.6 %row_products.6 = (bf16[768,1536]{1,0:T(8,128)(2,1)}, bf16[768,1536]{1,0:T(8,128)(2,1)}) custom-call(bf16[512,768]{1,0:T(8,128)(2,1)} %get-tuple-element.238.refs_0_, bf16[1024,768]{1,0:T(8,128)(2,1)} %copy-done.97, bf16[512,768]{1,0:T(8,128)(2,1)} %copy-done.78, bf16[512,384]{1,0:T(8,128)(2,1)} %get-tuple-element.151.refs_3_, ...), custom_call_target="tpu_custom_call" | custom-call | flops 3623878656 | bytes 4718592 | tf_op jit(solution)/shard_map/row_products/pallas_call | solution.py:445
  499.5 4.3 add_convert_fusion
  503.9 3.3 maximum_maximum_fusion
  507.3 4.5 fusion.114
  511.9 3.5 multiply_reduce_fusion.3
  517.2 4.0 fusion.119
  522.5 13.1 %attend_back.7 = (bf16[512,384]{1,0:T(8,128)(2,1)}, bf16[1024,768]{1,0:T(8,128)(2,1)}) custom-call(s32[2]{0:T(128)} %pad_add_fusion.start_ref, bf16[512,384]{1,0:T(8,128)(2,1)} %convolution_convert_fusion.10.query_ref, bf16[1024,768]{1,0:T(8,128)(2,1)} %convolution_convert_fusion.2.pair_ref, s32[1,512]{1,0:T(1,128)} %broadcast_select_fusion.2.limit_ref, ...), custom_call_target="tpu_custom_call" | custom-call | flops 3145728 | bytes 12288 | tf_op jit(solution)/shard_map/attend_back/pallas_call | solution.py:381
  538.0 13.0 %attend_back.6 = (bf16[512,384]{1,0:T(8,128)(2,1)}, bf16[1024,768]{1,0:T(8,128)(2,1)}) custom-call(s32[2]{0:T(128)} %pad_add_fusion.start_ref, bf16[512,384]{1,0:T(8,128)(2,1)} %convolution_convert_fusion.11.query_ref, bf16[1024,768]{1,0:T(8,128)(2,1)} %convolution_convert_fusion.3.pair_ref, s32[1,512]{1,0:T(1,128)} %broadcast_select_fusion.2.limit_ref, ...), custom_call_target="tpu_custom_call" | custom-call | flops 3145728 | bytes 12288 | tf_op jit(solution)/shard_map/attend_back/pallas_call | solution.py:381
  551.0 3.4 fusion.144
  557.7 8.9 %row_products.7 = (bf16[768,1536]{1,0:T(8,128)(2,1)}, bf16[768,1536]{1,0:T(8,128)(2,1)}) custom-call(bf16[512,768]{1,0:T(8,128)(2,1)} %copy-done.34, bf16[1024,768]{1,0:T(8,128)(2,1)} %pad_maximum_fusion.4.refs_1_, bf16[512,768]{1,0:T(8,128)(2,1)} %copy-done.81, bf16[512,384]{1,0:T(8,128)(2,1)} %get-tuple-element.163.refs_3_, ...), custom_call_target="tpu_custom_call" | custom-call | flops 3623878656 | bytes 4718592 | tf_op jit(solution)/shard_map/row_products/pallas_call | solution.py:445
  583.6 6.6 collective-permute-done.48
  593.4 8.6 %collective-permute-done.49 = bf16[112,1536]{1,0:T(8,128)(2,1)S(1)} collective-permute-done((bf16[112,1536]{1,0:T(8,128)(2,1)S(1)}, bf16[112,1536]{1,0:T(8,128)(2,1)S(1)}, u32[]{:S(2)}, u32[]{:S(2)}) %collective-permute-start.49) | collective-permute-done | bytes 344096 | tf_op jit(solution)/shard_map/ppermute | solution.py:39
  606.2 18.2 %collective-permute-done.56 = bf16[112,1536]{1,0:T(8,128)(2,1)S(1)} collective-permute-done((bf16[112,1536]{1,0:T(8,128)(2,1)S(1)}, bf16[112,1536]{1,0:T(8,128)(2,1)S(1)}, u32[]{:S(2)}, u32[]{:S(2)}) %collective-permute-start.56) | collective-permute-done | bytes 344096 | tf_op jit(solution)/shard_map/ppermute | solution.py:39
  629.1 8.3 %all-to-all-start.2 = ((bf16[8,33,768]{2,1,0:T(8,128)(2,1)}), bf16[8,33,768]{2,1,0:T(8,128)(2,1)}, u32[]{:S(2)}, u32[]{:S(2)}) async-start(bf16[8,33,768]{2,1,0:T(8,128)(2,1)} %pad_maximum_fusion.8), calls=%async_computation.2 | async-start | bytes 983040 | tf_op jit(solution)/shard_map/all_to_all | solution.py:232
  638.0 15.6 %collective-permute-done.57 = bf16[112,1536]{1,0:T(8,128)(2,1)} collective-permute-done((bf16[112,1536]{1,0:T(8,128)(2,1)}, bf16[112,1536]{1,0:T(8,128)(2,1)}, u32[]{:S(2)}, u32[]{:S(2)}) %collective-permute-start.57) | collective-permute-done | bytes 344096 | tf_op jit(solution)/shard_map/ppermute | solution.py:39
  655.8 3.9 all-to-all-done.2
  662.2 4.1 all-to-all-start.3
  673.1 3.2 all-to-all-done.3
  677.3 4.7 collective-permute-start.51
  697.1 4.7 collective-permute-done.58
  (649 shorter events, 236.5 us)
Async XLA Ops:
  8.4 17.4 %collective-permute-start = (bf16[256,768]{1,0:T(8,128)(2,1)S(1)}, bf16[256,768]{1,0:T(8,128)(2,1)S(1)}, u32[]{:S(2)}, u32[]{:S(2)}) collective-permute-start(bf16[256,768]{1,0:T(8,128)(2,1)S(1)} %slice_bitcast_fusion.3), channel_id=1, source_target_pairs={{16,0},{17,1},{18,2},{19,3},{20,4},{21,5},{22,6},{23,7},{24,8},{25... | collective-permute-start | bytes 1179656 | tf_op jit(solution)/shard_map/ppermute | solution.py:28
  12.7 11.1 %collective-permute-start.3 = (bf16[112,1536]{1,0:T(8,128)(2,1)S(1)}, bf16[112,1536]{1,0:T(8,128)(2,1)S(1)}, u32[]{:S(2)}, u32[]{:S(2)}) collective-permute-start(bf16[112,1536]{1,0:T(8,128)(2,1)S(1)} %concatenate.225.refs_0_), channel_id=1, source_target_pairs={{0,2},{4,0},{8,4},{12,8},{14,12},{10,14},{6,10},{2,6},{1,3},{5,1},... | collective-permute-start | bytes 1032200 | tf_op jit(solution)/shard_map/ppermute | solution.py:39
  15.7 9.8 %collective-permute-start.2 = (bf16[112,1536]{1,0:T(8,128)(2,1)S(1)}, bf16[112,1536]{1,0:T(8,128)(2,1)S(1)}, u32[]{:S(2)}, u32[]{:S(2)}) collective-permute-start(bf16[112,1536]{1,0:T(8,128)(2,1)S(1)} %concatenate.225.refs_0_), channel_id=1, source_target_pairs={{0,4},{4,8},{8,12},{12,14},{14,10},{10,6},{6,2},{2,0},{1,5},{5,9},... | collective-permute-start | bytes 1032200 | tf_op jit(solution)/shard_map/ppermute | solution.py:39
  23.8 14.3 %collective-permute-start.5 = (bf16[112,1536]{1,0:T(8,128)(2,1)S(1)}, bf16[112,1536]{1,0:T(8,128)(2,1)}, u32[]{:S(2)}, u32[]{:S(2)}) collective-permute-start(bf16[112,1536]{1,0:T(8,128)(2,1)S(1)} %collective-permute-done.3.refs_2_), channel_id=1, source_target_pairs={{0,2},{4,0},{8,4},{12,8},{14,12},{10,14},{6,10},{2,6},{1,3},{5,1},... | collective-permute-start | bytes 1032200 | tf_op jit(solution)/shard_map/ppermute | solution.py:39
  25.5 14.7 %collective-permute-start.4 = (bf16[112,1536]{1,0:T(8,128)(2,1)S(1)}, bf16[112,1536]{1,0:T(8,128)(2,1)}, u32[]{:S(2)}, u32[]{:S(2)}) collective-permute-start(bf16[112,1536]{1,0:T(8,128)(2,1)S(1)} %collective-permute-done.2.refs_1_), channel_id=1, source_target_pairs={{0,4},{4,8},{8,12},{12,14},{14,10},{10,6},{6,2},{2,0},{1,5},{5,9},... | collective-permute-start | bytes 1032200 | tf_op jit(solution)/shard_map/ppermute | solution.py:39
  26.6 18.0 %all-to-all-start = ((bf16[8,32,768]{2,1,0:T(8,128)(2,1)}), bf16[8,32,768]{2,1,0:T(8,128)(2,1)S(1)}, u32[]{:S(2)}, u32[]{:S(2)}) async-start(bf16[8,32,768]{2,1,0:T(8,128)(2,1)} %bitcast.2), calls=%async_computation | async-start | bytes 786432 | tf_op jit(solution)/shard_map/all_to_all | solution.py:232
  33.7 26.6 %collective-permute-start.10 = (bf16[48,1536]{1,0:T(8,128)(2,1)}, bf16[48,1536]{1,0:T(8,128)(2,1)S(1)}, u32[]{:S(2)}, u32[]{:S(2)}) collective-permute-start(bf16[48,1536]{1,0:T(8,128)(2,1)} %pad_maximum_fusion.13), channel_id=1, source_target_pairs={{0,16},{1,17},{2,18},{3,19},{4,20},{5,21},{6,22},{7,23},{8,24},{9,... | collective-permute-start | bytes 442376 | tf_op jit(solution)/shard_map/ppermute | solution.py:32
  38.1 12.0 %collective-permute-start.7 = (bf16[112,1536]{1,0:T(8,128)(2,1)}, bf16[112,1536]{1,0:T(8,128)(2,1)S(1)}, u32[]{:S(2)}, u32[]{:S(2)}) collective-permute-start(bf16[112,1536]{1,0:T(8,128)(2,1)} %collective-permute-done.5.refs_4_), channel_id=1, source_target_pairs={{0,2},{4,0},{8,4},{12,8},{14,12},{10,14},{6,10},{2,6},{1,3},{5,1},... | collective-permute-start | bytes 1032200 | tf_op jit(solution)/shard_map/ppermute | solution.py:39
  40.2 12.6 %collective-permute-start.6 = (bf16[112,1536]{1,0:T(8,128)(2,1)}, bf16[112,1536]{1,0:T(8,128)(2,1)S(1)}, u32[]{:S(2)}, u32[]{:S(2)}) collective-permute-start(bf16[112,1536]{1,0:T(8,128)(2,1)} %collective-permute-done.4.refs_3_), channel_id=1, source_target_pairs={{0,4},{4,8},{8,12},{12,14},{14,10},{10,6},{6,2},{2,0},{1,5},{5,9},... | collective-permute-start | bytes 1032200 | tf_op jit(solution)/shard_map/ppermute | solution.py:39
  46.0 21.1 %all-to-all-start.1 = ((bf16[8,32,768]{2,1,0:T(8,128)(2,1)}), bf16[8,32,768]{2,1,0:T(8,128)(2,1)S(1)}, u32[]{:S(2)}, u32[]{:S(2)}) async-start(bf16[8,32,768]{2,1,0:T(8,128)(2,1)} %gather_fusion), calls=%async_computation.1 | async-start | bytes 786432 | tf_op jit(solution)/shard_map/all_to_all | solution.py:233
  49.5 253.6 %all-gather.2.cloned.1.call-start = ((), (), s32[]{:S(2)}) async-start(), calls=%async_computation.6 | async-start | bytes 7077888 | tf_op jit(solution)/shard_map/all_gather | solution.py:632
  50.8 11.8 %collective-permute-start.9 = (bf16[56,1536]{1,0:T(8,128)(2,1)}, bf16[56,1536]{1,0:T(8,128)(2,1)}, u32[]{:S(2)}, u32[]{:S(2)}) collective-permute-start(bf16[56,1536]{1,0:T(8,128)(2,1)} %slice.388), channel_id=1, source_target_pairs={{0,2},{4,0},{8,4},{12,8},{14,12},{10,14},{6,10},{2,6},{1,3},{5,1},... | collective-permute-start | bytes 516104 | tf_op jit(solution)/shard_map/ppermute | solution.py:39
  59.1 29.2 %collective-permute-start.14 = (bf16[1,8,96,768]{3,2,1,0:T(8,128)(2,1)}, bf16[1,8,96,768]{3,2,1,0:T(8,128)(2,1)}, u32[]{:S(2)}, u32[]{:S(2)}) collective-permute-start(bf16[1,8,96,768]{3,2,1,0:T(8,128)(2,1)} %get-tuple-element.114.refs_1_), channel_id=1, source_target_pairs={{0,1},{1,0},{2,3},{3,2},{4,5},{5,4},{6,7},{7,6},{8,9},{9,8},{10,11... | collective-permute-start | bytes 3538952 | tf_op jit(solution)/shard_map/ppermute | solution.py:20
  60.2 6.9 collective-permute-start.8
  62.1 18.4 %collective-permute-start.16 = (bf16[1,8,16,1536]{3,2,1,0:T(8,128)(2,1)S(1)}, bf16[1,8,16,1536]{3,2,1,0:T(8,128)(2,1)S(1)}, u32[]{:S(2)}, u32[]{:S(2)}) collective-permute-start(bf16[1,8,16,1536]{3,2,1,0:T(8,128)(2,1)S(1)} %copy-done.90), channel_id=1, source_target_pairs={{0,1},{1,0},{2,3},{3,2},{4,5},{5,4},{6,7},{7,6},{8,9},{9,8},{10,11... | collective-permute-start | bytes 1179656 | tf_op jit(solution)/shard_map/ppermute | solution.py:20
  62.6 21.9 %collective-permute-start.11 = (bf16[96,4608]{1,0:T(8,128)(2,1)S(1)}, bf16[96,4608]{1,0:T(8,128)(2,1)}, u32[]{:S(2)}, u32[]{:S(2)}) collective-permute-start(bf16[96,4608]{1,0:T(8,128)(2,1)S(1)} %maximum_maximum_fusion.1.refs_0_), channel_id=1, source_target_pairs={{0,2},{4,0},{8,4},{12,8},{14,12},{10,14},{6,10},{2,6},{1,3},{5,1},... | collective-permute-start | bytes 2654216 | tf_op jit(solution)/shard_map/ppermute | solution.py:39
  64.3 22.3 %collective-permute-start.21 = (bf16[96,4608]{1,0:T(8,128)(2,1)S(1)}, bf16[96,4608]{1,0:T(8,128)(2,1)}, u32[]{:S(2)}, u32[]{:S(2)}) collective-permute-start(bf16[96,4608]{1,0:T(8,128)(2,1)S(1)} %maximum_maximum_fusion.1.refs_0_), channel_id=1, source_target_pairs={{0,4},{4,8},{8,12},{12,14},{14,10},{10,6},{6,2},{2,0},{1,5},{5,9},... | collective-permute-start | bytes 2654216 | tf_op jit(solution)/shard_map/ppermute | solution.py:39
  67.1 13.5 %collective-permute-start.1 = (bf16[256,768]{1,0:T(8,128)(2,1)S(1)}, bf16[256,768]{1,0:T(8,128)(2,1)}, u32[]{:S(2)}, u32[]{:S(2)}) collective-permute-start(bf16[256,768]{1,0:T(8,128)(2,1)S(1)} %bitcast.374), channel_id=1, source_target_pairs={{0,16},{1,17},{2,18},{3,19},{4,20},{5,21},{6,22},{7,23},{8,24},{9,... | collective-permute-start | bytes 1179656 | tf_op jit(solution)/shard_map/ppermute | solution.py:32
  80.5 6.2 collective-permute-start.13
  80.6 6.2 collective-permute-start.15
  84.5 21.6 %collective-permute-start.18 = (bf16[96,4608]{1,0:T(8,128)(2,1)}, bf16[96,4608]{1,0:T(8,128)(2,1)}, u32[]{:S(2)}, u32[]{:S(2)}) collective-permute-start(bf16[96,4608]{1,0:T(8,128)(2,1)} %collective-permute-done.11.refs_2_), channel_id=1, source_target_pairs={{0,2},{4,0},{8,4},{12,8},{14,12},{10,14},{6,10},{2,6},{1,3},{5,1},... | collective-permute-start | bytes 2654216 | tf_op jit(solution)/shard_map/ppermute | solution.py:39
  86.6 21.8 %collective-permute-start.22 = (bf16[96,4608]{1,0:T(8,128)(2,1)}, bf16[96,4608]{1,0:T(8,128)(2,1)}, u32[]{:S(2)}, u32[]{:S(2)}) collective-permute-start(bf16[96,4608]{1,0:T(8,128)(2,1)} %collective-permute-done.21.refs_1_), channel_id=1, source_target_pairs={{0,4},{4,8},{8,12},{12,14},{14,10},{10,6},{6,2},{2,0},{1,5},{5,9},... | collective-permute-start | bytes 2654216 | tf_op jit(solution)/shard_map/ppermute | solution.py:39
  86.7 10.3 %collective-permute-start.17 = (bf16[112,1536]{1,0:T(8,128)(2,1)}, bf16[112,1536]{1,0:T(8,128)(2,1)S(1)}, u32[]{:S(2)}, u32[]{:S(2)}) collective-permute-start(bf16[112,1536]{1,0:T(8,128)(2,1)} %constant_dynamic-update-slice_fusion.refs_4_), channel_id=1, source_target_pairs={{0,1},{1,0},{2,3},{3,2},{4,5},{5,4},{6,7},{7,6},{8,9},{9,8},{10,11... | collective-permute-start | bytes 1032200 | tf_op jit(solution)/shard_map/ppermute | solution.py:20
  88.3 25.3 %collective-permute-start.12 = (bf16[512,768]{1,0:T(8,128)(2,1)S(1)}, bf16[512,768]{1,0:T(8,128)(2,1)S(1)}, u32[]{:S(2)}, u32[]{:S(2)}) collective-permute-start(bf16[512,768]{1,0:T(8,128)(2,1)S(1)} %get-tuple-element.208), channel_id=1, source_target_pairs={{0,1},{1,0},{2,3},{3,2},{4,5},{5,4},{6,7},{7,6},{8,9},{9,8},{10,11... | collective-permute-start | bytes 2359304 | tf_op jit(solution)/shard_map/ppermute | solution.py:20
  92.0 21.6 %collective-permute-start.20 = (f32[384]{0:T(512)S(1)}, f32[384]{0:T(512)S(1)}, u32[]{:S(2)}, u32[]{:S(2)}) collective-permute-start(f32[384]{0:T(512)S(1)} %reshape.965), channel_id=1, source_target_pairs={{0,16},{1,17},{2,18},{3,19},{4,20},{5,21},{6,22},{7,23},{8,24},{9,... | collective-permute-start | bytes 4616 | tf_op jit(solution)/shard_map/ppermute | solution.py:32
  106.1 20.8 %collective-permute-start.19 = (bf16[96,4608]{1,0:T(8,128)(2,1)}, bf16[96,4608]{1,0:T(8,128)(2,1)}, u32[]{:S(2)}, u32[]{:S(2)}) collective-permute-start(bf16[96,4608]{1,0:T(8,128)(2,1)} %collective-permute-done.18.refs_4_), channel_id=1, source_target_pairs={{0,2},{4,0},{8,4},{12,8},{14,12},{10,14},{6,10},{2,6},{1,3},{5,1},... | collective-permute-start | bytes 2654216 | tf_op jit(solution)/shard_map/ppermute | solution.py:39
  108.4 20.7 %collective-permute-start.23 = (bf16[96,4608]{1,0:T(8,128)(2,1)}, bf16[96,4608]{1,0:T(8,128)(2,1)}, u32[]{:S(2)}, u32[]{:S(2)}) collective-permute-start(bf16[96,4608]{1,0:T(8,128)(2,1)} %collective-permute-done.22.refs_3_), channel_id=1, source_target_pairs={{0,4},{4,8},{8,12},{12,14},{14,10},{10,6},{6,2},{2,0},{1,5},{5,9},... | collective-permute-start | bytes 2654216 | tf_op jit(solution)/shard_map/ppermute | solution.py:39
  136.8 47.6 %collective-permute-start.26 = (bf16[1,8,96,2048]{3,2,1,0:T(8,128)(2,1)}, bf16[1,8,96,2048]{3,2,1,0:T(8,128)(2,1)}, u32[]{:S(2)}, u32[]{:S(2)}) collective-permute-start(bf16[1,8,96,2048]{3,2,1,0:T(8,128)(2,1)} %get-tuple-element.130.refs_0_), channel_id=1, source_target_pairs={{0,1},{1,0},{2,3},{3,2},{4,5},{5,4},{6,7},{7,6},{8,9},{9,8},{10,11... | collective-permute-start | bytes 9437192 | tf_op jit(solution)/shard_map/ppermute | solution.py:20
  143.5 25.4 %collective-permute-start.24 = (bf16[48,4608]{1,0:T(8,128)(2,1)}, bf16[48,4608]{1,0:T(8,128)(2,1)}, u32[]{:S(2)}, u32[]{:S(2)}) collective-permute-start(bf16[48,4608]{1,0:T(8,128)(2,1)} %slice.392), channel_id=1, source_target_pairs={{0,4},{4,8},{8,12},{12,14},{14,10},{10,6},{6,2},{2,0},{1,5},{5,9},... | collective-permute-start | bytes 1327112 | tf_op jit(solution)/shard_map/ppermute | solution.py:39
  166.5 12.4 %collective-permute-start.25 = (bf16[48,4608]{1,0:T(8,128)(2,1)S(1)}, bf16[48,4608]{1,0:T(8,128)(2,1)S(1)}, u32[]{:S(2)}, u32[]{:S(2)}) collective-permute-start(bf16[48,4608]{1,0:T(8,128)(2,1)S(1)} %slice.393), channel_id=1, source_target_pairs={{0,2},{4,0},{8,4},{12,8},{14,12},{10,14},{6,10},{2,6},{1,3},{5,1},... | collective-permute-start | bytes 1327112 | tf_op jit(solution)/shard_map/ppermute | solution.py:39
  168.3 16.0 %collective-permute-start.27 = (bf16[1,8,96,1024]{3,2,1,0:T(8,128)(2,1)}, bf16[1,8,96,1024]{3,2,1,0:T(8,128)(2,1)}, u32[]{:S(2)}, u32[]{:S(2)}) collective-permute-start(bf16[1,8,96,1024]{3,2,1,0:T(8,128)(2,1)} %get-tuple-element.131.refs_1_), channel_id=1, source_target_pairs={{0,1},{1,0},{2,3},{3,2},{4,5},{5,4},{6,7},{7,6},{8,9},{9,8},{10,11... | collective-permute-start | bytes 4718600 | tf_op jit(solution)/shard_map/ppermute | solution.py:20
  168.3 13.1 %collective-permute-start.28 = (bf16[2,8,48,384]{3,2,1,0:T(8,128)(2,1)S(1)}, bf16[2,8,48,384]{3,2,1,0:T(8,128)(2,1)}, u32[]{:S(2)}, u32[]{:S(2)}) collective-permute-start(bf16[2,8,48,384]{3,2,1,0:T(8,128)(2,1)S(1)} %copy-done.43), channel_id=1, source_target_pairs={{0,1},{1,0},{2,3},{3,2},{4,5},{5,4},{6,7},{7,6},{8,9},{9,8},{10,11... | collective-permute-start | bytes 1769480 | tf_op jit(solution)/shard_map/ppermute | solution.py:20
  168.9 15.4 %collective-permute-start.29 = (bf16[2,8,48,768]{3,2,1,0:T(8,128)(2,1)S(1)}, bf16[2,8,48,768]{3,2,1,0:T(8,128)(2,1)}, u32[]{:S(2)}, u32[]{:S(2)}) collective-permute-start(bf16[2,8,48,768]{3,2,1,0:T(8,128)(2,1)S(1)} %copy-done.14), channel_id=1, source_target_pairs={{0,1},{1,0},{2,3},{3,2},{4,5},{5,4},{6,7},{7,6},{8,9},{9,8},{10,11... | collective-permute-start | bytes 3538952 | tf_op jit(solution)/shard_map/ppermute | solution.py:20
  179.7 7.4 %collective-permute-start.31 = (bf16[96,4608]{1,0:T(8,128)(2,1)}, bf16[96,4608]{1,0:T(8,128)(2,1)}, u32[]{:S(2)}, u32[]{:S(2)}) collective-permute-start(bf16[96,4608]{1,0:T(8,128)(2,1)} %constant_dynamic-update-slice_fusion.2.refs_5_), channel_id=1, source_target_pairs={{0,1},{1,0},{2,3},{3,2},{4,5},{5,4},{6,7},{7,6},{8,9},{9,8},{10,11... | collective-permute-start | bytes 2654216 | tf_op jit(solution)/shard_map/ppermute | solution.py:20
  181.4 2.9 collective-permute-start.30
  183.7 506.6 %reduce-scatter.5.cloned.1.call-start = ((), (), s32[]{:S(2)}) async-start(), calls=%async_computation.8 | async-start | bytes 7077888 | tf_op jit(solution)/shard_map/reduce_scatter | solution.py:685
  204.1 21.4 %collective-permute-start.32 = (bf16[512,768]{1,0:T(8,128)(2,1)S(1)}, bf16[512,768]{1,0:T(8,128)(2,1)S(1)}, u32[]{:S(2)}, u32[]{:S(2)}) collective-permute-start(bf16[512,768]{1,0:T(8,128)(2,1)S(1)} %multiply_convert_fusion.11), channel_id=1, source_target_pairs={{0,16},{1,17},{2,18},{3,19},{4,20},{5,21},{6,22},{7,23},{8,24},{9,... | collective-permute-start | bytes 2359304 | tf_op jit(solution)/shard_map/ppermute | solution.py:32
  225.5 3.8 collective-permute-start.33
  276.0 22.4 %collective-permute-start.34 = (bf16[512,768]{1,0:T(8,128)(2,1)}, bf16[512,768]{1,0:T(8,128)(2,1)}, u32[]{:S(2)}, u32[]{:S(2)}) collective-permute-start(bf16[512,768]{1,0:T(8,128)(2,1)} %multiply_convert_fusion.9), channel_id=1, source_target_pairs={{16,0},{17,1},{18,2},{19,3},{20,4},{21,5},{22,6},{23,7},{24,8},{25... | collective-permute-start | bytes 2359304 | tf_op jit(solution)/shard_map/ppermute | solution.py:28
  300.7 2.4 collective-permute-start.35
  322.5 3.8 collective-permute-start.37
  343.4 2.4 collective-permute-start.38
  347.4 19.3 %collective-permute-start.39 = (bf16[512,768]{1,0:T(8,128)(2,1)}, bf16[512,768]{1,0:T(8,128)(2,1)}, u32[]{:S(2)}, u32[]{:S(2)}) collective-permute-start(bf16[512,768]{1,0:T(8,128)(2,1)} %get-tuple-element.197), channel_id=1, source_target_pairs={{0,16},{1,17},{2,18},{3,19},{4,20},{5,21},{6,22},{7,23},{8,24},{9,... | collective-permute-start | bytes 2359304 | tf_op jit(solution)/shard_map/ppermute | solution.py:32
  361.4 331.3 %reduce-scatter.3.cloned.1.call-start = ((), (), s32[]{:S(2)}) async-start(), calls=%async_computation.7 | async-start | bytes 7962624 | tf_op jit(solution)/shard_map/reduce_scatter | solution.py:732
  425.8 2.4 collective-permute-start.40
  429.3 21.9 %collective-permute-start.41 = (bf16[512,768]{1,0:T(8,128)(2,1)}, bf16[512,768]{1,0:T(8,128)(2,1)}, u32[]{:S(2)}, u32[]{:S(2)}) collective-permute-start(bf16[512,768]{1,0:T(8,128)(2,1)} %slice_add_fusion.1), channel_id=1, source_target_pairs={{16,0},{17,1},{18,2},{19,3},{20,4},{21,5},{22,6},{23,7},{24,8},{25... | collective-permute-start | bytes 2359304 | tf_op jit(solution)/shard_map/ppermute | solution.py:28
  479.7 19.6 %collective-permute-start.42 = (bf16[768,3072]{1,0:T(8,128)(2,1)}, bf16[768,3072]{1,0:T(8,128)(2,1)}, u32[]{:S(2)}, u32[]{:S(2)}) collective-permute-start(bf16[768,3072]{1,0:T(8,128)(2,1)} %get-tuple-element.158), channel_id=1, source_target_pairs={{0,1},{1,0},{2,3},{3,2},{4,5},{5,4},{6,7},{7,6},{8,9},{9,8},{10,11... | collective-permute-start | bytes 14155784 | tf_op jit(solution)/shard_map/ppermute | solution.py:20
  488.4 8.2 %collective-permute-start.43 = (bf16[768,1536]{1,0:T(8,128)(2,1)}, bf16[768,1536]{1,0:T(8,128)(2,1)}, u32[]{:S(2)}, u32[]{:S(2)}) collective-permute-start(bf16[768,1536]{1,0:T(8,128)(2,1)} %get-tuple-element.161), channel_id=1, source_target_pairs={{0,1},{1,0},{2,3},{3,2},{4,5},{5,4},{6,7},{7,6},{8,9},{9,8},{10,11... | collective-permute-start | bytes 7077896 | tf_op jit(solution)/shard_map/ppermute | solution.py:20
  515.4 51.7 %collective-permute-start.45 = (bf16[384]{0:T(512)(128)(2,1)S(1)}, bf16[384]{0:T(512)(128)(2,1)S(1)}, u32[]{:S(2)}, u32[]{:S(2)}) collective-permute-start(bf16[384]{0:T(512)(128)(2,1)S(1)} %slice.347), channel_id=1, source_target_pairs={{16,0},{17,1},{18,2},{19,3},{20,4},{21,5},{22,6},{23,7},{24,8},{25... | collective-permute-start | bytes 2312 | tf_op jit(solution)/shard_map/ppermute | solution.py:28
  557.5 12.8 %collective-permute-start.44 = (bf16[512,768]{1,0:T(8,128)(2,1)S(1)}, bf16[512,768]{1,0:T(8,128)(2,1)}, u32[]{:S(2)}, u32[]{:S(2)}) collective-permute-start(bf16[512,768]{1,0:T(8,128)(2,1)S(1)} %slice.561), channel_id=1, source_target_pairs={{0,1},{1,0},{2,3},{3,2},{4,5},{5,4},{6,7},{7,6},{8,9},{9,8},{10,11... | collective-permute-start | bytes 2359304 | tf_op jit(solution)/shard_map/ppermute | solution.py:20
  566.6 11.8 %collective-permute-start.46 = (bf16[768,1536]{1,0:T(8,128)(2,1)}, bf16[768,1536]{1,0:T(8,128)(2,1)}, u32[]{:S(2)}, u32[]{:S(2)}) collective-permute-start(bf16[768,1536]{1,0:T(8,128)(2,1)} %get-tuple-element.169), channel_id=1, source_target_pairs={{0,1},{1,0},{2,3},{3,2},{4,5},{5,4},{6,7},{7,6},{8,9},{9,8},{10,11... | collective-permute-start | bytes 7077896 | tf_op jit(solution)/shard_map/ppermute | solution.py:20
  581.2 9.0 %collective-permute-start.48 = (bf16[56,1536]{1,0:T(8,128)(2,1)S(1)}, bf16[56,1536]{1,0:T(8,128)(2,1)S(1)}, u32[]{:S(2)}, u32[]{:S(2)}) collective-permute-start(bf16[56,1536]{1,0:T(8,128)(2,1)S(1)} %get-tuple-element.264), channel_id=1, source_target_pairs={{0,2},{4,0},{8,4},{12,8},{14,12},{10,14},{6,10},{2,6},{1,3},{5,1},... | collective-permute-start | bytes 516104 | tf_op jit(solution)/shard_map/ppermute | solution.py:39
  582.6 10.6 %collective-permute-start.52 = (bf16[56,1536]{1,0:T(8,128)(2,1)S(1)}, bf16[56,1536]{1,0:T(8,128)(2,1)S(1)}, u32[]{:S(2)}, u32[]{:S(2)}) collective-permute-start(bf16[56,1536]{1,0:T(8,128)(2,1)S(1)} %get-tuple-element.263), channel_id=1, source_target_pairs={{0,4},{4,8},{8,12},{12,14},{14,10},{10,6},{6,2},{2,0},{1,5},{5,9},... | collective-permute-start | bytes 516104 | tf_op jit(solution)/shard_map/ppermute | solution.py:39
  590.2 11.7 %collective-permute-start.49 = (bf16[112,1536]{1,0:T(8,128)(2,1)S(1)}, bf16[112,1536]{1,0:T(8,128)(2,1)S(1)}, u32[]{:S(2)}, u32[]{:S(2)}) collective-permute-start(bf16[112,1536]{1,0:T(8,128)(2,1)S(1)} %pad_maximum_fusion.9), channel_id=1, source_target_pairs={{0,2},{4,0},{8,4},{12,8},{14,12},{10,14},{6,10},{2,6},{1,3},{5,1},... | collective-permute-start | bytes 1032200 | tf_op jit(solution)/shard_map/ppermute | solution.py:39
  593.3 12.7 %collective-permute-start.53 = (bf16[112,1536]{1,0:T(8,128)(2,1)S(1)}, bf16[112,1536]{1,0:T(8,128)(2,1)S(1)}, u32[]{:S(2)}, u32[]{:S(2)}) collective-permute-start(bf16[112,1536]{1,0:T(8,128)(2,1)S(1)} %pad_maximum_fusion.10), channel_id=1, source_target_pairs={{0,4},{4,8},{8,12},{12,14},{14,10},{10,6},{6,2},{2,0},{1,5},{5,9},... | collective-permute-start | bytes 1032200 | tf_op jit(solution)/shard_map/ppermute | solution.py:39
  602.0 26.2 %collective-permute-start.50 = (bf16[256,768]{1,0:T(8,128)(2,1)S(1)}, bf16[256,768]{1,0:T(8,128)(2,1)S(1)}, u32[]{:S(2)}, u32[]{:S(2)}) collective-permute-start(bf16[256,768]{1,0:T(8,128)(2,1)S(1)} %slice.352), channel_id=1, source_target_pairs={{16,0},{17,1},{18,2},{19,3},{20,4},{21,5},{22,6},{23,7},{24,8},{25... | collective-permute-start | bytes 1179656 | tf_op jit(solution)/shard_map/ppermute | solution.py:28
  603.4 21.0 %collective-permute-start.56 = (bf16[112,1536]{1,0:T(8,128)(2,1)S(1)}, bf16[112,1536]{1,0:T(8,128)(2,1)S(1)}, u32[]{:S(2)}, u32[]{:S(2)}) collective-permute-start(bf16[112,1536]{1,0:T(8,128)(2,1)S(1)} %add_convert_fusion.3), channel_id=1, source_target_pairs={{0,2},{4,0},{8,4},{12,8},{14,12},{10,14},{6,10},{2,6},{1,3},{5,1},... | collective-permute-start | bytes 1032200 | tf_op jit(solution)/shard_map/ppermute | solution.py:39
  606.1 19.2 %collective-permute-start.54 = (bf16[112,1536]{1,0:T(8,128)(2,1)S(1)}, bf16[112,1536]{1,0:T(8,128)(2,1)S(1)}, u32[]{:S(2)}, u32[]{:S(2)}) collective-permute-start(bf16[112,1536]{1,0:T(8,128)(2,1)S(1)} %add_convert_fusion.5), channel_id=1, source_target_pairs={{0,4},{4,8},{8,12},{12,14},{14,10},{10,6},{6,2},{2,0},{1,5},{5,9},... | collective-permute-start | bytes 1032200 | tf_op jit(solution)/shard_map/ppermute | solution.py:39
  625.3 28.3 %collective-permute-start.57 = (bf16[112,1536]{1,0:T(8,128)(2,1)}, bf16[112,1536]{1,0:T(8,128)(2,1)}, u32[]{:S(2)}, u32[]{:S(2)}) collective-permute-start(bf16[112,1536]{1,0:T(8,128)(2,1)} %add_convert_fusion.2), channel_id=1, source_target_pairs={{0,2},{4,0},{8,4},{12,8},{14,12},{10,14},{6,10},{2,6},{1,3},{5,1},... | collective-permute-start | bytes 1032200 | tf_op jit(solution)/shard_map/ppermute | solution.py:39
  626.2 27.4 %collective-permute-start.55 = (bf16[112,1536]{1,0:T(8,128)(2,1)}, bf16[112,1536]{1,0:T(8,128)(2,1)}, u32[]{:S(2)}, u32[]{:S(2)}) collective-permute-start(bf16[112,1536]{1,0:T(8,128)(2,1)} %add_convert_fusion.4), channel_id=1, source_target_pairs={{0,4},{4,8},{8,12},{12,14},{14,10},{10,6},{6,2},{2,0},{1,5},{5,9},... | collective-permute-start | bytes 1032200 | tf_op jit(solution)/shard_map/ppermute | solution.py:39
  629.1 30.7 %all-to-all-start.2 = ((bf16[8,33,768]{2,1,0:T(8,128)(2,1)}), bf16[8,33,768]{2,1,0:T(8,128)(2,1)}, u32[]{:S(2)}, u32[]{:S(2)}) async-start(bf16[8,33,768]{2,1,0:T(8,128)(2,1)} %pad_maximum_fusion.8), calls=%async_computation.2 | async-start | bytes 983040 | tf_op jit(solution)/shard_map/all_to_all | solution.py:232
  662.2 14.1 %all-to-all-start.3 = ((bf16[8,33,768]{2,1,0:T(8,128)(2,1)}), bf16[8,33,768]{2,1,0:T(8,128)(2,1)}, u32[]{:S(2)}, u32[]{:S(2)}) async-start(bf16[8,33,768]{2,1,0:T(8,128)(2,1)} %gather_fusion.1), calls=%async_computation.3 | async-start | bytes 983040 | tf_op jit(solution)/shard_map/all_to_all | solution.py:233
  677.3 10.0 %collective-permute-start.51 = (bf16[256,768]{1,0:T(8,128)(2,1)S(1)}, bf16[256,768]{1,0:T(8,128)(2,1)S(1)}, u32[]{:S(2)}, u32[]{:S(2)}) collective-permute-start(bf16[256,768]{1,0:T(8,128)(2,1)S(1)} %bitcast.371), channel_id=1, source_target_pairs={{0,16},{1,17},{2,18},{3,19},{4,20},{5,21},{6,22},{7,23},{8,24},{9,... | collective-permute-start | bytes 1179656 | tf_op jit(solution)/shard_map/ppermute | solution.py:32
  694.8 7.0 collective-permute-start.58
  (162 other events, 1478.5 us)
Sparse Core Ops, SparseCore 0:
  183.8 100.0 all-gather.1
  361.5 117.2 reduce-scatter.4
  507.3 150.8 reduce-scatter.2

commit v5 on v4

--- a/solution.py
+++ b/solution.py
@@ -427,7 +427,7 @@
 
 
 def row_products(lefts, rights):
-    tile = 256
+    tile = 384
     flat = [right for group in rights for _, right in group]
     widths = [sum(right.shape[1] for _, right in group) for group in rights]
     height = lefts[0].shape[1]

time: 723 us -> 723 us (level)
  no operation moved by 1% of the time
where the time goes in v5:
time: 723 us; the launch traced here: 713 us
  waiting for transfers between devices  177 us (24%)
  matrix products  140 us (19%)
  Pallas kernels  138 us (19%)
  starting transfers between devices  89.4 us (12%)
  other arithmetic  86.8 us (12%)
  local copies, waits for them, and re-layouts  59.8 us (8%)
  between operations  22.4 us (3%)
    ppermute x24, waiting for transfers between devices, loop_step(): return lax.ppermute(value, 'dp', pairs)  89.4 us
    dot_general x21, matrix products, matmul(): return jnp.dot(a, b, preferred_element_type=f32)  70.5 us
    dot_general x21, matrix products, contract_last(): lax.dot_general(a, b, (((1,), (1,)), ((), ())), preferred_element_type=f32)  58.3 us
    pallas_call x4, Pallas kernels, attend_back(): pl.pallas_call(attend_back_body, out_shape=[jax.ShapeDtypeStruct((rows, w...  52.4 us
    ppermute x6, waiting for transfers between devices, to_encoder(): return lax.ppermute(value, 'slab', [(1, 0)])  40.7 us
    pallas_call x4, Pallas kernels, attend(): pl.pallas_call(attend_body, out_shape=[jax.ShapeDtypeStruct((rows, width)...  34.5 us
    ppermute x24, starting transfers between devices, loop_step(): return lax.ppermute(value, 'dp', pairs)  27.6 us
    pallas_call x3, Pallas kernels, row_products(): pl.pallas_call(body, out_shape=[jax.ShapeDtypeStruct((height, width), bf1...  27.4 us
  transfers between devices with their start and end apart: 66, of which 26 were waited for; matrix products, arithmetic and copies ran while one was open for 32% of the time, Pallas kernels for 18%

profile of v5, /device:TPU:0, one launch (start us, length us, event | category | flops | bytes accessed | tf_op | source)
XLA Modules:
  0.0 713.5 jit_solution(2902063817321096422)
XLA Ops:
  15.9 7.9 %collective-permute-done.3.refs_2_ = bf16[112,1536]{1,0:T(8,128)(2,1)S(1)} collective-permute-done((bf16[112,1536]{1,0:T(8,128)(2,1)S(1)}, bf16[112,1536]{1,0:T(8,128)(2,1)S(1)}, u32[]{:S(2)}, u32[]{:S(2)}) %collective-permute-start.3) | collective-permute-done | bytes 344096 | tf_op jit(solution)/shard_map/ppermute | solution.py:39
  26.6 6.1 all-to-all-start
  33.7 4.3 collective-permute-start.10
  40.3 4.4 all-to-all-done
  46.0 3.5 all-to-all-start.1
  53.6 5.5 assemble.2
  67.1 5.0 collective-permute-start.1
  92.0 4.9 collective-permute-start.20
  100.0 6.0 collective-permute-done.18.refs_4_
  113.9 13.0 %collective-permute-done.19.refs_6_ = bf16[96,4608]{1,0:T(8,128)(2,1)} collective-permute-done((bf16[96,4608]{1,0:T(8,128)(2,1)}, bf16[96,4608]{1,0:T(8,128)(2,1)}, u32[]{:S(2)}, u32[]{:S(2)}) %collective-permute-start.19) | collective-permute-done | bytes 884768 | tf_op jit(solution)/shard_map/ppermute | solution.py:39
  129.1 7.7 %assemble.3 = (bf16[1,8,96,2048]{3,2,1,0:T(8,128)(2,1)}, bf16[1,8,96,1024]{3,2,1,0:T(8,128)(2,1)}, bf16[2,8,48,384]{3,2,1,0:T(8,128)(2,1)}, bf16[2,8,48,768]{3,2,1,0:T(8,128)(2,1)}, bf16[2,8,48,384]{3,2,1,0:T(8,128)(2,1)}) custom-call(s32[7]{0:T(128)} %bitcast.432, bf16[96,4608]{1,0:T(8,128)(2,1)} %copy-done.27, ...), custom_call_target="tpu_custom_call" | custom-call | bytes 12386304 | tf_op jit(solution)/shard_map/assemble/pallas_call | solution.py:168
  137.2 4.4 convolution_convert_fusion.2.pair_ref
  146.6 8.6 %attend.4 = (bf16[512,384]{1,0:T(8,128)(2,1)}, f32[3,2,512]{2,1,0:T(2,128)}) custom-call(s32[2]{0:T(128)} %pad_add_fusion.start_ref, bf16[512,384]{1,0:T(8,128)(2,1)} %convolution_convert_fusion.11.query_ref, bf16[1024,768]{1,0:T(8,128)(2,1)} %convolution_convert_fusion.3.pair_ref, s32[1,512]{1,0:T(1,128)} %broadcast_select_fusion.2.limit_ref), custom_call_target="tpu_custom_call" | custom-call | flops 3145728 | bytes 12288 | tf_op jit(solution)/shard_map/attend/pallas_call | solution.py:357
  155.2 8.5 %attend.5 = (bf16[512,384]{1,0:T(8,128)(2,1)}, f32[3,2,512]{2,1,0:T(2,128)}) custom-call(s32[2]{0:T(128)} %pad_add_fusion.start_ref, bf16[512,384]{1,0:T(8,128)(2,1)} %convolution_convert_fusion.10.query_ref, bf16[1024,768]{1,0:T(8,128)(2,1)} %convolution_convert_fusion.2.pair_ref, s32[1,512]{1,0:T(1,128)} %broadcast_select_fusion.2.limit_ref), custom_call_target="tpu_custom_call" | custom-call | flops 3145728 | bytes 12288 | tf_op jit(solution)/shard_map/attend/pallas_call | solution.py:357
  170.8 8.2 %collective-permute-done.25 = bf16[48,4608]{1,0:T(8,128)(2,1)S(1)} collective-permute-done((bf16[48,4608]{1,0:T(8,128)(2,1)S(1)}, bf16[48,4608]{1,0:T(8,128)(2,1)S(1)}, u32[]{:S(2)}, u32[]{:S(2)}) %collective-permute-start.25) | collective-permute-done | bytes 442400 | tf_op jit(solution)/shard_map/ppermute | solution.py:39
  190.0 3.9 fusion.135
  198.0 3.2 fusion.136
  204.1 4.8 collective-permute-start.32
  208.9 16.7 %collective-permute-done.32 = bf16[512,768]{1,0:T(8,128)(2,1)S(1)} collective-permute-done((bf16[512,768]{1,0:T(8,128)(2,1)S(1)}, bf16[512,768]{1,0:T(8,128)(2,1)S(1)}, u32[]{:S(2)}, u32[]{:S(2)}) %collective-permute-start.32) | collective-permute-done | bytes 786464 | tf_op jit(solution)/shard_map/ppermute | solution.py:32
  229.4 4.4 convolution_convert_fusion.pair_ref
  234.3 8.5 %attend.7 = (bf16[512,384]{1,0:T(8,128)(2,1)}, f32[3,2,512]{2,1,0:T(2,128)}) custom-call(s32[2]{0:T(128)} %pad_add_fusion.start_ref, bf16[512,384]{1,0:T(8,128)(2,1)} %convolution_convert_fusion.8.query_ref, bf16[1024,768]{1,0:T(8,128)(2,1)} %convolution_convert_fusion.pair_ref, s32[1,512]{1,0:T(1,128)} %broadcast_in_dim.60.limit_ref), custom_call_target="tpu_custom_call" | custom-call | flops 3145728 | bytes 12288 | tf_op jit(solution)/shard_map/attend/pallas_call | solution.py:357
  242.8 4.0 convolution_convert_fusion.1.pair_ref
  246.8 8.9 %attend.6 = (bf16[512,384]{1,0:T(8,128)(2,1)}, f32[3,2,512]{2,1,0:T(2,128)}) custom-call(s32[2]{0:T(128)} %pad_add_fusion.start_ref, bf16[512,384]{1,0:T(8,128)(2,1)} %convolution_convert_fusion.9.query_ref, bf16[1024,768]{1,0:T(8,128)(2,1)} %convolution_convert_fusion.1.pair_ref, s32[1,512]{1,0:T(1,128)} %broadcast_in_dim.60.limit_ref), custom_call_target="tpu_custom_call" | custom-call | flops 3145728 | bytes 12288 | tf_op jit(solution)/shard_map/attend/pallas_call | solution.py:357
  258.8 4.4 fusion.139
  278.1 20.3 %collective-permute-done.34 = bf16[512,768]{1,0:T(8,128)(2,1)} collective-permute-done((bf16[512,768]{1,0:T(8,128)(2,1)}, bf16[512,768]{1,0:T(8,128)(2,1)}, u32[]{:S(2)}, u32[]{:S(2)}) %collective-permute-start.34) | collective-permute-done | bytes 786464 | tf_op jit(solution)/shard_map/ppermute | solution.py:28
  303.1 9.8 %multiply_reduce_fusion = (f32[1024]{0:T(1024)S(1)}, f32[1024,4096]{1,0:T(8,128)S(1)}) fusion(bf16[4096,768]{1,0:T(8,128)(2,1)} %all-gather.2.cloned.1.call-done, bf16[512,768]{1,0:T(8,128)(2,1)} %collective-permute-done.35, bf16[512,768]{1,0:T(8,128)(2,1)} %copy-done.86), kind=kOutput, calls=%fused_computation.9 | convolution fusion | flops 6453984256 | bytes 24645632 | tf_op jit(solution)/shard_map/dot_general | solution.py:241
  313.0 7.6 %exponential_reduce_fusion = (f32[1024]{0:T(1024)S(1)}, f32[1024]{0:T(1024)S(1)}) fusion(f32[1024,4096]{1,0:T(8,128)S(1)} %get-tuple-element.293, f32[1024]{0:T(1024)S(1)} %get-tuple-element.292, s32[1024]{0:T(1024)S(1)} %add_select_fusion.2, s32[4096]{0:T(1024)S(1)} %fusion.79), kind=kLoop, calls=%fused_computation.8 | loop fusion | flops 25163776 | bytes 16809984 | tf_op jit(solution)/shard_map/reduce_sum | solution.py:668
  323.2 3.1 collective-permute-done.37
  326.3 6.3 fusion.3
  332.6 10.7 %convolution_multiply_fusion = f32[1024,768]{1,0:T(8,128)S(1)} fusion(bf16[1024,4096]{1,0:T(8,128)(2,1)S(1)} %fusion.3, bf16[4096,768]{1,0:T(8,128)(2,1)} %all-gather.2.cloned.1.call-done), kind=kOutput, calls=%fused_computation.76 | convolution fusion | flops 6443237376 | bytes 17825792 | tf_op jit(solution)/shard_map/dot_general | solution.py:237
  350.2 11.1 %multiply_convert_fusion = bf16[4096,768]{1,0:T(8,128)(2,1)} fusion(bf16[1024,4096]{1,0:T(8,128)(2,1)} %copy-done.10, bf16[512,768]{1,0:T(8,128)(2,1)} %collective-permute-done.35, bf16[512,768]{1,0:T(8,128)(2,1)S(1)} %copy-done.87), kind=kOutput, calls=%fused_computation.10 | convolution fusion | flops 6451888128 | bytes 16252928 | tf_op jit(solution)/shard_map/dot_general | solution.py:245
  361.6 5.1 collective-permute-done.39
  366.7 3.1 multiply_reduce_fusion.2
  372.2 4.1 fusion.31
  376.4 4.5 fusion.24
  380.9 4.5 fusion.115
  388.1 3.1 fusion.120
  392.6 13.3 %attend_back.5 = (bf16[512,384]{1,0:T(8,128)(2,1)}, bf16[1024,768]{1,0:T(8,128)(2,1)}) custom-call(s32[2]{0:T(128)} %pad_add_fusion.start_ref, bf16[512,384]{1,0:T(8,128)(2,1)} %convolution_convert_fusion.8.query_ref, bf16[1024,768]{1,0:T(8,128)(2,1)} %convolution_convert_fusion.pair_ref, s32[1,512]{1,0:T(1,128)} %broadcast_in_dim.60.limit_ref, ...), custom_call_target="tpu_custom_call" | custom-call | flops 3145728 | bytes 12288 | tf_op jit(solution)/shard_map/attend_back/pallas_call | solution.py:381
  408.3 13.1 %attend_back.4 = (bf16[512,384]{1,0:T(8,128)(2,1)}, bf16[1024,768]{1,0:T(8,128)(2,1)}) custom-call(s32[2]{0:T(128)} %pad_add_fusion.start_ref, bf16[512,384]{1,0:T(8,128)(2,1)} %convolution_convert_fusion.9.query_ref, bf16[1024,768]{1,0:T(8,128)(2,1)} %convolution_convert_fusion.1.pair_ref, s32[1,512]{1,0:T(1,128)} %broadcast_in_dim.60.limit_ref, ...), custom_call_target="tpu_custom_call" | custom-call | flops 3145728 | bytes 12288 | tf_op jit(solution)/shard_map/attend_back/pallas_call | solution.py:381
  435.5 15.7 %collective-permute-done.41 = bf16[512,768]{1,0:T(8,128)(2,1)} collective-permute-done((bf16[512,768]{1,0:T(8,128)(2,1)}, bf16[512,768]{1,0:T(8,128)(2,1)}, u32[]{:S(2)}, u32[]{:S(2)}) %collective-permute-start.41) | collective-permute-done | bytes 786464 | tf_op jit(solution)/shard_map/ppermute | solution.py:28
  456.0 4.0 fusion.10
  463.7 4.0 fusion.17
  469.8 10.0 %conditional.1 = ((bf16[768,3072]{1,0:T(8,128)(2,1)}, bf16[768,3072]{1,0:T(8,128)(2,1)})) conditional(s32[]{:T(128)} %convert_element_type.429, (bf16[512,768]{1,0:T(8,128)(2,1)}, bf16[512,768]{1,0:T(8,128)(2,1)}, bf16[512,2048]{1,0:T(8,128)(2,1)}, bf16[512,1024]{1,0:T(8,128)(2,1)}, bf16[512,2048]{1,0:T(8,128)(2,1)}, ...), branch_computations={%region_15.16_spmd, %region_16.17_spmd} | conditional | flops 4831838208 | bytes 9437192 | solution.py:719
  469.8 9.9 %row_products.4 = (bf16[768,3072]{1,0:T(8,128)(2,1)}, bf16[768,3072]{1,0:T(8,128)(2,1)}) custom-call(bf16[512,768]{1,0:T(8,128)(2,1)} %get-tuple-element.24.refs_0_, bf16[512,768]{1,0:T(8,128)(2,1)} %get-tuple-element.25.refs_1_, bf16[512,2048]{1,0:T(8,128)(2,1)} %get-tuple-element.26.refs_2_, bf16[512,1024]{1,0:T(8,128)(2,1)} %get-tuple-element.27.refs_3_, ...), custom_call_target="tpu_custom_call" | custom-call | flops 4831838208 | bytes 9437184 | tf_op jit(solution)/shard_map/cond/branch_0_fun/row_products/pallas_call | solution.py:445
  479.9 8.6 %row_products.6 = (bf16[768,1536]{1,0:T(8,128)(2,1)}, bf16[768,1536]{1,0:T(8,128)(2,1)}) custom-call(bf16[512,768]{1,0:T(8,128)(2,1)} %get-tuple-element.238.refs_0_, bf16[1024,768]{1,0:T(8,128)(2,1)} %copy-done.97, bf16[512,768]{1,0:T(8,128)(2,1)} %copy-done.78, bf16[512,384]{1,0:T(8,128)(2,1)} %get-tuple-element.151.refs_3_, ...), custom_call_target="tpu_custom_call" | custom-call | flops 3623878656 | bytes 4718592 | tf_op jit(solution)/shard_map/row_products/pallas_call | solution.py:445
  499.6 4.3 add_convert_fusion
  503.9 3.3 maximum_maximum_fusion
  507.3 4.5 fusion.114
  512.0 3.5 multiply_reduce_fusion.3
  517.2 4.0 fusion.119
  522.6 13.0 %attend_back.7 = (bf16[512,384]{1,0:T(8,128)(2,1)}, bf16[1024,768]{1,0:T(8,128)(2,1)}) custom-call(s32[2]{0:T(128)} %pad_add_fusion.start_ref, bf16[512,384]{1,0:T(8,128)(2,1)} %convolution_convert_fusion.10.query_ref, bf16[1024,768]{1,0:T(8,128)(2,1)} %convolution_convert_fusion.2.pair_ref, s32[1,512]{1,0:T(1,128)} %broadcast_select_fusion.2.limit_ref, ...), custom_call_target="tpu_custom_call" | custom-call | flops 3145728 | bytes 12288 | tf_op jit(solution)/shard_map/attend_back/pallas_call | solution.py:381
  538.0 13.0 %attend_back.6 = (bf16[512,384]{1,0:T(8,128)(2,1)}, bf16[1024,768]{1,0:T(8,128)(2,1)}) custom-call(s32[2]{0:T(128)} %pad_add_fusion.start_ref, bf16[512,384]{1,0:T(8,128)(2,1)} %convolution_convert_fusion.11.query_ref, bf16[1024,768]{1,0:T(8,128)(2,1)} %convolution_convert_fusion.3.pair_ref, s32[1,512]{1,0:T(1,128)} %broadcast_select_fusion.2.limit_ref, ...), custom_call_target="tpu_custom_call" | custom-call | flops 3145728 | bytes 12288 | tf_op jit(solution)/shard_map/attend_back/pallas_call | solution.py:381
  551.0 3.4 fusion.144
  557.8 8.9 %row_products.7 = (bf16[768,1536]{1,0:T(8,128)(2,1)}, bf16[768,1536]{1,0:T(8,128)(2,1)}) custom-call(bf16[512,768]{1,0:T(8,128)(2,1)} %copy-done.34, bf16[1024,768]{1,0:T(8,128)(2,1)} %pad_maximum_fusion.4.refs_1_, bf16[512,768]{1,0:T(8,128)(2,1)} %copy-done.81, bf16[512,384]{1,0:T(8,128)(2,1)} %get-tuple-element.163.refs_3_, ...), custom_call_target="tpu_custom_call" | custom-call | flops 3623878656 | bytes 4718592 | tf_op jit(solution)/shard_map/row_products/pallas_call | solution.py:445
  583.7 6.6 collective-permute-done.48
  593.4 8.6 %collective-permute-done.49 = bf16[112,1536]{1,0:T(8,128)(2,1)S(1)} collective-permute-done((bf16[112,1536]{1,0:T(8,128)(2,1)S(1)}, bf16[112,1536]{1,0:T(8,128)(2,1)S(1)}, u32[]{:S(2)}, u32[]{:S(2)}) %collective-permute-start.49) | collective-permute-done | bytes 344096 | tf_op jit(solution)/shard_map/ppermute | solution.py:39
  606.3 18.2 %collective-permute-done.56 = bf16[112,1536]{1,0:T(8,128)(2,1)S(1)} collective-permute-done((bf16[112,1536]{1,0:T(8,128)(2,1)S(1)}, bf16[112,1536]{1,0:T(8,128)(2,1)S(1)}, u32[]{:S(2)}, u32[]{:S(2)}) %collective-permute-start.56) | collective-permute-done | bytes 344096 | tf_op jit(solution)/shard_map/ppermute | solution.py:39
  629.2 8.5 %all-to-all-start.2 = ((bf16[8,33,768]{2,1,0:T(8,128)(2,1)}), bf16[8,33,768]{2,1,0:T(8,128)(2,1)}, u32[]{:S(2)}, u32[]{:S(2)}) async-start(bf16[8,33,768]{2,1,0:T(8,128)(2,1)} %pad_maximum_fusion.8), calls=%async_computation.2 | async-start | bytes 983040 | tf_op jit(solution)/shard_map/all_to_all | solution.py:232
  638.3 15.4 %collective-permute-done.57 = bf16[112,1536]{1,0:T(8,128)(2,1)} collective-permute-done((bf16[112,1536]{1,0:T(8,128)(2,1)}, bf16[112,1536]{1,0:T(8,128)(2,1)}, u32[]{:S(2)}, u32[]{:S(2)}) %collective-permute-start.57) | collective-permute-done | bytes 344096 | tf_op jit(solution)/shard_map/ppermute | solution.py:39
  656.0 4.1 all-to-all-done.2
  662.4 4.1 all-to-all-start.3
  673.4 3.2 all-to-all-done.3
  677.5 4.6 collective-permute-start.51
  697.3 4.7 collective-permute-done.58
  (649 shorter events, 236.6 us)
Async XLA Ops:
  8.4 17.4 %collective-permute-start = (bf16[256,768]{1,0:T(8,128)(2,1)S(1)}, bf16[256,768]{1,0:T(8,128)(2,1)S(1)}, u32[]{:S(2)}, u32[]{:S(2)}) collective-permute-start(bf16[256,768]{1,0:T(8,128)(2,1)S(1)} %slice_bitcast_fusion.3), channel_id=1, source_target_pairs={{16,0},{17,1},{18,2},{19,3},{20,4},{21,5},{22,6},{23,7},{24,8},{25... | collective-permute-start | bytes 1179656 | tf_op jit(solution)/shard_map/ppermute | solution.py:28
  12.7 11.1 %collective-permute-start.3 = (bf16[112,1536]{1,0:T(8,128)(2,1)S(1)}, bf16[112,1536]{1,0:T(8,128)(2,1)S(1)}, u32[]{:S(2)}, u32[]{:S(2)}) collective-permute-start(bf16[112,1536]{1,0:T(8,128)(2,1)S(1)} %concatenate.225.refs_0_), channel_id=1, source_target_pairs={{0,2},{4,0},{8,4},{12,8},{14,12},{10,14},{6,10},{2,6},{1,3},{5,1},... | collective-permute-start | bytes 1032200 | tf_op jit(solution)/shard_map/ppermute | solution.py:39
  15.7 9.8 %collective-permute-start.2 = (bf16[112,1536]{1,0:T(8,128)(2,1)S(1)}, bf16[112,1536]{1,0:T(8,128)(2,1)S(1)}, u32[]{:S(2)}, u32[]{:S(2)}) collective-permute-start(bf16[112,1536]{1,0:T(8,128)(2,1)S(1)} %concatenate.225.refs_0_), channel_id=1, source_target_pairs={{0,4},{4,8},{8,12},{12,14},{14,10},{10,6},{6,2},{2,0},{1,5},{5,9},... | collective-permute-start | bytes 1032200 | tf_op jit(solution)/shard_map/ppermute | solution.py:39
  23.8 14.3 %collective-permute-start.5 = (bf16[112,1536]{1,0:T(8,128)(2,1)S(1)}, bf16[112,1536]{1,0:T(8,128)(2,1)}, u32[]{:S(2)}, u32[]{:S(2)}) collective-permute-start(bf16[112,1536]{1,0:T(8,128)(2,1)S(1)} %collective-permute-done.3.refs_2_), channel_id=1, source_target_pairs={{0,2},{4,0},{8,4},{12,8},{14,12},{10,14},{6,10},{2,6},{1,3},{5,1},... | collective-permute-start | bytes 1032200 | tf_op jit(solution)/shard_map/ppermute | solution.py:39
  25.5 14.7 %collective-permute-start.4 = (bf16[112,1536]{1,0:T(8,128)(2,1)S(1)}, bf16[112,1536]{1,0:T(8,128)(2,1)}, u32[]{:S(2)}, u32[]{:S(2)}) collective-permute-start(bf16[112,1536]{1,0:T(8,128)(2,1)S(1)} %collective-permute-done.2.refs_1_), channel_id=1, source_target_pairs={{0,4},{4,8},{8,12},{12,14},{14,10},{10,6},{6,2},{2,0},{1,5},{5,9},... | collective-permute-start | bytes 1032200 | tf_op jit(solution)/shard_map/ppermute | solution.py:39
  26.6 18.0 %all-to-all-start = ((bf16[8,32,768]{2,1,0:T(8,128)(2,1)}), bf16[8,32,768]{2,1,0:T(8,128)(2,1)S(1)}, u32[]{:S(2)}, u32[]{:S(2)}) async-start(bf16[8,32,768]{2,1,0:T(8,128)(2,1)} %bitcast.2), calls=%async_computation | async-start | bytes 786432 | tf_op jit(solution)/shard_map/all_to_all | solution.py:232
  33.7 26.6 %collective-permute-start.10 = (bf16[48,1536]{1,0:T(8,128)(2,1)}, bf16[48,1536]{1,0:T(8,128)(2,1)S(1)}, u32[]{:S(2)}, u32[]{:S(2)}) collective-permute-start(bf16[48,1536]{1,0:T(8,128)(2,1)} %pad_maximum_fusion.13), channel_id=1, source_target_pairs={{0,16},{1,17},{2,18},{3,19},{4,20},{5,21},{6,22},{7,23},{8,24},{9,... | collective-permute-start | bytes 442376 | tf_op jit(solution)/shard_map/ppermute | solution.py:32
  38.1 12.0 %collective-permute-start.7 = (bf16[112,1536]{1,0:T(8,128)(2,1)}, bf16[112,1536]{1,0:T(8,128)(2,1)S(1)}, u32[]{:S(2)}, u32[]{:S(2)}) collective-permute-start(bf16[112,1536]{1,0:T(8,128)(2,1)} %collective-permute-done.5.refs_4_), channel_id=1, source_target_pairs={{0,2},{4,0},{8,4},{12,8},{14,12},{10,14},{6,10},{2,6},{1,3},{5,1},... | collective-permute-start | bytes 1032200 | tf_op jit(solution)/shard_map/ppermute | solution.py:39
  40.2 12.6 %collective-permute-start.6 = (bf16[112,1536]{1,0:T(8,128)(2,1)}, bf16[112,1536]{1,0:T(8,128)(2,1)S(1)}, u32[]{:S(2)}, u32[]{:S(2)}) collective-permute-start(bf16[112,1536]{1,0:T(8,128)(2,1)} %collective-permute-done.4.refs_3_), channel_id=1, source_target_pairs={{0,4},{4,8},{8,12},{12,14},{14,10},{10,6},{6,2},{2,0},{1,5},{5,9},... | collective-permute-start | bytes 1032200 | tf_op jit(solution)/shard_map/ppermute | solution.py:39
  46.0 21.1 %all-to-all-start.1 = ((bf16[8,32,768]{2,1,0:T(8,128)(2,1)}), bf16[8,32,768]{2,1,0:T(8,128)(2,1)S(1)}, u32[]{:S(2)}, u32[]{:S(2)}) async-start(bf16[8,32,768]{2,1,0:T(8,128)(2,1)} %gather_fusion), calls=%async_computation.1 | async-start | bytes 786432 | tf_op jit(solution)/shard_map/all_to_all | solution.py:233
  49.5 253.6 %all-gather.2.cloned.1.call-start = ((), (), s32[]{:S(2)}) async-start(), calls=%async_computation.6 | async-start | bytes 7077888 | tf_op jit(solution)/shard_map/all_gather | solution.py:632
  50.8 11.8 %collective-permute-start.9 = (bf16[56,1536]{1,0:T(8,128)(2,1)}, bf16[56,1536]{1,0:T(8,128)(2,1)}, u32[]{:S(2)}, u32[]{:S(2)}) collective-permute-start(bf16[56,1536]{1,0:T(8,128)(2,1)} %slice.388), channel_id=1, source_target_pairs={{0,2},{4,0},{8,4},{12,8},{14,12},{10,14},{6,10},{2,6},{1,3},{5,1},... | collective-permute-start | bytes 516104 | tf_op jit(solution)/shard_map/ppermute | solution.py:39
  59.1 29.2 %collective-permute-start.14 = (bf16[1,8,96,768]{3,2,1,0:T(8,128)(2,1)}, bf16[1,8,96,768]{3,2,1,0:T(8,128)(2,1)}, u32[]{:S(2)}, u32[]{:S(2)}) collective-permute-start(bf16[1,8,96,768]{3,2,1,0:T(8,128)(2,1)} %get-tuple-element.114.refs_1_), channel_id=1, source_target_pairs={{0,1},{1,0},{2,3},{3,2},{4,5},{5,4},{6,7},{7,6},{8,9},{9,8},{10,11... | collective-permute-start | bytes 3538952 | tf_op jit(solution)/shard_map/ppermute | solution.py:20
  60.2 6.9 collective-permute-start.8
  62.1 18.4 %collective-permute-start.16 = (bf16[1,8,16,1536]{3,2,1,0:T(8,128)(2,1)S(1)}, bf16[1,8,16,1536]{3,2,1,0:T(8,128)(2,1)S(1)}, u32[]{:S(2)}, u32[]{:S(2)}) collective-permute-start(bf16[1,8,16,1536]{3,2,1,0:T(8,128)(2,1)S(1)} %copy-done.90), channel_id=1, source_target_pairs={{0,1},{1,0},{2,3},{3,2},{4,5},{5,4},{6,7},{7,6},{8,9},{9,8},{10,11... | collective-permute-start | bytes 1179656 | tf_op jit(solution)/shard_map/ppermute | solution.py:20
  62.6 21.9 %collective-permute-start.11 = (bf16[96,4608]{1,0:T(8,128)(2,1)S(1)}, bf16[96,4608]{1,0:T(8,128)(2,1)}, u32[]{:S(2)}, u32[]{:S(2)}) collective-permute-start(bf16[96,4608]{1,0:T(8,128)(2,1)S(1)} %maximum_maximum_fusion.1.refs_0_), channel_id=1, source_target_pairs={{0,2},{4,0},{8,4},{12,8},{14,12},{10,14},{6,10},{2,6},{1,3},{5,1},... | collective-permute-start | bytes 2654216 | tf_op jit(solution)/shard_map/ppermute | solution.py:39
  64.3 22.3 %collective-permute-start.21 = (bf16[96,4608]{1,0:T(8,128)(2,1)S(1)}, bf16[96,4608]{1,0:T(8,128)(2,1)}, u32[]{:S(2)}, u32[]{:S(2)}) collective-permute-start(bf16[96,4608]{1,0:T(8,128)(2,1)S(1)} %maximum_maximum_fusion.1.refs_0_), channel_id=1, source_target_pairs={{0,4},{4,8},{8,12},{12,14},{14,10},{10,6},{6,2},{2,0},{1,5},{5,9},... | collective-permute-start | bytes 2654216 | tf_op jit(solution)/shard_map/ppermute | solution.py:39
  67.1 13.5 %collective-permute-start.1 = (bf16[256,768]{1,0:T(8,128)(2,1)S(1)}, bf16[256,768]{1,0:T(8,128)(2,1)}, u32[]{:S(2)}, u32[]{:S(2)}) collective-permute-start(bf16[256,768]{1,0:T(8,128)(2,1)S(1)} %bitcast.374), channel_id=1, source_target_pairs={{0,16},{1,17},{2,18},{3,19},{4,20},{5,21},{6,22},{7,23},{8,24},{9,... | collective-permute-start | bytes 1179656 | tf_op jit(solution)/shard_map/ppermute | solution.py:32
  80.5 6.2 collective-permute-start.13
  80.6 6.2 collective-permute-start.15
  84.5 21.6 %collective-permute-start.18 = (bf16[96,4608]{1,0:T(8,128)(2,1)}, bf16[96,4608]{1,0:T(8,128)(2,1)}, u32[]{:S(2)}, u32[]{:S(2)}) collective-permute-start(bf16[96,4608]{1,0:T(8,128)(2,1)} %collective-permute-done.11.refs_2_), channel_id=1, source_target_pairs={{0,2},{4,0},{8,4},{12,8},{14,12},{10,14},{6,10},{2,6},{1,3},{5,1},... | collective-permute-start | bytes 2654216 | tf_op jit(solution)/shard_map/ppermute | solution.py:39
  86.6 21.8 %collective-permute-start.22 = (bf16[96,4608]{1,0:T(8,128)(2,1)}, bf16[96,4608]{1,0:T(8,128)(2,1)}, u32[]{:S(2)}, u32[]{:S(2)}) collective-permute-start(bf16[96,4608]{1,0:T(8,128)(2,1)} %collective-permute-done.21.refs_1_), channel_id=1, source_target_pairs={{0,4},{4,8},{8,12},{12,14},{14,10},{10,6},{6,2},{2,0},{1,5},{5,9},... | collective-permute-start | bytes 2654216 | tf_op jit(solution)/shard_map/ppermute | solution.py:39
  86.7 10.3 %collective-permute-start.17 = (bf16[112,1536]{1,0:T(8,128)(2,1)}, bf16[112,1536]{1,0:T(8,128)(2,1)S(1)}, u32[]{:S(2)}, u32[]{:S(2)}) collective-permute-start(bf16[112,1536]{1,0:T(8,128)(2,1)} %constant_dynamic-update-slice_fusion.refs_4_), channel_id=1, source_target_pairs={{0,1},{1,0},{2,3},{3,2},{4,5},{5,4},{6,7},{7,6},{8,9},{9,8},{10,11... | collective-permute-start | bytes 1032200 | tf_op jit(solution)/shard_map/ppermute | solution.py:20
  88.3 25.3 %collective-permute-start.12 = (bf16[512,768]{1,0:T(8,128)(2,1)S(1)}, bf16[512,768]{1,0:T(8,128)(2,1)S(1)}, u32[]{:S(2)}, u32[]{:S(2)}) collective-permute-start(bf16[512,768]{1,0:T(8,128)(2,1)S(1)} %get-tuple-element.208), channel_id=1, source_target_pairs={{0,1},{1,0},{2,3},{3,2},{4,5},{5,4},{6,7},{7,6},{8,9},{9,8},{10,11... | collective-permute-start | bytes 2359304 | tf_op jit(solution)/shard_map/ppermute | solution.py:20
  92.0 21.6 %collective-permute-start.20 = (f32[384]{0:T(512)S(1)}, f32[384]{0:T(512)S(1)}, u32[]{:S(2)}, u32[]{:S(2)}) collective-permute-start(f32[384]{0:T(512)S(1)} %reshape.965), channel_id=1, source_target_pairs={{0,16},{1,17},{2,18},{3,19},{4,20},{5,21},{6,22},{7,23},{8,24},{9,... | collective-permute-start | bytes 4616 | tf_op jit(solution)/shard_map/ppermute | solution.py:32
  106.1 20.8 %collective-permute-start.19 = (bf16[96,4608]{1,0:T(8,128)(2,1)}, bf16[96,4608]{1,0:T(8,128)(2,1)}, u32[]{:S(2)}, u32[]{:S(2)}) collective-permute-start(bf16[96,4608]{1,0:T(8,128)(2,1)} %collective-permute-done.18.refs_4_), channel_id=1, source_target_pairs={{0,2},{4,0},{8,4},{12,8},{14,12},{10,14},{6,10},{2,6},{1,3},{5,1},... | collective-permute-start | bytes 2654216 | tf_op jit(solution)/shard_map/ppermute | solution.py:39
  108.4 20.7 %collective-permute-start.23 = (bf16[96,4608]{1,0:T(8,128)(2,1)}, bf16[96,4608]{1,0:T(8,128)(2,1)}, u32[]{:S(2)}, u32[]{:S(2)}) collective-permute-start(bf16[96,4608]{1,0:T(8,128)(2,1)} %collective-permute-done.22.refs_3_), channel_id=1, source_target_pairs={{0,4},{4,8},{8,12},{12,14},{14,10},{10,6},{6,2},{2,0},{1,5},{5,9},... | collective-permute-start | bytes 2654216 | tf_op jit(solution)/shard_map/ppermute | solution.py:39
  136.8 47.6 %collective-permute-start.26 = (bf16[1,8,96,2048]{3,2,1,0:T(8,128)(2,1)}, bf16[1,8,96,2048]{3,2,1,0:T(8,128)(2,1)}, u32[]{:S(2)}, u32[]{:S(2)}) collective-permute-start(bf16[1,8,96,2048]{3,2,1,0:T(8,128)(2,1)} %get-tuple-element.130.refs_0_), channel_id=1, source_target_pairs={{0,1},{1,0},{2,3},{3,2},{4,5},{5,4},{6,7},{7,6},{8,9},{9,8},{10,11... | collective-permute-start | bytes 9437192 | tf_op jit(solution)/shard_map/ppermute | solution.py:20
  143.5 25.4 %collective-permute-start.24 = (bf16[48,4608]{1,0:T(8,128)(2,1)}, bf16[48,4608]{1,0:T(8,128)(2,1)}, u32[]{:S(2)}, u32[]{:S(2)}) collective-permute-start(bf16[48,4608]{1,0:T(8,128)(2,1)} %slice.392), channel_id=1, source_target_pairs={{0,4},{4,8},{8,12},{12,14},{14,10},{10,6},{6,2},{2,0},{1,5},{5,9},... | collective-permute-start | bytes 1327112 | tf_op jit(solution)/shard_map/ppermute | solution.py:39
  166.5 12.4 %collective-permute-start.25 = (bf16[48,4608]{1,0:T(8,128)(2,1)S(1)}, bf16[48,4608]{1,0:T(8,128)(2,1)S(1)}, u32[]{:S(2)}, u32[]{:S(2)}) collective-permute-start(bf16[48,4608]{1,0:T(8,128)(2,1)S(1)} %slice.393), channel_id=1, source_target_pairs={{0,2},{4,0},{8,4},{12,8},{14,12},{10,14},{6,10},{2,6},{1,3},{5,1},... | collective-permute-start | bytes 1327112 | tf_op jit(solution)/shard_map/ppermute | solution.py:39
  168.3 16.0 %collective-permute-start.27 = (bf16[1,8,96,1024]{3,2,1,0:T(8,128)(2,1)}, bf16[1,8,96,1024]{3,2,1,0:T(8,128)(2,1)}, u32[]{:S(2)}, u32[]{:S(2)}) collective-permute-start(bf16[1,8,96,1024]{3,2,1,0:T(8,128)(2,1)} %get-tuple-element.131.refs_1_), channel_id=1, source_target_pairs={{0,1},{1,0},{2,3},{3,2},{4,5},{5,4},{6,7},{7,6},{8,9},{9,8},{10,11... | collective-permute-start | bytes 4718600 | tf_op jit(solution)/shard_map/ppermute | solution.py:20
  168.3 13.1 %collective-permute-start.28 = (bf16[2,8,48,384]{3,2,1,0:T(8,128)(2,1)S(1)}, bf16[2,8,48,384]{3,2,1,0:T(8,128)(2,1)}, u32[]{:S(2)}, u32[]{:S(2)}) collective-permute-start(bf16[2,8,48,384]{3,2,1,0:T(8,128)(2,1)S(1)} %copy-done.43), channel_id=1, source_target_pairs={{0,1},{1,0},{2,3},{3,2},{4,5},{5,4},{6,7},{7,6},{8,9},{9,8},{10,11... | collective-permute-start | bytes 1769480 | tf_op jit(solution)/shard_map/ppermute | solution.py:20
  168.9 15.4 %collective-permute-start.29 = (bf16[2,8,48,768]{3,2,1,0:T(8,128)(2,1)S(1)}, bf16[2,8,48,768]{3,2,1,0:T(8,128)(2,1)}, u32[]{:S(2)}, u32[]{:S(2)}) collective-permute-start(bf16[2,8,48,768]{3,2,1,0:T(8,128)(2,1)S(1)} %copy-done.14), channel_id=1, source_target_pairs={{0,1},{1,0},{2,3},{3,2},{4,5},{5,4},{6,7},{7,6},{8,9},{9,8},{10,11... | collective-permute-start | bytes 3538952 | tf_op jit(solution)/shard_map/ppermute | solution.py:20
  179.7 7.4 %collective-permute-start.31 = (bf16[96,4608]{1,0:T(8,128)(2,1)}, bf16[96,4608]{1,0:T(8,128)(2,1)}, u32[]{:S(2)}, u32[]{:S(2)}) collective-permute-start(bf16[96,4608]{1,0:T(8,128)(2,1)} %constant_dynamic-update-slice_fusion.2.refs_5_), channel_id=1, source_target_pairs={{0,1},{1,0},{2,3},{3,2},{4,5},{5,4},{6,7},{7,6},{8,9},{9,8},{10,11... | collective-permute-start | bytes 2654216 | tf_op jit(solution)/shard_map/ppermute | solution.py:20
  181.4 2.9 collective-permute-start.30
  183.7 506.8 %reduce-scatter.5.cloned.1.call-start = ((), (), s32[]{:S(2)}) async-start(), calls=%async_computation.8 | async-start | bytes 7077888 | tf_op jit(solution)/shard_map/reduce_scatter | solution.py:685
  204.1 21.4 %collective-permute-start.32 = (bf16[512,768]{1,0:T(8,128)(2,1)S(1)}, bf16[512,768]{1,0:T(8,128)(2,1)S(1)}, u32[]{:S(2)}, u32[]{:S(2)}) collective-permute-start(bf16[512,768]{1,0:T(8,128)(2,1)S(1)} %multiply_convert_fusion.11), channel_id=1, source_target_pairs={{0,16},{1,17},{2,18},{3,19},{4,20},{5,21},{6,22},{7,23},{8,24},{9,... | collective-permute-start | bytes 2359304 | tf_op jit(solution)/shard_map/ppermute | solution.py:32
  225.5 3.8 collective-permute-start.33
  276.0 22.4 %collective-permute-start.34 = (bf16[512,768]{1,0:T(8,128)(2,1)}, bf16[512,768]{1,0:T(8,128)(2,1)}, u32[]{:S(2)}, u32[]{:S(2)}) collective-permute-start(bf16[512,768]{1,0:T(8,128)(2,1)} %multiply_convert_fusion.9), channel_id=1, source_target_pairs={{16,0},{17,1},{18,2},{19,3},{20,4},{21,5},{22,6},{23,7},{24,8},{25... | collective-permute-start | bytes 2359304 | tf_op jit(solution)/shard_map/ppermute | solution.py:28
  300.7 2.4 collective-permute-start.35
  322.5 3.8 collective-permute-start.37
  343.4 2.4 collective-permute-start.38
  347.4 19.3 %collective-permute-start.39 = (bf16[512,768]{1,0:T(8,128)(2,1)}, bf16[512,768]{1,0:T(8,128)(2,1)}, u32[]{:S(2)}, u32[]{:S(2)}) collective-permute-start(bf16[512,768]{1,0:T(8,128)(2,1)} %get-tuple-element.197), channel_id=1, source_target_pairs={{0,16},{1,17},{2,18},{3,19},{4,20},{5,21},{6,22},{7,23},{8,24},{9,... | collective-permute-start | bytes 2359304 | tf_op jit(solution)/shard_map/ppermute | solution.py:32
  361.4 331.5 %reduce-scatter.3.cloned.1.call-start = ((), (), s32[]{:S(2)}) async-start(), calls=%async_computation.7 | async-start | bytes 7962624 | tf_op jit(solution)/shard_map/reduce_scatter | solution.py:732
  425.8 2.4 collective-permute-start.40
  429.3 21.9 %collective-permute-start.41 = (bf16[512,768]{1,0:T(8,128)(2,1)}, bf16[512,768]{1,0:T(8,128)(2,1)}, u32[]{:S(2)}, u32[]{:S(2)}) collective-permute-start(bf16[512,768]{1,0:T(8,128)(2,1)} %slice_add_fusion.1), channel_id=1, source_target_pairs={{16,0},{17,1},{18,2},{19,3},{20,4},{21,5},{22,6},{23,7},{24,8},{25... | collective-permute-start | bytes 2359304 | tf_op jit(solution)/shard_map/ppermute | solution.py:28
  479.8 19.6 %collective-permute-start.42 = (bf16[768,3072]{1,0:T(8,128)(2,1)}, bf16[768,3072]{1,0:T(8,128)(2,1)}, u32[]{:S(2)}, u32[]{:S(2)}) collective-permute-start(bf16[768,3072]{1,0:T(8,128)(2,1)} %get-tuple-element.158), channel_id=1, source_target_pairs={{0,1},{1,0},{2,3},{3,2},{4,5},{5,4},{6,7},{7,6},{8,9},{9,8},{10,11... | collective-permute-start | bytes 14155784 | tf_op jit(solution)/shard_map/ppermute | solution.py:20
  488.4 8.2 %collective-permute-start.43 = (bf16[768,1536]{1,0:T(8,128)(2,1)}, bf16[768,1536]{1,0:T(8,128)(2,1)}, u32[]{:S(2)}, u32[]{:S(2)}) collective-permute-start(bf16[768,1536]{1,0:T(8,128)(2,1)} %get-tuple-element.161), channel_id=1, source_target_pairs={{0,1},{1,0},{2,3},{3,2},{4,5},{5,4},{6,7},{7,6},{8,9},{9,8},{10,11... | collective-permute-start | bytes 7077896 | tf_op jit(solution)/shard_map/ppermute | solution.py:20
  515.5 51.7 %collective-permute-start.45 = (bf16[384]{0:T(512)(128)(2,1)S(1)}, bf16[384]{0:T(512)(128)(2,1)S(1)}, u32[]{:S(2)}, u32[]{:S(2)}) collective-permute-start(bf16[384]{0:T(512)(128)(2,1)S(1)} %slice.347), channel_id=1, source_target_pairs={{16,0},{17,1},{18,2},{19,3},{20,4},{21,5},{22,6},{23,7},{24,8},{25... | collective-permute-start | bytes 2312 | tf_op jit(solution)/shard_map/ppermute | solution.py:28
  557.6 12.8 %collective-permute-start.44 = (bf16[512,768]{1,0:T(8,128)(2,1)S(1)}, bf16[512,768]{1,0:T(8,128)(2,1)}, u32[]{:S(2)}, u32[]{:S(2)}) collective-permute-start(bf16[512,768]{1,0:T(8,128)(2,1)S(1)} %slice.561), channel_id=1, source_target_pairs={{0,1},{1,0},{2,3},{3,2},{4,5},{5,4},{6,7},{7,6},{8,9},{9,8},{10,11... | collective-permute-start | bytes 2359304 | tf_op jit(solution)/shard_map/ppermute | solution.py:20
  566.7 11.8 %collective-permute-start.46 = (bf16[768,1536]{1,0:T(8,128)(2,1)}, bf16[768,1536]{1,0:T(8,128)(2,1)}, u32[]{:S(2)}, u32[]{:S(2)}) collective-permute-start(bf16[768,1536]{1,0:T(8,128)(2,1)} %get-tuple-element.169), channel_id=1, source_target_pairs={{0,1},{1,0},{2,3},{3,2},{4,5},{5,4},{6,7},{7,6},{8,9},{9,8},{10,11... | collective-permute-start | bytes 7077896 | tf_op jit(solution)/shard_map/ppermute | solution.py:20
  581.2 9.0 %collective-permute-start.48 = (bf16[56,1536]{1,0:T(8,128)(2,1)S(1)}, bf16[56,1536]{1,0:T(8,128)(2,1)S(1)}, u32[]{:S(2)}, u32[]{:S(2)}) collective-permute-start(bf16[56,1536]{1,0:T(8,128)(2,1)S(1)} %get-tuple-element.264), channel_id=1, source_target_pairs={{0,2},{4,0},{8,4},{12,8},{14,12},{10,14},{6,10},{2,6},{1,3},{5,1},... | collective-permute-start | bytes 516104 | tf_op jit(solution)/shard_map/ppermute | solution.py:39
  582.7 10.6 %collective-permute-start.52 = (bf16[56,1536]{1,0:T(8,128)(2,1)S(1)}, bf16[56,1536]{1,0:T(8,128)(2,1)S(1)}, u32[]{:S(2)}, u32[]{:S(2)}) collective-permute-start(bf16[56,1536]{1,0:T(8,128)(2,1)S(1)} %get-tuple-element.263), channel_id=1, source_target_pairs={{0,4},{4,8},{8,12},{12,14},{14,10},{10,6},{6,2},{2,0},{1,5},{5,9},... | collective-permute-start | bytes 516104 | tf_op jit(solution)/shard_map/ppermute | solution.py:39
  590.3 11.7 %collective-permute-start.49 = (bf16[112,1536]{1,0:T(8,128)(2,1)S(1)}, bf16[112,1536]{1,0:T(8,128)(2,1)S(1)}, u32[]{:S(2)}, u32[]{:S(2)}) collective-permute-start(bf16[112,1536]{1,0:T(8,128)(2,1)S(1)} %pad_maximum_fusion.9), channel_id=1, source_target_pairs={{0,2},{4,0},{8,4},{12,8},{14,12},{10,14},{6,10},{2,6},{1,3},{5,1},... | collective-permute-start | bytes 1032200 | tf_op jit(solution)/shard_map/ppermute | solution.py:39
  593.4 12.7 %collective-permute-start.53 = (bf16[112,1536]{1,0:T(8,128)(2,1)S(1)}, bf16[112,1536]{1,0:T(8,128)(2,1)S(1)}, u32[]{:S(2)}, u32[]{:S(2)}) collective-permute-start(bf16[112,1536]{1,0:T(8,128)(2,1)S(1)} %pad_maximum_fusion.10), channel_id=1, source_target_pairs={{0,4},{4,8},{8,12},{12,14},{14,10},{10,6},{6,2},{2,0},{1,5},{5,9},... | collective-permute-start | bytes 1032200 | tf_op jit(solution)/shard_map/ppermute | solution.py:39
  602.0 26.3 %collective-permute-start.50 = (bf16[256,768]{1,0:T(8,128)(2,1)S(1)}, bf16[256,768]{1,0:T(8,128)(2,1)S(1)}, u32[]{:S(2)}, u32[]{:S(2)}) collective-permute-start(bf16[256,768]{1,0:T(8,128)(2,1)S(1)} %slice.352), channel_id=1, source_target_pairs={{16,0},{17,1},{18,2},{19,3},{20,4},{21,5},{22,6},{23,7},{24,8},{25... | collective-permute-start | bytes 1179656 | tf_op jit(solution)/shard_map/ppermute | solution.py:28
  603.5 21.0 %collective-permute-start.56 = (bf16[112,1536]{1,0:T(8,128)(2,1)S(1)}, bf16[112,1536]{1,0:T(8,128)(2,1)S(1)}, u32[]{:S(2)}, u32[]{:S(2)}) collective-permute-start(bf16[112,1536]{1,0:T(8,128)(2,1)S(1)} %add_convert_fusion.3), channel_id=1, source_target_pairs={{0,2},{4,0},{8,4},{12,8},{14,12},{10,14},{6,10},{2,6},{1,3},{5,1},... | collective-permute-start | bytes 1032200 | tf_op jit(solution)/shard_map/ppermute | solution.py:39
  606.2 19.2 %collective-permute-start.54 = (bf16[112,1536]{1,0:T(8,128)(2,1)S(1)}, bf16[112,1536]{1,0:T(8,128)(2,1)S(1)}, u32[]{:S(2)}, u32[]{:S(2)}) collective-permute-start(bf16[112,1536]{1,0:T(8,128)(2,1)S(1)} %add_convert_fusion.5), channel_id=1, source_target_pairs={{0,4},{4,8},{8,12},{12,14},{14,10},{10,6},{6,2},{2,0},{1,5},{5,9},... | collective-permute-start | bytes 1032200 | tf_op jit(solution)/shard_map/ppermute | solution.py:39
  625.4 28.4 %collective-permute-start.57 = (bf16[112,1536]{1,0:T(8,128)(2,1)}, bf16[112,1536]{1,0:T(8,128)(2,1)}, u32[]{:S(2)}, u32[]{:S(2)}) collective-permute-start(bf16[112,1536]{1,0:T(8,128)(2,1)} %add_convert_fusion.2), channel_id=1, source_target_pairs={{0,2},{4,0},{8,4},{12,8},{14,12},{10,14},{6,10},{2,6},{1,3},{5,1},... | collective-permute-start | bytes 1032200 | tf_op jit(solution)/shard_map/ppermute | solution.py:39
  626.3 27.5 %collective-permute-start.55 = (bf16[112,1536]{1,0:T(8,128)(2,1)}, bf16[112,1536]{1,0:T(8,128)(2,1)}, u32[]{:S(2)}, u32[]{:S(2)}) collective-permute-start(bf16[112,1536]{1,0:T(8,128)(2,1)} %add_convert_fusion.4), channel_id=1, source_target_pairs={{0,4},{4,8},{8,12},{12,14},{14,10},{10,6},{6,2},{2,0},{1,5},{5,9},... | collective-permute-start | bytes 1032200 | tf_op jit(solution)/shard_map/ppermute | solution.py:39
  629.2 30.9 %all-to-all-start.2 = ((bf16[8,33,768]{2,1,0:T(8,128)(2,1)}), bf16[8,33,768]{2,1,0:T(8,128)(2,1)}, u32[]{:S(2)}, u32[]{:S(2)}) async-start(bf16[8,33,768]{2,1,0:T(8,128)(2,1)} %pad_maximum_fusion.8), calls=%async_computation.2 | async-start | bytes 983040 | tf_op jit(solution)/shard_map/all_to_all | solution.py:232
  662.4 14.1 %all-to-all-start.3 = ((bf16[8,33,768]{2,1,0:T(8,128)(2,1)}), bf16[8,33,768]{2,1,0:T(8,128)(2,1)}, u32[]{:S(2)}, u32[]{:S(2)}) async-start(bf16[8,33,768]{2,1,0:T(8,128)(2,1)} %gather_fusion.1), calls=%async_computation.3 | async-start | bytes 983040 | tf_op jit(solution)/shard_map/all_to_all | solution.py:233
  677.5 9.9 %collective-permute-start.51 = (bf16[256,768]{1,0:T(8,128)(2,1)S(1)}, bf16[256,768]{1,0:T(8,128)(2,1)S(1)}, u32[]{:S(2)}, u32[]{:S(2)}) collective-permute-start(bf16[256,768]{1,0:T(8,128)(2,1)S(1)} %bitcast.371), channel_id=1, source_target_pairs={{0,16},{1,17},{2,18},{3,19},{4,20},{5,21},{6,22},{7,23},{8,24},{9,... | collective-permute-start | bytes 1179656 | tf_op jit(solution)/shard_map/ppermute | solution.py:32
  694.9 7.0 collective-permute-start.58
  (162 other events, 1479.0 us)
Sparse Core Ops, SparseCore 0:
  183.8 100.0 all-gather.1
  361.5 117.2 reduce-scatter.4
  507.4 150.8 reduce-scatter.2
